TPU v7x, 32 devices: a whole 2x2x4 slice. The times are simulated.
32 devices in a mesh: seq: 16 (over z, y, x), head: 2 (over core).
Axes of the slice: x: 2, y: 2, z: 4, core: 2. Of those that a mesh axis runs over, the one named last changes fastest.
Arguments:
- queries: bfloat16 [8192, 2048], P(('seq', 'head')), may hold values from -6 to 6
- key_rows: bfloat16 [8192, 2048], P(('seq', 'head')), may hold values from -6 to 6
- values: bfloat16 [8192, 2048], P(('seq', 'head')), may hold values from -6 to 6
- out_grad: bfloat16 [8192, 2048], P(('seq', 'head')), may hold values from -6 to 6
- level_weights: float32 [16, 11], replicated, may hold values from 0.2 to 1
Outputs:
- query_grad: bfloat16 [8192, 2048], P(('seq', 'head'))
- key_grad: bfloat16 [8192, 2048], P(('seq', 'head'))
- value_grad: bfloat16 [8192, 2048], P(('seq', 'head'))
All inputs are finite; a program needn't handle non-finite values.
Results may differ from a plain program's by a relative error of at most 0.003.
Values may be sent and summed in bfloat16 or wider, within the bound.
No kernel may reach another device: no remote copies, remote signals or barrier semaphores. Data moves between devices by JAX's collectives and lax.ppermute only.
A program may use at most 128 MiB of HBM per device.

v0:
```python
import jax
import jax.numpy as jnp
from jax import lax
from jax.sharding import PartitionSpec as P

DH = 128
BLOCK = 128


def partner(array, axis, distance):
    return lax.ppermute(array, axis, [(i, i ^ 1 << distance) for i in range(lax.axis_size(axis))])


def fenwick_local(kv_blocks, qo_blocks, level_scale):
    block_count = kv_blocks.shape[0]
    inner_shape = kv_blocks.shape[1:]
    earlier = jnp.zeros_like(kv_blocks)
    later = jnp.zeros_like(qo_blocks)
    for level_index in range(1, block_count.bit_length()):
        half_span = 1 << level_index - 1
        group_count = block_count >> level_index
        weight = level_scale[:, level_index][:, None, None]
        kv_groups = kv_blocks.reshape((group_count, 2, half_span) + inner_shape)
        qo_groups = qo_blocks.reshape((group_count, 2, half_span) + inner_shape)
        lower_sum = jnp.sum(kv_groups[:, 0], axis=1) * weight
        upper_sum = jnp.sum(qo_groups[:, 1], axis=1) * weight
        zero_block = jnp.zeros_like(lower_sum)
        add_earlier = jnp.stack([zero_block, lower_sum], axis=1)[:, :, None]
        add_later = jnp.stack([upper_sum, zero_block], axis=1)[:, :, None]
        full_shape = (group_count, 2, half_span) + inner_shape
        earlier = earlier + jnp.broadcast_to(add_earlier, full_shape).reshape(kv_blocks.shape)
        later = later + jnp.broadcast_to(add_later, full_shape).reshape(qo_blocks.shape)
    return (earlier, later)


def cross_states(kv_total, qo_total, level_scale, local_levels, swapper, position, chain_len):
    earlier = jnp.zeros_like(kv_total)
    later = jnp.zeros_like(qo_total)
    group_kv = kv_total
    group_qo = qo_total
    for bit_index in range(chain_len.bit_length() - 1):
        other_kv, other_qo = swapper((group_kv, group_qo), bit_index)
        upper_half = (position // (1 << bit_index) % 2).astype(jnp.float32)
        weight = level_scale[:, local_levels + 1 + bit_index][:, None, None]
        earlier = earlier + upper_half * weight * other_kv
        later = later + (1.0 - upper_half) * weight * other_qo
        group_kv = group_kv + other_kv
        group_qo = group_qo + other_qo
    return (earlier, later)


def range_grads(
    query_rows, key_part, value_rows, grad_rows, level_scale, swapper, position, chain_len
):
    high = lax.Precision.HIGHEST
    token_count = query_rows.shape[0]
    head_count = query_rows.shape[1] // DH
    block_count = token_count // BLOCK
    shape_four = (block_count, BLOCK, head_count, DH)
    query_blk = query_rows.reshape(shape_four)
    key_blk = key_part.reshape(shape_four)
    value_blk = value_rows.reshape(shape_four)
    grad_blk = grad_rows.reshape(shape_four)
    rows = lax.broadcasted_iota(jnp.int32, (BLOCK, BLOCK), 0)
    cols = lax.broadcasted_iota(jnp.int32, (BLOCK, BLOCK), 1)
    causal_mask = (rows >= cols).astype(jnp.float32)
    first_weight = level_scale[:, 0][None, :, None, None]
    kv_blocks = jnp.einsum(
        "nshd,nshe->nhde", key_blk, value_blk, preferred_element_type=jnp.float32
    )
    qo_blocks = jnp.einsum(
        "nthd,nthe->nhde", query_blk, grad_blk, preferred_element_type=jnp.float32
    )
    local_levels = block_count.bit_length() - 1
    earlier_dev, later_dev = cross_states(
        jnp.sum(kv_blocks, axis=0),
        jnp.sum(qo_blocks, axis=0),
        level_scale,
        local_levels,
        swapper,
        position,
        chain_len,
    )
    scores = jnp.einsum("nthd,nshd->nhts", query_blk, key_blk, preferred_element_type=jnp.float32)
    weighted = (scores * causal_mask * first_weight).astype(jnp.bfloat16)
    grad_prob = jnp.einsum(
        "nthe,nshe->nhts", grad_blk, value_blk, preferred_element_type=jnp.float32
    )
    grad_score = (grad_prob * causal_mask * first_weight).astype(jnp.bfloat16)
    value_local = jnp.einsum(
        "nhts,nthe->nshe", weighted, grad_blk, preferred_element_type=jnp.float32
    )
    query_local = jnp.einsum(
        "nhts,nshd->nthd", grad_score, key_blk, preferred_element_type=jnp.float32
    )
    key_local = jnp.einsum(
        "nhts,nthd->nshd", grad_score, query_blk, preferred_element_type=jnp.float32
    )
    earlier_local, later_local = fenwick_local(kv_blocks, qo_blocks, level_scale)
    earlier = earlier_local + earlier_dev[None]
    later = later_local + later_dev[None]
    query_cross = jnp.einsum(
        "nthe,nhde->nthd", grad_blk, earlier, precision=high, preferred_element_type=jnp.float32
    )
    key_cross = jnp.einsum(
        "nshe,nhde->nshd", value_blk, later, precision=high, preferred_element_type=jnp.float32
    )
    value_cross = jnp.einsum(
        "nshd,nhde->nshe", key_blk, later, precision=high, preferred_element_type=jnp.float32
    )
    flat_shape = (token_count, head_count * DH)
    return (
        (query_local + query_cross).astype(jnp.bfloat16).reshape(flat_shape),
        (key_local + key_cross).astype(jnp.bfloat16).reshape(flat_shape),
        (value_local + value_cross).astype(jnp.bfloat16).reshape(flat_shape),
    )


def body(queries, key_rows, values, out_grad, level_weights):
    level_ids = jnp.arange(level_weights.shape[1], dtype=jnp.float32)
    level_scale = (
        level_weights
        * jnp.exp2((1.0 - level_ids) / 2.0)[None, :]
        / jnp.sqrt(jnp.float32(DH * BLOCK))
    )
    query_rows, key_part, value_rows, grad_rows = (
        lax.all_to_all(queries, "head", split_axis=1, concat_axis=0, tiled=True),
        lax.all_to_all(key_rows, "head", split_axis=1, concat_axis=0, tiled=True),
        lax.all_to_all(values, "head", split_axis=1, concat_axis=0, tiled=True),
        lax.all_to_all(out_grad, "head", split_axis=1, concat_axis=0, tiled=True),
    )
    head_count = level_scale.shape[0] // lax.axis_size("head")
    head_scale = lax.dynamic_slice_in_dim(
        level_scale, lax.axis_index("head") * head_count, head_count, 0
    )

    def swap_heads(states, bit_index):
        return partner(states, "seq", bit_index)

    query_part, key_grad_part, value_part = range_grads(
        query_rows,
        key_part,
        value_rows,
        grad_rows,
        head_scale,
        swap_heads,
        lax.axis_index("seq"),
        lax.axis_size("seq"),
    )
    return (
        lax.all_to_all(query_part, "head", split_axis=0, concat_axis=1, tiled=True),
        lax.all_to_all(key_grad_part, "head", split_axis=0, concat_axis=1, tiled=True),
        lax.all_to_all(value_part, "head", split_axis=0, concat_axis=1, tiled=True),
    )


def solution(mesh):
    return jax.shard_map(
        body,
        mesh=mesh,
        in_specs=(
            P(("seq", "head"), None),
            P(("seq", "head"), None),
            P(("seq", "head"), None),
            P(("seq", "head"), None),
            P(),
        ),
        out_specs=(P(("seq", "head"), None), P(("seq", "head"), None), P(("seq", "head"), None)),
        check_vma=False,
    )
```

profile of v0, /device:TPU:31, one launch (start us, length us, event | category | flops | bytes accessed | tf_op | source)
XLA Modules:
  0.0 158.2 jit_solution(16164366697861797345)
XLA Ops:
  0.6 2.4 %copy.180 = bf16[32,2,8,1024]{3,2,0,1:T(8,128)(2,1)} copy(bf16[32,2,8,1024]{3,2,1,0:T(8,128)(2,1)} %bitcast.126) | data formatting | bytes 2097152 | tf_op jit(solution)/shard_map/all_to_all | solution.py:130
  3.0 4.2 %all-to-all-start = ((bf16[256,2,1024]{2,0,1:T(8,128)(2,1)}), bf16[256,2,1024]{2,0,1:T(8,128)(2,1)S(1)}, u32[]{:S(2)}, u32[]{:S(2)}) async-start(bf16[256,2,1024]{2,0,1:T(8,128)(2,1)} %bitcast.96), calls=%async_computation | async-start | bytes 2097152 | tf_op jit(solution)/shard_map/all_to_all | solution.py:130
  7.3 1.1 copy.177
  8.3 0.7 all-to-all-done
  9.0 3.9 %all-to-all-start.4 = ((bf16[256,2,1024]{2,0,1:T(8,128)(2,1)}), bf16[256,2,1024]{2,0,1:T(8,128)(2,1)S(1)}, u32[]{:S(2)}, u32[]{:S(2)}) async-start(bf16[256,2,1024]{2,0,1:T(8,128)(2,1)} %bitcast.93), calls=%async_computation.4 | async-start | bytes 2097152 | tf_op jit(solution)/shard_map/all_to_all | solution.py:127
  13.2 1.5 all-to-all-done.4
  15.0 2.7 %fusion.31 = (f32[8,128,128]{2,1,0:T(8,128)}, f32[4,8,128,128]{3,2,1,0:T(8,128)}) fusion(bf16[4,128,8,128]{3,2,1,0:T(8,128)(2,1)S(1)} %bitcast.101, bf16[4,128,8,128]{3,2,1,0:T(8,128)(2,1)S(1)} %bitcast.105), kind=kOutput, calls=%fused_computation.66 | convolution fusion | flops 134610944 | bytes 4718592 | tf_op jit(solution)/shard_map/nthd,nthe->nhde/dot_general | solution.py:71
  17.9 1.1 copy.178
  19.0 4.2 %all-to-all-start.2 = ((bf16[256,2,1024]{2,0,1:T(8,128)(2,1)}), bf16[256,2,1024]{2,0,1:T(8,128)(2,1)S(1)}, u32[]{:S(2)}, u32[]{:S(2)}) async-start(bf16[256,2,1024]{2,0,1:T(8,128)(2,1)} %bitcast.119), calls=%async_computation.2 | async-start | bytes 2097152 | tf_op jit(solution)/shard_map/all_to_all | solution.py:128
  23.2 2.3 %copy.179 = bf16[32,2,8,1024]{3,2,0,1:T(8,128)(2,1)} copy(bf16[32,2,8,1024]{3,2,1,0:T(8,128)(2,1)} %bitcast.129) | data formatting | bytes 2097152 | tf_op jit(solution)/shard_map/all_to_all | solution.py:129
  25.5 4.4 %all-to-all-start.1 = ((bf16[256,2,1024]{2,0,1:T(8,128)(2,1)}), bf16[256,2,1024]{2,0,1:T(8,128)(2,1)}, u32[]{:S(2)}, u32[]{:S(2)}) async-start(bf16[256,2,1024]{2,0,1:T(8,128)(2,1)} %bitcast.118), calls=%async_computation.1 | async-start | bytes 2097152 | tf_op jit(solution)/shard_map/all_to_all | solution.py:129
  29.9 1.5 copy.133
  31.4 0.4 all-to-all-done.1
  31.8 1.5 copy.132
  33.3 2.7 %fusion.30 = (f32[8,128,128]{2,1,0:T(8,128)}, f32[4,8,128,128]{3,2,1,0:T(8,128)}) fusion(bf16[4,128,8,128]{3,2,1,0:T(8,128)(2,1)S(1)} %bitcast.108, bf16[4,128,8,128]{3,2,1,0:T(8,128)(2,1)S(1)} %bitcast.97), kind=kOutput, calls=%fused_computation.65 | convolution fusion | flops 134610944 | bytes 4718592 | tf_op jit(solution)/shard_map/nshd,nshe->nhde/dot_general | solution.py:68
  36.0 1.2 collective-permute-start
  37.2 2.1 %slice_reduce_fusion = f32[8,128,128]{2,1,0:T(8,128)} fusion(f32[1,2,2,8,128,128]{5,4,3,2,1,0:T(8,128)} %bitcast.111), kind=kLoop, calls=%fused_computation.17 | loop fusion | flops 131072 | bytes 1572864 | tf_op jit(solution)/shard_map/reduce_sum | solution.py:26
  39.3 2.1 %slice_reduce_fusion.1 = f32[8,128,128]{2,1,0:T(8,128)} fusion(f32[1,2,2,8,128,128]{5,4,3,2,1,0:T(8,128)} %bitcast.113), kind=kLoop, calls=%fused_computation.20 | loop fusion | flops 131072 | bytes 1572864 | tf_op jit(solution)/shard_map/reduce_sum | solution.py:25
  41.8 1.5 bitcast_multiply_fusion
  43.4 1.1 pad_bitcast_fusion
  44.5 0.9 copy-done.7
  45.4 1.2 fusion.4
  46.6 2.1 %add.119 = f32[8,128,128]{2,1,0:T(8,128)} add(f32[8,128,128]{2,1,0:T(8,128)} %get-tuple-element.26, f32[8,128,128]{2,1,0:T(8,128)} %collective-permute-done.4) | non-fusion elementwise | flops 131072 | bytes 1572864 | tf_op jit(solution)/shard_map/add | solution.py:48
  48.9 1.5 pad_add_fusion
  50.4 2.9 %copy.102 = f32[2,2,8,128,128]{3,4,2,1,0:T(8,128)} copy(f32[2,2,8,128,128]{4,3,2,0,1:T(8,128)} %pad_add_fusion) | data formatting | bytes 4194304 | tf_op jit(solution)/shard_map/add | solution.py:32
  53.4 1.7 %pad_add_fusion.1 = f32[2,2,8,128,128]{4,3,2,0,1:T(8,128)S(1)} fusion(f32[2,1,8,128,128]{4,3,2,0,1:T(8,128)} %get-tuple-element.23, f32[2,8,128,128]{3,2,1,0:T(8,128)} %get-tuple-element.29), kind=kLoop, calls=%fused_computation.10 | loop fusion | flops 524288 | bytes 4194304 | tf_op jit(solution)/shard_map/add | solution.py:31
  55.1 1.5 copy.91
  56.6 1.3 add.106
  57.9 1.3 collective-permute-start.1
  59.3 2.6 %collective-permute-done.5 = f32[8,128,128]{2,1,0:T(8,128)} collective-permute-done((f32[8,128,128]{2,1,0:T(8,128)}, f32[8,128,128]{2,1,0:T(8,128)}, u32[]{:S(2)}, u32[]{:S(2)}) %collective-permute-start.5) | collective-permute-done | bytes 524320 | tf_op jit(solution)/shard_map/ppermute | solution.py:11
  61.9 1.3 add.121
  63.4 0.8 multiply_convert_fusion.1
  64.2 1.9 %fusion.12 = f32[4,8,128,128]{3,2,1,0:T(8,128)} fusion(bf16[4,8,128,128]{3,2,1,0:T(8,128)(2,1)S(1)} %multiply_convert_fusion.1, bf16[4,128,8,128]{3,2,1,0:T(8,128)(2,1)S(1)} %bitcast.106), kind=kOutput, calls=%fused_computation.30 | convolution fusion | flops 134217728 | bytes 4194304 | tf_op jit(solution)/shard_map/nhts,nthd->nshd/dot_general | solution.py:96
  66.1 6.9 %collective-permute-done.1 = f32[8,128,128]{2,1,0:T(8,128)S(1)} collective-permute-done((f32[8,128,128]{2,1,0:T(8,128)S(1)}, f32[8,128,128]{2,1,0:T(8,128)S(1)}, u32[]{:S(2)}, u32[]{:S(2)}) %collective-permute-start.1) | collective-permute-done | bytes 524320 | tf_op jit(solution)/shard_map/ppermute | solution.py:11
  73.0 0.9 add.109
  74.1 0.9 add.123
  75.1 1.7 %fusion.22 = f32[4,8,128,128]{3,2,1,0:T(8,128)} fusion(bf16[4,8,128,128]{3,2,1,0:T(8,128)(2,1)S(1)} %multiply_convert_fusion.1, bf16[4,128,8,128]{3,2,1,0:T(8,128)(2,1)S(1)} %bitcast.98), kind=kOutput, calls=%fused_computation.39 | convolution fusion | flops 134217728 | bytes 4194304 | tf_op jit(solution)/shard_map/nhts,nshd->nthd/dot_general | solution.py:93
  76.8 2.6 %fusion.3 = f32[4,8,128,128]{3,2,1,0:T(8,128)} fusion(f32[8]{0:T(128)S(1)} %get-tuple-element.18, f32[128,128]{1,0:T(8,128)S(1)} %fusion.28, bf16[4,128,8,128]{3,2,1,0:T(8,128)(2,1)S(1)} %bitcast.107, bf16[4,128,8,128]{3,2,1,0:T(8,128)(2,1)S(1)} %bitcast.99, bf16[4,128,8,128]{3,2,1,0:T(8,128)(2,1)S(1)} %bitcast.103), kind=kOutput, calls=%fused_computation.12 | convolution fusion | flops 270008320 | bytes 5308448 | tf_op jit(solution)/shard_map/nhts,nthe->nshe/dot_general | solution.py:90
  79.4 16.8 %collective-permute-done.2 = f32[8,128,128]{2,1,0:T(8,128)} collective-permute-done((f32[8,128,128]{2,1,0:T(8,128)}, f32[8,128,128]{2,1,0:T(8,128)}, u32[]{:S(2)}, u32[]{:S(2)}) %collective-permute-start.2) | collective-permute-done | bytes 524320 | tf_op jit(solution)/shard_map/ppermute | solution.py:11
  96.2 2.1 %add.112 = f32[8,128,128]{2,1,0:T(8,128)} add(f32[8,128,128]{2,1,0:T(8,128)} %add.109, f32[8,128,128]{2,1,0:T(8,128)} %collective-permute-done.2) | non-fusion elementwise | flops 131072 | bytes 1572864 | tf_op jit(solution)/shard_map/add | solution.py:47
  98.2 1.7 %multiply_add_fusion = f32[8,128,128]{2,1,0:T(8,128)S(1)} fusion(f32[8,128,128]{2,1,0:T(8,128)} %collective-permute-done.7, f32[8,128,128]{2,1,0:T(8,128)} %copy-done.13, f32[8,128,128]{2,1,0:T(8,128)} %collective-permute-done.5, f32[8,128,128]{2,1,0:T(8,128)} %collective-permute-done.4, f32[8]{0:T(128)S(1)} %get-tuple-element.12, ...), kind=kLoop, calls=%fused_computation.47 | loop fusion | flops 917504 | bytes 2621568 | tf_op jit(solution)/shard_map/add | solution.py:46
  100.0 1.0 copy.103
  101.0 2.1 %bitcast_add_fusion.2 = f32[4,8,128,128]{2,3,1,0:T(8,128)S(1)} fusion(f32[2,2,8,128,128]{3,4,2,1,0:T(8,128)} %copy.102, f32[8,128,128]{1,2,0:T(8,128)} %copy.103), kind=kLoop, calls=%fused_computation.4 | loop fusion | flops 524288 | bytes 4718592 | tf_op jit(solution)/shard_map/add | solution.py:101
  103.4 2.3 %fusion = bf16[4,128,8,128]{3,1,2,0:T(8,128)(2,1)S(1)} fusion(f32[4,8,128,128]{3,2,1,0:T(8,128)S(1)} %copy-done.6, f32[4,8,128,128]{2,3,1,0:T(8,128)S(1)} %bitcast_add_fusion.2, bf16[4,128,8,128]{3,2,1,0:T(8,128)(2,1)S(1)} %bitcast.100), kind=kOutput, calls=%fused_computation.1 | convolution fusion | flops 806354944 | bytes 6291456 | tf_op jit(solution)/shard_map/nshd,nhde->nshe/dot_general | solution.py:108
  105.7 0.7 copy.115
  106.4 1.3 all_to_all.110
  107.7 21.3 %all_to_all.121 = bf16[2,256,1024]{2,1,0:T(8,128)(2,1)} all-to-all(bf16[2,256,1024]{2,1,0:T(8,128)(2,1)} %all_to_all.110), channel_id=1, replica_groups=mesh['seq'=16,'head'=2] {'head'}, dimensions={0} | all-to-all | bytes 2097152 | tf_op jit(solution)/shard_map/all_to_all | solution.py:153
  129.0 2.3 %copy.116 = bf16[256,2,1024]{0,2,1:T(8,128)(2,1)} copy(bf16[256,2,1024]{2,0,1:T(8,128)(2,1)} %bitcast.120) | data formatting | bytes 2097152 | tf_op jit(solution)/shard_map/all_to_all | solution.py:153
  131.3 2.3 %copy.119 = bf16[256,2048]{1,0:T(8,128)(2,1)} copy(bf16[256,2048]{0,1:T(8,128)(2,1)} %bitcast.121) | data formatting | bytes 2097152
  133.6 2.9 %fusion.1 = bf16[4,128,8,128]{3,1,2,0:T(8,128)(2,1)S(1)} fusion(f32[4,8,128,128]{3,2,1,0:T(8,128)} %fusion.12, f32[4,8,128,128]{2,3,1,0:T(8,128)S(1)} %bitcast_add_fusion.2, bf16[4,128,8,128]{3,2,1,0:T(8,128)(2,1)S(1)} %bitcast.110), kind=kOutput, calls=%fused_computation.3 | convolution fusion | flops 806354944 | bytes 6291456 | tf_op jit(solution)/shard_map/nshe,nhde->nshd/dot_general | solution.py:105
  136.5 0.7 copy.107
  137.2 0.5 all_to_all.106
  137.7 4.5 %all_to_all.122 = bf16[2,256,1024]{2,1,0:T(8,128)(2,1)S(1)} all-to-all(bf16[2,256,1024]{2,1,0:T(8,128)(2,1)S(1)} %all_to_all.106), channel_id=1, replica_groups=mesh['seq'=16,'head'=2] {'head'}, dimensions={0} | all-to-all | bytes 2097152 | tf_op jit(solution)/shard_map/all_to_all | solution.py:152
  142.2 0.5 copy.108
  142.7 1.4 copy.118
  144.2 1.7 %multiply_add_fusion.1 = f32[8,128,128]{2,1,0:T(8,128)S(1)} fusion(f32[8,128,128]{2,1,0:T(8,128)} %collective-permute-done.3, f32[8,128,128]{2,1,0:T(8,128)} %collective-permute-done.2, f32[8,128,128]{2,1,0:T(8,128)S(1)} %copy-done.12, f32[8,128,128]{2,1,0:T(8,128)} %collective-permute-done, f32[8]{0:T(128)S(1)} %get-tuple-element.19, ...), kind=kLoop, calls=%fused_computation.48 | loop fusion | flops 917504 | bytes 2621568 | tf_op jit(solution)/shard_map/add | solution.py:45
  146.5 0.9 copy-done.1
  147.5 0.7 copy-done.5
  148.2 2.3 %fusion.2 = bf16[4,128,8,128]{3,1,2,0:T(8,128)(2,1)S(1)} fusion(f32[4,8,128,128]{3,2,1,0:T(8,128)S(1)} %copy-done.5, f32[4,8,128,128]{3,2,1,0:T(8,128)S(1)} %bitcast_add_fusion.4, bf16[4,128,8,128]{3,2,1,0:T(8,128)(2,1)S(1)} %bitcast.104), kind=kOutput, calls=%fused_computation.6 | convolution fusion | flops 806354944 | bytes 6291456 | tf_op jit(solution)/shard_map/nthe,nhde->nthd/dot_general | solution.py:102
  150.5 0.7 copy.94
  151.2 0.5 all_to_all.99
  151.7 4.6 %all_to_all.123 = bf16[2,256,1024]{2,1,0:T(8,128)(2,1)S(1)} all-to-all(bf16[2,256,1024]{2,1,0:T(8,128)(2,1)S(1)} %all_to_all.99), channel_id=1, replica_groups=mesh['seq'=16,'head'=2] {'head'}, dimensions={0} | all-to-all | bytes 2097152 | tf_op jit(solution)/shard_map/all_to_all | solution.py:151
  156.3 0.5 copy.95
  156.8 1.4 copy.117
  (50 shorter events, 2.9 us)
Async XLA Ops:
  0.6 6.6 %copy-start.14 = (bf16[256,2048]{1,0:T(8,128)(2,1)S(1)}, bf16[256,2048]{1,0:T(8,128)(2,1)}, u32[]{:S(2)}) copy-start(bf16[256,2048]{1,0:T(8,128)(2,1)} %param.5) | copy-start | bytes 3145732
  3.0 6.0 %all-to-all-start = ((bf16[256,2,1024]{2,0,1:T(8,128)(2,1)}), bf16[256,2,1024]{2,0,1:T(8,128)(2,1)S(1)}, u32[]{:S(2)}, u32[]{:S(2)}) async-start(bf16[256,2,1024]{2,0,1:T(8,128)(2,1)} %bitcast.96), calls=%async_computation | async-start | bytes 2097152 | tf_op jit(solution)/shard_map/all_to_all | solution.py:130
  9.0 5.7 %all-to-all-start.4 = ((bf16[256,2,1024]{2,0,1:T(8,128)(2,1)}), bf16[256,2,1024]{2,0,1:T(8,128)(2,1)S(1)}, u32[]{:S(2)}, u32[]{:S(2)}) async-start(bf16[256,2,1024]{2,0,1:T(8,128)(2,1)} %bitcast.93), calls=%async_computation.4 | async-start | bytes 2097152 | tf_op jit(solution)/shard_map/all_to_all | solution.py:127
  13.2 63.6 %copy-start = (bf16[64,8,8,128]{3,2,1,0:T(8,128)(2,1)}, bf16[64,8,8,128]{3,2,1,0:T(8,128)(2,1)S(1)}, u32[]{:S(2)}) copy-start(bf16[64,8,8,128]{3,2,1,0:T(8,128)(2,1)S(1)} %copy.131) | copy-start | bytes 3145732
  15.0 3.0 %copy-start.15 = (bf16[256,2048]{1,0:T(8,128)(2,1)S(1)}, bf16[256,2048]{1,0:T(8,128)(2,1)}, u32[]{:S(2)}) copy-start(bf16[256,2048]{1,0:T(8,128)(2,1)} %param.6) | copy-start | bytes 3145732
  17.7 28.9 %collective-permute-start.4 = (f32[8,128,128]{2,1,0:T(8,128)}, f32[8,128,128]{2,1,0:T(8,128)}, u32[]{:S(2)}, u32[]{:S(2)}) collective-permute-start(f32[8,128,128]{2,1,0:T(8,128)} %get-tuple-element.26), channel_id=1, source_target_pairs={{0,2},{2,0},{4,6},{6,4},{8,10},{10,8},{12,14},{14,12},{16,18},{18,... | collective-permute-start | bytes 1572872 | tf_op jit(solution)/shard_map/ppermute | solution.py:11
  19.0 6.5 %all-to-all-start.2 = ((bf16[256,2,1024]{2,0,1:T(8,128)(2,1)}), bf16[256,2,1024]{2,0,1:T(8,128)(2,1)S(1)}, u32[]{:S(2)}, u32[]{:S(2)}) async-start(bf16[256,2,1024]{2,0,1:T(8,128)(2,1)} %bitcast.119), calls=%async_computation.2 | async-start | bytes 2097152 | tf_op jit(solution)/shard_map/all_to_all | solution.py:128
  25.5 4.4 %copy-start.10 = (bf16[256,2,1024]{2,0,1:T(8,128)(2,1)}, bf16[256,2,1024]{2,0,1:T(8,128)(2,1)S(1)}, u32[]{:S(2)}) copy-start(bf16[256,2,1024]{2,0,1:T(8,128)(2,1)S(1)} %all-to-all-done.2) | copy-start | bytes 3145732
  25.5 6.3 %all-to-all-start.1 = ((bf16[256,2,1024]{2,0,1:T(8,128)(2,1)}), bf16[256,2,1024]{2,0,1:T(8,128)(2,1)}, u32[]{:S(2)}, u32[]{:S(2)}) async-start(bf16[256,2,1024]{2,0,1:T(8,128)(2,1)} %bitcast.118), calls=%async_computation.1 | async-start | bytes 2097152 | tf_op jit(solution)/shard_map/all_to_all | solution.py:129
  33.3 2.7 %copy-start.2 = (bf16[64,8,8,128]{3,2,1,0:T(8,128)(2,1)}, bf16[64,8,8,128]{3,2,1,0:T(8,128)(2,1)S(1)}, u32[]{:S(2)}) copy-start(bf16[64,8,8,128]{3,2,1,0:T(8,128)(2,1)S(1)} %copy.132) | copy-start | bytes 3145732
  36.0 5.5 %copy-start.16 = (f32[16,11]{1,0:T(8,128)S(1)}, f32[16,11]{1,0:T(8,128)}, u32[]{:S(2)}) copy-start(f32[16,11]{1,0:T(8,128)} %param.9) | copy-start | bytes 2116
  36.0 20.6 %collective-permute-start = (f32[8,128,128]{2,1,0:T(8,128)}, f32[8,128,128]{2,1,0:T(8,128)}, u32[]{:S(2)}, u32[]{:S(2)}) collective-permute-start(f32[8,128,128]{2,1,0:T(8,128)} %get-tuple-element.24), channel_id=1, source_target_pairs={{0,2},{2,0},{4,6},{6,4},{8,10},{10,8},{12,14},{14,12},{16,18},{18,... | collective-permute-start | bytes 1572872 | tf_op jit(solution)/shard_map/ppermute | solution.py:11
  41.8 2.7 %copy-start.8 = (f32[4,8,128,128]{3,2,1,0:T(8,128)S(1)}, f32[4,8,128,128]{3,2,1,0:T(8,128)}, u32[]{:S(2)}) copy-start(f32[4,8,128,128]{3,2,1,0:T(8,128)} %get-tuple-element.25) | copy-start | bytes 6291460
  43.4 2.1 %copy-start.7 = (f32[4,8,128,128]{3,2,1,0:T(8,128)S(1)}, f32[4,8,128,128]{3,2,1,0:T(8,128)}, u32[]{:S(2)}) copy-start(f32[4,8,128,128]{3,2,1,0:T(8,128)} %get-tuple-element.27) | copy-start | bytes 6291460
  48.7 13.1 %collective-permute-start.5 = (f32[8,128,128]{2,1,0:T(8,128)}, f32[8,128,128]{2,1,0:T(8,128)}, u32[]{:S(2)}, u32[]{:S(2)}) collective-permute-start(f32[8,128,128]{2,1,0:T(8,128)} %add.119), channel_id=1, source_target_pairs={{0,4},{2,6},{4,0},{6,2},{8,12},{10,14},{12,8},{14,10},{16,20},{18,... | collective-permute-start | bytes 1572872 | tf_op jit(solution)/shard_map/ppermute | solution.py:11
  56.6 6.8 %copy-start.3 = (bf16[64,8,8,128]{3,2,1,0:T(8,128)(2,1)S(1)}, bf16[64,8,8,128]{3,2,1,0:T(8,128)(2,1)}, u32[]{:S(2)}) copy-start(bf16[64,8,8,128]{3,2,1,0:T(8,128)(2,1)} %copy-done.2) | copy-start | bytes 3145732
  57.9 15.0 %collective-permute-start.1 = (f32[8,128,128]{2,1,0:T(8,128)S(1)}, f32[8,128,128]{2,1,0:T(8,128)S(1)}, u32[]{:S(2)}, u32[]{:S(2)}) collective-permute-start(f32[8,128,128]{2,1,0:T(8,128)S(1)} %add.106), channel_id=1, source_target_pairs={{0,4},{2,6},{4,0},{6,2},{8,12},{10,14},{12,8},{14,10},{16,20},{18,... | collective-permute-start | bytes 1572872 | tf_op jit(solution)/shard_map/ppermute | solution.py:11
  63.1 11.0 %collective-permute-start.6 = (f32[8,128,128]{2,1,0:T(8,128)S(1)}, f32[8,128,128]{2,1,0:T(8,128)S(1)}, u32[]{:S(2)}, u32[]{:S(2)}) collective-permute-start(f32[8,128,128]{2,1,0:T(8,128)S(1)} %add.121), channel_id=1, source_target_pairs={{0,8},{2,10},{4,12},{6,14},{8,0},{10,2},{12,4},{14,6},{16,24},{18,... | collective-permute-start | bytes 1572872 | tf_op jit(solution)/shard_map/ppermute | solution.py:11
  73.0 2.0 %copy-start.11 = (f32[8,128,128]{2,1,0:T(8,128)}, f32[8,128,128]{2,1,0:T(8,128)S(1)}, u32[]{:S(2)}) copy-start(f32[8,128,128]{2,1,0:T(8,128)S(1)} %collective-permute-done.1) | copy-start | bytes 1572868
  73.9 22.3 %collective-permute-start.2 = (f32[8,128,128]{2,1,0:T(8,128)}, f32[8,128,128]{2,1,0:T(8,128)}, u32[]{:S(2)}, u32[]{:S(2)}) collective-permute-start(f32[8,128,128]{2,1,0:T(8,128)} %add.109), channel_id=1, source_target_pairs={{0,8},{2,10},{4,12},{6,14},{8,0},{10,2},{12,4},{14,6},{16,24},{18,... | collective-permute-start | bytes 1572872 | tf_op jit(solution)/shard_map/ppermute | solution.py:11
  74.1 1.0 copy-start.13
  75.0 23.2 %collective-permute-start.7 = (f32[8,128,128]{2,1,0:T(8,128)}, f32[8,128,128]{2,1,0:T(8,128)}, u32[]{:S(2)}, u32[]{:S(2)}) collective-permute-start(f32[8,128,128]{2,1,0:T(8,128)} %add.123), channel_id=1, source_target_pairs={{0,16},{2,18},{4,20},{6,22},{8,24},{10,26},{12,28},{14,30},{16,0},... | collective-permute-start | bytes 1572872 | tf_op jit(solution)/shard_map/ppermute | solution.py:11
  98.2 45.9 %collective-permute-start.3 = (f32[8,128,128]{2,1,0:T(8,128)}, f32[8,128,128]{2,1,0:T(8,128)}, u32[]{:S(2)}, u32[]{:S(2)}) collective-permute-start(f32[8,128,128]{2,1,0:T(8,128)} %add.112), channel_id=1, source_target_pairs={{0,16},{2,18},{4,20},{6,22},{8,24},{10,26},{12,28},{14,30},{16,0},... | collective-permute-start | bytes 1572872 | tf_op jit(solution)/shard_map/ppermute | solution.py:11
  101.0 2.4 %copy-start.6 = (f32[4,8,128,128]{3,2,1,0:T(8,128)S(1)}, f32[4,8,128,128]{3,2,1,0:T(8,128)}, u32[]{:S(2)}) copy-start(f32[4,8,128,128]{3,2,1,0:T(8,128)} %fusion.3) | copy-start | bytes 6291460
  129.0 4.6 %copy-start.4 = (bf16[64,8,8,128]{3,2,1,0:T(8,128)(2,1)S(1)}, bf16[64,8,8,128]{3,2,1,0:T(8,128)(2,1)}, u32[]{:S(2)}) copy-start(bf16[64,8,8,128]{3,2,1,0:T(8,128)(2,1)} %copy-done.2) | copy-start | bytes 3145732
  142.2 2.0 %copy-start.12 = (f32[8,128,128]{2,1,0:T(8,128)S(1)}, f32[8,128,128]{2,1,0:T(8,128)}, u32[]{:S(2)}) copy-start(f32[8,128,128]{2,1,0:T(8,128)} %copy-done.11) | copy-start | bytes 1572868
  144.2 2.1 %copy-start.9 = (f32[2,2,8,128,128]{4,3,2,1,0:T(8,128)S(1)}, f32[2,2,8,128,128]{4,3,2,1,0:T(8,128)}, u32[]{:S(2)}) copy-start(f32[2,2,8,128,128]{4,3,2,1,0:T(8,128)} %copy.91) | copy-start | bytes 6291460
  146.2 1.2 copy-start.1
  146.2 1.9 %copy-start.5 = (f32[4,8,128,128]{3,2,1,0:T(8,128)S(1)}, f32[4,8,128,128]{3,2,1,0:T(8,128)}, u32[]{:S(2)}) copy-start(f32[4,8,128,128]{3,2,1,0:T(8,128)} %fusion.22) | copy-start | bytes 6291460
where the time goes:
time: 159 us; the launch traced here: 158 us
  local copies, waits for them, and re-layouts  32.8 us (21%)
  blocking collectives  30.4 us (19%)
  waiting for transfers between devices  28.9 us (18%)
  other arithmetic  25 us (16%)
  starting transfers between devices  20.3 us (13%)
  matrix products  20 us (13%)
    ppermute x8, waiting for transfers between devices, partner(): lax.ppermute(array, axis, [(i, i ^ 1 << distance) for i in range(lax.axis...  26.3 us
    all_to_all x1, blocking collectives, body(): lax.all_to_all(value_part, 'head', split_axis=0, concat_axis=1, tiled=True)  21.3 us
    unnamed x41, local copies, waits for them, and re-layouts  11.8 us
    all_to_all x1, blocking collectives, body(): lax.all_to_all(query_part, 'head', split_axis=0, concat_axis=1, tiled=True)  4.57 us
    all_to_all x1, blocking collectives, body(): lax.all_to_all(key_grad_part, 'head', split_axis=0, concat_axis=1, tiled=...  4.51 us
    all_to_all x1, starting transfers between devices, body(): lax.all_to_all(values, 'head', split_axis=1, concat_axis=0, tiled=True)  4.42 us
    add x3, other arithmetic, cross_states(): group_kv = group_kv + other_kv  4.33 us
    add x3, other arithmetic, cross_states(): group_qo = group_qo + other_qo  4.27 us
  transfers between devices with their start and end apart: 12, of which 6 were waited for; matrix products, arithmetic and copies ran while one was open for 38% of the time, Pallas kernels for 0%

commit v1 on v0

v1 whole, which is shorter than its diff:
```python
import functools
import math

import jax
import jax.numpy as jnp
from jax import lax
from jax.experimental import pallas as pl
from jax.experimental.pallas import tpu as pltpu
from jax.sharding import PartitionSpec as P

DH = 128
BLOCK = 128
F32 = jnp.float32
BF16 = jnp.bfloat16
NT = (((1,), (1,)), ((), ()))
TN = (((0,), (0,)), ((), ()))


def dot(a, b, dims=None):
    if dims is None:
        dims = (((1,), (0,)), ((), ()))
    return lax.dot_general(a, b, dims, preferred_element_type=F32)


def split(x):
    hi = x.astype(BF16)
    return hi, (x - hi.astype(F32)).astype(BF16)


def partner(array, axis, distance):
    return lax.ppermute(array, axis, [(i, i ^ distance) for i in range(lax.axis_size(axis))])


def state_kernel(pos_ref, q_ref, k_ref, v_ref, o_ref, out_ref):
    for j in range(out_ref.shape[2]):
        cols = slice(j * DH, (j + 1) * DH)
        out_ref[0, 0, j] = dot(v_ref[:, cols], k_ref[:, cols], TN)
        out_ref[0, 1, j] = dot(o_ref[:, cols], q_ref[:, cols], TN)


def device_states(pos, q, k, v, o, slices, width):
    tokens = q.shape[0]
    spec = pl.BlockSpec(
        (tokens, width * DH), lambda d, pos: (0, pos[0] * slices + (pos[1] ^ d))
    )
    return pl.pallas_call(
        state_kernel,
        grid_spec=pltpu.PrefetchScalarGridSpec(
            num_scalar_prefetch=1,
            grid=(slices,),
            in_specs=[spec] * 4,
            out_specs=pl.BlockSpec((1, 2, width, DH, DH), lambda d, pos: (d, 0, 0, 0, 0)),
        ),
        out_shape=jax.ShapeDtypeStruct((slices, 2, width, DH, DH), F32),
        cost_estimate=pl.CostEstimate(
            flops=4 * slices * width * tokens * DH * DH,
            bytes_accessed=8 * slices * width * DH * (tokens + DH),
            transcendentals=0,
        ),
        name="states",
    )(pos, q, k, v, o)


def local_kernel(scale_ref, q_ref, k_ref, v_ref, o_ref, qg_ref, kg_ref, vg_ref):
    tokens = q_ref.shape[0]
    blocks = tokens // BLOCK
    width = q_ref.shape[1] // DH
    step = pl.program_id(0)
    rows = lax.broadcasted_iota(jnp.int32, (BLOCK, BLOCK), 0)
    cols = lax.broadcasted_iota(jnp.int32, (BLOCK, BLOCK), 1)
    lower = rows >= cols
    upper = rows <= cols
    for j in range(width):
        head = step * width + j
        cs = slice(j * DH, (j + 1) * DH)
        for n in range(blocks):
            here = slice(n * BLOCK, (n + 1) * BLOCK)
            q, k, v, o = q_ref[here, cs], k_ref[here, cs], v_ref[here, cs], o_ref[here, cs]
            first = scale_ref[head, 0]
            score_t = jnp.where(upper, dot(k, q, NT) * first, 0.0).astype(BF16)
            grad = jnp.where(lower, dot(o, v, NT) * first, 0.0).astype(BF16)
            grad_t = jnp.where(upper, dot(v, o, NT) * first, 0.0).astype(BF16)
            vg = dot(score_t, o)
            qg = dot(grad, k)
            kg = dot(grad_t, q)
            for m in range(blocks):
                if m == n:
                    continue
                there = slice(m * BLOCK, (m + 1) * BLOCK)
                weight = scale_ref[head, (m ^ n).bit_length()]
                if m < n:
                    hi, lo = split(dot(o, v_ref[there, cs], NT) * weight)
                    other = k_ref[there, cs]
                    qg = qg + dot(hi, other) + dot(lo, other)
                else:
                    hi, lo = split(dot(v, o_ref[there, cs], NT) * weight)
                    other = q_ref[there, cs]
                    kg = kg + dot(hi, other) + dot(lo, other)
                    hi, lo = split(dot(k, q_ref[there, cs], NT) * weight)
                    other = o_ref[there, cs]
                    vg = vg + dot(hi, other) + dot(lo, other)
            qg_ref[here, cs] = qg
            kg_ref[here, cs] = kg
            vg_ref[here, cs] = vg


def local_grads(level_scale, q, k, v, o, width):
    tokens, model = q.shape
    spec = pl.BlockSpec((tokens, width * DH), lambda i: (0, i))
    return pl.pallas_call(
        local_kernel,
        grid=(model // (width * DH),),
        in_specs=[pl.BlockSpec(memory_space=pltpu.SMEM)] + [spec] * 4,
        out_specs=[spec] * 3,
        out_shape=[jax.ShapeDtypeStruct((tokens, model), F32)] * 3,
        cost_estimate=pl.CostEstimate(
            flops=24 * tokens * BLOCK * model, bytes_accessed=20 * tokens * model, transcendentals=0
        ),
        name="local",
    )(level_scale, q, k, v, o)


def cross_kernel(pos_ref, mine_ref, other_ref, k_ref, v_ref, o_ref, ql_ref, kl_ref, vl_ref, qg_ref, kg_ref, vg_ref):
    width = mine_ref.shape[2]
    own = pl.program_id(0) == 0
    for j in range(width):
        cs = slice(j * DH, (j + 1) * DH)
        early = jnp.where(own, mine_ref[0, 0, j], other_ref[0, 0, j])
        late = jnp.where(own, mine_ref[0, 1, j], other_ref[0, 1, j])
        hi, lo = split(early)
        o = o_ref[:, cs]
        qg_ref[:, cs] = (ql_ref[:, cs] + (dot(o, hi) + dot(o, lo))).astype(BF16)
        hi, lo = split(late)
        v = v_ref[:, cs]
        kg_ref[:, cs] = (kl_ref[:, cs] + (dot(v, hi) + dot(v, lo))).astype(BF16)
        k = k_ref[:, cs]
        vg_ref[:, cs] = (vl_ref[:, cs] + (dot(k, hi, NT) + dot(k, lo, NT))).astype(BF16)


def finish(pos, mine, other, k, v, o, local, slices, width):
    tokens, model = k.shape
    spec = pl.BlockSpec(
        (tokens, width * DH),
        lambda half, d, pos: (0, (pos[0] ^ half) * slices + (pos[1] ^ d)),
    )
    state = (1, 2, width, DH, DH)
    last = slices - 1
    return pl.pallas_call(
        cross_kernel,
        grid_spec=pltpu.PrefetchScalarGridSpec(
            num_scalar_prefetch=1,
            grid=(2, slices),
            in_specs=[
                pl.BlockSpec(state, lambda half, d, pos: (d * (1 - half) + last * half, 0, 0, 0, 0)),
                pl.BlockSpec(state, lambda half, d, pos: (d * half, 0, 0, 0, 0)),
            ]
            + [spec] * 6,
            out_specs=[spec] * 3,
        ),
        out_shape=[jax.ShapeDtypeStruct((tokens, model), BF16)] * 3,
        cost_estimate=pl.CostEstimate(
            flops=12 * tokens * DH * model, bytes_accessed=24 * tokens * model, transcendentals=0
        ),
        name="finish",
    )(pos, mine, other, k, v, o, *local)


def body(queries, key_rows, values, out_grad, level_weights):
    level_ids = jnp.arange(level_weights.shape[1], dtype=F32)
    level_scale = level_weights * jnp.exp2((1.0 - level_ids) / 2.0)[None, :] / jnp.sqrt(F32(DH * BLOCK))
    heads = level_weights.shape[0]
    tokens = queries.shape[0]
    chain = lax.axis_size("seq")
    halves = lax.axis_size("head")
    bits = chain.bit_length() - 1
    plane_bits = min(2, bits)
    slices = 1 << plane_bits
    width = heads // (halves * slices)
    local_levels = (tokens // BLOCK).bit_length() - 1
    core = lax.axis_index("head")
    seq = lax.axis_index("seq")
    place = seq % slices
    row = seq // slices

    args = (queries, key_rows, values, out_grad)
    sent = device_states(jnp.stack([1 - core, place]).astype(jnp.int32), *args, slices, width)
    other = partner(sent, "head", 1)
    pos = jnp.stack([core, place]).astype(jnp.int32)
    own = device_states(pos, *args, slices, width)
    local = local_grads(level_scale, *args, width)

    by_slice = level_scale.reshape(halves, slices, width, -1)[core]
    relative = jnp.stack([by_slice[place ^ d] for d in range(slices)])
    mine_scale = relative[0]

    def weigh(level):
        return mine_scale[:, level][:, None, None]

    def bit_of(value, index):
        return ((value >> index) & 1).astype(F32)

    base = local_levels + 2
    chip = own + other
    parts = [chip[0]] + [partner(chip[d], "seq", d) for d in range(1, slices)]
    earlier = [jnp.zeros((width, DH, DH), F32) for _ in range(slices)]
    later = [jnp.zeros((width, DH, DH), F32) for _ in range(slices)]
    for d in range(slices):
        for e in range(slices):
            if e == d:
                continue
            top = (d ^ e).bit_length() - 1
            up = bit_of(place ^ d, top)
            earlier[d] = earlier[d] + (up * weigh(base + top)) * parts[e][0]
            later[d] = later[d] + ((1.0 - up) * weigh(base + top)) * parts[e][1]
    total = functools.reduce(jnp.add, parts)
    far_early = jnp.zeros((width, DH, DH), F32)
    far_late = jnp.zeros((width, DH, DH), F32)
    rest = bits - plane_bits
    direct = min(2, rest)
    for index in range(rest - direct):
        got = partner(total, "seq", slices << index)
        up = bit_of(row, index)
        weight = weigh(base + plane_bits + index)
        far_early = far_early + up * weight * got[0]
        far_late = far_late + (1.0 - up) * weight * got[1]
        total = total + got
    for step in range(1, 1 << direct):
        top = step.bit_length() - 1 + rest - direct
        up = bit_of(row, top)
        give = jnp.where(up > 0, total[1], total[0])
        got = partner(give, "seq", slices << (rest - direct) if step == 1 else (slices << (rest - direct)) * step)
        weight = weigh(base + plane_bits + top)
        far_early = far_early + (up * weight) * got
        far_late = far_late + ((1.0 - up) * weight) * got
    result = [jnp.stack([earlier[d] + far_early, later[d] + far_late]) for d in range(slices)]
    back = [result[0]] + [partner(result[d], "seq", d) for d in range(1, slices)]
    states = jnp.stack(back)
    weight = relative[:, :, local_levels + 1]
    second = core.astype(F32)
    to_other = jnp.stack([(1.0 - second) * weight, second * weight], axis=1)[..., None, None]
    to_mine = jnp.stack([second * weight, (1.0 - second) * weight], axis=1)[..., None, None]
    theirs = partner(states + to_other * own, "head", 1)
    mine = states + to_mine * other
    return tuple(finish(pos, mine, theirs, key_rows, values, out_grad, local, slices, width))


def solution(mesh):
    rows = P(("seq", "head"), None)
    return jax.shard_map(
        body,
        mesh=mesh,
        in_specs=(rows, rows, rows, rows, P()),
        out_specs=(rows, rows, rows),
        check_vma=False,
    )
```

time: 159 us -> 91.7 us (0.58)
  the two profiles are of different devices: /device:TPU:31 before, /device:TPU:1 now
where the time goes in v1:
time: 91.7 us; the launch traced here: 91.1 us
  Pallas kernels  32.2 us (35%)
  waiting for transfers between devices  30.1 us (33%)
  starting transfers between devices  13.1 us (14%)
  other arithmetic  12.5 us (14%)
  local copies, waits for them, and re-layouts  2.38 us (3%)
    ppermute x11, waiting for transfers between devices, partner(): lax.ppermute(array, axis, [(i, i ^ distance) for i in range(lax.axis_size...  30.1 us
    ppermute x11, starting transfers between devices, partner(): lax.ppermute(array, axis, [(i, i ^ distance) for i in range(lax.axis_size...  13.1 us
    pallas_call x1, Pallas kernels, local_grads(): pl.pallas_call(local_kernel, grid=(model // (width * DH),), in_specs=[pl....  13 us
    pallas_call x2, Pallas kernels, device_states(): pl.pallas_call(state_kernel, grid_spec=pltpu.PrefetchScalarGridSpec(num_s...  9.65 us
    pallas_call x1, Pallas kernels, finish(): pl.pallas_call(cross_kernel, grid_spec=pltpu.PrefetchScalarGridSpec(num_s...  9.54 us
    another operation x7, other arithmetic, body(): jnp.stack([earlier[d] + far_early, later[d] + far_late])  5.27 us
    add x1, other arithmetic, body(): theirs = partner(states + to_other * own, 'head', 1)  2.32 us
  transfers between devices with their start and end apart: 11, of which 7 were waited for; matrix products, arithmetic and copies ran while one was open for 6% of the time, Pallas kernels for 20%

profile of v1, /device:TPU:1, one launch (start us, length us, event | category | flops | bytes accessed | tf_op | source)
XLA Modules:
  0.0 91.1 jit_solution(7604587437212286867)
XLA Ops:
  0.6 0.7 pad_add_fusion.1.pos_ref
  1.3 4.8 %states.3 = f32[4,2,2,128,128]{4,3,2,1,0:T(8,128)} custom-call(s32[2]{0:T(128)} %pad_add_fusion.1.pos_ref, bf16[256,2048]{1,0:T(8,128)(2,1)} %q_ref.5, bf16[256,2048]{1,0:T(8,128)(2,1)} %k_ref.7, bf16[256,2048]{1,0:T(8,128)(2,1)} %v_ref.7, bf16[256,2048]{1,0:T(8,128)(2,1)} %o_ref.7), custom_call_target="tpu_custom_call" | custom-call | flops 134217728 | bytes 3145728 | tf_op jit(solution)/shard_map/states/pallas_call | solution.py:46
  6.1 0.0 collective-permute-start
  6.2 0.6 pad_add_fusion.pos_ref
  6.7 4.8 %states.2 = f32[4,2,2,128,128]{4,3,2,1,0:T(8,128)} custom-call(s32[2]{0:T(128)} %pad_add_fusion.pos_ref, bf16[256,2048]{1,0:T(8,128)(2,1)} %q_ref.5, bf16[256,2048]{1,0:T(8,128)(2,1)} %k_ref.7, bf16[256,2048]{1,0:T(8,128)(2,1)} %v_ref.7, bf16[256,2048]{1,0:T(8,128)(2,1)} %o_ref.7), custom_call_target="tpu_custom_call" | custom-call | flops 134217728 | bytes 3145728 | tf_op jit(solution)/shard_map/states/pallas_call | solution.py:46
  11.6 0.0 copy-start.6
  11.6 0.0 collective-permute-done
  11.6 1.3 %add.141 = f32[4,2,2,128,128]{4,3,2,1,0:T(8,128)S(1)} add(f32[4,2,2,128,128]{4,3,2,1,0:T(8,128)} %states.2, f32[4,2,2,128,128]{4,3,2,1,0:T(8,128)S(1)} %collective-permute-done) | non-fusion elementwise | flops 262144 | bytes 3145728 | tf_op jit(solution)/shard_map/add | solution.py:203
  12.9 0.8 slice_bitcast_fusion.1
  13.7 3.6 %collective-permute-start.3 = (f32[2,2,128,128]{3,2,1,0:T(8,128)}, f32[2,2,128,128]{3,2,1,0:T(8,128)S(1)}, u32[]{:S(2)}, u32[]{:S(2)}) collective-permute-start(f32[2,2,128,128]{3,2,1,0:T(8,128)} %get-tuple-element.45), channel_id=1, source_target_pairs={{0,6},{2,4},{4,2},{6,0},{8,14},{10,12},{12,10},{14,8},{16,22},{18,... | collective-permute-start | bytes 786440 | tf_op jit(solution)/shard_map/ppermute | solution.py:31
  17.3 0.2 collective-permute-start.2
  17.5 0.1 collective-permute-start.1
  17.6 0.0 copy-done.6
  17.6 0.0 copy-start.5
  17.7 0.1 copy.29
  17.8 0.1 copy.32
  17.9 0.1 copy.31
  18.0 0.1 copy.30
  18.1 0.9 multiply_reduce_fusion.19
  19.0 5.3 %collective-permute-done.3 = f32[2,2,128,128]{3,2,1,0:T(8,128)S(1)} collective-permute-done((f32[2,2,128,128]{3,2,1,0:T(8,128)}, f32[2,2,128,128]{3,2,1,0:T(8,128)S(1)}, u32[]{:S(2)}, u32[]{:S(2)}) %collective-permute-start.3) | collective-permute-done | bytes 262176 | tf_op jit(solution)/shard_map/ppermute | solution.py:31
  24.3 0.0 copy-start.3
  24.3 5.7 %collective-permute-done.2 = f32[2,2,128,128]{3,2,1,0:T(8,128)S(1)} collective-permute-done((f32[2,2,128,128]{3,2,1,0:T(8,128)S(1)}, f32[2,2,128,128]{3,2,1,0:T(8,128)S(1)}, u32[]{:S(2)}, u32[]{:S(2)}) %collective-permute-start.2) | collective-permute-done | bytes 262176 | tf_op jit(solution)/shard_map/ppermute | solution.py:31
  29.9 0.0 collective-permute-done.1
  29.9 0.0 copy-start.1
  29.9 0.1 fusion.2
  30.0 3.6 %collective-permute-start.6 = (f32[2,128,128]{2,1,0:T(8,128)S(1)}, f32[2,128,128]{2,1,0:T(8,128)S(1)}, u32[]{:S(2)}, u32[]{:S(2)}) collective-permute-start(f32[2,128,128]{2,1,0:T(8,128)S(1)} %get-tuple-element.49), channel_id=1, source_target_pairs={{0,24},{2,26},{4,28},{6,30},{8,16},{10,18},{12,20},{14,22},{16,8},... | collective-permute-start | bytes 393224 | tf_op jit(solution)/shard_map/ppermute | solution.py:31
  33.6 0.0 collective-permute-start.5
  33.6 0.4 collective-permute-start.4
  34.0 0.1 multiply_bitcast_fusion.1
  34.1 0.4 multiply_reduce_fusion.17
  34.4 7.2 %collective-permute-done.4 = f32[2,128,128]{2,1,0:T(8,128)} collective-permute-done((f32[2,128,128]{2,1,0:T(8,128)S(1)}, f32[2,128,128]{2,1,0:T(8,128)}, u32[]{:S(2)}, u32[]{:S(2)}) %collective-permute-start.4) | collective-permute-done | bytes 131104 | tf_op jit(solution)/shard_map/ppermute | solution.py:31
  41.6 0.0 collective-permute-done.6
  41.6 2.7 %collective-permute-done.5 = f32[2,128,128]{2,1,0:T(8,128)S(1)} collective-permute-done((f32[2,128,128]{2,1,0:T(8,128)S(1)}, f32[2,128,128]{2,1,0:T(8,128)S(1)}, u32[]{:S(2)}, u32[]{:S(2)}) %collective-permute-start.5) | collective-permute-done | bytes 131104 | tf_op jit(solution)/shard_map/ppermute | solution.py:31
  44.3 1.7 %add_bitcast_fusion.3 = (f32[1,2,128,128]{3,2,1,0:T(8,128)S(1)}, f32[2,128,128]{2,1,0:T(8,128)S(1)}, f32[1,2,128,128]{3,2,1,0:T(8,128)}, f32[2,128,128]{2,1,0:T(8,128)S(1)}) fusion(f32[2,2,128,128]{3,2,1,0:T(8,128)S(1)} %collective-permute-done.1, f32[2,2,128,128]{3,2,1,0:T(8,128)S(1)} %collective-permute-done.2, ...), kind=kLoop, calls=%fused_computation.38 | loop fusion | flops 720896 | bytes 1704000 | tf_op jit(solution)/shard_map/stack | solution.py:235
  46.0 0.0 copy-start.7
  46.0 0.8 fusion.10
  46.8 0.0 copy-done.5
  46.8 0.0 copy-done.1
  46.8 0.0 copy-start.2
  46.8 0.7 pad_maximum_fusion.2
  47.6 1.3 %collective-permute-start.8 = (f32[2,2,128,128]{3,2,1,0:T(8,128)}, f32[2,2,128,128]{3,2,1,0:T(8,128)}, u32[]{:S(2)}, u32[]{:S(2)}) collective-permute-start(f32[2,2,128,128]{3,2,1,0:T(8,128)} %pad_maximum_fusion.2), channel_id=1, source_target_pairs={{0,4},{2,6},{4,0},{6,2},{8,12},{10,14},{12,8},{14,10},{16,20},{18,... | collective-permute-start | bytes 786440 | tf_op jit(solution)/shard_map/ppermute | solution.py:31
  48.8 0.0 copy-done.3
  48.8 1.2 %add_bitcast_fusion.1 = (f32[1,2,128,128]{3,2,1,0:T(8,128)S(1)}, f32[1,2,128,128]{3,2,1,0:T(8,128)S(1)}) fusion(f32[2,128,128]{2,1,0:T(8,128)S(1)} %get-tuple-element.32, f32[4,2,2,128,128]{4,3,2,1,0:T(8,128)S(1)} %add.141, f32[2,2,128,128]{3,2,1,0:T(8,128)S(1)} %collective-permute-done.2, f32[2,2,128,128]{3,2,1,0:T(8,128)} %copy-done.3, ...), kind=kLoop, calls=%fused_computation.35 | loop fusion | flops 393216 | bytes 1310752 | tf_op jit(solution)/shard_map/stack | solution.py:235
  50.0 0.7 pad_maximum_fusion.1
  50.8 0.0 collective-permute-start.7
  50.8 0.0 copy-done.7
  50.8 0.0 copy-done.8
  50.8 0.0 copy-done.2
  50.8 0.1 fusion.6
  50.9 1.4 %collective-permute-start.9 = (f32[2,2,128,128]{3,2,1,0:T(8,128)S(1)}, f32[2,2,128,128]{3,2,1,0:T(8,128)S(1)}, u32[]{:S(2)}, u32[]{:S(2)}) collective-permute-start(f32[2,2,128,128]{3,2,1,0:T(8,128)S(1)} %pad_maximum_fusion.3), channel_id=1, source_target_pairs={{0,6},{2,4},{4,2},{6,0},{8,14},{10,12},{12,10},{14,8},{16,22},{18,... | collective-permute-start | bytes 786440 | tf_op jit(solution)/shard_map/ppermute | solution.py:31
  52.4 0.1 copy.34
  52.5 0.1 copy.33
  52.6 0.9 %maximum_bitcast_fusion = f32[1,2,2,128,128]{4,3,2,1,0:T(8,128)S(1)} fusion(f32[1,2,128,128]{3,2,1,0:T(8,128)} %get-tuple-element.41, f32[1,2,128,128]{3,2,1,0:T(8,128)S(1)} %get-tuple-element.31), kind=kLoop, calls=%fused_computation.10 | loop fusion | flops 65536 | bytes 524288 | tf_op jit(solution)/shard_map/stack | solution.py:237
  53.5 0.9 %collective-permute-done.8 = f32[2,2,128,128]{3,2,1,0:T(8,128)} collective-permute-done((f32[2,2,128,128]{3,2,1,0:T(8,128)}, f32[2,2,128,128]{3,2,1,0:T(8,128)}, u32[]{:S(2)}, u32[]{:S(2)}) %collective-permute-start.8) | collective-permute-done | bytes 262176 | tf_op jit(solution)/shard_map/ppermute | solution.py:31
  54.4 2.9 %collective-permute-done.7 = f32[2,2,128,128]{3,2,1,0:T(8,128)} collective-permute-done((f32[2,2,128,128]{3,2,1,0:T(8,128)}, f32[2,2,128,128]{3,2,1,0:T(8,128)}, u32[]{:S(2)}, u32[]{:S(2)}) %collective-permute-start.7) | collective-permute-done | bytes 262176 | tf_op jit(solution)/shard_map/ppermute | solution.py:31
  57.4 5.4 %collective-permute-done.9 = f32[2,2,128,128]{3,2,1,0:T(8,128)S(1)} collective-permute-done((f32[2,2,128,128]{3,2,1,0:T(8,128)S(1)}, f32[2,2,128,128]{3,2,1,0:T(8,128)S(1)}, u32[]{:S(2)}, u32[]{:S(2)}) %collective-permute-start.9) | collective-permute-done | bytes 262176 | tf_op jit(solution)/shard_map/ppermute | solution.py:31
  62.7 0.0 copy-done
  62.7 2.3 %multiply_add_fusion = (f32[4,2,2,128,128]{4,3,2,1,0:T(8,128)S(1)}, f32[4,2,2,128,128]{4,3,2,1,0:T(8,128)}) fusion(f32[4,2,2,128,128]{4,3,2,1,0:T(8,128)S(1)} %copy-done, f32[1,2,2,128,128]{4,3,2,1,0:T(8,128)S(1)} %bitcast.129, f32[1,2,2,128,128]{4,3,2,1,0:T(8,128)} %bitcast.27, f32[1,2,2,128,128]{4,3,2,1,0:T(8,128)} %bitcast.24, ...), kind=kLoop, calls=%fused_computation.1 | loop fusion | flops 1835008 | bytes 5243008 | tf_op jit(solution)/shard_map/add | solution.py:242
  65.1 2.5 %collective-permute-start.10 = (f32[4,2,2,128,128]{4,3,2,1,0:T(8,128)S(1)}, f32[4,2,2,128,128]{4,3,2,1,0:T(8,128)S(1)}, u32[]{:S(2)}, u32[]{:S(2)}) collective-permute-start(f32[4,2,2,128,128]{4,3,2,1,0:T(8,128)S(1)} %get-tuple-element.43), channel_id=1, source_target_pairs={{0,1},{1,0},{2,3},{3,2},{4,5},{5,4},{6,7},{7,6},{8,9},{9,8},{10,11... | collective-permute-start | bytes 3145736 | tf_op jit(solution)/shard_map/ppermute | solution.py:31
  67.5 13.0 %local.1 = (f32[256,2048]{1,0:T(8,128)}, f32[256,2048]{1,0:T(8,128)}, f32[256,2048]{1,0:T(8,128)}) custom-call(f32[16,11]{1,0:T(8,128)} %copy-done.5, bf16[256,2048]{1,0:T(8,128)(2,1)} %q_ref.5, bf16[256,2048]{1,0:T(8,128)(2,1)} %k_ref.7, bf16[256,2048]{1,0:T(8,128)(2,1)} %v_ref.7, bf16[256,2048]{1,0:T(8,128)(2,1)} %o_ref.7), custom_call_target="tpu_custom_call" | custom-call | flops 1610612736 | bytes 10485760 | tf_op jit(solution)/shard_map/local/pallas_call | solution.py:110
  80.5 0.0 collective-permute-done.10.other_ref
  80.5 0.0 copy-start.4
  80.5 1.0 %copy-done.4 = f32[4,2,2,128,128]{4,3,2,1,0:T(8,128)} copy-done((f32[4,2,2,128,128]{4,3,2,1,0:T(8,128)}, f32[4,2,2,128,128]{4,3,2,1,0:T(8,128)S(1)}, u32[]{:S(2)}) %copy-start.4) | copy-done | bytes 1048600
  81.5 9.5 %finish.1 = (bf16[256,2048]{1,0:T(8,128)(2,1)}, bf16[256,2048]{1,0:T(8,128)(2,1)}, bf16[256,2048]{1,0:T(8,128)(2,1)}) custom-call(s32[2]{0:T(128)} %pad_add_fusion.pos_ref, f32[4,2,2,128,128]{4,3,2,1,0:T(8,128)} %get-tuple-element.44.mine_ref, f32[4,2,2,128,128]{4,3,2,1,0:T(8,128)} %copy-done.4, bf16[256,2048]{1,0:T(8,128)(2,1)} %k_ref.7, ...), custom_call_target="tpu_custom_call" | custom-call | flops 805306368 | bytes 12582912 | tf_op jit(solution)/shard_map/finish/pallas_call | solution.py:148
  (9 shorter events, 0.1 us)
Async XLA Ops:
  6.1 5.4 %collective-permute-start = (f32[4,2,2,128,128]{4,3,2,1,0:T(8,128)}, f32[4,2,2,128,128]{4,3,2,1,0:T(8,128)S(1)}, u32[]{:S(2)}, u32[]{:S(2)}) collective-permute-start(f32[4,2,2,128,128]{4,3,2,1,0:T(8,128)} %states.3), channel_id=1, source_target_pairs={{0,1},{1,0},{2,3},{3,2},{4,5},{5,4},{6,7},{7,6},{8,9},{9,8},{10,11... | collective-permute-start | bytes 3145736 | tf_op jit(solution)/shard_map/ppermute | solution.py:31
  11.6 6.1 %copy-start.6 = (f32[16,11]{1,0:T(8,128)S(1)}, f32[16,11]{1,0:T(8,128)}, u32[]{:S(2)}) copy-start(f32[16,11]{1,0:T(8,128)} %param.9) | copy-start | bytes 2116
  13.7 10.6 %collective-permute-start.3 = (f32[2,2,128,128]{3,2,1,0:T(8,128)}, f32[2,2,128,128]{3,2,1,0:T(8,128)S(1)}, u32[]{:S(2)}, u32[]{:S(2)}) collective-permute-start(f32[2,2,128,128]{3,2,1,0:T(8,128)} %get-tuple-element.45), channel_id=1, source_target_pairs={{0,6},{2,4},{4,2},{6,0},{8,14},{10,12},{12,10},{14,8},{16,22},{18,... | collective-permute-start | bytes 786440 | tf_op jit(solution)/shard_map/ppermute | solution.py:31
  17.3 12.6 %collective-permute-start.2 = (f32[2,2,128,128]{3,2,1,0:T(8,128)S(1)}, f32[2,2,128,128]{3,2,1,0:T(8,128)S(1)}, u32[]{:S(2)}, u32[]{:S(2)}) collective-permute-start(f32[2,2,128,128]{3,2,1,0:T(8,128)S(1)} %get-tuple-element.46), channel_id=1, source_target_pairs={{0,4},{2,6},{4,0},{6,2},{8,12},{10,14},{12,8},{14,10},{16,20},{18,... | collective-permute-start | bytes 786440 | tf_op jit(solution)/shard_map/ppermute | solution.py:31
  17.5 12.4 %collective-permute-start.1 = (f32[2,2,128,128]{3,2,1,0:T(8,128)S(1)}, f32[2,2,128,128]{3,2,1,0:T(8,128)S(1)}, u32[]{:S(2)}, u32[]{:S(2)}) collective-permute-start(f32[2,2,128,128]{3,2,1,0:T(8,128)S(1)} %get-tuple-element.47), channel_id=1, source_target_pairs={{0,2},{2,0},{4,6},{6,4},{8,10},{10,8},{12,14},{14,12},{16,18},{18,... | collective-permute-start | bytes 786440 | tf_op jit(solution)/shard_map/ppermute | solution.py:31
  17.6 29.2 %copy-start.5 = (f32[16,11]{1,0:T(8,128)}, f32[16,11]{1,0:T(8,128)S(1)}, u32[]{:S(2)}) copy-start(f32[16,11]{1,0:T(8,128)S(1)} %multiply_multiply_fusion.scale_ref) | copy-start | bytes 2116
  24.3 24.6 %copy-start.3 = (f32[2,2,128,128]{3,2,1,0:T(8,128)}, f32[2,2,128,128]{3,2,1,0:T(8,128)S(1)}, u32[]{:S(2)}) copy-start(f32[2,2,128,128]{3,2,1,0:T(8,128)S(1)} %collective-permute-done.3) | copy-start | bytes 786436
  29.9 16.9 %copy-start.1 = (f32[2,2,128,128]{3,2,1,0:T(8,128)}, f32[2,2,128,128]{3,2,1,0:T(8,128)S(1)}, u32[]{:S(2)}) copy-start(f32[2,2,128,128]{3,2,1,0:T(8,128)S(1)} %collective-permute-done.1) | copy-start | bytes 786436
  30.0 11.6 %collective-permute-start.6 = (f32[2,128,128]{2,1,0:T(8,128)S(1)}, f32[2,128,128]{2,1,0:T(8,128)S(1)}, u32[]{:S(2)}, u32[]{:S(2)}) collective-permute-start(f32[2,128,128]{2,1,0:T(8,128)S(1)} %get-tuple-element.49), channel_id=1, source_target_pairs={{0,24},{2,26},{4,28},{6,30},{8,16},{10,18},{12,20},{14,22},{16,8},... | collective-permute-start | bytes 393224 | tf_op jit(solution)/shard_map/ppermute | solution.py:31
  33.6 10.7 %collective-permute-start.5 = (f32[2,128,128]{2,1,0:T(8,128)S(1)}, f32[2,128,128]{2,1,0:T(8,128)S(1)}, u32[]{:S(2)}, u32[]{:S(2)}) collective-permute-start(f32[2,128,128]{2,1,0:T(8,128)S(1)} %get-tuple-element.49), channel_id=1, source_target_pairs={{0,16},{2,18},{4,20},{6,22},{8,24},{10,26},{12,28},{14,30},{16,0},... | collective-permute-start | bytes 393224 | tf_op jit(solution)/shard_map/ppermute | solution.py:31
  33.6 8.0 %collective-permute-start.4 = (f32[2,128,128]{2,1,0:T(8,128)S(1)}, f32[2,128,128]{2,1,0:T(8,128)}, u32[]{:S(2)}, u32[]{:S(2)}) collective-permute-start(f32[2,128,128]{2,1,0:T(8,128)S(1)} %get-tuple-element.48), channel_id=1, source_target_pairs={{0,8},{2,10},{4,12},{6,14},{8,0},{10,2},{12,4},{14,6},{16,24},{18,... | collective-permute-start | bytes 393224 | tf_op jit(solution)/shard_map/ppermute | solution.py:31
  46.0 4.7 %copy-start.7 = (f32[2]{0:T(128)S(1)}, f32[2]{0:T(128)}, u32[]{:S(2)}) copy-start(f32[2]{0:T(128)} %get-tuple-element.15) | copy-start | bytes 28
  46.0 4.7 %copy-start.8 = (f32[2]{0:T(128)S(1)}, f32[2]{0:T(128)}, u32[]{:S(2)}) copy-start(f32[2]{0:T(128)} %get-tuple-element.16) | copy-start | bytes 28
  46.8 3.9 %copy-start.2 = (f32[2,2,128,128]{3,2,1,0:T(8,128)S(1)}, f32[2,2,128,128]{3,2,1,0:T(8,128)}, u32[]{:S(2)}) copy-start(f32[2,2,128,128]{3,2,1,0:T(8,128)} %copy-done.1) | copy-start | bytes 786436
  47.6 6.8 %collective-permute-start.8 = (f32[2,2,128,128]{3,2,1,0:T(8,128)}, f32[2,2,128,128]{3,2,1,0:T(8,128)}, u32[]{:S(2)}, u32[]{:S(2)}) collective-permute-start(f32[2,2,128,128]{3,2,1,0:T(8,128)} %pad_maximum_fusion.2), channel_id=1, source_target_pairs={{0,4},{2,6},{4,0},{6,2},{8,12},{10,14},{12,8},{14,10},{16,20},{18,... | collective-permute-start | bytes 786440 | tf_op jit(solution)/shard_map/ppermute | solution.py:31
  48.8 13.9 %copy-start = (f32[4,2,2,128,128]{4,3,2,1,0:T(8,128)S(1)}, f32[4,2,2,128,128]{4,3,2,1,0:T(8,128)}, u32[]{:S(2)}) copy-start(f32[4,2,2,128,128]{4,3,2,1,0:T(8,128)} %states.2) | copy-start | bytes 3145732
  50.8 6.6 %collective-permute-start.7 = (f32[2,2,128,128]{3,2,1,0:T(8,128)}, f32[2,2,128,128]{3,2,1,0:T(8,128)}, u32[]{:S(2)}, u32[]{:S(2)}) collective-permute-start(f32[2,2,128,128]{3,2,1,0:T(8,128)} %pad_maximum_fusion.1), channel_id=1, source_target_pairs={{0,2},{2,0},{4,6},{6,4},{8,10},{10,8},{12,14},{14,12},{16,18},{18,... | collective-permute-start | bytes 786440 | tf_op jit(solution)/shard_map/ppermute | solution.py:31
  50.9 11.8 %collective-permute-start.9 = (f32[2,2,128,128]{3,2,1,0:T(8,128)S(1)}, f32[2,2,128,128]{3,2,1,0:T(8,128)S(1)}, u32[]{:S(2)}, u32[]{:S(2)}) collective-permute-start(f32[2,2,128,128]{3,2,1,0:T(8,128)S(1)} %pad_maximum_fusion.3), channel_id=1, source_target_pairs={{0,6},{2,4},{4,2},{6,0},{8,14},{10,12},{12,10},{14,8},{16,22},{18,... | collective-permute-start | bytes 786440 | tf_op jit(solution)/shard_map/ppermute | solution.py:31
  65.1 15.5 %collective-permute-start.10 = (f32[4,2,2,128,128]{4,3,2,1,0:T(8,128)S(1)}, f32[4,2,2,128,128]{4,3,2,1,0:T(8,128)S(1)}, u32[]{:S(2)}, u32[]{:S(2)}) collective-permute-start(f32[4,2,2,128,128]{4,3,2,1,0:T(8,128)S(1)} %get-tuple-element.43), channel_id=1, source_target_pairs={{0,1},{1,0},{2,3},{3,2},{4,5},{5,4},{6,7},{7,6},{8,9},{9,8},{10,11... | collective-permute-start | bytes 3145736 | tf_op jit(solution)/shard_map/ppermute | solution.py:31
  80.5 1.0 %copy-start.4 = (f32[4,2,2,128,128]{4,3,2,1,0:T(8,128)}, f32[4,2,2,128,128]{4,3,2,1,0:T(8,128)S(1)}, u32[]{:S(2)}) copy-start(f32[4,2,2,128,128]{4,3,2,1,0:T(8,128)S(1)} %collective-permute-done.10.other_ref) | copy-start | bytes 3145732

commit v2 on v1

v2 whole, which is shorter than its diff:
```python
import functools
import math

import jax
import jax.numpy as jnp
from jax import lax
from jax.experimental import pallas as pl
from jax.experimental.pallas import tpu as pltpu
from jax.sharding import PartitionSpec as P

DH = 128
BLOCK = 128
F32 = jnp.float32
BF16 = jnp.bfloat16
NT = (((1,), (1,)), ((), ()))
TN = (((0,), (0,)), ((), ()))


def dot(a, b, dims=None):
    if dims is None:
        dims = (((1,), (0,)), ((), ()))
    return lax.dot_general(a, b, dims, preferred_element_type=F32)


def split(x):
    hi = x.astype(BF16)
    return hi, (x - hi.astype(F32)).astype(BF16)


def partner(array, axis, distance):
    return lax.ppermute(array, axis, [(i, i ^ distance) for i in range(lax.axis_size(axis))])


VMEM = pl.BlockSpec(memory_space=pltpu.VMEM)
SMEM = pl.BlockSpec(memory_space=pltpu.SMEM)
HBM = pl.BlockSpec(memory_space=pl.ANY)


def columns(half, place, slices, width):
    core = lax.axis_index("head") ^ half
    return pl.multiple_of((core * slices + place) * (width * DH), DH)


def group_place(slices):
    return lax.axis_index("seq") & (slices - 1)


def state_kernel(half, q_ref, k_ref, v_ref, o_ref, out_ref):
    slices, _, width = out_ref.shape[:3]
    place = group_place(slices)
    for d in range(slices):
        start = columns(half, place ^ d, slices, width)
        for j in range(width):
            cols = pl.ds(pl.multiple_of(start + j * DH, DH), DH)
            out_ref[d, 0, j] = dot(v_ref[:, cols], k_ref[:, cols], TN)
            out_ref[d, 1, j] = dot(o_ref[:, cols], q_ref[:, cols], TN)


def device_states(half, q, k, v, o, slices, width):
    tokens = q.shape[0]
    return pl.pallas_call(
        functools.partial(state_kernel, half),
        in_specs=[VMEM] * 4,
        out_specs=VMEM,
        out_shape=pltpu.VMEM((slices, 2, width, DH, DH), F32),
        compiler_params=pltpu.CompilerParams(vmem_limit_bytes=4 << 20),
        cost_estimate=pl.CostEstimate(
            flops=4 * slices * width * tokens * DH * DH,
            bytes_accessed=8 * slices * width * DH * (tokens + DH),
            transcendentals=0,
        ),
        name=f"states_{half}",
    )(q, k, v, o)


def local_kernel(first_head, heads, scale_ref, q_ref, k_ref, v_ref, o_ref, qg_ref, kg_ref, vg_ref):
    tokens = q_ref.shape[0]
    blocks = tokens // BLOCK
    rows = lax.broadcasted_iota(jnp.int32, (BLOCK, BLOCK), 0)
    cols = lax.broadcasted_iota(jnp.int32, (BLOCK, BLOCK), 1)

    def blk(n, m=None):
        return slice(n * BLOCK, (n + 1 if m is None else m) * BLOCK)

    def product(left, right, weight, values, n, low, high, mask):
        raw = dot(left[blk(n)], right[blk(low, high)], NT)
        parts, rest = [], []
        for m in range(low, high):
            part = raw[:, blk(m - low)]
            if m == n:
                parts.append(jnp.where(mask, part * weight(0), 0.0).astype(BF16))
            else:
                hi, lo = split(part * weight((m ^ n).bit_length()))
                parts.append(hi)
                rest.append((m, lo))
        out = dot(jnp.concatenate(parts, axis=1) if len(parts) > 1 else parts[0], values[blk(low, high)])
        for m, lo in rest:
            out = out + dot(lo, values[blk(m)])
        return out

    def one(index, _):
        head = first_head + index
        here = pl.ds(pl.multiple_of(head * DH, DH), DH)
        there = pl.ds(pl.multiple_of(index * DH, DH), DH)
        q, k, v, o = q_ref[:, here], k_ref[:, here], v_ref[:, here], o_ref[:, here]

        def weight(level):
            return scale_ref[head, level]

        for n in range(blocks):
            vg_ref[blk(n), there] = product(k, q, weight, o, n, n, blocks, rows <= cols)
            kg_ref[blk(n), there] = product(v, o, weight, q, n, n, blocks, rows <= cols)
            qg_ref[blk(n), there] = product(o, v, weight, k, n, 0, n + 1, rows >= cols)
        return 0

    lax.fori_loop(0, heads, one, 0, unroll=2)


def local_grads(level_scale, q, k, v, o, first_head, heads):
    tokens = q.shape[0]
    out = pltpu.VMEM((tokens, heads * DH), F32)
    return pl.pallas_call(
        functools.partial(local_kernel, first_head, heads),
        in_specs=[SMEM] + [VMEM] * 4,
        out_specs=[VMEM] * 3,
        out_shape=[out] * 3,
        compiler_params=pltpu.CompilerParams(vmem_limit_bytes=4 << 20),
        cost_estimate=pl.CostEstimate(
            flops=24 * tokens * BLOCK * heads * DH, bytes_accessed=20 * tokens * heads * DH, transcendentals=0
        ),
        name=f"local_{first_head}",
    )(level_scale, q, k, v, o)


def cross_kernel(count, mine_ref, other_ref, k_ref, v_ref, o_ref, *refs):
    slices, _, width = mine_ref.shape[:3]
    place = group_place(slices)
    local = [refs[3 * i : 3 * i + 3] for i in range(count)]
    outs = refs[3 * count : 3 * count + 3]
    held = refs[3 * count + 3 : 3 * count + 6]
    sems = refs[3 * count + 6]
    heads = k_ref.shape[1] // DH
    per = heads // count
    copies = []
    for half in range(2):
        state_ref = (mine_ref, other_ref)[half]
        for d in range(slices):
            start = columns(half, place ^ d, slices, width)
            for j in range(width):
                at = pl.multiple_of(start + j * DH, DH)
                cs = pl.ds(at, DH)
                o, v, k = o_ref[:, cs], v_ref[:, cs], k_ref[:, cs]
                hi, lo = split(state_ref[d, 0, j])
                qg = dot(o, hi) + dot(o, lo)
                hi, lo = split(state_ref[d, 1, j])
                kg = dot(v, hi) + dot(v, lo)
                vg = dot(k, hi, NT) + dot(k, lo, NT)
                for i, cross in enumerate((qg, kg, vg)):
                    held[i][:, cs] = (cross + local[0][i][:, cs]).astype(BF16)
            cs = pl.ds(start, width * DH)
            for i in range(3):
                copy = pltpu.make_async_copy(
                    held[i].at[:, cs], outs[i].at[:, cs], sems.at[half * slices + d, i]
                )
                copy.start()
                copies.append(copy)
    for copy in copies:
        copy.wait()


def finish(mine, other, k, v, o, local):
    tokens, model = k.shape
    slices = mine.shape[0]
    flat = [part for group in local for part in group]
    return pl.pallas_call(
        functools.partial(cross_kernel, len(local)),
        in_specs=[VMEM] * (5 + len(flat)),
        out_specs=[HBM] * 3,
        out_shape=[jax.ShapeDtypeStruct((tokens, model), BF16)] * 3,
        scratch_shapes=[pltpu.VMEM((tokens, model), BF16)] * 3 + [pltpu.SemaphoreType.DMA((2 * slices, 3))],
        compiler_params=pltpu.CompilerParams(vmem_limit_bytes=8 << 20),
        cost_estimate=pl.CostEstimate(
            flops=12 * tokens * DH * model, bytes_accessed=24 * tokens * model, transcendentals=0
        ),
        name="finish",
    )(mine, other, k, v, o, *flat)


def body(queries, key_rows, values, out_grad, level_weights):
    level_ids = jnp.arange(level_weights.shape[1], dtype=F32)
    level_scale = level_weights * jnp.exp2((1.0 - level_ids) / 2.0)[None, :] / jnp.sqrt(F32(DH * BLOCK))
    heads = level_weights.shape[0]
    tokens = queries.shape[0]
    chain = lax.axis_size("seq")
    halves = lax.axis_size("head")
    bits = chain.bit_length() - 1
    plane_bits = min(2, bits)
    slices = 1 << plane_bits
    width = heads // (halves * slices)
    local_levels = (tokens // BLOCK).bit_length() - 1
    core = lax.axis_index("head")
    seq = lax.axis_index("seq")
    place = seq % slices
    row = seq // slices

    args = (queries, key_rows, values, out_grad)
    sent = device_states(1, *args, slices, width)
    other = partner(sent, "head", 1)
    own = device_states(0, *args, slices, width)
    local = [local_grads(level_scale, *args, 0, heads)]

    by_slice = level_scale.reshape(halves, slices, width, -1)[core]
    relative = jnp.stack([by_slice[place ^ d] for d in range(slices)])
    mine_scale = relative[0]

    def weigh(level):
        return mine_scale[:, level][:, None, None]

    def bit_of(value, index):
        return ((value >> index) & 1).astype(F32)

    base = local_levels + 2
    chip = own + other
    parts = [chip[0]] + [partner(chip[d], "seq", d) for d in range(1, slices)]
    earlier = [jnp.zeros((width, DH, DH), F32) for _ in range(slices)]
    later = [jnp.zeros((width, DH, DH), F32) for _ in range(slices)]
    for d in range(slices):
        for e in range(slices):
            if e == d:
                continue
            top = (d ^ e).bit_length() - 1
            up = bit_of(place ^ d, top)
            earlier[d] = earlier[d] + (up * weigh(base + top)) * parts[e][0]
            later[d] = later[d] + ((1.0 - up) * weigh(base + top)) * parts[e][1]
    total = functools.reduce(jnp.add, parts)
    far_early = jnp.zeros((width, DH, DH), F32)
    far_late = jnp.zeros((width, DH, DH), F32)
    rest = bits - plane_bits
    direct = min(2, rest)
    for index in range(rest - direct):
        got = partner(total, "seq", slices << index)
        up = bit_of(row, index)
        weight = weigh(base + plane_bits + index)
        far_early = far_early + up * weight * got[0]
        far_late = far_late + (1.0 - up) * weight * got[1]
        total = total + got
    for step in range(1, 1 << direct):
        top = step.bit_length() - 1 + rest - direct
        up = bit_of(row, top)
        give = jnp.where(up > 0, total[1], total[0])
        got = partner(give, "seq", slices << (rest - direct) if step == 1 else (slices << (rest - direct)) * step)
        weight = weigh(base + plane_bits + top)
        far_early = far_early + (up * weight) * got
        far_late = far_late + ((1.0 - up) * weight) * got
    result = [jnp.stack([earlier[d] + far_early, later[d] + far_late]) for d in range(slices)]
    back = [result[0]] + [partner(result[d], "seq", d) for d in range(1, slices)]
    states = jnp.stack(back)
    weight = relative[:, :, local_levels + 1]
    second = core.astype(F32)
    to_other = jnp.stack([(1.0 - second) * weight, second * weight], axis=1)[..., None, None]
    to_mine = jnp.stack([second * weight, (1.0 - second) * weight], axis=1)[..., None, None]
    theirs = partner(states + to_other * own, "head", 1)
    mine = states + to_mine * other
    return tuple(finish(mine, theirs, key_rows, values, out_grad, local))


def solution(mesh):
    rows = P(("seq", "head"), None)
    return jax.shard_map(
        body,
        mesh=mesh,
        in_specs=(rows, rows, rows, rows, P()),
        out_specs=(rows, rows, rows),
        check_vma=False,
    )
```

time: 91.7 us -> 81.4 us (0.89)
  Pallas kernels: 32.2 us -> 16.4 us
  local copies, waits for them, and re-layouts: 2.38 us -> 8.79 us
  waiting for transfers between devices: 30.1 us -> 27.5 us
  other arithmetic: 12.5 us -> 13.9 us
    pallas_call x4, Pallas kernels: 32.2 us -> 16.4 us  [the longest x1 11.8 us: local_grads(): pl.pallas_call(functools.partial(local_kernel, first_head, heads), in_spe...]
    unnamed x18 -> x24, local copies, waits for them, and re-layouts: 1 us -> 4.93 us
    ppermute x11, waiting for transfers between devices: 30.1 us -> 27.5 us  [partner(): lax.ppermute(array, axis, [(i, i ^ distance) for i in range(lax.axis_size...]
    dynamic_slice x5, local copies, waits for them, and re-layouts: 0.42 us -> 2.78 us  [body(): relative = jnp.stack([by_slice[place ^ d] for d in range(slices)])]
    another operation x7, other arithmetic: 5.27 us -> 6.97 us  [body(): jnp.stack([earlier[d] + far_early, later[d] + far_late])]
    mul x1, other arithmetic: 0.08 us -> 1.34 us  [body(): second * weight]
    add x1, other arithmetic: 1.34 us -> 0.12 us  [body(): chip = own + other]
    another operation x2 -> x0, other arithmetic: 1.22 us -> none  [the longest x1 0.67 us: body(): jnp.stack([1 - core, place]).astype(jnp.int32)]
  transfers between devices with their start and end apart: 11 -> 11, of which waited for: 7 -> 7; matrix products, arithmetic and copies ran while one was open for 6% -> 12% of each run, Pallas kernels for 20% -> 16%
where the time goes in v2:
time: 81.4 us; the launch traced here: 80.2 us
  waiting for transfers between devices  27.5 us (34%)
  Pallas kernels  16.4 us (20%)
  other arithmetic  13.9 us (17%)
  starting transfers between devices  12.7 us (16%)
  local copies, waits for them, and re-layouts  8.79 us (11%)
  between operations  0.82 us (1%)
    ppermute x11, waiting for transfers between devices, partner(): lax.ppermute(array, axis, [(i, i ^ distance) for i in range(lax.axis_size...  27.5 us
    ppermute x11, starting transfers between devices, partner(): lax.ppermute(array, axis, [(i, i ^ distance) for i in range(lax.axis_size...  12.7 us
    pallas_call x1, Pallas kernels, local_grads(): pl.pallas_call(functools.partial(local_kernel, first_head, heads), in_spe...  11.8 us
    another operation x7, other arithmetic, body(): jnp.stack([earlier[d] + far_early, later[d] + far_late])  6.97 us
    unnamed x24, local copies, waits for them, and re-layouts  4.93 us
    pallas_call x1, Pallas kernels, finish(): pl.pallas_call(functools.partial(cross_kernel, len(local)), in_specs=[VME...  3.03 us
    dynamic_slice x5, local copies, waits for them, and re-layouts, body(): relative = jnp.stack([by_slice[place ^ d] for d in range(slices)])  2.78 us
    pallas_call x2, Pallas kernels, device_states(): pl.pallas_call(functools.partial(state_kernel, half), in_specs=[VMEM] * 4...  1.64 us
  transfers between devices with their start and end apart: 11, of which 7 were waited for; matrix products, arithmetic and copies ran while one was open for 12% of the time, Pallas kernels for 16%

profile of v2, /device:TPU:1, one launch (start us, length us, event | category | flops | bytes accessed | tf_op | source)
XLA Modules:
  0.0 80.2 jit_solution(8473840736413369561)
XLA Ops:
  0.6 0.0 copy-start
  0.6 1.2 %copy-done = bf16[256,2048]{1,0:T(8,128)(2,1)S(1)} copy-done((bf16[256,2048]{1,0:T(8,128)(2,1)S(1)}, bf16[256,2048]{1,0:T(8,128)(2,1)}, u32[]{:S(2)}) %copy-start) | copy-done | bytes 1048600
  1.9 0.0 copy-start.2
  1.9 1.2 %copy-done.2 = bf16[256,2048]{1,0:T(8,128)(2,1)S(1)} copy-done((bf16[256,2048]{1,0:T(8,128)(2,1)S(1)}, bf16[256,2048]{1,0:T(8,128)(2,1)}, u32[]{:S(2)}) %copy-start.2) | copy-done | bytes 1048600
  3.1 0.0 copy-start.4
  3.1 1.2 %copy-done.4 = bf16[256,2048]{1,0:T(8,128)(2,1)S(1)} copy-done((bf16[256,2048]{1,0:T(8,128)(2,1)S(1)}, bf16[256,2048]{1,0:T(8,128)(2,1)}, u32[]{:S(2)}) %copy-start.4) | copy-done | bytes 1048600
  4.3 1.2 %copy-done.6 = bf16[256,2048]{1,0:T(8,128)(2,1)S(1)} copy-done((bf16[256,2048]{1,0:T(8,128)(2,1)S(1)}, bf16[256,2048]{1,0:T(8,128)(2,1)}, u32[]{:S(2)}) %copy-start.6) | copy-done | bytes 1048600
  5.5 0.8 %states_1.1 = f32[4,2,2,128,128]{4,3,2,1,0:T(8,128)S(1)} custom-call(bf16[256,2048]{1,0:T(8,128)(2,1)S(1)} %copy-done.6, bf16[256,2048]{1,0:T(8,128)(2,1)S(1)} %copy-done, bf16[256,2048]{1,0:T(8,128)(2,1)S(1)} %copy-done.2, bf16[256,2048]{1,0:T(8,128)(2,1)S(1)} %copy-done.4), custom_call_target="tpu_custom_call" | custom-call | flops 134217728 | bytes 3145728 | tf_op jit(solution)/shard_map/states_1/pallas_call | solution.py:61
  6.4 0.1 collective-permute-start
  6.4 0.8 %states_0.1 = f32[4,2,2,128,128]{4,3,2,1,0:T(8,128)S(1)} custom-call(bf16[256,2048]{1,0:T(8,128)(2,1)S(1)} %copy-done.6, bf16[256,2048]{1,0:T(8,128)(2,1)S(1)} %copy-done, bf16[256,2048]{1,0:T(8,128)(2,1)S(1)} %copy-done.2, bf16[256,2048]{1,0:T(8,128)(2,1)S(1)} %copy-done.4), custom_call_target="tpu_custom_call" | custom-call | flops 134217728 | bytes 3145728 | tf_op jit(solution)/shard_map/states_0/pallas_call | solution.py:61
  7.3 0.0 copy-start.8
  7.3 1.8 %collective-permute-done = f32[4,2,2,128,128]{4,3,2,1,0:T(8,128)S(1)} collective-permute-done((f32[4,2,2,128,128]{4,3,2,1,0:T(8,128)S(1)}, f32[4,2,2,128,128]{4,3,2,1,0:T(8,128)S(1)}, u32[]{:S(2)}, u32[]{:S(2)}) %collective-permute-start) | collective-permute-done | bytes 1048608 | tf_op jit(solution)/shard_map/ppermute | solution.py:31
  9.1 0.1 add.141
  9.2 0.9 %slice_bitcast_fusion.1 = (f32[2,2,128,128]{3,2,1,0:T(8,128)}, f32[2,2,128,128]{3,2,1,0:T(8,128)}, f32[2,2,128,128]{3,2,1,0:T(8,128)}) fusion(f32[4,2,2,128,128]{4,3,2,1,0:T(8,128)S(1)} %add.141), kind=kLoop, calls=%fused_computation.7 | loop fusion | bytes 1572864 | tf_op jit(solution)/shard_map/squeeze | solution.py:224
  10.1 3.3 %collective-permute-start.3 = (f32[2,2,128,128]{3,2,1,0:T(8,128)}, f32[2,2,128,128]{3,2,1,0:T(8,128)}, u32[]{:S(2)}, u32[]{:S(2)}) collective-permute-start(f32[2,2,128,128]{3,2,1,0:T(8,128)} %get-tuple-element.45), channel_id=1, source_target_pairs={{0,6},{2,4},{4,2},{6,0},{8,14},{10,12},{12,10},{14,8},{16,22},{18,... | collective-permute-start | bytes 786440 | tf_op jit(solution)/shard_map/ppermute | solution.py:31
  13.4 0.2 collective-permute-start.2
  13.6 0.1 collective-permute-start.1
  13.7 0.0 copy-done.8
  13.8 0.7 copy.29
  14.4 0.7 copy.32
  15.1 0.7 copy.31
  15.8 0.7 copy.30
  16.5 0.9 %multiply_reduce_fusion.19 = (f32[2]{0:T(128)}, f32[2]{0:T(128)}, f32[2]{0:T(128)}, f32[2]{0:T(128)}, f32[2]{0:T(128)}, /*index=5*/f32[2]{0:T(128)}, f32[2]{0:T(128)}, f32[2]{0:T(128)}, f32[2]{0:T(128)}) fusion(f32[]{:T(128)S(6)} %convert_element_type.38, f32[2,11]{1,0:T(2,128)S(1)} %get-tuple-element.54, f32[]{:T(128)S(6)} %sub.52, ...), kind=kLoop, calls=%fused_computation.74 | loop fusion | flops 18 | bytes 124 | tf_op jit(solution)/shard_map/mul | solution.py:233
  17.4 2.6 %collective-permute-done.3 = f32[2,2,128,128]{3,2,1,0:T(8,128)} collective-permute-done((f32[2,2,128,128]{3,2,1,0:T(8,128)}, f32[2,2,128,128]{3,2,1,0:T(8,128)}, u32[]{:S(2)}, u32[]{:S(2)}) %collective-permute-start.3) | collective-permute-done | bytes 262176 | tf_op jit(solution)/shard_map/ppermute | solution.py:31
  20.0 6.0 %collective-permute-done.2 = f32[2,2,128,128]{3,2,1,0:T(8,128)S(1)} collective-permute-done((f32[2,2,128,128]{3,2,1,0:T(8,128)}, f32[2,2,128,128]{3,2,1,0:T(8,128)S(1)}, u32[]{:S(2)}, u32[]{:S(2)}) %collective-permute-start.2) | collective-permute-done | bytes 262176 | tf_op jit(solution)/shard_map/ppermute | solution.py:31
  26.1 0.0 collective-permute-done.1
  26.1 1.1 %fusion.2 = f32[2,2,128,128]{3,2,1,0:T(8,128)S(1)} fusion(f32[2,2,128,128]{3,2,1,0:T(8,128)} %collective-permute-done.3, f32[2,2,128,128]{3,2,1,0:T(8,128)S(1)} %collective-permute-done.2, f32[2,2,128,128]{3,2,1,0:T(8,128)} %collective-permute-done.1, f32[4,2,2,128,128]{4,3,2,1,0:T(8,128)S(1)} %add.141), kind=kLoop, calls=%fused_computation.6 | loop fusion | flops 196608 | bytes 1310720 | tf_op jit(solution)/shard_map/add | solution.py:235
  27.2 0.7 select_bitcast_fusion.1
  27.9 3.5 %collective-permute-start.6 = (f32[2,128,128]{2,1,0:T(8,128)S(1)}, f32[2,128,128]{2,1,0:T(8,128)}, u32[]{:S(2)}, u32[]{:S(2)}) collective-permute-start(f32[2,128,128]{2,1,0:T(8,128)S(1)} %get-tuple-element.49), channel_id=1, source_target_pairs={{0,24},{2,26},{4,28},{6,30},{8,16},{10,18},{12,20},{14,22},{16,8},... | collective-permute-start | bytes 393224 | tf_op jit(solution)/shard_map/ppermute | solution.py:31
  31.4 0.0 collective-permute-start.5
  31.4 0.3 collective-permute-start.4
  31.7 1.3 %multiply_bitcast_fusion.1 = (f32[4,1,2]{0,2,1:T(2,128)}, f32[4,2,1]{0,1,2:T(2,128)S(1)}) fusion(f32[]{:T(128)S(6)} %convert_element_type.48, f32[1,2,11]{0,1,2:T(2,128)} %copy.32, f32[1,2,11]{0,1,2:T(2,128)} %copy.31, f32[1,2,11]{0,1,2:T(2,128)} %copy.30, f32[1,2,11]{0,1,2:T(2,128)} %copy.29), kind=kLoop, calls=%fused_computation.51 | loop fusion | flops 32 | bytes 420 | tf_op jit(solution)/shard_map/mul | solution.py:261
  33.0 0.4 multiply_reduce_fusion.17
  33.4 6.1 %collective-permute-done.4 = f32[2,128,128]{2,1,0:T(8,128)} collective-permute-done((f32[2,128,128]{2,1,0:T(8,128)}, f32[2,128,128]{2,1,0:T(8,128)}, u32[]{:S(2)}, u32[]{:S(2)}) %collective-permute-start.4) | collective-permute-done | bytes 131104 | tf_op jit(solution)/shard_map/ppermute | solution.py:31
  39.5 0.0 collective-permute-done.6
  39.5 2.7 %collective-permute-done.5 = f32[2,128,128]{2,1,0:T(8,128)} collective-permute-done((f32[2,128,128]{2,1,0:T(8,128)S(1)}, f32[2,128,128]{2,1,0:T(8,128)}, u32[]{:S(2)}, u32[]{:S(2)}) %collective-permute-start.5) | collective-permute-done | bytes 131104 | tf_op jit(solution)/shard_map/ppermute | solution.py:31
  42.2 2.1 %add_bitcast_fusion.3 = (f32[1,2,128,128]{3,2,1,0:T(8,128)S(1)}, f32[2,128,128]{2,1,0:T(8,128)S(1)}, f32[1,2,128,128]{3,2,1,0:T(8,128)}, f32[2,128,128]{2,1,0:T(8,128)S(1)}) fusion(f32[2,2,128,128]{3,2,1,0:T(8,128)} %collective-permute-done.1, f32[2,2,128,128]{3,2,1,0:T(8,128)S(1)} %collective-permute-done.2, f32[2,2,128,128]{3,2,1,0:T(8,128)} %collective-permute-done.3, ...), kind=kLoop, calls=%fused_computation.38 | loop fusion | flops 720896 | bytes 1704000 | tf_op jit(solution)/shard_map/stack | solution.py:255
  44.3 1.2 %fusion.10 = (f32[1,2,128,128]{3,2,1,0:T(8,128)S(1)}, f32[1,2,128,128]{3,2,1,0:T(8,128)S(1)}) fusion(f32[2,128,128]{2,1,0:T(8,128)S(1)} %get-tuple-element.32, f32[2,2,128,128]{3,2,1,0:T(8,128)} %collective-permute-done.3, f32[2]{0:T(128)} %get-tuple-element.13, f32[2]{0:T(128)S(1)} %get-tuple-element.62, f32[2,2,128,128]{3,2,1,0:T(8,128)} %collective-permute-done.1, ...), kind=kLoop, calls=%fused_computation.33 | loop fusion | flops 327680 | bytes 1310752 | tf_op jit(solution)/shard_map/stack | solution.py:255
  45.5 0.0 copy-start.9
  45.5 0.7 pad_maximum_fusion.2
  46.2 1.1 %collective-permute-start.8 = (f32[2,2,128,128]{3,2,1,0:T(8,128)}, f32[2,2,128,128]{3,2,1,0:T(8,128)}, u32[]{:S(2)}, u32[]{:S(2)}) collective-permute-start(f32[2,2,128,128]{3,2,1,0:T(8,128)} %pad_maximum_fusion.2), channel_id=1, source_target_pairs={{0,4},{2,6},{4,0},{6,2},{8,12},{10,14},{12,8},{14,10},{16,20},{18,... | collective-permute-start | bytes 786440 | tf_op jit(solution)/shard_map/ppermute | solution.py:31
  47.4 1.1 %add_bitcast_fusion.1 = (f32[1,2,128,128]{3,2,1,0:T(8,128)S(1)}, f32[1,2,128,128]{3,2,1,0:T(8,128)S(1)}) fusion(f32[2,128,128]{2,1,0:T(8,128)S(1)} %get-tuple-element.32, f32[4,2,2,128,128]{4,3,2,1,0:T(8,128)S(1)} %add.141, f32[2,2,128,128]{3,2,1,0:T(8,128)S(1)} %collective-permute-done.2, f32[2,2,128,128]{3,2,1,0:T(8,128)} %collective-permute-done.3, ...), kind=kLoop, calls=%fused_computation.35 | loop fusion | flops 393216 | bytes 1310752 | tf_op jit(solution)/shard_map/stack | solution.py:255
  48.5 0.7 pad_maximum_fusion.1
  49.2 0.1 collective-permute-start.7
  49.3 0.0 copy-done.10
  49.3 0.0 copy-done.11
  49.3 1.1 %fusion.6 = (f32[1,2,128,128]{3,2,1,0:T(8,128)S(1)}, f32[1,2,128,128]{3,2,1,0:T(8,128)S(1)}) fusion(f32[2,128,128]{2,1,0:T(8,128)S(1)} %get-tuple-element.32, f32[2,2,128,128]{3,2,1,0:T(8,128)S(1)} %collective-permute-done.2, f32[2]{0:T(128)S(1)} %copy-done.10, f32[2]{0:T(128)S(1)} %get-tuple-element.60, f32[2,2,128,128]{3,2,1,0:T(8,128)} %collective-permute-done.1, ...), kind=kLoop, calls=%fused_computation.27 | loop fusion | flops 327680 | bytes 1310752 | tf_op jit(solution)/shard_map/stack | solution.py:255
  50.4 1.5 %collective-permute-start.9 = (f32[2,2,128,128]{3,2,1,0:T(8,128)S(1)}, f32[2,2,128,128]{3,2,1,0:T(8,128)S(1)}, u32[]{:S(2)}, u32[]{:S(2)}) collective-permute-start(f32[2,2,128,128]{3,2,1,0:T(8,128)S(1)} %pad_maximum_fusion.3), channel_id=1, source_target_pairs={{0,6},{2,4},{4,2},{6,0},{8,14},{10,12},{12,10},{14,8},{16,22},{18,... | collective-permute-start | bytes 786440 | tf_op jit(solution)/shard_map/ppermute | solution.py:31
  51.9 0.0 copy-done.9
  51.9 0.1 copy.34
  52.0 0.1 copy.33
  52.1 0.9 %maximum_bitcast_fusion = f32[1,2,2,128,128]{4,3,2,1,0:T(8,128)S(1)} fusion(f32[1,2,128,128]{3,2,1,0:T(8,128)} %get-tuple-element.41, f32[1,2,128,128]{3,2,1,0:T(8,128)S(1)} %get-tuple-element.31), kind=kLoop, calls=%fused_computation.10 | loop fusion | flops 65536 | bytes 524288 | tf_op jit(solution)/shard_map/stack | solution.py:257
  53.1 0.0 collective-permute-done.8
  53.1 2.7 %collective-permute-done.7 = f32[2,2,128,128]{3,2,1,0:T(8,128)} collective-permute-done((f32[2,2,128,128]{3,2,1,0:T(8,128)}, f32[2,2,128,128]{3,2,1,0:T(8,128)}, u32[]{:S(2)}, u32[]{:S(2)}) %collective-permute-start.7) | collective-permute-done | bytes 262176 | tf_op jit(solution)/shard_map/ppermute | solution.py:31
  55.8 5.5 %collective-permute-done.9 = f32[2,2,128,128]{3,2,1,0:T(8,128)S(1)} collective-permute-done((f32[2,2,128,128]{3,2,1,0:T(8,128)S(1)}, f32[2,2,128,128]{3,2,1,0:T(8,128)S(1)}, u32[]{:S(2)}, u32[]{:S(2)}) %collective-permute-start.9) | collective-permute-done | bytes 262176 | tf_op jit(solution)/shard_map/ppermute | solution.py:31
  61.4 1.4 %multiply_add_fusion = (f32[4,2,2,128,128]{4,3,2,1,0:T(8,128)S(1)}, f32[4,2,2,128,128]{4,3,2,1,0:T(8,128)S(1)}) fusion(f32[4,2,2,128,128]{4,3,2,1,0:T(8,128)S(1)} %states_0.1, f32[1,2,2,128,128]{4,3,2,1,0:T(8,128)S(1)} %bitcast.127, f32[1,2,2,128,128]{4,3,2,1,0:T(8,128)} %bitcast.24, f32[1,2,2,128,128]{4,3,2,1,0:T(8,128)} %bitcast.21, ...), kind=kLoop, calls=%fused_computation.1 | loop fusion | flops 1835008 | bytes 5243008 | tf_op jit(solution)/shard_map/add | solution.py:262
  62.8 2.5 %collective-permute-start.10 = (f32[4,2,2,128,128]{4,3,2,1,0:T(8,128)S(1)}, f32[4,2,2,128,128]{4,3,2,1,0:T(8,128)S(1)}, u32[]{:S(2)}, u32[]{:S(2)}) collective-permute-start(f32[4,2,2,128,128]{4,3,2,1,0:T(8,128)S(1)} %get-tuple-element.43), channel_id=1, source_target_pairs={{0,1},{1,0},{2,3},{3,2},{4,5},{5,4},{6,7},{7,6},{8,9},{9,8},{10,11... | collective-permute-start | bytes 3145736 | tf_op jit(solution)/shard_map/ppermute | solution.py:31
  65.3 0.0 copy-done.1
  65.3 0.0 copy-done.3
  65.3 0.0 copy-done.5
  65.3 0.0 copy-done.7
  65.4 11.8 %local_0.1 = (f32[256,2048]{1,0:T(8,128)S(1)}, f32[256,2048]{1,0:T(8,128)S(1)}, f32[256,2048]{1,0:T(8,128)S(1)}) custom-call(f32[16,11]{1,0:T(8,128)S(1)} %multiply_multiply_fusion.scale_ref, bf16[256,2048]{1,0:T(8,128)(2,1)S(1)} %copy-done.7, bf16[256,2048]{1,0:T(8,128)(2,1)S(1)} %copy-done.1, bf16[256,2048]{1,0:T(8,128)(2,1)S(1)} %copy-done.3, ...), custom_call_target="tpu_custom_call" | custom-call | flops 1610612736 | bytes 10485760 | tf_op jit(solution)/shard_map/local_0/pallas_call | solution.py:122
  77.1 0.0 collective-permute-done.10.other_ref
  77.2 3.0 %finish.1 = (bf16[256,2048]{1,0:T(8,128)(2,1)}, bf16[256,2048]{1,0:T(8,128)(2,1)}, bf16[256,2048]{1,0:T(8,128)(2,1)}) custom-call(f32[4,2,2,128,128]{4,3,2,1,0:T(8,128)S(1)} %get-tuple-element.44.mine_ref, f32[4,2,2,128,128]{4,3,2,1,0:T(8,128)S(1)} %collective-permute-done.10.other_ref, bf16[256,2048]{1,0:T(8,128)(2,1)S(1)} %copy-done.1, ...), custom_call_target="tpu_custom_call" | custom-call | flops 805306368 | bytes 12582912 | tf_op jit(solution)/shard_map/finish/pallas_call | solution.py:175
  (13 shorter events, 0.1 us)
Async XLA Ops:
  0.6 1.2 %copy-start = (bf16[256,2048]{1,0:T(8,128)(2,1)S(1)}, bf16[256,2048]{1,0:T(8,128)(2,1)}, u32[]{:S(2)}) copy-start(bf16[256,2048]{1,0:T(8,128)(2,1)} %k_ref.7) | copy-start | bytes 3145732
  1.9 1.2 %copy-start.2 = (bf16[256,2048]{1,0:T(8,128)(2,1)S(1)}, bf16[256,2048]{1,0:T(8,128)(2,1)}, u32[]{:S(2)}) copy-start(bf16[256,2048]{1,0:T(8,128)(2,1)} %v_ref.7) | copy-start | bytes 3145732
  3.1 1.2 %copy-start.4 = (bf16[256,2048]{1,0:T(8,128)(2,1)S(1)}, bf16[256,2048]{1,0:T(8,128)(2,1)}, u32[]{:S(2)}) copy-start(bf16[256,2048]{1,0:T(8,128)(2,1)} %o_ref.7) | copy-start | bytes 3145732
  4.3 1.2 %copy-start.6 = (bf16[256,2048]{1,0:T(8,128)(2,1)S(1)}, bf16[256,2048]{1,0:T(8,128)(2,1)}, u32[]{:S(2)}) copy-start(bf16[256,2048]{1,0:T(8,128)(2,1)} %q_ref.5) | copy-start | bytes 3145732
  6.4 2.7 %collective-permute-start = (f32[4,2,2,128,128]{4,3,2,1,0:T(8,128)S(1)}, f32[4,2,2,128,128]{4,3,2,1,0:T(8,128)S(1)}, u32[]{:S(2)}, u32[]{:S(2)}) collective-permute-start(f32[4,2,2,128,128]{4,3,2,1,0:T(8,128)S(1)} %states_1.1), channel_id=1, source_target_pairs={{0,1},{1,0},{2,3},{3,2},{4,5},{5,4},{6,7},{7,6},{8,9},{9,8},{10,11... | collective-permute-start | bytes 3145736 | tf_op jit(solution)/shard_map/ppermute | solution.py:31
  7.3 6.4 %copy-start.8 = (f32[16,11]{1,0:T(8,128)S(1)}, f32[16,11]{1,0:T(8,128)}, u32[]{:S(2)}) copy-start(f32[16,11]{1,0:T(8,128)} %param.9) | copy-start | bytes 2116
  10.1 9.9 %collective-permute-start.3 = (f32[2,2,128,128]{3,2,1,0:T(8,128)}, f32[2,2,128,128]{3,2,1,0:T(8,128)}, u32[]{:S(2)}, u32[]{:S(2)}) collective-permute-start(f32[2,2,128,128]{3,2,1,0:T(8,128)} %get-tuple-element.45), channel_id=1, source_target_pairs={{0,6},{2,4},{4,2},{6,0},{8,14},{10,12},{12,10},{14,8},{16,22},{18,... | collective-permute-start | bytes 786440 | tf_op jit(solution)/shard_map/ppermute | solution.py:31
  13.4 12.7 %collective-permute-start.2 = (f32[2,2,128,128]{3,2,1,0:T(8,128)}, f32[2,2,128,128]{3,2,1,0:T(8,128)S(1)}, u32[]{:S(2)}, u32[]{:S(2)}) collective-permute-start(f32[2,2,128,128]{3,2,1,0:T(8,128)} %get-tuple-element.46), channel_id=1, source_target_pairs={{0,4},{2,6},{4,0},{6,2},{8,12},{10,14},{12,8},{14,10},{16,20},{18,... | collective-permute-start | bytes 786440 | tf_op jit(solution)/shard_map/ppermute | solution.py:31
  13.6 12.5 %collective-permute-start.1 = (f32[2,2,128,128]{3,2,1,0:T(8,128)}, f32[2,2,128,128]{3,2,1,0:T(8,128)}, u32[]{:S(2)}, u32[]{:S(2)}) collective-permute-start(f32[2,2,128,128]{3,2,1,0:T(8,128)} %get-tuple-element.47), channel_id=1, source_target_pairs={{0,2},{2,0},{4,6},{6,4},{8,10},{10,8},{12,14},{14,12},{16,18},{18,... | collective-permute-start | bytes 786440 | tf_op jit(solution)/shard_map/ppermute | solution.py:31
  27.9 11.6 %collective-permute-start.6 = (f32[2,128,128]{2,1,0:T(8,128)S(1)}, f32[2,128,128]{2,1,0:T(8,128)}, u32[]{:S(2)}, u32[]{:S(2)}) collective-permute-start(f32[2,128,128]{2,1,0:T(8,128)S(1)} %get-tuple-element.49), channel_id=1, source_target_pairs={{0,24},{2,26},{4,28},{6,30},{8,16},{10,18},{12,20},{14,22},{16,8},... | collective-permute-start | bytes 393224 | tf_op jit(solution)/shard_map/ppermute | solution.py:31
  31.4 10.8 %collective-permute-start.5 = (f32[2,128,128]{2,1,0:T(8,128)S(1)}, f32[2,128,128]{2,1,0:T(8,128)}, u32[]{:S(2)}, u32[]{:S(2)}) collective-permute-start(f32[2,128,128]{2,1,0:T(8,128)S(1)} %get-tuple-element.49), channel_id=1, source_target_pairs={{0,16},{2,18},{4,20},{6,22},{8,24},{10,26},{12,28},{14,30},{16,0},... | collective-permute-start | bytes 393224 | tf_op jit(solution)/shard_map/ppermute | solution.py:31
  31.4 8.1 %collective-permute-start.4 = (f32[2,128,128]{2,1,0:T(8,128)}, f32[2,128,128]{2,1,0:T(8,128)}, u32[]{:S(2)}, u32[]{:S(2)}) collective-permute-start(f32[2,128,128]{2,1,0:T(8,128)} %get-tuple-element.48), channel_id=1, source_target_pairs={{0,8},{2,10},{4,12},{6,14},{8,0},{10,2},{12,4},{14,6},{16,24},{18,... | collective-permute-start | bytes 393224 | tf_op jit(solution)/shard_map/ppermute | solution.py:31
  44.3 5.0 %copy-start.10 = (f32[2]{0:T(128)S(1)}, f32[2]{0:T(128)}, u32[]{:S(2)}) copy-start(f32[2]{0:T(128)} %get-tuple-element.15) | copy-start | bytes 28
  44.3 5.0 %copy-start.11 = (f32[2]{0:T(128)S(1)}, f32[2]{0:T(128)}, u32[]{:S(2)}) copy-start(f32[2]{0:T(128)} %get-tuple-element.16) | copy-start | bytes 28
  45.5 6.4 %copy-start.9 = (f32[4,1,2]{0,2,1:T(2,128)S(1)}, f32[4,1,2]{0,2,1:T(2,128)}, u32[]{:S(2)}) copy-start(f32[4,1,2]{0,2,1:T(2,128)} %get-tuple-element.29) | copy-start | bytes 100
  46.2 6.8 %collective-permute-start.8 = (f32[2,2,128,128]{3,2,1,0:T(8,128)}, f32[2,2,128,128]{3,2,1,0:T(8,128)}, u32[]{:S(2)}, u32[]{:S(2)}) collective-permute-start(f32[2,2,128,128]{3,2,1,0:T(8,128)} %pad_maximum_fusion.2), channel_id=1, source_target_pairs={{0,4},{2,6},{4,0},{6,2},{8,12},{10,14},{12,8},{14,10},{16,20},{18,... | collective-permute-start | bytes 786440 | tf_op jit(solution)/shard_map/ppermute | solution.py:31
  49.2 6.6 %collective-permute-start.7 = (f32[2,2,128,128]{3,2,1,0:T(8,128)}, f32[2,2,128,128]{3,2,1,0:T(8,128)}, u32[]{:S(2)}, u32[]{:S(2)}) collective-permute-start(f32[2,2,128,128]{3,2,1,0:T(8,128)} %pad_maximum_fusion.1), channel_id=1, source_target_pairs={{0,2},{2,0},{4,6},{6,4},{8,10},{10,8},{12,14},{14,12},{16,18},{18,... | collective-permute-start | bytes 786440 | tf_op jit(solution)/shard_map/ppermute | solution.py:31
  50.4 10.9 %collective-permute-start.9 = (f32[2,2,128,128]{3,2,1,0:T(8,128)S(1)}, f32[2,2,128,128]{3,2,1,0:T(8,128)S(1)}, u32[]{:S(2)}, u32[]{:S(2)}) collective-permute-start(f32[2,2,128,128]{3,2,1,0:T(8,128)S(1)} %pad_maximum_fusion.3), channel_id=1, source_target_pairs={{0,6},{2,4},{4,2},{6,0},{8,14},{10,12},{12,10},{14,8},{16,22},{18,... | collective-permute-start | bytes 786440 | tf_op jit(solution)/shard_map/ppermute | solution.py:31
  61.3 4.0 %copy-start.1 = (bf16[256,2048]{1,0:T(8,128)(2,1)S(1)}, bf16[256,2048]{1,0:T(8,128)(2,1)}, u32[]{:S(2)}) copy-start(bf16[256,2048]{1,0:T(8,128)(2,1)} %k_ref.7) | copy-start | bytes 3145732
  61.4 4.0 %copy-start.3 = (bf16[256,2048]{1,0:T(8,128)(2,1)S(1)}, bf16[256,2048]{1,0:T(8,128)(2,1)}, u32[]{:S(2)}) copy-start(bf16[256,2048]{1,0:T(8,128)(2,1)} %v_ref.7) | copy-start | bytes 3145732
  61.4 4.0 %copy-start.5 = (bf16[256,2048]{1,0:T(8,128)(2,1)S(1)}, bf16[256,2048]{1,0:T(8,128)(2,1)}, u32[]{:S(2)}) copy-start(bf16[256,2048]{1,0:T(8,128)(2,1)} %o_ref.7) | copy-start | bytes 3145732
  61.4 4.0 %copy-start.7 = (bf16[256,2048]{1,0:T(8,128)(2,1)S(1)}, bf16[256,2048]{1,0:T(8,128)(2,1)}, u32[]{:S(2)}) copy-start(bf16[256,2048]{1,0:T(8,128)(2,1)} %q_ref.5) | copy-start | bytes 3145732
  62.8 14.4 %collective-permute-start.10 = (f32[4,2,2,128,128]{4,3,2,1,0:T(8,128)S(1)}, f32[4,2,2,128,128]{4,3,2,1,0:T(8,128)S(1)}, u32[]{:S(2)}, u32[]{:S(2)}) collective-permute-start(f32[4,2,2,128,128]{4,3,2,1,0:T(8,128)S(1)} %get-tuple-element.43), channel_id=1, source_target_pairs={{0,1},{1,0},{2,3},{3,2},{4,5},{5,4},{6,7},{7,6},{8,9},{9,8},{10,11... | collective-permute-start | bytes 3145736 | tf_op jit(solution)/shard_map/ppermute | solution.py:31

commit v3 on v2

v3 whole, which is shorter than its diff:
```python
import functools

import jax
import jax.numpy as jnp
from jax import lax
from jax.experimental import pallas as pl
from jax.experimental.pallas import tpu as pltpu
from jax.sharding import PartitionSpec as P

DH = 128
BLOCK = 128
EXTRA = 16
TOP = 14.0
F32 = jnp.float32
BF16 = jnp.bfloat16
F16 = jnp.float16
NT = (((1,), (1,)), ((), ()))
TN = (((0,), (0,)), ((), ()))
VMEM = pl.BlockSpec(memory_space=pltpu.VMEM)
SMEM = pl.BlockSpec(memory_space=pltpu.SMEM)
HBM = pl.BlockSpec(memory_space=pltpu.HBM)


def dot(a, b, dims=None):
    if dims is None:
        dims = (((1,), (0,)), ((), ()))
    return lax.dot_general(a, b, dims, preferred_element_type=F32)


def split(x):
    hi = x.astype(BF16)
    return hi, (x - hi.astype(F32)).astype(BF16)


def call(kernel, outs, args, specs=None, out_specs=None, scratch=(), flops=0, limit=2):
    moved = sum(x.size * x.dtype.itemsize for x in args)
    return pl.pallas_call(
        kernel,
        in_specs=specs or [VMEM] * len(args),
        out_specs=out_specs or [VMEM] * len(outs),
        out_shape=list(outs),
        scratch_shapes=list(scratch),
        compiler_params=pltpu.CompilerParams(vmem_limit_bytes=limit << 20),
        cost_estimate=pl.CostEstimate(flops=flops, bytes_accessed=moved, transcendentals=0),
    )(*args)


def partner(array, axis, distance):
    return lax.ppermute(array, axis, [(i, i ^ distance) for i in range(lax.axis_size(axis))])


def narrow(array, axis, distance):
    return partner(array.astype(F16), axis, distance).astype(F32)


def pack(out_ref, values):
    rows = 0
    marks = []
    for value in values:
        most = jnp.maximum(jnp.max(jnp.abs(value)), 1e-30)
        power = TOP - jnp.ceil(jnp.log2(jnp.full((8, DH), most, F32)))
        flat = value.reshape(-1, DH)
        factor = jnp.exp2(power)[:1]
        out_ref[rows : rows + flat.shape[0]] = flat * factor
        rows += flat.shape[0]
        marks.append(power)
    for i in range(EXTRA // 8):
        out_ref[rows + 8 * i : rows + 8 * i + 8] = marks[min(i, len(marks) - 1)]


def unpack(ref, shape, count):
    size = (ref.shape[0] - EXTRA) // count
    out = []
    for i in range(count):
        factor = jnp.exp2(-ref[count * size + 8 * i : count * size + 8 * i + 1])
        out.append((ref[i * size : (i + 1) * size] * factor).reshape(shape))
    return out


def column(half, d, slices, width):
    core = lax.axis_index("head") ^ half
    place = (lax.axis_index("seq") & (slices - 1)) ^ d
    return pl.multiple_of((core * slices + place) * (width * DH), DH)


def state_kernel(half, *refs):
    srcs, (out_ref, q_ref, k_ref, v_ref, o_ref), sems = refs[:4], refs[4:9], refs[9]
    slices, _, width = out_ref.shape[:3]
    held = (q_ref, k_ref, v_ref, o_ref)
    copies = []
    for d in range(slices):
        cols = pl.ds(column(half, d, slices, width), width * DH)
        for i in range(4):
            copy = pltpu.make_async_copy(srcs[i].at[:, cols], held[i].at[d], sems.at[d, i])
            copy.start()
            copies.append(copy)
    for d in range(slices):
        for i in range(4):
            copies[4 * d + i].wait()
        for j in range(width):
            cols = slice(j * DH, (j + 1) * DH)
            out_ref[d, 0, j] = dot(v_ref[d, :, cols], k_ref[d, :, cols], TN)
            out_ref[d, 1, j] = dot(o_ref[d, :, cols], q_ref[d, :, cols], TN)


def device_states(half, args, slices, width):
    tokens = args[0].shape[0]
    return call(
        functools.partial(state_kernel, half),
        [pltpu.VMEM((slices, 2, width, DH, DH), F32)] + [pltpu.VMEM((slices, tokens, width * DH), BF16)] * 4,
        args,
        specs=[HBM] * 4,
        scratch=[pltpu.SemaphoreType.DMA((slices, 4))],
        flops=4 * slices * width * tokens * DH * DH,
    )


def local_kernel(half, slices, lots, scale_ref, q_ref, k_ref, v_ref, o_ref, out_ref):
    tokens = q_ref.shape[1]
    width = q_ref.shape[2] // DH
    blocks = tokens // BLOCK
    rows = lax.broadcasted_iota(jnp.int32, (BLOCK, BLOCK), 0)
    cols = lax.broadcasted_iota(jnp.int32, (BLOCK, BLOCK), 1)

    def blk(n, m=None):
        return slice(n * BLOCK, (n + 1 if m is None else m) * BLOCK)

    def product(left, right, weight, values, n, low, high, mask):
        raw = dot(left[blk(n)], right[blk(low, high)], NT)
        parts, rest = [], []
        for m in range(low, high):
            part = raw[:, blk(m - low)]
            if m == n:
                parts.append(jnp.where(mask, part * weight(0), 0.0).astype(BF16))
            else:
                hi, lo = split(part * weight((m ^ n).bit_length()))
                parts.append(hi)
                rest.append((m, lo))
        out = dot(jnp.concatenate(parts, axis=1) if len(parts) > 1 else parts[0], values[blk(low, high)])
        for m, lo in rest:
            out = out + dot(lo, values[blk(m)])
        return out

    for i, d in enumerate(lots):
        first = column(half, d, slices, width) // DH
        for j in range(width):
            at = slice(j * DH, (j + 1) * DH)
            q, k, v, o = q_ref[d, :, at], k_ref[d, :, at], v_ref[d, :, at], o_ref[d, :, at]

            def weight(level, head=first + j):
                return scale_ref[head, level]

            for n in range(blocks):
                out_ref[i, 2, blk(n), at] = product(k, q, weight, o, n, n, blocks, rows <= cols)
                out_ref[i, 1, blk(n), at] = product(v, o, weight, q, n, n, blocks, rows <= cols)
                out_ref[i, 0, blk(n), at] = product(o, v, weight, k, n, 0, n + 1, rows >= cols)


def local_grads(half, lots, level_scale, held, slices):
    tokens, model = held[0].shape[1:]
    return call(
        functools.partial(local_kernel, half, slices, lots),
        [pltpu.VMEM((len(lots), 3, tokens, model), F32)],
        [level_scale, *held],
        specs=[SMEM] + [VMEM] * 4,
        flops=24 * tokens * BLOCK * len(lots) * model,
    )[0]


def chip_kernel(own_ref, other_ref, keep_ref, *out_refs):
    keep_ref[...] = own_ref[0] + other_ref[0]
    for d, out_ref in enumerate(out_refs, 1):
        pack(out_ref, [own_ref[d, t] + other_ref[d, t] for t in range(2)])


def bit_of(value, index):
    return ((value >> index) & 1).astype(F32)


def head_weight(scale_ref, d, slices, width, j, level):
    return scale_ref[column(0, d, slices, width) // DH + j, level]


def plane_kernel(plane_bits, base, rest, scale_ref, keep_ref, *refs):
    slices = 1 << plane_bits
    parts = refs[: slices - 1]
    near_ref, total_ref = refs[slices - 1], refs[slices]
    outs = refs[slices + 1 :]
    width = keep_ref.shape[1]
    place = lax.axis_index("seq") & (slices - 1)
    got = [[keep_ref[0], keep_ref[1]]] + [unpack(p, (width, DH, DH), 2) for p in parts]
    for t in range(2):
        total_ref[t] = functools.reduce(jnp.add, [g[t] for g in got])
    for j in range(width):
        weights = [head_weight(scale_ref, 0, slices, width, j, base + b) for b in range(plane_bits)]
        for d in range(slices):
            early = jnp.zeros((DH, DH), F32)
            late = jnp.zeros((DH, DH), F32)
            for b in range(plane_bits):
                group = [e for e in range(slices) if (d ^ e).bit_length() == b + 1]
                up = bit_of(place ^ d, b)
                early = early + (up * weights[b]) * functools.reduce(jnp.add, [got[e][0][j] for e in group])
                late = late + ((1.0 - up) * weights[b]) * functools.reduce(jnp.add, [got[e][1][j] for e in group])
            near_ref[d, 0, j] = early
            near_ref[d, 1, j] = late
    far_out(outs, total_ref, rest, slices)


def far_out(outs, total_ref, rest, slices):
    row = lax.axis_index("seq") // slices
    for i, out_ref in enumerate(outs):
        up = bit_of(row, rest - len(outs) + i)
        pack(out_ref, [jnp.where(up > 0, total_ref[1], total_ref[0])])


def merge_kernel(slices, index, level, rest, scale_ref, near_ref, total_ref, got_ref, near_out, total_out, *outs):
    width = total_ref.shape[1]
    row = lax.axis_index("seq") // slices
    up = bit_of(row, index)
    got = unpack(got_ref, (width, DH, DH), 2)
    for j in range(width):
        weight = head_weight(scale_ref, 0, slices, width, j, level)
        for d in range(slices):
            near_out[d, 0, j] = near_ref[d, 0, j] + (up * weight) * got[0][j]
            near_out[d, 1, j] = near_ref[d, 1, j] + ((1.0 - up) * weight) * got[1][j]
    for t in range(2):
        total_out[t] = total_ref[t] + got[t]
    far_out(outs, total_out, rest, slices)


def back_kernel(slices, levels, bits, scale_ref, near_ref, *refs):
    count = len(levels)
    gots, (keep_ref, *outs) = refs[:count], refs[count:]
    width = near_ref.shape[2]
    row = lax.axis_index("seq") // slices
    early = [jnp.zeros((DH, DH), F32)] * width
    late = [jnp.zeros((DH, DH), F32)] * width
    for got_ref, level, bit in zip(gots, levels, bits):
        up = bit_of(row, bit)
        (got,) = unpack(got_ref, (width, DH, DH), 1)
        for j in range(width):
            weight = head_weight(scale_ref, 0, slices, width, j, level)
            early[j] = early[j] + (up * weight) * got[j]
            late[j] = late[j] + ((1.0 - up) * weight) * got[j]
    far = (jnp.stack(early), jnp.stack(late))
    for t in range(2):
        keep_ref[t] = near_ref[0, t] + far[t]
    for d, out_ref in enumerate(outs, 1):
        pack(out_ref, [near_ref[d, t] + far[t] for t in range(2)])


def core_kernel(level, scale_ref, own_ref, other_ref, keep_ref, *refs):
    parts, (mine_ref, theirs_ref) = refs[:-2], refs[-2:]
    slices, _, width = own_ref.shape[:3]
    second = lax.axis_index("head").astype(F32)
    for d in range(slices):
        got = [keep_ref[0], keep_ref[1]] if d == 0 else unpack(parts[d - 1], (width, DH, DH), 2)
        for j in range(width):
            weight = head_weight(scale_ref, d, slices, width, j, level)
            high, low = second * weight, (1.0 - second) * weight
            mine_ref[d, 0, j] = got[0][j] + high * other_ref[d, 0, j]
            mine_ref[d, 1, j] = got[1][j] + low * other_ref[d, 1, j]
            theirs_ref[d, 0, j] = got[0][j] + low * own_ref[d, 0, j]
            theirs_ref[d, 1, j] = got[1][j] + high * own_ref[d, 1, j]


def cross_kernel(where, state_refs, held_refs, local_refs, outs, temps, sems):
    slices, _, width = state_refs[0].shape[:3]
    copies = []
    for half in range(2):
        k_ref, v_ref, o_ref = held_refs[half]
        for d in range(slices):
            part, index = where[half, d]
            for j in range(width):
                cs = slice(j * DH, (j + 1) * DH)
                o, v, k = o_ref[d, :, cs], v_ref[d, :, cs], k_ref[d, :, cs]
                hi, lo = split(state_refs[half][d, 0, j])
                qg = dot(o, hi) + dot(o, lo)
                hi, lo = split(state_refs[half][d, 1, j])
                kg = dot(v, hi) + dot(v, lo)
                vg = dot(k, hi, NT) + dot(k, lo, NT)
                for i, cross in enumerate((qg, kg, vg)):
                    temps[half, d, i, :, cs] = (cross + local_refs[part][index, i, :, cs]).astype(BF16)
            cols = pl.ds(column(half, d, slices, width), width * DH)
            for i in range(3):
                copy = pltpu.make_async_copy(temps.at[half, d, i], outs[i].at[:, cols], sems.at[half * slices + d, i])
                copy.start()
                copies.append(copy)
    for copy in copies:
        copy.wait()


def finish(states, held, local, model):
    slices, tokens, cols = held[0][0].shape
    where, parts = {}, []
    for half, lots, part in local:
        for index, d in enumerate(lots):
            where[half, d] = (len(parts), index)
        parts.append(part)

    def kernel(*refs):
        count = 8 + len(parts)
        ins, (o0, o1, o2, temps, sems) = refs[:count], refs[count:]
        cross_kernel(where, ins[:2], (ins[2:5], ins[5:8]), ins[8:], (o0, o1, o2), temps, sems)

    return call(
        kernel,
        [jax.ShapeDtypeStruct((tokens, model), BF16)] * 3,
        [*states, *held[0][1:], *held[1][1:], *parts],
        out_specs=[HBM] * 3,
        scratch=[pltpu.VMEM((2, slices, 3, tokens, cols), BF16), pltpu.SemaphoreType.DMA((2 * slices, 3))],
        flops=12 * tokens * DH * model,
        limit=6,
    )


def work(queries, key_rows, values, out_grad, level_weights):
    level_ids = jnp.arange(level_weights.shape[1], dtype=F32)
    level_scale = level_weights * jnp.exp2((1.0 - level_ids) / 2.0)[None, :] / jnp.sqrt(F32(DH * BLOCK))
    heads = level_weights.shape[0]
    tokens, model = queries.shape
    chain = lax.axis_size("seq")
    bits = chain.bit_length() - 1
    plane_bits = min(2, bits)
    slices = 1 << plane_bits
    width = heads // (lax.axis_size("head") * slices)
    local_levels = (tokens // BLOCK).bit_length() - 1
    base = local_levels + 2
    rest = bits - plane_bits
    direct = min(2, rest)

    args = [pltpu.with_memory_space_constraint(x, pltpu.HBM) for x in (queries, key_rows, values, out_grad)]
    sent, *held_there = device_states(1, args, slices, width)
    other = partner(sent, "head", 1)
    own, *held_here = device_states(0, args, slices, width)
    held = (held_here, held_there)
    local = []
    lots = [(half, lot) for half in range(2) for lot in (range(slices // 2), range(slices // 2, slices)) if lot]
    for half, lot in lots:
        local.append((half, tuple(lot), local_grads(half, tuple(lot), level_scale, held[half], slices)))

    state = pltpu.VMEM((2, width, DH, DH), F32)
    load = pltpu.VMEM((2 * width * DH + EXTRA, DH), F32)
    single = pltpu.VMEM((width * DH + EXTRA, DH), F32)
    near = pltpu.VMEM((slices, 2, width, DH, DH), F32)

    keep, *outs = call(chip_kernel, [state] + [load] * (slices - 1), [own, other])
    got = []
    for d in range(1, slices):
        got.append(narrow(outs[d - 1], "seq", d))
    sending = direct if rest == direct else 0
    near_sum, total, *outs = call(
        functools.partial(plane_kernel, plane_bits, base, rest),
        [near, state] + [single] * sending,
        [level_scale, keep, *got],
        specs=[SMEM] + [VMEM] * slices,
        limit=4,
    )
    for index in range(rest - direct):
        both = call(lambda ref, out: pack(out, [ref[0], ref[1]]), [load], [total])[0]
        arrived = narrow(both, "seq", slices << index)
        sending = direct if index + 1 == rest - direct else 0
        near_sum, total, *outs = call(
            functools.partial(merge_kernel, slices, index, base + plane_bits + index, rest),
            [near, state] + [single] * sending,
            [level_scale, near_sum, total, arrived],
            specs=[SMEM] + [VMEM] * 3,
        )
    got, levels, which = [], [], []
    for step in range(1, 1 << direct):
        top = step.bit_length() - 1
        got.append(narrow(outs[top], "seq", (slices << (rest - direct)) * step))
        which.append(rest - direct + top)
        levels.append(base + plane_bits + rest - direct + top)
    keep, *outs = call(
        functools.partial(back_kernel, slices, levels, which),
        [state] + [load] * (slices - 1),
        [level_scale, near_sum, *got],
        specs=[SMEM] + [VMEM] * (1 + len(got)),
        limit=4,
    )
    got = []
    for d in range(1, slices):
        got.append(narrow(outs[d - 1], "seq", d))
    mine, theirs = call(
        functools.partial(core_kernel, local_levels + 1),
        [near, near],
        [level_scale, own, other, keep, *got],
        specs=[SMEM] + [VMEM] * (3 + len(got)),
        limit=4,
    )
    theirs = partner(theirs, "head", 1)
    return tuple(finish((mine, theirs), held, local, model))


def solution(mesh):
    rows = P(("seq", "head"), None)
    return jax.shard_map(
        work,
        mesh=mesh,
        in_specs=(rows, rows, rows, rows, P()),
        out_specs=(rows, rows, rows),
        check_vma=False,
    )
```

time: 81.4 us -> 57.6 us (0.71); the launches traced: 80.2 us -> 57.4 us
  other arithmetic: 13.9 us -> 0.32 us
  local copies, waits for them, and re-layouts: 8.79 us -> 0.01 us
  Pallas kernels: 16.4 us -> 24.4 us
  waiting for transfers between devices: 27.5 us -> 20.6 us
  starting transfers between devices: 12.7 us -> 11.2 us
    pallas_call x4 -> x11, Pallas kernels: 16.4 us -> 24.4 us  [call(): pl.pallas_call(kernel, in_specs=specs or [VMEM] * len(args), out_specs=ou...]
    another operation x9 -> x0, other arithmetic: 7.92 us -> none  [the longest x7 6.97 us: body(): jnp.stack([earlier[d] + far_early, later[d] + far_late])]
    ppermute x11, waiting for transfers between devices: 27.5 us -> 20.6 us  [partner(): lax.ppermute(array, axis, [(i, i ^ distance) for i in range(lax.axis_size...]
    unnamed x24 -> x2, local copies, waits for them, and re-layouts: 4.93 us -> 0.01 us
    dynamic_slice x5 -> x0, local copies, waits for them, and re-layouts: 2.78 us -> none  [body(): relative = jnp.stack([by_slice[place ^ d] for d in range(slices)])]
    add x3 -> x0, other arithmetic: 2.67 us -> none  [the longest x1 1.43 us: body(): theirs = partner(states + to_other * own, 'head', 1)]
    mul x4 -> x0, other arithmetic: 2.61 us -> none  [the longest x1 1.34 us: body(): second * weight]
    ppermute x11, starting transfers between devices: 12.7 us -> 11.2 us  [partner(): lax.ppermute(array, axis, [(i, i ^ distance) for i in range(lax.axis_size...]
  transfers between devices with their start and end apart: 11 -> 11, of which waited for: 7 -> 7; matrix products, arithmetic and copies ran while one was open for 12% -> 0% of each run, Pallas kernels for 16% -> 27%
where the time goes in v3:
time: 57.6 us; the launch traced here: 57.4 us
  Pallas kernels  24.4 us (42%)
  waiting for transfers between devices  20.6 us (36%)
  starting transfers between devices  11.2 us (19%)
  between operations  0.83 us (1%)
    pallas_call x11, Pallas kernels, call(): pl.pallas_call(kernel, in_specs=specs or [VMEM] * len(args), out_specs=ou...  24.4 us
    ppermute x11, waiting for transfers between devices, partner(): lax.ppermute(array, axis, [(i, i ^ distance) for i in range(lax.axis_size...  20.6 us
    ppermute x11, starting transfers between devices, partner(): lax.ppermute(array, axis, [(i, i ^ distance) for i in range(lax.axis_size...  11.2 us
  transfers between devices with their start and end apart: 11, of which 7 were waited for; matrix products, arithmetic and copies ran while one was open for 0% of the time, Pallas kernels for 27%

profile of v3, /device:TPU:1, one launch (start us, length us, event | category | flops | bytes accessed | tf_op | source)
XLA Modules:
  0.0 57.4 jit_solution(5014065066241353985)
XLA Ops:
  0.6 2.4 %shard_map.77 = (f32[4,2,2,128,128]{4,3,2,1,0:T(8,128)S(1)}, bf16[4,256,256]{2,1,0:T(8,128)(2,1)S(1)}, bf16[4,256,256]{2,1,0:T(8,128)(2,1)S(1)}, bf16[4,256,256]...) custom-call(bf16[256,2048]{1,0:T(8,128)(2,1)} %refs_0_.3, bf16[256,2048]{1,0:T(8,128)(2,1)} %refs_1_.3, ...), custom_call_target="tpu_custom_call" | custom-call | flops 134217728 | bytes 4194304 | tf_op jit(solution)/shard_map/pallas_call | solution.py:37
  3.0 0.1 collective-permute-start
  3.1 2.4 %shard_map.76 = (f32[4,2,2,128,128]{4,3,2,1,0:T(8,128)S(1)}, bf16[4,256,256]{2,1,0:T(8,128)(2,1)S(1)}, bf16[4,256,256]{2,1,0:T(8,128)(2,1)S(1)}, bf16[4,256,256]...) custom-call(bf16[256,2048]{1,0:T(8,128)(2,1)} %refs_0_.3, bf16[256,2048]{1,0:T(8,128)(2,1)} %refs_1_.3, ...), custom_call_target="tpu_custom_call" | custom-call | flops 134217728 | bytes 4194304 | tf_op jit(solution)/shard_map/pallas_call | solution.py:37
  5.5 0.3 collective-permute-done.other_ref
  5.7 0.0 copy-start
  5.7 0.3 shard_map.78
  6.1 3.5 %collective-permute-start.3 = (f16[528,128]{1,0:T(8,128)(2,1)S(1)}, f16[528,128]{1,0:T(8,128)(2,1)S(1)}, u32[]{:S(2)}, u32[]{:S(2)}) collective-permute-start(f16[528,128]{1,0:T(8,128)(2,1)S(1)} %convert_element_type.56), channel_id=1, source_target_pairs={{0,6},{2,4},{4,2},{6,0},{8,14},{10,12},{12,10},{14,8},{16,22},{18,... | collective-permute-start | bytes 405512 | tf_op jit(solution)/shard_map/ppermute | solution.py:49
  9.6 0.2 collective-permute-start.2
  9.8 0.1 collective-permute-start.1
  9.9 0.0 copy-done
  9.9 3.3 %collective-permute-done.3 = f16[528,128]{1,0:T(8,128)(2,1)S(1)} collective-permute-done((f16[528,128]{1,0:T(8,128)(2,1)S(1)}, f16[528,128]{1,0:T(8,128)(2,1)S(1)}, u32[]{:S(2)}, u32[]{:S(2)}) %collective-permute-start.3) | collective-permute-done | bytes 135200 | tf_op jit(solution)/shard_map/ppermute | solution.py:49
  13.3 3.2 %collective-permute-done.2 = f16[528,128]{1,0:T(8,128)(2,1)S(1)} collective-permute-done((f16[528,128]{1,0:T(8,128)(2,1)S(1)}, f16[528,128]{1,0:T(8,128)(2,1)S(1)}, u32[]{:S(2)}, u32[]{:S(2)}) %collective-permute-start.2) | collective-permute-done | bytes 135200 | tf_op jit(solution)/shard_map/ppermute | solution.py:49
  16.5 0.0 collective-permute-done.1
  16.6 1.6 %shard_map.79 = (f32[4,2,2,128,128]{4,3,2,1,0:T(8,128)S(1)}, f32[2,2,128,128]{3,2,1,0:T(8,128)}, f32[272,128]{1,0:T(8,128)S(1)}, f32[272,128]{1,0:T(8,128)S(1)}) custom-call(f32[16,11]{1,0:T(8,128)S(1)} %multiply_multiply_fusion.scale_ref, f32[2,2,128,128]{3,2,1,0:T(8,128)S(1)} %get-tuple-element.28.keep_ref, f32[528,128]{1,0:T(8,128)S(1)} %convert_element_type.53.refs_0_, ...), custom_call_target="tpu_custom_call" | custom-call | bytes 1073856 | tf_op jit(solution)/shard_map/pallas_call | solution.py:37
  18.2 1.6 %collective-permute-start.4 = (f16[272,128]{1,0:T(8,128)(2,1)S(1)}, f16[272,128]{1,0:T(8,128)(2,1)S(1)}, u32[]{:S(2)}, u32[]{:S(2)}) collective-permute-start(f16[272,128]{1,0:T(8,128)(2,1)S(1)} %convert_element_type.58), channel_id=1, source_target_pairs={{0,8},{2,10},{4,12},{6,14},{8,0},{10,2},{12,4},{14,6},{16,24},{18,... | collective-permute-start | bytes 208904 | tf_op jit(solution)/shard_map/ppermute | solution.py:49
  19.8 2.3 %collective-permute-start.6 = (f16[272,128]{1,0:T(8,128)(2,1)S(1)}, f16[272,128]{1,0:T(8,128)(2,1)S(1)}, u32[]{:S(2)}, u32[]{:S(2)}) collective-permute-start(f16[272,128]{1,0:T(8,128)(2,1)S(1)} %convert_element_type.60), channel_id=1, source_target_pairs={{0,24},{2,26},{4,28},{6,30},{8,16},{10,18},{12,20},{14,22},{16,8},... | collective-permute-start | bytes 208904 | tf_op jit(solution)/shard_map/ppermute | solution.py:49
  22.0 0.2 collective-permute-start.5
  22.2 0.0 collective-permute-done.4
  22.2 3.5 %collective-permute-done.6 = f16[272,128]{1,0:T(8,128)(2,1)S(1)} collective-permute-done((f16[272,128]{1,0:T(8,128)(2,1)S(1)}, f16[272,128]{1,0:T(8,128)(2,1)S(1)}, u32[]{:S(2)}, u32[]{:S(2)}) %collective-permute-start.6) | collective-permute-done | bytes 69664 | tf_op jit(solution)/shard_map/ppermute | solution.py:49
  25.8 3.7 %collective-permute-done.5 = f16[272,128]{1,0:T(8,128)(2,1)S(1)} collective-permute-done((f16[272,128]{1,0:T(8,128)(2,1)S(1)}, f16[272,128]{1,0:T(8,128)(2,1)S(1)}, u32[]{:S(2)}, u32[]{:S(2)}) %collective-permute-start.5) | collective-permute-done | bytes 69664 | tf_op jit(solution)/shard_map/ppermute | solution.py:49
  29.5 1.0 %shard_map.80 = (f32[2,2,128,128]{3,2,1,0:T(8,128)S(1)}, f32[528,128]{1,0:T(8,128)S(1)}, f32[528,128]{1,0:T(8,128)S(1)}, f32[528,128]{1,0:T(8,128)S(1)}) custom-call(f32[16,11]{1,0:T(8,128)S(1)} %multiply_multiply_fusion.scale_ref, f32[4,2,2,128,128]{4,3,2,1,0:T(8,128)S(1)} %get-tuple-element.32.near_ref, f32[272,128]{1,0:T(8,128)S(1)} %convert_element_type.59.refs_0_, ...), custom_call_target="tpu_custom_call" | custom-call | bytes 1467072 | tf_op jit(solution)/shard_map/pallas_call | solution.py:37
  30.5 0.6 collective-permute-start.9
  31.1 1.9 %collective-permute-start.8 = (f16[528,128]{1,0:T(8,128)(2,1)S(1)}, f16[528,128]{1,0:T(8,128)(2,1)S(1)}, u32[]{:S(2)}, u32[]{:S(2)}) collective-permute-start(f16[528,128]{1,0:T(8,128)(2,1)S(1)} %convert_element_type.65), channel_id=1, source_target_pairs={{0,4},{2,6},{4,0},{6,2},{8,12},{10,14},{12,8},{14,10},{16,20},{18,... | collective-permute-start | bytes 405512 | tf_op jit(solution)/shard_map/ppermute | solution.py:49
  33.0 0.3 collective-permute-start.7
  33.3 2.8 %collective-permute-done.9 = f16[528,128]{1,0:T(8,128)(2,1)S(1)} collective-permute-done((f16[528,128]{1,0:T(8,128)(2,1)S(1)}, f16[528,128]{1,0:T(8,128)(2,1)S(1)}, u32[]{:S(2)}, u32[]{:S(2)}) %collective-permute-start.9) | collective-permute-done | bytes 135200 | tf_op jit(solution)/shard_map/ppermute | solution.py:49
  36.2 3.7 %collective-permute-done.8 = f16[528,128]{1,0:T(8,128)(2,1)S(1)} collective-permute-done((f16[528,128]{1,0:T(8,128)(2,1)S(1)}, f16[528,128]{1,0:T(8,128)(2,1)S(1)}, u32[]{:S(2)}, u32[]{:S(2)}) %collective-permute-start.8) | collective-permute-done | bytes 135200 | tf_op jit(solution)/shard_map/ppermute | solution.py:49
  39.9 0.0 collective-permute-done.7
  40.0 0.9 %shard_map.81 = (f32[4,2,2,128,128]{4,3,2,1,0:T(8,128)S(1)}, f32[4,2,2,128,128]{4,3,2,1,0:T(8,128)S(1)}) custom-call(f32[16,11]{1,0:T(8,128)S(1)} %multiply_multiply_fusion.scale_ref, f32[4,2,2,128,128]{4,3,2,1,0:T(8,128)S(1)} %get-tuple-element.26.own_ref, f32[4,2,2,128,128]{4,3,2,1,0:T(8,128)S(1)} %collective-permute-done.other_ref, ...), custom_call_target="tpu_custom_call" | custom-call | bytes 3171008 | tf_op jit(solution)/shard_map/pallas_call | solution.py:37
  40.9 0.6 collective-permute-start.10
  41.4 3.3 %shard_map.85.refs_11_ = f32[2,3,256,256]{3,2,1,0:T(8,128)S(1)} custom-call(f32[16,11]{1,0:T(8,128)S(1)} %multiply_multiply_fusion.scale_ref, bf16[4,256,256]{2,1,0:T(8,128)(2,1)S(1)} %get-tuple-element.48.q_ref, bf16[4,256,256]{2,1,0:T(8,128)(2,1)S(1)} %get-tuple-element.44.k_ref.refs_5_, bf16[4,256,256]{2,1,0:T(8,128)(2,1)S(1)} %get-tuple-element.45.v_ref.refs_6_, ...), custom_call_target="tpu_custom_call" | custom-call | flops 402653184 | bytes 2097856 | tf_op jit(solution)/shard_map/pallas_call | solution.py:37
  44.7 3.3 %shard_map.84.refs_10_ = f32[2,3,256,256]{3,2,1,0:T(8,128)S(1)} custom-call(f32[16,11]{1,0:T(8,128)S(1)} %multiply_multiply_fusion.scale_ref, bf16[4,256,256]{2,1,0:T(8,128)(2,1)S(1)} %get-tuple-element.48.q_ref, bf16[4,256,256]{2,1,0:T(8,128)(2,1)S(1)} %get-tuple-element.44.k_ref.refs_5_, bf16[4,256,256]{2,1,0:T(8,128)(2,1)S(1)} %get-tuple-element.45.v_ref.refs_6_, ...), custom_call_target="tpu_custom_call" | custom-call | flops 402653184 | bytes 2097856 | tf_op jit(solution)/shard_map/pallas_call | solution.py:37
  48.0 3.3 %shard_map.83.refs_9_ = f32[2,3,256,256]{3,2,1,0:T(8,128)S(1)} custom-call(f32[16,11]{1,0:T(8,128)S(1)} %multiply_multiply_fusion.scale_ref, bf16[4,256,256]{2,1,0:T(8,128)(2,1)S(1)} %get-tuple-element.47.q_ref, bf16[4,256,256]{2,1,0:T(8,128)(2,1)S(1)} %get-tuple-element.41.k_ref.refs_2_, bf16[4,256,256]{2,1,0:T(8,128)(2,1)S(1)} %get-tuple-element.42.v_ref.refs_3_, ...), custom_call_target="tpu_custom_call" | custom-call | flops 402653184 | bytes 2097856 | tf_op jit(solution)/shard_map/pallas_call | solution.py:37
  51.3 3.3 %shard_map.82.refs_8_ = f32[2,3,256,256]{3,2,1,0:T(8,128)S(1)} custom-call(f32[16,11]{1,0:T(8,128)S(1)} %multiply_multiply_fusion.scale_ref, bf16[4,256,256]{2,1,0:T(8,128)(2,1)S(1)} %get-tuple-element.47.q_ref, bf16[4,256,256]{2,1,0:T(8,128)(2,1)S(1)} %get-tuple-element.41.k_ref.refs_2_, bf16[4,256,256]{2,1,0:T(8,128)(2,1)S(1)} %get-tuple-element.42.v_ref.refs_3_, ...), custom_call_target="tpu_custom_call" | custom-call | flops 402653184 | bytes 2097856 | tf_op jit(solution)/shard_map/pallas_call | solution.py:37
  54.6 0.0 collective-permute-done.10.refs_1_
  54.6 2.8 %shard_map.86 = (bf16[256,2048]{1,0:T(8,128)(2,1)}, bf16[256,2048]{1,0:T(8,128)(2,1)}, bf16[256,2048]{1,0:T(8,128)(2,1)}) custom-call(f32[4,2,2,128,128]{4,3,2,1,0:T(8,128)S(1)} %get-tuple-element.39.refs_0_, f32[4,2,2,128,128]{4,3,2,1,0:T(8,128)S(1)} %collective-permute-done.10.refs_1_, bf16[4,256,256]{2,1,0:T(8,128)(2,1)S(1)} %get-tuple-element.41.k_ref.refs_2_, ...), custom_call_target="tpu_custom_call" | custom-call | flops 805306368 | bytes 11534336 | tf_op jit(solution)/shard_map/pallas_call | solution.py:37
  (19 shorter events, 0.3 us)
Async XLA Ops:
  3.0 2.7 %collective-permute-start = (f32[4,2,2,128,128]{4,3,2,1,0:T(8,128)S(1)}, f32[4,2,2,128,128]{4,3,2,1,0:T(8,128)S(1)}, u32[]{:S(2)}, u32[]{:S(2)}) collective-permute-start(f32[4,2,2,128,128]{4,3,2,1,0:T(8,128)S(1)} %get-tuple-element.27), channel_id=1, source_target_pairs={{0,1},{1,0},{2,3},{3,2},{4,5},{5,4},{6,7},{7,6},{8,9},{9,8},{10,11... | collective-permute-start | bytes 3145736 | tf_op jit(solution)/shard_map/ppermute | solution.py:49
  5.7 4.2 %copy-start = (f32[16,11]{1,0:T(8,128)S(1)}, f32[16,11]{1,0:T(8,128)}, u32[]{:S(2)}) copy-start(f32[16,11]{1,0:T(8,128)} %param.9) | copy-start | bytes 2116
  6.1 7.2 %collective-permute-start.3 = (f16[528,128]{1,0:T(8,128)(2,1)S(1)}, f16[528,128]{1,0:T(8,128)(2,1)S(1)}, u32[]{:S(2)}, u32[]{:S(2)}) collective-permute-start(f16[528,128]{1,0:T(8,128)(2,1)S(1)} %convert_element_type.56), channel_id=1, source_target_pairs={{0,6},{2,4},{4,2},{6,0},{8,14},{10,12},{12,10},{14,8},{16,22},{18,... | collective-permute-start | bytes 405512 | tf_op jit(solution)/shard_map/ppermute | solution.py:49
  9.6 6.9 %collective-permute-start.2 = (f16[528,128]{1,0:T(8,128)(2,1)S(1)}, f16[528,128]{1,0:T(8,128)(2,1)S(1)}, u32[]{:S(2)}, u32[]{:S(2)}) collective-permute-start(f16[528,128]{1,0:T(8,128)(2,1)S(1)} %convert_element_type.54), channel_id=1, source_target_pairs={{0,4},{2,6},{4,0},{6,2},{8,12},{10,14},{12,8},{14,10},{16,20},{18,... | collective-permute-start | bytes 405512 | tf_op jit(solution)/shard_map/ppermute | solution.py:49
  9.8 6.7 %collective-permute-start.1 = (f16[528,128]{1,0:T(8,128)(2,1)S(1)}, f16[528,128]{1,0:T(8,128)(2,1)S(1)}, u32[]{:S(2)}, u32[]{:S(2)}) collective-permute-start(f16[528,128]{1,0:T(8,128)(2,1)S(1)} %convert_element_type.52), channel_id=1, source_target_pairs={{0,2},{2,0},{4,6},{6,4},{8,10},{10,8},{12,14},{14,12},{16,18},{18,... | collective-permute-start | bytes 405512 | tf_op jit(solution)/shard_map/ppermute | solution.py:49
  18.2 4.0 %collective-permute-start.4 = (f16[272,128]{1,0:T(8,128)(2,1)S(1)}, f16[272,128]{1,0:T(8,128)(2,1)S(1)}, u32[]{:S(2)}, u32[]{:S(2)}) collective-permute-start(f16[272,128]{1,0:T(8,128)(2,1)S(1)} %convert_element_type.58), channel_id=1, source_target_pairs={{0,8},{2,10},{4,12},{6,14},{8,0},{10,2},{12,4},{14,6},{16,24},{18,... | collective-permute-start | bytes 208904 | tf_op jit(solution)/shard_map/ppermute | solution.py:49
  19.8 6.0 %collective-permute-start.6 = (f16[272,128]{1,0:T(8,128)(2,1)S(1)}, f16[272,128]{1,0:T(8,128)(2,1)S(1)}, u32[]{:S(2)}, u32[]{:S(2)}) collective-permute-start(f16[272,128]{1,0:T(8,128)(2,1)S(1)} %convert_element_type.60), channel_id=1, source_target_pairs={{0,24},{2,26},{4,28},{6,30},{8,16},{10,18},{12,20},{14,22},{16,8},... | collective-permute-start | bytes 208904 | tf_op jit(solution)/shard_map/ppermute | solution.py:49
  22.0 7.5 %collective-permute-start.5 = (f16[272,128]{1,0:T(8,128)(2,1)S(1)}, f16[272,128]{1,0:T(8,128)(2,1)S(1)}, u32[]{:S(2)}, u32[]{:S(2)}) collective-permute-start(f16[272,128]{1,0:T(8,128)(2,1)S(1)} %convert_element_type.60), channel_id=1, source_target_pairs={{0,16},{2,18},{4,20},{6,22},{8,24},{10,26},{12,28},{14,30},{16,0},... | collective-permute-start | bytes 208904 | tf_op jit(solution)/shard_map/ppermute | solution.py:49
  30.5 5.7 %collective-permute-start.9 = (f16[528,128]{1,0:T(8,128)(2,1)S(1)}, f16[528,128]{1,0:T(8,128)(2,1)S(1)}, u32[]{:S(2)}, u32[]{:S(2)}) collective-permute-start(f16[528,128]{1,0:T(8,128)(2,1)S(1)} %convert_element_type.67), channel_id=1, source_target_pairs={{0,6},{2,4},{4,2},{6,0},{8,14},{10,12},{12,10},{14,8},{16,22},{18,... | collective-permute-start | bytes 405512 | tf_op jit(solution)/shard_map/ppermute | solution.py:49
  31.1 8.8 %collective-permute-start.8 = (f16[528,128]{1,0:T(8,128)(2,1)S(1)}, f16[528,128]{1,0:T(8,128)(2,1)S(1)}, u32[]{:S(2)}, u32[]{:S(2)}) collective-permute-start(f16[528,128]{1,0:T(8,128)(2,1)S(1)} %convert_element_type.65), channel_id=1, source_target_pairs={{0,4},{2,6},{4,0},{6,2},{8,12},{10,14},{12,8},{14,10},{16,20},{18,... | collective-permute-start | bytes 405512 | tf_op jit(solution)/shard_map/ppermute | solution.py:49
  33.0 6.9 %collective-permute-start.7 = (f16[528,128]{1,0:T(8,128)(2,1)S(1)}, f16[528,128]{1,0:T(8,128)(2,1)S(1)}, u32[]{:S(2)}, u32[]{:S(2)}) collective-permute-start(f16[528,128]{1,0:T(8,128)(2,1)S(1)} %convert_element_type.63), channel_id=1, source_target_pairs={{0,2},{2,0},{4,6},{6,4},{8,10},{10,8},{12,14},{14,12},{16,18},{18,... | collective-permute-start | bytes 405512 | tf_op jit(solution)/shard_map/ppermute | solution.py:49
  40.9 13.7 %collective-permute-start.10 = (f32[4,2,2,128,128]{4,3,2,1,0:T(8,128)S(1)}, f32[4,2,2,128,128]{4,3,2,1,0:T(8,128)S(1)}, u32[]{:S(2)}, u32[]{:S(2)}) collective-permute-start(f32[4,2,2,128,128]{4,3,2,1,0:T(8,128)S(1)} %get-tuple-element.40), channel_id=1, source_target_pairs={{0,1},{1,0},{2,3},{3,2},{4,5},{5,4},{6,7},{7,6},{8,9},{9,8},{10,11... | collective-permute-start | bytes 3145736 | tf_op jit(solution)/shard_map/ppermute | solution.py:49

commit v4 on v3

v4 whole, which is shorter than its diff:
```python
import functools

import jax
import jax.numpy as jnp
from jax import lax
from jax.experimental import pallas as pl
from jax.experimental.pallas import tpu as pltpu
from jax.sharding import PartitionSpec as P

DH = 128
BLOCK = 128
EXTRA = 16
TOP = 14.0
PIECE = 32
F32 = jnp.float32
BF16 = jnp.bfloat16
F16 = jnp.float16
NT = (((1,), (1,)), ((), ()))
TN = (((0,), (0,)), ((), ()))
VMEM = pl.BlockSpec(memory_space=pltpu.VMEM)
SMEM = pl.BlockSpec(memory_space=pltpu.SMEM)
HBM = pl.BlockSpec(memory_space=pltpu.HBM)


def dot(a, b, dims=None):
    if dims is None:
        dims = (((1,), (0,)), ((), ()))
    return lax.dot_general(a, b, dims, preferred_element_type=F32)


def split(x):
    hi = x.astype(BF16)
    return hi, (x - hi.astype(F32)).astype(BF16)


def call(kernel, outs, args, specs=None, out_specs=None, scratch=(), flops=0, limit=2, aliases=None):
    moved = sum(x.size * x.dtype.itemsize for x in args)
    return pl.pallas_call(
        kernel,
        in_specs=specs or [VMEM] * len(args),
        out_specs=out_specs or [VMEM] * len(outs),
        out_shape=list(outs),
        scratch_shapes=list(scratch),
        input_output_aliases=aliases or {},
        compiler_params=pltpu.CompilerParams(vmem_limit_bytes=limit << 20),
        cost_estimate=pl.CostEstimate(flops=flops, bytes_accessed=moved, transcendentals=0),
    )(*args)


def partner(array, axis, distance):
    return lax.ppermute(array, axis, [(i, i ^ distance) for i in range(lax.axis_size(axis))])


def narrow(array, axis, distance):
    return partner(array.astype(F16), axis, distance).astype(F32)


def marks_of(value):
    most = jnp.maximum(jnp.max(jnp.abs(value)), 1e-30)
    return TOP - jnp.ceil(jnp.log2(jnp.full((8, DH), most, F32)))


def pack(out_ref, values):
    rows = 0
    marks = []
    for value in values:
        power = marks_of(value)
        flat = value.reshape(-1, DH)
        out_ref[rows : rows + flat.shape[0]] = flat * jnp.exp2(power)[:1]
        rows += flat.shape[0]
        marks.append(power)
    put_marks(out_ref, marks)


def put_marks(out_ref, marks):
    rows = out_ref.shape[0] - EXTRA
    for i in range(EXTRA // 8):
        out_ref[rows + 8 * i : rows + 8 * i + 8] = marks[min(i, len(marks) - 1)]


def mark(ref, index):
    rows = ref.shape[0] - EXTRA
    return ref[rows + 8 * index : rows + 8 * index + 8]


def bound_power(bound):
    return TOP - jnp.ceil(jnp.log2(jnp.maximum(bound, 1e-30)))


def unpack(ref, shape, count):
    size = (ref.shape[0] - EXTRA) // count
    return [
        (ref[i * size : (i + 1) * size] * jnp.exp2(-mark(ref, i)[:1])).reshape(shape) for i in range(count)
    ]


def pieces(width):
    return [(j, r, slice(r, r + PIECE)) for j in range(width) for r in range(0, DH, PIECE)]


def first_head(half, heads):
    return (lax.axis_index("head") ^ half) * heads


def near_place(slices):
    return lax.axis_index("seq") & (slices - 1)


def state_kernel(half, cuts, *refs):
    srcs, (out_ref, q_ref, k_ref, v_ref, o_ref), sems = refs[:4], refs[4:9], refs[9]
    slices, _, width = out_ref.shape[:3]
    held = (q_ref, k_ref, v_ref, o_ref)
    model = q_ref.shape[1]
    place = near_place(slices)
    size = model // cuts
    copies = []
    for c in range(cuts):
        start = pl.multiple_of(first_head(half, model // DH) * DH + c * size, DH)
        for i in range(4):
            copy = pltpu.make_async_copy(
                srcs[i].at[:, pl.ds(start, size)], held[i].at[:, c * size : (c + 1) * size], sems.at[c, i]
            )
            copy.start()
            copies.append(copy)
    for c in range(cuts):
        for i in range(4):
            copies[4 * c + i].wait()
        for head in range(c * size // DH, (c + 1) * size // DH):
            d, j = place ^ (head // width), head % width
            cols = slice(head * DH, (head + 1) * DH)
            out_ref[d, 0, j] = dot(v_ref[:, cols], k_ref[:, cols], TN)
            out_ref[d, 1, j] = dot(o_ref[:, cols], q_ref[:, cols], TN)


def device_states(half, args, slices, width):
    tokens = args[0].shape[0]
    cuts = 2 if slices % 2 == 0 else 1
    return call(
        functools.partial(state_kernel, half, cuts),
        [pltpu.VMEM((slices, 2, width, DH, DH), F32)] + [pltpu.VMEM((tokens, slices * width * DH), BF16)] * 4,
        args,
        specs=[HBM] * 4,
        scratch=[pltpu.SemaphoreType.DMA((cuts, 4))],
        flops=4 * slices * width * tokens * DH * DH,
    )


def local_kernel(half, group, width, scale_ref, q_ref, k_ref, v_ref, o_ref, out_ref):
    tokens = q_ref.shape[0]
    blocks = tokens // BLOCK
    rows = lax.broadcasted_iota(jnp.int32, (BLOCK, BLOCK), 0)
    cols = lax.broadcasted_iota(jnp.int32, (BLOCK, BLOCK), 1)

    def blk(n, m=None):
        return slice(n * BLOCK, (n + 1 if m is None else m) * BLOCK)

    def product(left, right, weight, values, n, low, high, mask):
        raw = dot(left[blk(n)], right[blk(low, high)], NT)
        parts, rest = [], []
        for m in range(low, high):
            part = raw[:, blk(m - low)]
            if m == n:
                parts.append(jnp.where(mask, part * weight(0), 0.0).astype(BF16))
            else:
                hi, lo = split(part * weight((m ^ n).bit_length()))
                parts.append(hi)
                rest.append((m, lo))
        out = dot(jnp.concatenate(parts, axis=1) if len(parts) > 1 else parts[0], values[blk(low, high)])
        for m, lo in rest:
            out = out + dot(lo, values[blk(m)])
        return out

    for j in range(width):
        at = slice((group * width + j) * DH, (group * width + j + 1) * DH)
        to = slice(j * DH, (j + 1) * DH)
        q, k, v, o = q_ref[:, at], k_ref[:, at], v_ref[:, at], o_ref[:, at]
        head = first_head(half, q_ref.shape[1] // DH) + group * width + j

        def weight(level, head=head):
            return scale_ref[head, level]

        for n in range(blocks):
            out_ref[2, blk(n), to] = product(k, q, weight, o, n, n, blocks, rows <= cols)
            out_ref[1, blk(n), to] = product(v, o, weight, q, n, n, blocks, rows <= cols)
            out_ref[0, blk(n), to] = product(o, v, weight, k, n, 0, n + 1, rows >= cols)


def local_grads(half, group, level_scale, held, width):
    tokens = held[0].shape[0]
    return call(
        functools.partial(local_kernel, half, group, width),
        [pltpu.VMEM((3, tokens, width * DH), F32)],
        [level_scale, *held],
        specs=[SMEM] + [VMEM] * 4,
        flops=24 * tokens * BLOCK * width * DH,
    )[0]


def chip_kernel(own_ref, other_ref, keep_ref, *out_refs):
    rows = (keep_ref.shape[0] - EXTRA) // 2
    marks = []
    for t in range(2):
        value = own_ref[0, t] + other_ref[0, t]
        keep_ref[t * rows : (t + 1) * rows] = value.reshape(rows, DH)
        marks.append(marks_of(value))
    put_marks(keep_ref, marks)
    for d, out_ref in enumerate(out_refs, 1):
        pack(out_ref, [own_ref[d, t] + other_ref[d, t] for t in range(2)])


def bit_of(value, index):
    return ((value >> index) & 1).astype(F32)


def head_weight(scale_ref, place, slices, width, j, level):
    return scale_ref[first_head(0, slices * width) + place * width + j, level]


def top_weight(scale_ref):
    return scale_ref[scale_ref.shape[0] - 1, 0]


def plane_kernel(plane_bits, base, rest, wide, scale_ref, keep_ref, *refs):
    slices = 1 << plane_bits
    parts, refs = (keep_ref, *refs[: slices - 1]), refs[slices - 1 :]
    near_ref, bound_ref, refs = refs[0], refs[1], refs[2:]
    total_ref = refs[0] if wide else None
    outs = refs[1:] if wide else refs
    width = near_ref.shape[2]
    place = near_place(slices)
    row = lax.axis_index("seq") // slices
    factors = [[None if e == 0 else jnp.exp2(-mark(parts[e], t)[:1]) for t in range(2)] for e in range(slices)]
    bounds = [
        functools.reduce(jnp.add, [jnp.exp2(TOP - mark(parts[e], t)) for e in range(slices)]) for t in range(2)
    ]
    for t in range(2):
        bound_ref[8 * t : 8 * t + 8] = bounds[t]
    ups = [bit_of(row, rest - len(outs) + i) for i in range(len(outs))]
    factor_out = []
    for out_ref, up in zip(outs, ups):
        power = bound_power(jnp.where(up > 0, bounds[1], bounds[0]))
        put_marks(out_ref, [power])
        factor_out.append(jnp.exp2(power)[:1])
    sides = [[bit_of(place ^ d, b) for b in range(plane_bits)] for d in range(slices)]
    for j, r, rows in pieces(width):
        weights = [head_weight(scale_ref, place, slices, width, j, base + b) for b in range(plane_bits)]
        values = []
        for t in range(2):
            at = (t * width + j) * DH + r
            loaded = [parts[e][at : at + PIECE] for e in range(slices)]
            loaded = [x if f[t] is None else x * f[t] for x, f in zip(loaded, factors)]
            sums = {}
            for b in range(plane_bits + 1):
                for first in range(0, slices, 1 << b):
                    half = 1 << (b - 1) if b else 0
                    sums[b, first] = loaded[first] if b == 0 else sums[b - 1, first] + sums[b - 1, first + half]
            values.append(sums)
        for d in range(slices):
            early, late = [], []
            for b in range(plane_bits):
                first = ((d >> b) ^ 1) << b
                up = sides[d][b]
                early.append((up * weights[b]) * values[0][b, first])
                late.append(((1.0 - up) * weights[b]) * values[1][b, first])
            zero = jnp.zeros((PIECE, DH), F32)
            near_ref[d, 0, j, rows] = functools.reduce(jnp.add, early) if early else zero
            near_ref[d, 1, j, rows] = functools.reduce(jnp.add, late) if late else zero
        total = [values[t][plane_bits, 0] for t in range(2)]
        for t in range(2):
            if wide:
                total_ref[t, j, rows] = total[t]
        at = j * DH + r
        for out_ref, up, factor in zip(outs, ups, factor_out):
            out_ref[at : at + PIECE] = jnp.where(up > 0, total[1], total[0]) * factor


def far_out(outs, total_ref, rest, slices):
    row = lax.axis_index("seq") // slices
    for i, out_ref in enumerate(outs):
        up = bit_of(row, rest - len(outs) + i)
        pack(out_ref, [jnp.where(up > 0, total_ref[1], total_ref[0])])


def merge_kernel(slices, index, level, rest, scale_ref, near_ref, bound_ref, total_ref, got_ref, near_out, bound_out, total_out, *outs):
    width = total_ref.shape[1]
    row = lax.axis_index("seq") // slices
    place = near_place(slices)
    up = bit_of(row, index)
    got = unpack(got_ref, (width, DH, DH), 2)
    for t in range(2):
        bound_out[8 * t : 8 * t + 8] = bound_ref[8 * t : 8 * t + 8] + jnp.exp2(TOP - mark(got_ref, t))
    for j in range(width):
        weight = head_weight(scale_ref, place, slices, width, j, level)
        for d in range(slices):
            near_out[d, 0, j] = near_ref[d, 0, j] + (up * weight) * got[0][j]
            near_out[d, 1, j] = near_ref[d, 1, j] + ((1.0 - up) * weight) * got[1][j]
    for t in range(2):
        total_out[t] = total_ref[t] + got[t]
    far_out(outs, total_out, rest, slices)


def back_kernel(slices, levels, bits, scale_ref, near_ref, bound_ref, *refs):
    count = len(levels)
    gots, (keep_ref, *outs) = refs[:count], refs[count:]
    width = near_ref.shape[2]
    row = lax.axis_index("seq") // slices
    place = near_place(slices)
    ups = [bit_of(row, bit) for bit in bits]
    bounds = [bound_ref[:8], bound_ref[8:]]
    for got_ref, up in zip(gots, ups):
        size = jnp.exp2(TOP - mark(got_ref, 0))
        bounds = [bounds[0] + up * size, bounds[1] + (1.0 - up) * size]
    powers = [bound_power(top_weight(scale_ref) * bound) for bound in bounds]
    factors = [jnp.exp2(power)[:1] for power in powers]
    for out_ref in (keep_ref, *outs):
        put_marks(out_ref, powers)
    opened = [jnp.exp2(-mark(got_ref, 0)[:1]) for got_ref in gots]
    for j, r, rows in pieces(width):
        far = [jnp.zeros((PIECE, DH), F32)] * 2
        at = j * DH + r
        for got_ref, level, up, factor in zip(gots, levels, ups, opened):
            weight = head_weight(scale_ref, place, slices, width, j, level)
            got = got_ref[at : at + PIECE] * factor
            far = [far[0] + (up * weight) * got, far[1] + ((1.0 - up) * weight) * got]
        for d, out_ref in enumerate((keep_ref, *outs)):
            for t in range(2):
                value = near_ref[d, t, j, rows] + far[t]
                to = t * width * DH + at
                out_ref[to : to + PIECE] = value if d == 0 else value * factors[t]


def core_kernel(level, mine, scale_ref, source_ref, keep_ref, *refs):
    parts, out_ref = (keep_ref, *refs[:-1]), refs[-1]
    slices, _, width = source_ref.shape[:3]
    place = near_place(slices)
    second = lax.axis_index("head").astype(F32)
    sides = (second, 1.0 - second) if mine else (1.0 - second, second)
    for d in range(slices):
        factors = [None if d == 0 else jnp.exp2(-mark(parts[d], t)[:1]) for t in range(2)]
        for j, r, rows in pieces(width):
            weight = head_weight(scale_ref, place ^ d, slices, width, j, level)
            for t in range(2):
                at = (t * width + j) * DH + r
                got = parts[d][at : at + PIECE]
                if d:
                    got = got * factors[t]
                out_ref[d, t, j, rows] = got + (sides[t] * weight) * source_ref[d, t, j, rows]


def cross_kernel(half, cuts, state_ref, k_ref, v_ref, o_ref, local_refs, outs, temps, sems):
    slices, _, width = state_ref.shape[:3]
    model = k_ref.shape[1]
    place = near_place(slices)
    size = model // cuts
    copies = []
    for c in range(cuts):
        for head in range(c * size // DH, (c + 1) * size // DH):
            group, j = head // width, head % width
            d = place ^ group
            cs = slice(head * DH, (head + 1) * DH)
            to = slice(j * DH, (j + 1) * DH)
            o, v, k = o_ref[:, cs], v_ref[:, cs], k_ref[:, cs]
            hi, lo = split(state_ref[d, 0, j])
            qg = dot(o, hi) + dot(o, lo)
            hi, lo = split(state_ref[d, 1, j])
            kg = dot(v, hi) + dot(v, lo)
            vg = dot(k, hi, NT) + dot(k, lo, NT)
            for i, cross in enumerate((qg, kg, vg)):
                temps[i, :, cs] = (cross + local_refs[group][i, :, to]).astype(BF16)
        cs = slice(c * size, (c + 1) * size)
        cols = pl.ds(pl.multiple_of(first_head(half, model // DH) * DH + c * size, DH), size)
        for i in range(3):
            copy = pltpu.make_async_copy(temps.at[i, :, cs], outs[i].at[:, cols], sems.at[c, i])
            copy.start()
            copies.append(copy)
    for copy in copies:
        copy.wait()


def finish(half, states, held, local, model, before):
    tokens, cols = held[0].shape
    slices = states.shape[0]
    cuts = 2 if slices % 2 == 0 else 1
    args = [states, *held[1:], *local]
    specs = [VMEM] * len(args) + [HBM] * len(before)

    def kernel(*refs):
        parts = refs[4 : len(args)]
        outs = refs[len(specs) : len(specs) + 3]
        cross_kernel(half, cuts, *refs[:4], parts, outs, refs[-2], refs[-1])

    return call(
        kernel,
        [jax.ShapeDtypeStruct((tokens, model), BF16)] * 3,
        args + list(before),
        specs=specs,
        out_specs=[HBM] * 3,
        scratch=[pltpu.VMEM((3, tokens, cols), BF16), pltpu.SemaphoreType.DMA((cuts, 3))],
        flops=12 * tokens * DH * cols,
        limit=4,
        aliases={len(args) + i: i for i in range(len(before))},
    )


def work(queries, key_rows, values, out_grad, level_weights):
    level_ids = jnp.arange(level_weights.shape[1], dtype=F32)
    level_scale = level_weights * jnp.exp2((1.0 - level_ids) / 2.0)[None, :] / jnp.sqrt(F32(DH * BLOCK))
    heads = level_weights.shape[0]
    tokens, model = queries.shape
    chain = lax.axis_size("seq")
    bits = chain.bit_length() - 1
    plane_bits = min(2, bits)
    slices = 1 << plane_bits
    width = heads // (lax.axis_size("head") * slices)
    local_levels = (tokens // BLOCK).bit_length() - 1
    base = local_levels + 2
    rest = bits - plane_bits
    direct = min(2, rest)

    most = jnp.full((1, level_scale.shape[1]), jnp.max(jnp.abs(level_scale)))
    level_scale = jnp.concatenate([level_scale, most])

    args = [pltpu.with_memory_space_constraint(x, pltpu.HBM) for x in (queries, key_rows, values, out_grad)]
    sent, *held_there = device_states(1, args, slices, width)
    other = partner(sent, "head", 1)
    own, *held_here = device_states(0, args, slices, width)
    held = (held_here, held_there)
    local = [[], []]
    for half in range(2):
        for group in range(slices):
            local[half].append(local_grads(half, group, level_scale, held[half], width))

    state = pltpu.VMEM((2, width, DH, DH), F32)
    load = pltpu.VMEM((2 * width * DH + EXTRA, DH), F32)
    single = pltpu.VMEM((width * DH + EXTRA, DH), F32)
    near = pltpu.VMEM((slices, 2, width, DH, DH), F32)
    bound = pltpu.VMEM((16, DH), F32)

    keep, *outs = call(chip_kernel, [load] * slices, [own, other])
    got = []
    for d in range(1, slices):
        got.append(narrow(outs[d - 1], "seq", d))
    wide = rest > direct
    near_sum, bounds, *outs = call(
        functools.partial(plane_kernel, plane_bits, base, rest, wide),
        [near, bound] + ([state] if wide else [single] * direct),
        [level_scale, keep, *got],
        specs=[SMEM] + [VMEM] * slices,
    )
    total = outs[0] if wide else None
    for index in range(rest - direct):
        both = call(lambda ref, out: pack(out, [ref[0], ref[1]]), [load], [total])[0]
        arrived = narrow(both, "seq", slices << index)
        sending = direct if index + 1 == rest - direct else 0
        near_sum, bounds, total, *outs = call(
            functools.partial(merge_kernel, slices, index, base + plane_bits + index, rest),
            [near, bound, state] + [single] * sending,
            [level_scale, near_sum, bounds, total, arrived],
            specs=[SMEM] + [VMEM] * 4,
        )
    got, levels, which = [], [], []
    for step in range(1, 1 << direct):
        top = step.bit_length() - 1
        got.append(narrow(outs[top], "seq", (slices << (rest - direct)) * step))
        which.append(rest - direct + top)
        levels.append(base + plane_bits + rest - direct + top)
    keep, *outs = call(
        functools.partial(back_kernel, slices, levels, which),
        [load] * slices,
        [level_scale, near_sum, bounds, *got],
        specs=[SMEM] + [VMEM] * (2 + len(got)),
    )
    got = []
    for d in range(1, slices):
        got.append(narrow(outs[d - 1], "seq", d))
    gathered = []
    for mine, source in ((False, own), (True, other)):
        gathered += call(
            functools.partial(core_kernel, local_levels + 1, mine),
            [near],
            [level_scale, source, keep, *got],
            specs=[SMEM] + [VMEM] * (2 + len(got)),
        )
    theirs = partner(gathered[0], "head", 1)
    half_done = finish(0, gathered[1], held[0], local[0], model, [])
    return tuple(finish(1, theirs, held[1], local[1], model, half_done))


def solution(mesh):
    rows = P(("seq", "head"), None)
    return jax.shard_map(
        work,
        mesh=mesh,
        in_specs=(rows, rows, rows, rows, P()),
        out_specs=(rows, rows, rows),
        check_vma=False,
    )
```

time: 57.6 us -> 59.6 us (1.035)
  waiting for transfers between devices: 20.6 us -> 12.5 us
  Pallas kernels: 24.4 us -> 28.9 us
  starting transfers between devices: 11.2 us -> 14.9 us
  local copies, waits for them, and re-layouts: 0.01 us -> 1.24 us
  other arithmetic: 0.32 us -> 0.92 us
    ppermute x11, waiting for transfers between devices: 20.6 us -> 12.5 us  [partner(): lax.ppermute(array, axis, [(i, i ^ distance) for i in range(lax.axis_size...]
    pallas_call x11 -> x17, Pallas kernels: 24.4 us -> 28.9 us  [call(): pl.pallas_call(kernel, in_specs=specs or [VMEM] * len(args), out_specs=ou...]
    ppermute x11, starting transfers between devices: 11.2 us -> 14.9 us  [partner(): lax.ppermute(array, axis, [(i, i ^ distance) for i in range(lax.axis_size...]
    concatenate x0 -> x1, local copies, waits for them, and re-layouts: none -> 0.65 us  [work(): level_scale = jnp.concatenate([level_scale, most])]
    reduce_max x0 -> x1, other arithmetic: none -> 0.6 us  [work(): most = jnp.full((1, level_scale.shape[1]), jnp.max(jnp.abs(level_scale)))]
  transfers between devices with their start and end apart: 11 -> 11, of which waited for: 7 -> 9; matrix products, arithmetic and copies ran while one was open for 0% -> 2% of each run, Pallas kernels for 27% -> 37%
where the time goes in v4:
time: 59.6 us; the launch traced here: 59.4 us
  Pallas kernels  28.9 us (48%)
  starting transfers between devices  14.9 us (25%)
  waiting for transfers between devices  12.5 us (21%)
  local copies, waits for them, and re-layouts  1.24 us (2%)
  other arithmetic  0.92 us (2%)
  between operations  0.85 us (1%)
    pallas_call x17, Pallas kernels, call(): pl.pallas_call(kernel, in_specs=specs or [VMEM] * len(args), out_specs=ou...  28.9 us
    ppermute x11, starting transfers between devices, partner(): lax.ppermute(array, axis, [(i, i ^ distance) for i in range(lax.axis_size...  14.9 us
    ppermute x11, waiting for transfers between devices, partner(): lax.ppermute(array, axis, [(i, i ^ distance) for i in range(lax.axis_size...  12.5 us
  transfers between devices with their start and end apart: 11, of which 9 were waited for; matrix products, arithmetic and copies ran while one was open for 2% of the time, Pallas kernels for 37%

profile of v4, /device:TPU:1, one launch (start us, length us, event | category | flops | bytes accessed | tf_op | source)
XLA Modules:
  0.0 59.4 jit_solution(7454946612293372950)
XLA Ops:
  0.6 2.0 %shard_map.77 = (f32[4,2,2,128,128]{4,3,2,1,0:T(8,128)S(1)}, bf16[256,1024]{1,0:T(8,128)(2,1)S(1)}, bf16[256,1024]{1,0:T(8,128)(2,1)S(1)}, bf16[256,1024]{1,0:T(8,128)(2,1)S(1)}, bf16[256,1024]{1,0:T(8,128)(2,1)S(1)}) custom-call(bf16[256,2048]{1,0:T(8,128)(2,1)} %refs_0_.3, bf16[256,2048]{1,0:T(8,128)(2,1)} %refs_1_.3, bf16[256,2048]{1,0:T(8,128)(2,1)} %refs_2_.3, ...), custom_call_target="tpu_custom_call" | custom-call | flops 134217728 | bytes 4194304 | tf_op jit(solution)/shard_map/pallas_call | solution.py:38
  2.7 0.1 collective-permute-start
  2.8 2.0 %shard_map.76 = (f32[4,2,2,128,128]{4,3,2,1,0:T(8,128)S(1)}, bf16[256,1024]{1,0:T(8,128)(2,1)S(1)}, bf16[256,1024]{1,0:T(8,128)(2,1)S(1)}, bf16[256,1024]{1,0:T(8,128)(2,1)S(1)}, bf16[256,1024]{1,0:T(8,128)(2,1)S(1)}) custom-call(bf16[256,2048]{1,0:T(8,128)(2,1)} %refs_0_.3, bf16[256,2048]{1,0:T(8,128)(2,1)} %refs_1_.3, bf16[256,2048]{1,0:T(8,128)(2,1)} %refs_2_.3, ...), custom_call_target="tpu_custom_call" | custom-call | flops 134217728 | bytes 4194304 | tf_op jit(solution)/shard_map/pallas_call | solution.py:38
  4.8 0.6 collective-permute-done.other_ref.source_ref
  5.4 0.3 shard_map.78
  5.7 2.4 %collective-permute-start.1 = (f16[528,128]{1,0:T(8,128)(2,1)S(1)}, f16[528,128]{1,0:T(8,128)(2,1)S(1)}, u32[]{:S(2)}, u32[]{:S(2)}) collective-permute-start(f16[528,128]{1,0:T(8,128)(2,1)S(1)} %convert_element_type.52), channel_id=1, source_target_pairs={{0,2},{2,0},{4,6},{6,4},{8,10},{10,8},{12,14},{14,12},{16,18},{18,... | collective-permute-start | bytes 405512 | tf_op jit(solution)/shard_map/ppermute | solution.py:51
  8.1 1.3 %collective-permute-start.2 = (f16[528,128]{1,0:T(8,128)(2,1)S(1)}, f16[528,128]{1,0:T(8,128)(2,1)S(1)}, u32[]{:S(2)}, u32[]{:S(2)}) collective-permute-start(f16[528,128]{1,0:T(8,128)(2,1)S(1)} %convert_element_type.54), channel_id=1, source_target_pairs={{0,4},{2,6},{4,0},{6,2},{8,12},{10,14},{12,8},{14,10},{16,20},{18,... | collective-permute-start | bytes 405512 | tf_op jit(solution)/shard_map/ppermute | solution.py:51
  9.4 0.0 copy-start
  9.5 0.1 collective-permute-start.3
  9.5 0.6 copy-done
  10.1 0.6 %abs_reduce_fusion = (f32[]{:T(128)}, f32[16,11]{1,0:T(8,128)S(1)}) fusion(f32[16,11]{1,0:T(8,128)S(1)} %copy-done, f32[11]{0:T(128)S(1)} %multiply_exponential_fusion), kind=kLoop, calls=%fused_computation | loop fusion | flops 703 | bytes 1456 | tf_op jit(solution)/shard_map/reduce_max | solution.py:420
  10.7 0.6 %concatenate.3.scale_ref = f32[17,11]{1,0:T(8,128)S(1)} pad(f32[16,11]{1,0:T(8,128)S(1)} %get-tuple-element.54, f32[]{:T(128)} %get-tuple-element.53), padding=0_1x0_0 | pad | bytes 1456 | tf_op jit(solution)/shard_map/concatenate | solution.py:421
  11.4 0.3 collective-permute-done.1
  11.7 2.7 %collective-permute-done.2 = f16[528,128]{1,0:T(8,128)(2,1)S(1)} collective-permute-done((f16[528,128]{1,0:T(8,128)(2,1)S(1)}, f16[528,128]{1,0:T(8,128)(2,1)S(1)}, u32[]{:S(2)}, u32[]{:S(2)}) %collective-permute-start.2) | collective-permute-done | bytes 135200 | tf_op jit(solution)/shard_map/ppermute | solution.py:51
  14.5 0.8 %collective-permute-done.3 = f16[528,128]{1,0:T(8,128)(2,1)S(1)} collective-permute-done((f16[528,128]{1,0:T(8,128)(2,1)S(1)}, f16[528,128]{1,0:T(8,128)(2,1)S(1)}, u32[]{:S(2)}, u32[]{:S(2)}) %collective-permute-start.3) | collective-permute-done | bytes 135200 | tf_op jit(solution)/shard_map/ppermute | solution.py:51
  15.4 1.0 %shard_map.79 = (f32[4,2,2,128,128]{4,3,2,1,0:T(8,128)S(1)}, f32[16,128]{1,0:T(8,128)S(1)}, f32[272,128]{1,0:T(8,128)S(1)}, f32[272,128]{1,0:T(8,128)S(1)}) custom-call(f32[17,11]{1,0:T(8,128)S(1)} %concatenate.3.scale_ref, f32[528,128]{1,0:T(8,128)S(1)} %get-tuple-element.30.keep_ref, f32[528,128]{1,0:T(8,128)S(1)} %convert_element_type.53.refs_0_, ...), custom_call_target="tpu_custom_call" | custom-call | bytes 1082092 | tf_op jit(solution)/shard_map/pallas_call | solution.py:38
  16.3 2.4 %collective-permute-start.5 = (f16[272,128]{1,0:T(8,128)(2,1)S(1)}, f16[272,128]{1,0:T(8,128)(2,1)S(1)}, u32[]{:S(2)}, u32[]{:S(2)}) collective-permute-start(f16[272,128]{1,0:T(8,128)(2,1)S(1)} %convert_element_type.60), channel_id=1, source_target_pairs={{0,16},{2,18},{4,20},{6,22},{8,24},{10,26},{12,28},{14,30},{16,0},... | collective-permute-start | bytes 208904 | tf_op jit(solution)/shard_map/ppermute | solution.py:51
  18.7 1.1 %collective-permute-start.6 = (f16[272,128]{1,0:T(8,128)(2,1)S(1)}, f16[272,128]{1,0:T(8,128)(2,1)S(1)}, u32[]{:S(2)}, u32[]{:S(2)}) collective-permute-start(f16[272,128]{1,0:T(8,128)(2,1)S(1)} %convert_element_type.60), channel_id=1, source_target_pairs={{0,24},{2,26},{4,28},{6,30},{8,16},{10,18},{12,20},{14,22},{16,8},... | collective-permute-start | bytes 208904 | tf_op jit(solution)/shard_map/ppermute | solution.py:51
  19.8 0.3 collective-permute-start.4
  20.1 0.4 collective-permute-done.5
  20.5 3.9 %collective-permute-done.6 = f16[272,128]{1,0:T(8,128)(2,1)S(1)} collective-permute-done((f16[272,128]{1,0:T(8,128)(2,1)S(1)}, f16[272,128]{1,0:T(8,128)(2,1)S(1)}, u32[]{:S(2)}, u32[]{:S(2)}) %collective-permute-start.6) | collective-permute-done | bytes 69664 | tf_op jit(solution)/shard_map/ppermute | solution.py:51
  24.4 0.0 collective-permute-done.4
  24.4 0.9 %shard_map.80 = (f32[528,128]{1,0:T(8,128)S(1)}, f32[528,128]{1,0:T(8,128)S(1)}, f32[528,128]{1,0:T(8,128)S(1)}, f32[528,128]{1,0:T(8,128)S(1)}) custom-call(f32[17,11]{1,0:T(8,128)S(1)} %concatenate.3.scale_ref, f32[4,2,2,128,128]{4,3,2,1,0:T(8,128)S(1)} %get-tuple-element.34.near_ref, f32[16,128]{1,0:T(8,128)S(1)} %get-tuple-element.35.bound_ref, ...), custom_call_target="tpu_custom_call" | custom-call | bytes 1475308 | tf_op jit(solution)/shard_map/pallas_call | solution.py:38
  25.4 1.1 %collective-permute-start.7 = (f16[528,128]{1,0:T(8,128)(2,1)S(1)}, f16[528,128]{1,0:T(8,128)(2,1)S(1)}, u32[]{:S(2)}, u32[]{:S(2)}) collective-permute-start(f16[528,128]{1,0:T(8,128)(2,1)S(1)} %convert_element_type.63), channel_id=1, source_target_pairs={{0,2},{2,0},{4,6},{6,4},{8,10},{10,8},{12,14},{14,12},{16,18},{18,... | collective-permute-start | bytes 405512 | tf_op jit(solution)/shard_map/ppermute | solution.py:51
  26.5 0.7 %collective-permute-start.8 = (f16[528,128]{1,0:T(8,128)(2,1)S(1)}, f16[528,128]{1,0:T(8,128)(2,1)S(1)}, u32[]{:S(2)}, u32[]{:S(2)}) collective-permute-start(f16[528,128]{1,0:T(8,128)(2,1)S(1)} %convert_element_type.65), channel_id=1, source_target_pairs={{0,4},{2,6},{4,0},{6,2},{8,12},{10,14},{12,8},{14,10},{16,20},{18,... | collective-permute-start | bytes 405512 | tf_op jit(solution)/shard_map/ppermute | solution.py:51
  27.2 1.0 %collective-permute-start.9 = (f16[528,128]{1,0:T(8,128)(2,1)S(1)}, f16[528,128]{1,0:T(8,128)(2,1)S(1)}, u32[]{:S(2)}, u32[]{:S(2)}) collective-permute-start(f16[528,128]{1,0:T(8,128)(2,1)S(1)} %convert_element_type.67), channel_id=1, source_target_pairs={{0,6},{2,4},{4,2},{6,0},{8,14},{10,12},{12,10},{14,8},{16,22},{18,... | collective-permute-start | bytes 405512 | tf_op jit(solution)/shard_map/ppermute | solution.py:51
  28.3 1.0 %collective-permute-done.7 = f16[528,128]{1,0:T(8,128)(2,1)S(1)} collective-permute-done((f16[528,128]{1,0:T(8,128)(2,1)S(1)}, f16[528,128]{1,0:T(8,128)(2,1)S(1)}, u32[]{:S(2)}, u32[]{:S(2)}) %collective-permute-start.7) | collective-permute-done | bytes 135200 | tf_op jit(solution)/shard_map/ppermute | solution.py:51
  29.3 1.1 %collective-permute-done.8 = f16[528,128]{1,0:T(8,128)(2,1)S(1)} collective-permute-done((f16[528,128]{1,0:T(8,128)(2,1)S(1)}, f16[528,128]{1,0:T(8,128)(2,1)S(1)}, u32[]{:S(2)}, u32[]{:S(2)}) %collective-permute-start.8) | collective-permute-done | bytes 135200 | tf_op jit(solution)/shard_map/ppermute | solution.py:51
  30.4 1.6 %collective-permute-done.9 = f16[528,128]{1,0:T(8,128)(2,1)S(1)} collective-permute-done((f16[528,128]{1,0:T(8,128)(2,1)S(1)}, f16[528,128]{1,0:T(8,128)(2,1)S(1)}, u32[]{:S(2)}, u32[]{:S(2)}) %collective-permute-start.9) | collective-permute-done | bytes 135200 | tf_op jit(solution)/shard_map/ppermute | solution.py:51
  32.1 0.9 %shard_map.81 = f32[4,2,2,128,128]{4,3,2,1,0:T(8,128)S(1)} custom-call(f32[17,11]{1,0:T(8,128)S(1)} %concatenate.3.scale_ref, f32[4,2,2,128,128]{4,3,2,1,0:T(8,128)S(1)} %get-tuple-element.28.own_ref.source_ref, f32[528,128]{1,0:T(8,128)S(1)} %get-tuple-element.38.keep_ref, f32[528,128]{1,0:T(8,128)S(1)} %convert_element_type.64.refs_0_, ...), custom_call_target="tpu_custom_call" | custom-call | bytes 2130668 | tf_op jit(solution)/shard_map/pallas_call | solution.py:38
  33.0 4.4 %collective-permute-start.10 = (f32[4,2,2,128,128]{4,3,2,1,0:T(8,128)S(1)}, f32[4,2,2,128,128]{4,3,2,1,0:T(8,128)S(1)}, u32[]{:S(2)}, u32[]{:S(2)}) collective-permute-start(f32[4,2,2,128,128]{4,3,2,1,0:T(8,128)S(1)} %shard_map.81), channel_id=1, source_target_pairs={{0,1},{1,0},{2,3},{3,2},{4,5},{5,4},{6,7},{7,6},{8,9},{9,8},{10,11... | collective-permute-start | bytes 3145736 | tf_op jit(solution)/shard_map/ppermute | solution.py:51
  37.4 2.1 %shard_map.87.refs_4_ = f32[3,256,256]{2,1,0:T(8,128)S(1)} custom-call(f32[17,11]{1,0:T(8,128)S(1)} %concatenate.3.scale_ref, bf16[256,1024]{1,0:T(8,128)(2,1)S(1)} %get-tuple-element.49.q_ref, bf16[256,1024]{1,0:T(8,128)(2,1)S(1)} %get-tuple-element.46.k_ref.refs_1_, bf16[256,1024]{1,0:T(8,128)(2,1)S(1)} %get-tuple-element.47.v_ref.refs_2_, ...), custom_call_target="tpu_custom_call" | custom-call | flops 201326592 | bytes 2097900 | tf_op jit(solution)/shard_map/pallas_call | solution.py:38
  39.5 2.1 %shard_map.88.refs_5_ = f32[3,256,256]{2,1,0:T(8,128)S(1)} custom-call(f32[17,11]{1,0:T(8,128)S(1)} %concatenate.3.scale_ref, bf16[256,1024]{1,0:T(8,128)(2,1)S(1)} %get-tuple-element.49.q_ref, bf16[256,1024]{1,0:T(8,128)(2,1)S(1)} %get-tuple-element.46.k_ref.refs_1_, bf16[256,1024]{1,0:T(8,128)(2,1)S(1)} %get-tuple-element.47.v_ref.refs_2_, ...), custom_call_target="tpu_custom_call" | custom-call | flops 201326592 | bytes 2097900 | tf_op jit(solution)/shard_map/pallas_call | solution.py:38
  41.7 2.1 %shard_map.89.refs_6_ = f32[3,256,256]{2,1,0:T(8,128)S(1)} custom-call(f32[17,11]{1,0:T(8,128)S(1)} %concatenate.3.scale_ref, bf16[256,1024]{1,0:T(8,128)(2,1)S(1)} %get-tuple-element.49.q_ref, bf16[256,1024]{1,0:T(8,128)(2,1)S(1)} %get-tuple-element.46.k_ref.refs_1_, bf16[256,1024]{1,0:T(8,128)(2,1)S(1)} %get-tuple-element.47.v_ref.refs_2_, ...), custom_call_target="tpu_custom_call" | custom-call | flops 201326592 | bytes 2097900 | tf_op jit(solution)/shard_map/pallas_call | solution.py:38
  43.8 2.1 %shard_map.90.refs_7_ = f32[3,256,256]{2,1,0:T(8,128)S(1)} custom-call(f32[17,11]{1,0:T(8,128)S(1)} %concatenate.3.scale_ref, bf16[256,1024]{1,0:T(8,128)(2,1)S(1)} %get-tuple-element.49.q_ref, bf16[256,1024]{1,0:T(8,128)(2,1)S(1)} %get-tuple-element.46.k_ref.refs_1_, bf16[256,1024]{1,0:T(8,128)(2,1)S(1)} %get-tuple-element.47.v_ref.refs_2_, ...), custom_call_target="tpu_custom_call" | custom-call | flops 201326592 | bytes 2097900 | tf_op jit(solution)/shard_map/pallas_call | solution.py:38
  45.9 2.1 %shard_map.82.refs_4_ = f32[3,256,256]{2,1,0:T(8,128)S(1)} custom-call(f32[17,11]{1,0:T(8,128)S(1)} %concatenate.3.scale_ref, bf16[256,1024]{1,0:T(8,128)(2,1)S(1)} %get-tuple-element.45.q_ref, bf16[256,1024]{1,0:T(8,128)(2,1)S(1)} %get-tuple-element.42.k_ref.refs_1_, bf16[256,1024]{1,0:T(8,128)(2,1)S(1)} %get-tuple-element.43.v_ref.refs_2_, ...), custom_call_target="tpu_custom_call" | custom-call | flops 201326592 | bytes 2097900 | tf_op jit(solution)/shard_map/pallas_call | solution.py:38
  48.0 2.1 %shard_map.83.refs_5_ = f32[3,256,256]{2,1,0:T(8,128)S(1)} custom-call(f32[17,11]{1,0:T(8,128)S(1)} %concatenate.3.scale_ref, bf16[256,1024]{1,0:T(8,128)(2,1)S(1)} %get-tuple-element.45.q_ref, bf16[256,1024]{1,0:T(8,128)(2,1)S(1)} %get-tuple-element.42.k_ref.refs_1_, bf16[256,1024]{1,0:T(8,128)(2,1)S(1)} %get-tuple-element.43.v_ref.refs_2_, ...), custom_call_target="tpu_custom_call" | custom-call | flops 201326592 | bytes 2097900 | tf_op jit(solution)/shard_map/pallas_call | solution.py:38
  50.1 2.1 %shard_map.84.refs_6_ = f32[3,256,256]{2,1,0:T(8,128)S(1)} custom-call(f32[17,11]{1,0:T(8,128)S(1)} %concatenate.3.scale_ref, bf16[256,1024]{1,0:T(8,128)(2,1)S(1)} %get-tuple-element.45.q_ref, bf16[256,1024]{1,0:T(8,128)(2,1)S(1)} %get-tuple-element.42.k_ref.refs_1_, bf16[256,1024]{1,0:T(8,128)(2,1)S(1)} %get-tuple-element.43.v_ref.refs_2_, ...), custom_call_target="tpu_custom_call" | custom-call | flops 201326592 | bytes 2097900 | tf_op jit(solution)/shard_map/pallas_call | solution.py:38
  52.3 2.1 %shard_map.85.refs_7_ = f32[3,256,256]{2,1,0:T(8,128)S(1)} custom-call(f32[17,11]{1,0:T(8,128)S(1)} %concatenate.3.scale_ref, bf16[256,1024]{1,0:T(8,128)(2,1)S(1)} %get-tuple-element.45.q_ref, bf16[256,1024]{1,0:T(8,128)(2,1)S(1)} %get-tuple-element.42.k_ref.refs_1_, bf16[256,1024]{1,0:T(8,128)(2,1)S(1)} %get-tuple-element.43.v_ref.refs_2_, ...), custom_call_target="tpu_custom_call" | custom-call | flops 201326592 | bytes 2097900 | tf_op jit(solution)/shard_map/pallas_call | solution.py:38
  54.4 0.9 %shard_map.86.refs_0_ = f32[4,2,2,128,128]{4,3,2,1,0:T(8,128)S(1)} custom-call(f32[17,11]{1,0:T(8,128)S(1)} %concatenate.3.scale_ref, f32[4,2,2,128,128]{4,3,2,1,0:T(8,128)S(1)} %collective-permute-done.other_ref.source_ref, f32[528,128]{1,0:T(8,128)S(1)} %get-tuple-element.38.keep_ref, f32[528,128]{1,0:T(8,128)S(1)} %convert_element_type.64.refs_0_, ...), custom_call_target="tpu_custom_call" | custom-call | bytes 2130668 | tf_op jit(solution)/shard_map/pallas_call | solution.py:38
  55.3 2.0 %shard_map.91 = (bf16[256,2048]{1,0:T(8,128)(2,1)}, bf16[256,2048]{1,0:T(8,128)(2,1)}, bf16[256,2048]{1,0:T(8,128)(2,1)}) custom-call(f32[4,2,2,128,128]{4,3,2,1,0:T(8,128)S(1)} %shard_map.86.refs_0_, bf16[256,1024]{1,0:T(8,128)(2,1)S(1)} %get-tuple-element.46.k_ref.refs_1_, bf16[256,1024]{1,0:T(8,128)(2,1)S(1)} %get-tuple-element.47.v_ref.refs_2_, ...), custom_call_target="tpu_custom_call" | custom-call | flops 402653184 | bytes 5767168 | tf_op jit(solution)/shard_map/pallas_call | solution.py:38
  57.3 0.0 collective-permute-done.10.refs_0_
  57.3 2.0 %shard_map.92 = (bf16[256,2048]{1,0:T(8,128)(2,1)}, bf16[256,2048]{1,0:T(8,128)(2,1)}, bf16[256,2048]{1,0:T(8,128)(2,1)}) custom-call(f32[4,2,2,128,128]{4,3,2,1,0:T(8,128)S(1)} %collective-permute-done.10.refs_0_, bf16[256,1024]{1,0:T(8,128)(2,1)S(1)} %get-tuple-element.42.k_ref.refs_1_, ...), custom_call_target="tpu_custom_call", output_to_operand_aliasing={{0}: (8, {}), {1}: (9, {}), {2}: (10, {})} | custom-call | flops 402653184 | bytes 8912896 | tf_op jit(solution)/shard_map/pallas_call | solution.py:38
  (18 shorter events, 0.3 us)
Async XLA Ops:
  2.7 2.7 %collective-permute-start = (f32[4,2,2,128,128]{4,3,2,1,0:T(8,128)S(1)}, f32[4,2,2,128,128]{4,3,2,1,0:T(8,128)S(1)}, u32[]{:S(2)}, u32[]{:S(2)}) collective-permute-start(f32[4,2,2,128,128]{4,3,2,1,0:T(8,128)S(1)} %get-tuple-element.29), channel_id=1, source_target_pairs={{0,1},{1,0},{2,3},{3,2},{4,5},{5,4},{6,7},{7,6},{8,9},{9,8},{10,11... | collective-permute-start | bytes 3145736 | tf_op jit(solution)/shard_map/ppermute | solution.py:51
  5.7 6.0 %collective-permute-start.1 = (f16[528,128]{1,0:T(8,128)(2,1)S(1)}, f16[528,128]{1,0:T(8,128)(2,1)S(1)}, u32[]{:S(2)}, u32[]{:S(2)}) collective-permute-start(f16[528,128]{1,0:T(8,128)(2,1)S(1)} %convert_element_type.52), channel_id=1, source_target_pairs={{0,2},{2,0},{4,6},{6,4},{8,10},{10,8},{12,14},{14,12},{16,18},{18,... | collective-permute-start | bytes 405512 | tf_op jit(solution)/shard_map/ppermute | solution.py:51
  8.1 6.3 %collective-permute-start.2 = (f16[528,128]{1,0:T(8,128)(2,1)S(1)}, f16[528,128]{1,0:T(8,128)(2,1)S(1)}, u32[]{:S(2)}, u32[]{:S(2)}) collective-permute-start(f16[528,128]{1,0:T(8,128)(2,1)S(1)} %convert_element_type.54), channel_id=1, source_target_pairs={{0,4},{2,6},{4,0},{6,2},{8,12},{10,14},{12,8},{14,10},{16,20},{18,... | collective-permute-start | bytes 405512 | tf_op jit(solution)/shard_map/ppermute | solution.py:51
  9.4 0.7 %copy-start = (f32[16,11]{1,0:T(8,128)S(1)}, f32[16,11]{1,0:T(8,128)}, u32[]{:S(2)}) copy-start(f32[16,11]{1,0:T(8,128)} %param.9) | copy-start | bytes 2116
  9.5 5.9 %collective-permute-start.3 = (f16[528,128]{1,0:T(8,128)(2,1)S(1)}, f16[528,128]{1,0:T(8,128)(2,1)S(1)}, u32[]{:S(2)}, u32[]{:S(2)}) collective-permute-start(f16[528,128]{1,0:T(8,128)(2,1)S(1)} %convert_element_type.56), channel_id=1, source_target_pairs={{0,6},{2,4},{4,2},{6,0},{8,14},{10,12},{12,10},{14,8},{16,22},{18,... | collective-permute-start | bytes 405512 | tf_op jit(solution)/shard_map/ppermute | solution.py:51
  16.3 4.1 %collective-permute-start.5 = (f16[272,128]{1,0:T(8,128)(2,1)S(1)}, f16[272,128]{1,0:T(8,128)(2,1)S(1)}, u32[]{:S(2)}, u32[]{:S(2)}) collective-permute-start(f16[272,128]{1,0:T(8,128)(2,1)S(1)} %convert_element_type.60), channel_id=1, source_target_pairs={{0,16},{2,18},{4,20},{6,22},{8,24},{10,26},{12,28},{14,30},{16,0},... | collective-permute-start | bytes 208904 | tf_op jit(solution)/shard_map/ppermute | solution.py:51
  18.7 5.7 %collective-permute-start.6 = (f16[272,128]{1,0:T(8,128)(2,1)S(1)}, f16[272,128]{1,0:T(8,128)(2,1)S(1)}, u32[]{:S(2)}, u32[]{:S(2)}) collective-permute-start(f16[272,128]{1,0:T(8,128)(2,1)S(1)} %convert_element_type.60), channel_id=1, source_target_pairs={{0,24},{2,26},{4,28},{6,30},{8,16},{10,18},{12,20},{14,22},{16,8},... | collective-permute-start | bytes 208904 | tf_op jit(solution)/shard_map/ppermute | solution.py:51
  19.8 4.6 %collective-permute-start.4 = (f16[272,128]{1,0:T(8,128)(2,1)S(1)}, f16[272,128]{1,0:T(8,128)(2,1)S(1)}, u32[]{:S(2)}, u32[]{:S(2)}) collective-permute-start(f16[272,128]{1,0:T(8,128)(2,1)S(1)} %convert_element_type.58), channel_id=1, source_target_pairs={{0,8},{2,10},{4,12},{6,14},{8,0},{10,2},{12,4},{14,6},{16,24},{18,... | collective-permute-start | bytes 208904 | tf_op jit(solution)/shard_map/ppermute | solution.py:51
  25.4 3.9 %collective-permute-start.7 = (f16[528,128]{1,0:T(8,128)(2,1)S(1)}, f16[528,128]{1,0:T(8,128)(2,1)S(1)}, u32[]{:S(2)}, u32[]{:S(2)}) collective-permute-start(f16[528,128]{1,0:T(8,128)(2,1)S(1)} %convert_element_type.63), channel_id=1, source_target_pairs={{0,2},{2,0},{4,6},{6,4},{8,10},{10,8},{12,14},{14,12},{16,18},{18,... | collective-permute-start | bytes 405512 | tf_op jit(solution)/shard_map/ppermute | solution.py:51
  26.5 3.9 %collective-permute-start.8 = (f16[528,128]{1,0:T(8,128)(2,1)S(1)}, f16[528,128]{1,0:T(8,128)(2,1)S(1)}, u32[]{:S(2)}, u32[]{:S(2)}) collective-permute-start(f16[528,128]{1,0:T(8,128)(2,1)S(1)} %convert_element_type.65), channel_id=1, source_target_pairs={{0,4},{2,6},{4,0},{6,2},{8,12},{10,14},{12,8},{14,10},{16,20},{18,... | collective-permute-start | bytes 405512 | tf_op jit(solution)/shard_map/ppermute | solution.py:51
  27.2 4.8 %collective-permute-start.9 = (f16[528,128]{1,0:T(8,128)(2,1)S(1)}, f16[528,128]{1,0:T(8,128)(2,1)S(1)}, u32[]{:S(2)}, u32[]{:S(2)}) collective-permute-start(f16[528,128]{1,0:T(8,128)(2,1)S(1)} %convert_element_type.67), channel_id=1, source_target_pairs={{0,6},{2,4},{4,2},{6,0},{8,14},{10,12},{12,10},{14,8},{16,22},{18,... | collective-permute-start | bytes 405512 | tf_op jit(solution)/shard_map/ppermute | solution.py:51
  33.0 24.4 %collective-permute-start.10 = (f32[4,2,2,128,128]{4,3,2,1,0:T(8,128)S(1)}, f32[4,2,2,128,128]{4,3,2,1,0:T(8,128)S(1)}, u32[]{:S(2)}, u32[]{:S(2)}) collective-permute-start(f32[4,2,2,128,128]{4,3,2,1,0:T(8,128)S(1)} %shard_map.81), channel_id=1, source_target_pairs={{0,1},{1,0},{2,3},{3,2},{4,5},{5,4},{6,7},{7,6},{8,9},{9,8},{10,11... | collective-permute-start | bytes 3145736 | tf_op jit(solution)/shard_map/ppermute | solution.py:51

commit v5 on v4

--- a/solution.py
+++ b/solution.py
@@ -18,7 +18,6 @@
 NT = (((1,), (1,)), ((), ()))
 TN = (((0,), (0,)), ((), ()))
 VMEM = pl.BlockSpec(memory_space=pltpu.VMEM)
-SMEM = pl.BlockSpec(memory_space=pltpu.SMEM)
 HBM = pl.BlockSpec(memory_space=pltpu.HBM)
 
 
@@ -145,8 +144,9 @@
     )
 
 
-def local_kernel(half, group, width, scale_ref, q_ref, k_ref, v_ref, o_ref, out_ref):
-    tokens = q_ref.shape[0]
+def local_kernel(lot, width, scale_ref, *refs):
+    held, out_ref = (refs[:4], refs[4:8]), refs[8]
+    tokens, model = refs[0].shape
     blocks = tokens // BLOCK
     rows = lax.broadcasted_iota(jnp.int32, (BLOCK, BLOCK), 0)
     cols = lax.broadcasted_iota(jnp.int32, (BLOCK, BLOCK), 1)
@@ -170,29 +170,31 @@
             out = out + dot(lo, values[blk(m)])
         return out
 
-    for j in range(width):
-        at = slice((group * width + j) * DH, (group * width + j + 1) * DH)
-        to = slice(j * DH, (j + 1) * DH)
-        q, k, v, o = q_ref[:, at], k_ref[:, at], v_ref[:, at], o_ref[:, at]
-        head = first_head(half, q_ref.shape[1] // DH) + group * width + j
-
-        def weight(level, head=head):
-            return scale_ref[head, level]
-
-        for n in range(blocks):
-            out_ref[2, blk(n), to] = product(k, q, weight, o, n, n, blocks, rows <= cols)
-            out_ref[1, blk(n), to] = product(v, o, weight, q, n, n, blocks, rows <= cols)
-            out_ref[0, blk(n), to] = product(o, v, weight, k, n, 0, n + 1, rows >= cols)
-
-
-def local_grads(half, group, level_scale, held, width):
-    tokens = held[0].shape[0]
+    place = near_place(model // (width * DH))
+    for index, (half, d) in enumerate(lot):
+        group = place ^ d
+        for j in range(width):
+            at = pl.ds(pl.multiple_of((group * width + j) * DH, DH), DH)
+            to = slice(j * DH, (j + 1) * DH)
+            q, k, v, o = (ref[:, at] for ref in held[half])
+            head = first_head(half, model // DH) + group * width + j
+
+            def weight(level, head=head):
+                return scale_ref[head, level : level + 1]
+
+            for n in range(blocks):
+                out_ref[index, 2, blk(n), to] = product(k, q, weight, o, n, n, blocks, rows <= cols)
+                out_ref[index, 1, blk(n), to] = product(v, o, weight, q, n, n, blocks, rows <= cols)
+                out_ref[index, 0, blk(n), to] = product(o, v, weight, k, n, 0, n + 1, rows >= cols)
+
+
+def local_grads(lot, scales, held, width):
+    tokens = held[0][0].shape[0]
     return call(
-        functools.partial(local_kernel, half, group, width),
-        [pltpu.VMEM((3, tokens, width * DH), F32)],
-        [level_scale, *held],
-        specs=[SMEM] + [VMEM] * 4,
-        flops=24 * tokens * BLOCK * width * DH,
+        functools.partial(local_kernel, lot, width),
+        [pltpu.VMEM((len(lot), 3, tokens, width * DH), F32)],
+        [scales, *held[0], *held[1]],
+        flops=24 * tokens * BLOCK * width * DH * len(lot),
     )[0]
 
 
@@ -213,11 +215,7 @@
 
 
 def head_weight(scale_ref, place, slices, width, j, level):
-    return scale_ref[first_head(0, slices * width) + place * width + j, level]
-
-
-def top_weight(scale_ref):
-    return scale_ref[scale_ref.shape[0] - 1, 0]
+    return scale_ref[first_head(0, slices * width) + place * width + j, level : level + 1]
 
 
 def plane_kernel(plane_bits, base, rest, wide, scale_ref, keep_ref, *refs):
@@ -310,7 +308,10 @@
     for got_ref, up in zip(gots, ups):
         size = jnp.exp2(TOP - mark(got_ref, 0))
         bounds = [bounds[0] + up * size, bounds[1] + (1.0 - up) * size]
-    powers = [bound_power(top_weight(scale_ref) * bound) for bound in bounds]
+    head = first_head(0, scale_ref.shape[0] // lax.axis_size("head")) + place * width
+    most = functools.reduce(jnp.maximum, [jnp.abs(scale_ref[head + j]) for j in range(width)])
+    most = jnp.max(most, axis=0, keepdims=True)
+    powers = [bound_power(most * bound) for bound in bounds]
     factors = [jnp.exp2(power)[:1] for power in powers]
     for out_ref in (keep_ref, *outs):
         put_marks(out_ref, powers)
@@ -329,12 +330,16 @@
                 out_ref[to : to + PIECE] = value if d == 0 else value * factors[t]
 
 
-def core_kernel(level, mine, scale_ref, source_ref, keep_ref, *refs):
+def core_side(mine):
+    second = lax.axis_index("head").astype(F32)
+    return (second, 1.0 - second) if mine else (1.0 - second, second)
+
+
+def core_kernel(level, scale_ref, source_ref, keep_ref, *refs):
     parts, out_ref = (keep_ref, *refs[:-1]), refs[-1]
     slices, _, width = source_ref.shape[:3]
     place = near_place(slices)
-    second = lax.axis_index("head").astype(F32)
-    sides = (second, 1.0 - second) if mine else (1.0 - second, second)
+    sides = core_side(False)
     for d in range(slices):
         factors = [None if d == 0 else jnp.exp2(-mark(parts[d], t)[:1]) for t in range(2)]
         for j, r, rows in pieces(width):
@@ -347,47 +352,66 @@
                 out_ref[d, t, j, rows] = got + (sides[t] * weight) * source_ref[d, t, j, rows]
 
 
-def cross_kernel(half, cuts, state_ref, k_ref, v_ref, o_ref, local_refs, outs, temps, sems):
-    slices, _, width = state_ref.shape[:3]
+def cross_kernel(half, states_of, k_ref, v_ref, o_ref, local_of, outs, temps, sems):
+    slices, width = temps.shape[0], temps.shape[3] // DH
     model = k_ref.shape[1]
     place = near_place(slices)
-    size = model // cuts
     copies = []
-    for c in range(cuts):
-        for head in range(c * size // DH, (c + 1) * size // DH):
-            group, j = head // width, head % width
-            d = place ^ group
-            cs = slice(head * DH, (head + 1) * DH)
+    for d in range(slices):
+        group = place ^ d
+        for j in range(width):
+            at = pl.ds(pl.multiple_of((group * width + j) * DH, DH), DH)
             to = slice(j * DH, (j + 1) * DH)
-            o, v, k = o_ref[:, cs], v_ref[:, cs], k_ref[:, cs]
-            hi, lo = split(state_ref[d, 0, j])
+            o, v, k = o_ref[:, at], v_ref[:, at], k_ref[:, at]
+            early, late = states_of(d, j)
+            hi, lo = split(early)
             qg = dot(o, hi) + dot(o, lo)
-            hi, lo = split(state_ref[d, 1, j])
+            hi, lo = split(late)
             kg = dot(v, hi) + dot(v, lo)
             vg = dot(k, hi, NT) + dot(k, lo, NT)
             for i, cross in enumerate((qg, kg, vg)):
-                temps[i, :, cs] = (cross + local_refs[group][i, :, to]).astype(BF16)
-        cs = slice(c * size, (c + 1) * size)
-        cols = pl.ds(pl.multiple_of(first_head(half, model // DH) * DH + c * size, DH), size)
+                temps[d, i, :, to] = (cross + local_of(d, i, to)).astype(BF16)
+        start = first_head(half, model // DH) * DH + group * (width * DH)
+        cols = pl.ds(pl.multiple_of(start, DH), width * DH)
         for i in range(3):
-            copy = pltpu.make_async_copy(temps.at[i, :, cs], outs[i].at[:, cols], sems.at[c, i])
+            copy = pltpu.make_async_copy(temps.at[d, i], outs[i].at[:, cols], sems.at[d, i])
             copy.start()
             copies.append(copy)
     for copy in copies:
         copy.wait()
 
 
-def finish(half, states, held, local, model, before):
+def finish(half, source, held, parts, where, scales, level, model, before):
     tokens, cols = held[0].shape
-    slices = states.shape[0]
-    cuts = 2 if slices % 2 == 0 else 1
-    args = [states, *held[1:], *local]
+    slices, _, width = source[0].shape[:3]
+    count = len(source)
+    args = [*source, scales, *held[1:], *parts]
     specs = [VMEM] * len(args) + [HBM] * len(before)
 
     def kernel(*refs):
-        parts = refs[4 : len(args)]
-        outs = refs[len(specs) : len(specs) + 3]
-        cross_kernel(half, cuts, *refs[:4], parts, outs, refs[-2], refs[-1])
+        states, scale_ref, held_refs = refs[:count], refs[count], refs[count + 1 : count + 4]
+        local_refs, outs = refs[count + 4 : len(args)], refs[len(specs) : len(specs) + 3]
+        place = near_place(slices)
+        sides = core_side(True)
+
+        def states_of(d, j):
+            if count == 1:
+                return [states[0][d, t, j] for t in range(2)]
+            weight = head_weight(scale_ref, place ^ d, slices, width, j, level)
+            out = []
+            for t in range(2):
+                ref = states[1 + d]
+                got = ref[(t * width + j) * DH : (t * width + j + 1) * DH]
+                if d:
+                    got = got * jnp.exp2(-mark(ref, t)[:1])
+                out.append(got + (sides[t] * weight) * states[0][d, t, j])
+            return out
+
+        def local_of(d, i, to):
+            part, index = where[half, d]
+            return local_refs[part][index, i, :, to]
+
+        cross_kernel(half, states_of, *held_refs, local_of, outs, refs[-2], refs[-1])
 
     return call(
         kernel,
@@ -395,7 +419,7 @@
         args + list(before),
         specs=specs,
         out_specs=[HBM] * 3,
-        scratch=[pltpu.VMEM((3, tokens, cols), BF16), pltpu.SemaphoreType.DMA((cuts, 3))],
+        scratch=[pltpu.VMEM((slices, 3, tokens, width * DH), BF16), pltpu.SemaphoreType.DMA((slices, 3))],
         flops=12 * tokens * DH * cols,
         limit=4,
         aliases={len(args) + i: i for i in range(len(before))},
@@ -417,18 +441,23 @@
     rest = bits - plane_bits
     direct = min(2, rest)
 
-    most = jnp.full((1, level_scale.shape[1]), jnp.max(jnp.abs(level_scale)))
-    level_scale = jnp.concatenate([level_scale, most])
+    padded = jnp.pad(level_scale, ((0, 0), (0, -level_scale.shape[1] % 8)))
+    scales = jnp.broadcast_to(padded[:, :, None], (*padded.shape, DH))
 
     args = [pltpu.with_memory_space_constraint(x, pltpu.HBM) for x in (queries, key_rows, values, out_grad)]
     sent, *held_there = device_states(1, args, slices, width)
     other = partner(sent, "head", 1)
     own, *held_here = device_states(0, args, slices, width)
     held = (held_here, held_there)
-    local = [[], []]
-    for half in range(2):
-        for group in range(slices):
-            local[half].append(local_grads(half, group, level_scale, held[half], width))
+    every = [(half, d) for half in range(2) for d in range(slices)]
+    ends = [0, 3 * len(every) // 8, 6 * len(every) // 8, len(every)]
+    where, local = {}, []
+    for low, high in zip(ends, ends[1:]):
+        if low == high:
+            continue
+        for i, key in enumerate(every[low:high]):
+            where[key] = (len(local), i)
+        local.append(local_grads(tuple(every[low:high]), scales, held, width))
 
     state = pltpu.VMEM((2, width, DH, DH), F32)
     load = pltpu.VMEM((2 * width * DH + EXTRA, DH), F32)
@@ -444,8 +473,7 @@
     near_sum, bounds, *outs = call(
         functools.partial(plane_kernel, plane_bits, base, rest, wide),
         [near, bound] + ([state] if wide else [single] * direct),
-        [level_scale, keep, *got],
-        specs=[SMEM] + [VMEM] * slices,
+        [scales, keep, *got],
     )
     total = outs[0] if wide else None
     for index in range(rest - direct):
@@ -455,8 +483,7 @@
         near_sum, bounds, total, *outs = call(
             functools.partial(merge_kernel, slices, index, base + plane_bits + index, rest),
             [near, bound, state] + [single] * sending,
-            [level_scale, near_sum, bounds, total, arrived],
-            specs=[SMEM] + [VMEM] * 4,
+            [scales, near_sum, bounds, total, arrived],
         )
     got, levels, which = [], [], []
     for step in range(1, 1 << direct):
@@ -465,25 +492,16 @@
         which.append(rest - direct + top)
         levels.append(base + plane_bits + rest - direct + top)
     keep, *outs = call(
-        functools.partial(back_kernel, slices, levels, which),
-        [load] * slices,
-        [level_scale, near_sum, bounds, *got],
-        specs=[SMEM] + [VMEM] * (2 + len(got)),
+        functools.partial(back_kernel, slices, levels, which), [load] * slices, [scales, near_sum, bounds, *got]
     )
     got = []
     for d in range(1, slices):
         got.append(narrow(outs[d - 1], "seq", d))
-    gathered = []
-    for mine, source in ((False, own), (True, other)):
-        gathered += call(
-            functools.partial(core_kernel, local_levels + 1, mine),
-            [near],
-            [level_scale, source, keep, *got],
-            specs=[SMEM] + [VMEM] * (2 + len(got)),
-        )
-    theirs = partner(gathered[0], "head", 1)
-    half_done = finish(0, gathered[1], held[0], local[0], model, [])
-    return tuple(finish(1, theirs, held[1], local[1], model, half_done))
+    level = local_levels + 1
+    theirs = call(functools.partial(core_kernel, level), [near], [scales, own, keep, *got])[0]
+    theirs = partner(theirs, "head", 1)
+    half_done = finish(0, [other, keep, *got], held[0], local, where, scales, level, model, [])
+    return tuple(finish(1, [theirs], held[1], local, where, scales, level, model, half_done))
 
 
 def solution(mesh):

time: 59.6 us -> 52.6 us (0.88)
  Pallas kernels: 28.9 us -> 19.1 us
  waiting for transfers between devices: 12.5 us -> 20.9 us
  starting transfers between devices: 14.9 us -> 11.1 us
  local copies, waits for them, and re-layouts: 1.24 us -> 0.1 us
  other arithmetic: 0.92 us -> 0.32 us
    pallas_call x17 -> x11, Pallas kernels: 28.9 us -> 19.1 us  [call(): pl.pallas_call(kernel, in_specs=specs or [VMEM] * len(args), out_specs=ou...]
    ppermute x11, waiting for transfers between devices: 12.5 us -> 20.9 us  [partner(): lax.ppermute(array, axis, [(i, i ^ distance) for i in range(lax.axis_size...]
    ppermute x11, starting transfers between devices: 14.9 us -> 11.1 us  [partner(): lax.ppermute(array, axis, [(i, i ^ distance) for i in range(lax.axis_size...]
    concatenate x1 -> x0, local copies, waits for them, and re-layouts: 0.65 us -> none  [work(): level_scale = jnp.concatenate([level_scale, most])]
    reduce_max x1 -> x0, other arithmetic: 0.6 us -> none  [work(): most = jnp.full((1, level_scale.shape[1]), jnp.max(jnp.abs(level_scale)))]
  transfers between devices with their start and end apart: 11 -> 11, of which waited for: 9 -> 7; matrix products, arithmetic and copies ran while one was open for 2% -> 0% of each run, Pallas kernels for 37% -> 27%
where the time goes in v5:
time: 52.6 us; the launch traced here: 52.4 us
  waiting for transfers between devices  20.9 us (40%)
  Pallas kernels  19.1 us (36%)
  starting transfers between devices  11.1 us (21%)
  between operations  0.85 us (2%)
    ppermute x11, waiting for transfers between devices, partner(): lax.ppermute(array, axis, [(i, i ^ distance) for i in range(lax.axis_size...  20.9 us
    pallas_call x11, Pallas kernels, call(): pl.pallas_call(kernel, in_specs=specs or [VMEM] * len(args), out_specs=ou...  19.1 us
    ppermute x11, starting transfers between devices, partner(): lax.ppermute(array, axis, [(i, i ^ distance) for i in range(lax.axis_size...  11.1 us
  transfers between devices with their start and end apart: 11, of which 7 were waited for; matrix products, arithmetic and copies ran while one was open for 0% of the time, Pallas kernels for 27%

profile of v5, /device:TPU:1, one launch (start us, length us, event | category | flops | bytes accessed | tf_op | source)
XLA Modules:
  0.0 52.4 jit_solution(11225148638928174784)
XLA Ops:
  0.6 2.0 %shard_map.77 = (f32[4,2,2,128,128]{4,3,2,1,0:T(8,128)S(1)}, bf16[256,1024]{1,0:T(8,128)(2,1)S(1)}, bf16[256,1024]{1,0:T(8,128)(2,1)S(1)}, bf16[256,1024]{1,0:T(8,128)(2,1)S(1)}, bf16[256,1024]{1,0:T(8,128)(2,1)S(1)}) custom-call(bf16[256,2048]{1,0:T(8,128)(2,1)} %refs_0_.3, bf16[256,2048]{1,0:T(8,128)(2,1)} %refs_1_.3, bf16[256,2048]{1,0:T(8,128)(2,1)} %refs_2_.3, ...), custom_call_target="tpu_custom_call" | custom-call | flops 134217728 | bytes 4194304 | tf_op jit(solution)/shard_map/pallas_call | solution.py:37
  2.7 0.1 collective-permute-start
  2.8 2.0 %shard_map.76 = (f32[4,2,2,128,128]{4,3,2,1,0:T(8,128)S(1)}, bf16[256,1024]{1,0:T(8,128)(2,1)S(1)}, bf16[256,1024]{1,0:T(8,128)(2,1)S(1)}, bf16[256,1024]{1,0:T(8,128)(2,1)S(1)}, bf16[256,1024]{1,0:T(8,128)(2,1)S(1)}) custom-call(bf16[256,2048]{1,0:T(8,128)(2,1)} %refs_0_.3, bf16[256,2048]{1,0:T(8,128)(2,1)} %refs_1_.3, bf16[256,2048]{1,0:T(8,128)(2,1)} %refs_2_.3, ...), custom_call_target="tpu_custom_call" | custom-call | flops 134217728 | bytes 4194304 | tf_op jit(solution)/shard_map/pallas_call | solution.py:37
  4.8 0.0 copy-start
  4.8 0.6 %collective-permute-done.other_ref.refs_0_ = f32[4,2,2,128,128]{4,3,2,1,0:T(8,128)S(1)} collective-permute-done((f32[4,2,2,128,128]{4,3,2,1,0:T(8,128)S(1)}, f32[4,2,2,128,128]{4,3,2,1,0:T(8,128)S(1)}, u32[]{:S(2)}, u32[]{:S(2)}) %collective-permute-start) | collective-permute-done | bytes 1048608 | tf_op jit(solution)/shard_map/ppermute | solution.py:50
  5.4 0.3 shard_map.78
  5.8 3.3 %collective-permute-start.3 = (f16[528,128]{1,0:T(8,128)(2,1)S(1)}, f16[528,128]{1,0:T(8,128)(2,1)S(1)}, u32[]{:S(2)}, u32[]{:S(2)}) collective-permute-start(f16[528,128]{1,0:T(8,128)(2,1)S(1)} %convert_element_type.58), channel_id=1, source_target_pairs={{0,6},{2,4},{4,2},{6,0},{8,14},{10,12},{12,10},{14,8},{16,22},{18,... | collective-permute-start | bytes 405512 | tf_op jit(solution)/shard_map/ppermute | solution.py:50
  9.1 0.2 collective-permute-start.2
  9.3 0.1 collective-permute-start.1
  9.5 0.0 copy-done
  9.5 3.2 %collective-permute-done.3 = f16[528,128]{1,0:T(8,128)(2,1)S(1)} collective-permute-done((f16[528,128]{1,0:T(8,128)(2,1)S(1)}, f16[528,128]{1,0:T(8,128)(2,1)S(1)}, u32[]{:S(2)}, u32[]{:S(2)}) %collective-permute-start.3) | collective-permute-done | bytes 135200 | tf_op jit(solution)/shard_map/ppermute | solution.py:50
  12.7 3.3 %collective-permute-done.2 = f16[528,128]{1,0:T(8,128)(2,1)S(1)} collective-permute-done((f16[528,128]{1,0:T(8,128)(2,1)S(1)}, f16[528,128]{1,0:T(8,128)(2,1)S(1)}, u32[]{:S(2)}, u32[]{:S(2)}) %collective-permute-start.2) | collective-permute-done | bytes 135200 | tf_op jit(solution)/shard_map/ppermute | solution.py:50
  16.1 0.0 collective-permute-done.1
  16.1 0.1 broadcast_in_dim.2.scale_ref.refs_5_.refs_1_
  16.2 0.2 shard_map.79
  16.5 1.6 %collective-permute-start.4 = (f16[272,128]{1,0:T(8,128)(2,1)S(1)}, f16[272,128]{1,0:T(8,128)(2,1)S(1)}, u32[]{:S(2)}, u32[]{:S(2)}) collective-permute-start(f16[272,128]{1,0:T(8,128)(2,1)S(1)} %convert_element_type.60), channel_id=1, source_target_pairs={{0,8},{2,10},{4,12},{6,14},{8,0},{10,2},{12,4},{14,6},{16,24},{18,... | collective-permute-start | bytes 208904 | tf_op jit(solution)/shard_map/ppermute | solution.py:50
  18.1 2.3 %collective-permute-start.6 = (f16[272,128]{1,0:T(8,128)(2,1)S(1)}, f16[272,128]{1,0:T(8,128)(2,1)S(1)}, u32[]{:S(2)}, u32[]{:S(2)}) collective-permute-start(f16[272,128]{1,0:T(8,128)(2,1)S(1)} %convert_element_type.62), channel_id=1, source_target_pairs={{0,24},{2,26},{4,28},{6,30},{8,16},{10,18},{12,20},{14,22},{16,8},... | collective-permute-start | bytes 208904 | tf_op jit(solution)/shard_map/ppermute | solution.py:50
  20.3 0.2 collective-permute-start.5
  20.5 0.0 collective-permute-done.4
  20.5 3.5 %collective-permute-done.6 = f16[272,128]{1,0:T(8,128)(2,1)S(1)} collective-permute-done((f16[272,128]{1,0:T(8,128)(2,1)S(1)}, f16[272,128]{1,0:T(8,128)(2,1)S(1)}, u32[]{:S(2)}, u32[]{:S(2)}) %collective-permute-start.6) | collective-permute-done | bytes 69664 | tf_op jit(solution)/shard_map/ppermute | solution.py:50
  24.1 3.7 %collective-permute-done.5 = f16[272,128]{1,0:T(8,128)(2,1)S(1)} collective-permute-done((f16[272,128]{1,0:T(8,128)(2,1)S(1)}, f16[272,128]{1,0:T(8,128)(2,1)S(1)}, u32[]{:S(2)}, u32[]{:S(2)}) %collective-permute-start.5) | collective-permute-done | bytes 69664 | tf_op jit(solution)/shard_map/ppermute | solution.py:50
  27.8 0.2 shard_map.80
  28.0 0.6 %collective-permute-start.9 = (f16[528,128]{1,0:T(8,128)(2,1)S(1)}, f16[528,128]{1,0:T(8,128)(2,1)S(1)}, u32[]{:S(2)}, u32[]{:S(2)}) collective-permute-start(f16[528,128]{1,0:T(8,128)(2,1)S(1)} %convert_element_type.69), channel_id=1, source_target_pairs={{0,6},{2,4},{4,2},{6,0},{8,14},{10,12},{12,10},{14,8},{16,22},{18,... | collective-permute-start | bytes 405512 | tf_op jit(solution)/shard_map/ppermute | solution.py:50
  28.6 1.9 %collective-permute-start.8 = (f16[528,128]{1,0:T(8,128)(2,1)S(1)}, f16[528,128]{1,0:T(8,128)(2,1)S(1)}, u32[]{:S(2)}, u32[]{:S(2)}) collective-permute-start(f16[528,128]{1,0:T(8,128)(2,1)S(1)} %convert_element_type.67), channel_id=1, source_target_pairs={{0,4},{2,6},{4,0},{6,2},{8,12},{10,14},{12,8},{14,10},{16,20},{18,... | collective-permute-start | bytes 405512 | tf_op jit(solution)/shard_map/ppermute | solution.py:50
  30.5 0.3 collective-permute-start.7
  30.8 2.9 %collective-permute-done.9 = f16[528,128]{1,0:T(8,128)(2,1)S(1)} collective-permute-done((f16[528,128]{1,0:T(8,128)(2,1)S(1)}, f16[528,128]{1,0:T(8,128)(2,1)S(1)}, u32[]{:S(2)}, u32[]{:S(2)}) %collective-permute-start.9) | collective-permute-done | bytes 135200 | tf_op jit(solution)/shard_map/ppermute | solution.py:50
  33.7 3.7 %collective-permute-done.8 = f16[528,128]{1,0:T(8,128)(2,1)S(1)} collective-permute-done((f16[528,128]{1,0:T(8,128)(2,1)S(1)}, f16[528,128]{1,0:T(8,128)(2,1)S(1)}, u32[]{:S(2)}, u32[]{:S(2)}) %collective-permute-start.8) | collective-permute-done | bytes 135200 | tf_op jit(solution)/shard_map/ppermute | solution.py:50
  37.4 0.0 collective-permute-done.7
  37.5 0.1 shard_map.81
  37.6 0.6 %collective-permute-start.10 = (f32[4,2,2,128,128]{4,3,2,1,0:T(8,128)S(1)}, f32[4,2,2,128,128]{4,3,2,1,0:T(8,128)S(1)}, u32[]{:S(2)}, u32[]{:S(2)}) collective-permute-start(f32[4,2,2,128,128]{4,3,2,1,0:T(8,128)S(1)} %shard_map.81), channel_id=1, source_target_pairs={{0,1},{1,0},{2,3},{3,2},{4,5},{5,4},{6,7},{7,6},{8,9},{9,8},{10,11... | collective-permute-start | bytes 3145736 | tf_op jit(solution)/shard_map/ppermute | solution.py:50
  38.2 2.6 %shard_map.84.refs_11_.refs_7_ = f32[2,3,256,256]{3,2,1,0:T(8,128)S(1)} custom-call(f32[16,16,128]{2,1,0:T(8,128)S(1)} %broadcast_in_dim.2.scale_ref.refs_5_.refs_1_, bf16[256,1024]{1,0:T(8,128)(2,1)S(1)} %get-tuple-element.45.refs_0_, bf16[256,1024]{1,0:T(8,128)(2,1)S(1)} %get-tuple-element.46.refs_1_.refs_6_, ...), custom_call_target="tpu_custom_call" | custom-call | flops 402653184 | bytes 4325376 | tf_op jit(solution)/shard_map/pallas_call | solution.py:37
  40.8 3.9 %shard_map.83.refs_10_.refs_6_ = f32[3,3,256,256]{3,2,1,0:T(8,128)S(1)} custom-call(f32[16,16,128]{2,1,0:T(8,128)S(1)} %broadcast_in_dim.2.scale_ref.refs_5_.refs_1_, bf16[256,1024]{1,0:T(8,128)(2,1)S(1)} %get-tuple-element.45.refs_0_, bf16[256,1024]{1,0:T(8,128)(2,1)S(1)} %get-tuple-element.46.refs_1_.refs_6_, ...), custom_call_target="tpu_custom_call" | custom-call | flops 603979776 | bytes 4325376 | tf_op jit(solution)/shard_map/pallas_call | solution.py:37
  44.7 3.9 %shard_map.82.refs_9_.refs_5_ = f32[3,3,256,256]{3,2,1,0:T(8,128)S(1)} custom-call(f32[16,16,128]{2,1,0:T(8,128)S(1)} %broadcast_in_dim.2.scale_ref.refs_5_.refs_1_, bf16[256,1024]{1,0:T(8,128)(2,1)S(1)} %get-tuple-element.45.refs_0_, bf16[256,1024]{1,0:T(8,128)(2,1)S(1)} %get-tuple-element.46.refs_1_.refs_6_, ...), custom_call_target="tpu_custom_call" | custom-call | flops 603979776 | bytes 4325376 | tf_op jit(solution)/shard_map/pallas_call | solution.py:37
  48.6 1.9 %shard_map.85 = (bf16[256,2048]{1,0:T(8,128)(2,1)}, bf16[256,2048]{1,0:T(8,128)(2,1)}, bf16[256,2048]{1,0:T(8,128)(2,1)}) custom-call(f32[4,2,2,128,128]{4,3,2,1,0:T(8,128)S(1)} %collective-permute-done.other_ref.refs_0_, f32[528,128]{1,0:T(8,128)S(1)} %get-tuple-element.38.keep_ref.refs_1_, f32[528,128]{1,0:T(8,128)S(1)} %convert_element_type.66.refs_0_.refs_2_, ...), custom_call_target="tpu_custom_call" | custom-call | flops 402653184 | bytes 10125312 | tf_op jit(solution)/shard_map/pallas_call | solution.py:37
  50.5 0.0 collective-permute-done.10.refs_0_
  50.5 1.9 %shard_map.86 = (bf16[256,2048]{1,0:T(8,128)(2,1)}, bf16[256,2048]{1,0:T(8,128)(2,1)}, bf16[256,2048]{1,0:T(8,128)(2,1)}) custom-call(f32[4,2,2,128,128]{4,3,2,1,0:T(8,128)S(1)} %collective-permute-done.10.refs_0_, f32[16,16,128]{2,1,0:T(8,128)S(1)} %broadcast_in_dim.2.scale_ref.refs_5_.refs_1_, ...), custom_call_target="tpu_custom_call", output_to_operand_aliasing={{0}: (8, {}), {1}: (9, {}), {2}: (10, {})} | custom-call | flops 402653184 | bytes 12189696 | tf_op jit(solution)/shard_map/pallas_call | solution.py:37
  (20 shorter events, 0.3 us)
Async XLA Ops:
  2.7 2.7 %collective-permute-start = (f32[4,2,2,128,128]{4,3,2,1,0:T(8,128)S(1)}, f32[4,2,2,128,128]{4,3,2,1,0:T(8,128)S(1)}, u32[]{:S(2)}, u32[]{:S(2)}) collective-permute-start(f32[4,2,2,128,128]{4,3,2,1,0:T(8,128)S(1)} %get-tuple-element.29), channel_id=1, source_target_pairs={{0,1},{1,0},{2,3},{3,2},{4,5},{5,4},{6,7},{7,6},{8,9},{9,8},{10,11... | collective-permute-start | bytes 3145736 | tf_op jit(solution)/shard_map/ppermute | solution.py:50
  4.8 4.7 %copy-start = (f32[16,11]{1,0:T(8,128)S(1)}, f32[16,11]{1,0:T(8,128)}, u32[]{:S(2)}) copy-start(f32[16,11]{1,0:T(8,128)} %param.9) | copy-start | bytes 2116
  5.8 6.9 %collective-permute-start.3 = (f16[528,128]{1,0:T(8,128)(2,1)S(1)}, f16[528,128]{1,0:T(8,128)(2,1)S(1)}, u32[]{:S(2)}, u32[]{:S(2)}) collective-permute-start(f16[528,128]{1,0:T(8,128)(2,1)S(1)} %convert_element_type.58), channel_id=1, source_target_pairs={{0,6},{2,4},{4,2},{6,0},{8,14},{10,12},{12,10},{14,8},{16,22},{18,... | collective-permute-start | bytes 405512 | tf_op jit(solution)/shard_map/ppermute | solution.py:50
  9.1 6.9 %collective-permute-start.2 = (f16[528,128]{1,0:T(8,128)(2,1)S(1)}, f16[528,128]{1,0:T(8,128)(2,1)S(1)}, u32[]{:S(2)}, u32[]{:S(2)}) collective-permute-start(f16[528,128]{1,0:T(8,128)(2,1)S(1)} %convert_element_type.56), channel_id=1, source_target_pairs={{0,4},{2,6},{4,0},{6,2},{8,12},{10,14},{12,8},{14,10},{16,20},{18,... | collective-permute-start | bytes 405512 | tf_op jit(solution)/shard_map/ppermute | solution.py:50
  9.3 6.7 %collective-permute-start.1 = (f16[528,128]{1,0:T(8,128)(2,1)S(1)}, f16[528,128]{1,0:T(8,128)(2,1)S(1)}, u32[]{:S(2)}, u32[]{:S(2)}) collective-permute-start(f16[528,128]{1,0:T(8,128)(2,1)S(1)} %convert_element_type.54), channel_id=1, source_target_pairs={{0,2},{2,0},{4,6},{6,4},{8,10},{10,8},{12,14},{14,12},{16,18},{18,... | collective-permute-start | bytes 405512 | tf_op jit(solution)/shard_map/ppermute | solution.py:50
  16.5 4.0 %collective-permute-start.4 = (f16[272,128]{1,0:T(8,128)(2,1)S(1)}, f16[272,128]{1,0:T(8,128)(2,1)S(1)}, u32[]{:S(2)}, u32[]{:S(2)}) collective-permute-start(f16[272,128]{1,0:T(8,128)(2,1)S(1)} %convert_element_type.60), channel_id=1, source_target_pairs={{0,8},{2,10},{4,12},{6,14},{8,0},{10,2},{12,4},{14,6},{16,24},{18,... | collective-permute-start | bytes 208904 | tf_op jit(solution)/shard_map/ppermute | solution.py:50
  18.1 6.0 %collective-permute-start.6 = (f16[272,128]{1,0:T(8,128)(2,1)S(1)}, f16[272,128]{1,0:T(8,128)(2,1)S(1)}, u32[]{:S(2)}, u32[]{:S(2)}) collective-permute-start(f16[272,128]{1,0:T(8,128)(2,1)S(1)} %convert_element_type.62), channel_id=1, source_target_pairs={{0,24},{2,26},{4,28},{6,30},{8,16},{10,18},{12,20},{14,22},{16,8},... | collective-permute-start | bytes 208904 | tf_op jit(solution)/shard_map/ppermute | solution.py:50
  20.3 7.5 %collective-permute-start.5 = (f16[272,128]{1,0:T(8,128)(2,1)S(1)}, f16[272,128]{1,0:T(8,128)(2,1)S(1)}, u32[]{:S(2)}, u32[]{:S(2)}) collective-permute-start(f16[272,128]{1,0:T(8,128)(2,1)S(1)} %convert_element_type.62), channel_id=1, source_target_pairs={{0,16},{2,18},{4,20},{6,22},{8,24},{10,26},{12,28},{14,30},{16,0},... | collective-permute-start | bytes 208904 | tf_op jit(solution)/shard_map/ppermute | solution.py:50
  28.0 5.7 %collective-permute-start.9 = (f16[528,128]{1,0:T(8,128)(2,1)S(1)}, f16[528,128]{1,0:T(8,128)(2,1)S(1)}, u32[]{:S(2)}, u32[]{:S(2)}) collective-permute-start(f16[528,128]{1,0:T(8,128)(2,1)S(1)} %convert_element_type.69), channel_id=1, source_target_pairs={{0,6},{2,4},{4,2},{6,0},{8,14},{10,12},{12,10},{14,8},{16,22},{18,... | collective-permute-start | bytes 405512 | tf_op jit(solution)/shard_map/ppermute | solution.py:50
  28.6 8.8 %collective-permute-start.8 = (f16[528,128]{1,0:T(8,128)(2,1)S(1)}, f16[528,128]{1,0:T(8,128)(2,1)S(1)}, u32[]{:S(2)}, u32[]{:S(2)}) collective-permute-start(f16[528,128]{1,0:T(8,128)(2,1)S(1)} %convert_element_type.67), channel_id=1, source_target_pairs={{0,4},{2,6},{4,0},{6,2},{8,12},{10,14},{12,8},{14,10},{16,20},{18,... | collective-permute-start | bytes 405512 | tf_op jit(solution)/shard_map/ppermute | solution.py:50
  30.5 6.9 %collective-permute-start.7 = (f16[528,128]{1,0:T(8,128)(2,1)S(1)}, f16[528,128]{1,0:T(8,128)(2,1)S(1)}, u32[]{:S(2)}, u32[]{:S(2)}) collective-permute-start(f16[528,128]{1,0:T(8,128)(2,1)S(1)} %convert_element_type.65), channel_id=1, source_target_pairs={{0,2},{2,0},{4,6},{6,4},{8,10},{10,8},{12,14},{14,12},{16,18},{18,... | collective-permute-start | bytes 405512 | tf_op jit(solution)/shard_map/ppermute | solution.py:50
  37.6 12.9 %collective-permute-start.10 = (f32[4,2,2,128,128]{4,3,2,1,0:T(8,128)S(1)}, f32[4,2,2,128,128]{4,3,2,1,0:T(8,128)S(1)}, u32[]{:S(2)}, u32[]{:S(2)}) collective-permute-start(f32[4,2,2,128,128]{4,3,2,1,0:T(8,128)S(1)} %shard_map.81), channel_id=1, source_target_pairs={{0,1},{1,0},{2,3},{3,2},{4,5},{5,4},{6,7},{7,6},{8,9},{9,8},{10,11... | collective-permute-start | bytes 3145736 | tf_op jit(solution)/shard_map/ppermute | solution.py:50

commit v6 on v5

--- a/solution.py
+++ b/solution.py
@@ -105,38 +105,49 @@
     return lax.axis_index("seq") & (slices - 1)
 
 
-def state_kernel(half, cuts, *refs):
-    srcs, (out_ref, q_ref, k_ref, v_ref, o_ref), sems = refs[:4], refs[4:9], refs[9]
-    slices, _, width = out_ref.shape[:3]
+def state_kernel(half, slices, cuts, counts, *refs):
+    srcs, outs, (mark_ref, q_ref, k_ref, v_ref, o_ref, sems) = refs[:4], refs[4 : 4 + len(counts)], refs[4 + len(counts) :]
+    width = outs[0].shape[2]
     held = (q_ref, k_ref, v_ref, o_ref)
     model = q_ref.shape[1]
     place = near_place(slices)
     size = model // cuts
-    copies = []
-    for c in range(cuts):
-        start = pl.multiple_of(first_head(half, model // DH) * DH + c * size, DH)
+    per = slices // cuts
+    copies = {}
+    for c in reversed(range(cuts)):
+        at = pl.multiple_of((place // per ^ c) * size, DH)
+        start = pl.multiple_of(first_head(half, model // DH) * DH + at, DH)
         for i in range(4):
-            copy = pltpu.make_async_copy(
-                srcs[i].at[:, pl.ds(start, size)], held[i].at[:, c * size : (c + 1) * size], sems.at[c, i]
+            copies[c, i] = pltpu.make_async_copy(
+                srcs[i].at[:, pl.ds(start, size)], held[i].at[:, pl.ds(at, size)], sems.at[c, i]
             )
-            copy.start()
-            copies.append(copy)
-    for c in range(cuts):
-        for i in range(4):
-            copies[4 * c + i].wait()
-        for head in range(c * size // DH, (c + 1) * size // DH):
-            d, j = place ^ (head // width), head % width
-            cols = slice(head * DH, (head + 1) * DH)
-            out_ref[d, 0, j] = dot(v_ref[:, cols], k_ref[:, cols], TN)
-            out_ref[d, 1, j] = dot(o_ref[:, cols], q_ref[:, cols], TN)
-
-
-def device_states(half, args, slices, width):
+            copies[c, i].start()
+    most = [jnp.zeros((8, DH), F32)] * 2
+    for d in reversed(range(slices)):
+        if d % per == per - 1:
+            for i in range(4):
+                copies[d // per, i].wait()
+        part = sum(d >= sum(counts[: n + 1]) for n in range(len(counts)))
+        index = d - sum(counts[:part])
+        for j in range(width):
+            cols = pl.ds(pl.multiple_of(((place ^ d) * width + j) * DH, DH), DH)
+            pairs = (dot(v_ref[:, cols], k_ref[:, cols], TN), dot(o_ref[:, cols], q_ref[:, cols], TN))
+            for t in range(2):
+                outs[part][index, t, j] = pairs[t]
+                if half == 0:
+                    most[t] = jnp.maximum(most[t], jnp.max(jnp.abs(pairs[t]).reshape(-1, 8, DH), axis=0))
+    for t in range(2):
+        mark_ref[8 * t : 8 * t + 8] = jnp.full((8, DH), jnp.max(most[t]), F32)
+
+
+def device_states(half, args, slices, width, counts):
     tokens = args[0].shape[0]
     cuts = 2 if slices % 2 == 0 else 1
     return call(
-        functools.partial(state_kernel, half, cuts),
-        [pltpu.VMEM((slices, 2, width, DH, DH), F32)] + [pltpu.VMEM((tokens, slices * width * DH), BF16)] * 4,
+        functools.partial(state_kernel, half, slices, cuts, counts),
+        [pltpu.VMEM((n, 2, width, DH, DH), F32) for n in counts]
+        + [pltpu.VMEM((16, DH), F32)]
+        + [pltpu.VMEM((tokens, slices * width * DH), BF16)] * 4,
         args,
         specs=[HBM] * 4,
         scratch=[pltpu.SemaphoreType.DMA((cuts, 4))],
@@ -198,16 +209,17 @@
     )[0]
 
 
-def chip_kernel(own_ref, other_ref, keep_ref, *out_refs):
-    rows = (keep_ref.shape[0] - EXTRA) // 2
-    marks = []
-    for t in range(2):
-        value = own_ref[0, t] + other_ref[0, t]
-        keep_ref[t * rows : (t + 1) * rows] = value.reshape(rows, DH)
-        marks.append(marks_of(value))
-    put_marks(keep_ref, marks)
-    for d, out_ref in enumerate(out_refs, 1):
-        pack(out_ref, [own_ref[d, t] + other_ref[d, t] for t in range(2)])
+def chip_kernel(first, own_ref, other_ref, *out_refs):
+    for index, out_ref in enumerate(out_refs):
+        d = first + index
+        values = [own_ref[d, t] + other_ref[index, t] for t in range(2)]
+        if d:
+            pack(out_ref, values)
+            continue
+        rows = (out_ref.shape[0] - EXTRA) // 2
+        for t in range(2):
+            out_ref[t * rows : (t + 1) * rows] = values[t].reshape(rows, DH)
+        put_marks(out_ref, [marks_of(value) for value in values])
 
 
 def bit_of(value, index):
@@ -335,83 +347,102 @@
     return (second, 1.0 - second) if mine else (1.0 - second, second)
 
 
-def core_kernel(level, scale_ref, source_ref, keep_ref, *refs):
-    parts, out_ref = (keep_ref, *refs[:-1]), refs[-1]
-    slices, _, width = source_ref.shape[:3]
+def near_core_kernel(level, slices, scale_ref, own_ref, keep_ref, out_ref):
+    width = out_ref.shape[1]
     place = near_place(slices)
     sides = core_side(False)
-    for d in range(slices):
-        factors = [None if d == 0 else jnp.exp2(-mark(parts[d], t)[:1]) for t in range(2)]
-        for j, r, rows in pieces(width):
-            weight = head_weight(scale_ref, place ^ d, slices, width, j, level)
-            for t in range(2):
+    for j, r, rows in pieces(width):
+        weight = head_weight(scale_ref, place, slices, width, j, level)
+        for t in range(2):
+            at = (t * width + j) * DH + r
+            out_ref[t, j, rows] = keep_ref[at : at + PIECE] + (sides[t] * weight) * own_ref[0, t, j, rows]
+
+
+def core_kernel(level, scale_ref, own_ref, most_ref, *refs):
+    parts, out_ref = refs[:-1], refs[-1]
+    slices, _, width = own_ref.shape[:3]
+    place = near_place(slices)
+    sides = core_side(False)
+    first = first_head(0, scale_ref.shape[0] // lax.axis_size("head"))
+    weights = [jnp.abs(scale_ref[first + h, level : level + 1]) for h in range(slices * width)]
+    heaviest = functools.reduce(jnp.maximum, weights)
+    powers = []
+    for t in range(2):
+        bound = functools.reduce(jnp.maximum, [jnp.exp2(TOP - mark(part, t)) for part in parts])
+        powers.append(bound_power(bound + heaviest * most_ref[8 * t : 8 * t + 8]))
+    put_marks(out_ref, powers)
+    for d, part in enumerate(parts, 1):
+        for t in range(2):
+            opened = jnp.exp2(powers[t][:1] - mark(part, t)[:1])
+            closed = sides[t] * jnp.exp2(powers[t][:1])
+            for j, r, rows in pieces(width):
+                weight = head_weight(scale_ref, place ^ d, slices, width, j, level)
                 at = (t * width + j) * DH + r
-                got = parts[d][at : at + PIECE]
-                if d:
-                    got = got * factors[t]
-                out_ref[d, t, j, rows] = got + (sides[t] * weight) * source_ref[d, t, j, rows]
-
-
-def cross_kernel(half, states_of, k_ref, v_ref, o_ref, local_of, outs, temps, sems):
-    slices, width = temps.shape[0], temps.shape[3] // DH
-    model = k_ref.shape[1]
-    place = near_place(slices)
-    copies = []
-    for d in range(slices):
-        group = place ^ d
-        for j in range(width):
-            at = pl.ds(pl.multiple_of((group * width + j) * DH, DH), DH)
-            to = slice(j * DH, (j + 1) * DH)
-            o, v, k = o_ref[:, at], v_ref[:, at], k_ref[:, at]
-            early, late = states_of(d, j)
-            hi, lo = split(early)
-            qg = dot(o, hi) + dot(o, lo)
-            hi, lo = split(late)
-            kg = dot(v, hi) + dot(v, lo)
-            vg = dot(k, hi, NT) + dot(k, lo, NT)
-            for i, cross in enumerate((qg, kg, vg)):
-                temps[d, i, :, to] = (cross + local_of(d, i, to)).astype(BF16)
-        start = first_head(half, model // DH) * DH + group * (width * DH)
-        cols = pl.ds(pl.multiple_of(start, DH), width * DH)
-        for i in range(3):
-            copy = pltpu.make_async_copy(temps.at[d, i], outs[i].at[:, cols], sems.at[d, i])
-            copy.start()
-            copies.append(copy)
-    for copy in copies:
-        copy.wait()
-
-
-def finish(half, source, held, parts, where, scales, level, model, before):
-    tokens, cols = held[0].shape
-    slices, _, width = source[0].shape[:3]
-    count = len(source)
-    args = [*source, scales, *held[1:], *parts]
+                to = (((d - 1) * 2 + t) * width + j) * DH + r
+                out_ref[to : to + PIECE] = part[at : at + PIECE] * opened + (closed * weight) * own_ref[d, t, j, rows]
+
+
+def finish(items, kinds, states, held, parts, where, scales, level, model, before):
+    tokens, cols = held[0][0].shape
+    width = parts[0].shape[3] // DH
+    slices = cols // (width * DH)
+    halves = sorted({half for half, _ in items})
+    args = [*states, scales, *[x for half in halves for x in held[half][1:]], *parts]
     specs = [VMEM] * len(args) + [HBM] * len(before)
 
     def kernel(*refs):
-        states, scale_ref, held_refs = refs[:count], refs[count], refs[count + 1 : count + 4]
-        local_refs, outs = refs[count + 4 : len(args)], refs[len(specs) : len(specs) + 3]
+        given = dict(zip(kinds, refs))
+        rest = refs[len(kinds) :]
+        scale_ref, rest = rest[0], rest[1:]
+        held_refs = {half: rest[3 * i : 3 * i + 3] for i, half in enumerate(halves)}
+        local_refs, outs = rest[3 * len(halves) :], refs[len(specs) : len(specs) + 3]
+        temps, sems = refs[-2], refs[-1]
         place = near_place(slices)
         sides = core_side(True)
-
-        def states_of(d, j):
-            if count == 1:
-                return [states[0][d, t, j] for t in range(2)]
-            weight = head_weight(scale_ref, place ^ d, slices, width, j, level)
-            out = []
-            for t in range(2):
-                ref = states[1 + d]
-                got = ref[(t * width + j) * DH : (t * width + j + 1) * DH]
+        copies = []
+
+        def state_of(half, d, j, t):
+            rows = slice((t * width + j) * DH, (t * width + j + 1) * DH)
+            if half == 0:
+                got = given["got", d][rows]
                 if d:
-                    got = got * jnp.exp2(-mark(ref, t)[:1])
-                out.append(got + (sides[t] * weight) * states[0][d, t, j])
-            return out
-
-        def local_of(d, i, to):
-            part, index = where[half, d]
-            return local_refs[part][index, i, :, to]
-
-        cross_kernel(half, states_of, *held_refs, local_of, outs, refs[-2], refs[-1])
+                    got = got * jnp.exp2(-mark(given["got", d], t)[:1])
+                weight = head_weight(scale_ref, place ^ d, slices, width, j, level)
+                return got + (sides[t] * weight) * given["other", d][given["index", d], t, j]
+            if d == 0:
+                return given["near", 0][t, j]
+            ref = given["far", 0]
+            at = (((d - 1) * 2 + t) * width + j) * DH
+            return ref[at : at + DH] * jnp.exp2(-mark(ref, t)[:1])
+
+        for d in range(slices):
+            other = "other_a" if d == slices - 1 else "other_b"
+            if other in given:
+                given["other", d] = given[other]
+                given["index", d] = 0 if d == slices - 1 else d
+        for index, (half, d) in enumerate(items):
+            k_ref, v_ref, o_ref = held_refs[half]
+            group = place ^ d
+            part, at_part = where[half, d]
+            for j in range(width):
+                at = pl.ds(pl.multiple_of((group * width + j) * DH, DH), DH)
+                to = slice(j * DH, (j + 1) * DH)
+                o, v, k = o_ref[:, at], v_ref[:, at], k_ref[:, at]
+                hi, lo = split(state_of(half, d, j, 0))
+                qg = dot(o, hi) + dot(o, lo)
+                hi, lo = split(state_of(half, d, j, 1))
+                kg = dot(v, hi) + dot(v, lo)
+                vg = dot(k, hi, NT) + dot(k, lo, NT)
+                for i, cross in enumerate((qg, kg, vg)):
+                    temps[index, i, :, to] = (cross + local_refs[part][at_part, i, :, to]).astype(BF16)
+            start = first_head(half, cols // DH) * DH + group * (width * DH)
+            wide = pl.ds(pl.multiple_of(start, DH), width * DH)
+            for i in range(3):
+                copy = pltpu.make_async_copy(temps.at[index, i], outs[i].at[:, wide], sems.at[index, i])
+                copy.start()
+                copies.append(copy)
+        for copy in copies:
+            copy.wait()
 
     return call(
         kernel,
@@ -419,8 +450,8 @@
         args + list(before),
         specs=specs,
         out_specs=[HBM] * 3,
-        scratch=[pltpu.VMEM((slices, 3, tokens, width * DH), BF16), pltpu.SemaphoreType.DMA((slices, 3))],
-        flops=12 * tokens * DH * cols,
+        scratch=[pltpu.VMEM((len(items), 3, tokens, width * DH), BF16), pltpu.SemaphoreType.DMA((len(items), 3))],
+        flops=12 * tokens * DH * width * DH * len(items),
         limit=4,
         aliases={len(args) + i: i for i in range(len(before))},
     )
@@ -445,9 +476,10 @@
     scales = jnp.broadcast_to(padded[:, :, None], (*padded.shape, DH))
 
     args = [pltpu.with_memory_space_constraint(x, pltpu.HBM) for x in (queries, key_rows, values, out_grad)]
-    sent, *held_there = device_states(1, args, slices, width)
-    other = partner(sent, "head", 1)
-    own, *held_here = device_states(0, args, slices, width)
+    sent_b, sent_a, _, *held_there = device_states(1, args, slices, width, (slices - 1, 1))
+    other_a = partner(sent_a, "head", 1)
+    other_b = partner(sent_b, "head", 1)
+    own, most, *held_here = device_states(0, args, slices, width, (slices,))
     held = (held_here, held_there)
     every = [(half, d) for half in range(2) for d in range(slices)]
     ends = [0, 3 * len(every) // 8, 6 * len(every) // 8, len(every)]
@@ -465,7 +497,9 @@
     near = pltpu.VMEM((slices, 2, width, DH, DH), F32)
     bound = pltpu.VMEM((16, DH), F32)
 
-    keep, *outs = call(chip_kernel, [load] * slices, [own, other])
+    last = call(functools.partial(chip_kernel, slices - 1), [load], [own, other_a])
+    keep, *outs = call(functools.partial(chip_kernel, 0), [load] * (slices - 1), [own, other_b])
+    outs += last
     got = []
     for d in range(1, slices):
         got.append(narrow(outs[d - 1], "seq", d))
@@ -498,10 +532,17 @@
     for d in range(1, slices):
         got.append(narrow(outs[d - 1], "seq", d))
     level = local_levels + 1
-    theirs = call(functools.partial(core_kernel, level), [near], [scales, own, keep, *got])[0]
-    theirs = partner(theirs, "head", 1)
-    half_done = finish(0, [other, keep, *got], held[0], local, where, scales, level, model, [])
-    return tuple(finish(1, [theirs], held[1], local, where, scales, level, model, half_done))
+    near_theirs = call(functools.partial(near_core_kernel, level, slices), [state], [scales, own, keep])[0]
+    near_theirs = partner(near_theirs, "head", 1)
+    rest_rows = pltpu.VMEM((2 * (slices - 1) * width * DH + EXTRA, DH), F32)
+    theirs = call(functools.partial(core_kernel, level), [rest_rows], [scales, own, most, *got])[0]
+    theirs = narrow(theirs, "head", 1)
+    others = ["other_b", "other_a"]
+    common = (held, local, where, scales, level, model)
+    done = finish([(0, 0), (1, 0)], ["other_b", ("got", 0), ("near", 0)], [other_b, keep, near_theirs], *common, [])
+    away = range(1, slices)
+    done = finish([(0, d) for d in away], others + [("got", d) for d in away], [other_b, other_a, *got], *common, done)
+    return tuple(finish([(1, d) for d in away], [("far", 0)], [theirs], *common, done))
 
 
 def solution(mesh):

time: 52.6 us -> 55 us (1.046)
  Pallas kernels: 19.1 us -> 21.2 us
  waiting for transfers between devices: 20.9 us -> 20 us
  starting transfers between devices: 11.1 us -> 11.7 us
    pallas_call x11 -> x14, Pallas kernels: 19.1 us -> 21.2 us  [call(): pl.pallas_call(kernel, in_specs=specs or [VMEM] * len(args), out_specs=ou...]
    ppermute x11 -> x13, waiting for transfers between devices: 20.9 us -> 20 us  [partner(): lax.ppermute(array, axis, [(i, i ^ distance) for i in range(lax.axis_size...]
    ppermute x11 -> x13, starting transfers between devices: 11.1 us -> 11.7 us  [partner(): lax.ppermute(array, axis, [(i, i ^ distance) for i in range(lax.axis_size...]
  transfers between devices with their start and end apart: 11 -> 13, of which waited for: 7 -> 6; matrix products, arithmetic and copies ran while one was open for 0% -> 0% of each run, Pallas kernels for 27% -> 30%
where the time goes in v6:
time: 55 us; the launch traced here: 54.3 us
  Pallas kernels  21.2 us (39%)
  waiting for transfers between devices  20 us (36%)
  starting transfers between devices  11.7 us (21%)
  between operations  0.9 us (2%)
    pallas_call x14, Pallas kernels, call(): pl.pallas_call(kernel, in_specs=specs or [VMEM] * len(args), out_specs=ou...  21.2 us
    ppermute x13, waiting for transfers between devices, partner(): lax.ppermute(array, axis, [(i, i ^ distance) for i in range(lax.axis_size...  20 us
    ppermute x13, starting transfers between devices, partner(): lax.ppermute(array, axis, [(i, i ^ distance) for i in range(lax.axis_size...  11.7 us
  transfers between devices with their start and end apart: 13, of which 6 were waited for; matrix products, arithmetic and copies ran while one was open for 0% of the time, Pallas kernels for 30%

profile of v6, /device:TPU:1, one launch (start us, length us, event | category | flops | bytes accessed | tf_op | source)
XLA Modules:
  0.0 54.3 jit_solution(16109107812004055383)
XLA Ops:
  0.6 2.8 %shard_map.77 = (f32[3,2,2,128,128]{4,3,2,1,0:T(8,128)S(1)}, f32[1,2,2,128,128]{4,3,2,1,0:T(8,128)S(1)}, f32[16,128]{1,0:T(8,128)}, bf16[256,1024]{1,0:T(8,128)(...) custom-call(bf16[256,2048]{1,0:T(8,128)(2,1)} %refs_0_.3, ...), custom_call_target="tpu_custom_call" | custom-call | flops 134217728 | bytes 4194304 | tf_op jit(solution)/shard_map/pallas_call | solution.py:37
  3.4 0.1 collective-permute-start
  3.5 0.5 collective-permute-start.3
  4.0 2.4 %shard_map.76 = (f32[4,2,2,128,128]{4,3,2,1,0:T(8,128)S(1)}, f32[16,128]{1,0:T(8,128)S(1)}, bf16[256,1024]{1,0:T(8,128)(2,1)S(1)}, bf16[256,1024]{1,0:T(8,128)(2...) custom-call(bf16[256,2048]{1,0:T(8,128)(2,1)} %refs_0_.3, bf16[256,2048]{1,0:T(8,128)(2,1)} %refs_1_.3, ...), custom_call_target="tpu_custom_call" | custom-call | flops 134217728 | bytes 4194304 | tf_op jit(solution)/shard_map/pallas_call | solution.py:37
  6.3 0.0 copy-start
  6.4 0.0 collective-permute-done.3.other_ref.refs_1_
  6.4 0.2 shard_map.79
  6.6 3.3 %collective-permute-start.4 = (f16[528,128]{1,0:T(8,128)(2,1)S(1)}, f16[528,128]{1,0:T(8,128)(2,1)S(1)}, u32[]{:S(2)}, u32[]{:S(2)}) collective-permute-start(f16[528,128]{1,0:T(8,128)(2,1)S(1)} %convert_element_type.64), channel_id=1, source_target_pairs={{0,6},{2,4},{4,2},{6,0},{8,14},{10,12},{12,10},{14,8},{16,22},{18,... | collective-permute-start | bytes 405512 | tf_op jit(solution)/shard_map/ppermute | solution.py:50
  9.9 0.0 collective-permute-done.other_ref.refs_0_
  9.9 0.2 shard_map.78
  10.2 0.3 collective-permute-start.2
  10.5 0.1 collective-permute-start.1
  10.6 0.0 copy-done
  10.6 2.8 %collective-permute-done.4 = f16[528,128]{1,0:T(8,128)(2,1)S(1)} collective-permute-done((f16[528,128]{1,0:T(8,128)(2,1)S(1)}, f16[528,128]{1,0:T(8,128)(2,1)S(1)}, u32[]{:S(2)}, u32[]{:S(2)}) %collective-permute-start.4) | collective-permute-done | bytes 135200 | tf_op jit(solution)/shard_map/ppermute | solution.py:50
  13.4 3.4 %collective-permute-done.2 = f16[528,128]{1,0:T(8,128)(2,1)S(1)} collective-permute-done((f16[528,128]{1,0:T(8,128)(2,1)S(1)}, f16[528,128]{1,0:T(8,128)(2,1)S(1)}, u32[]{:S(2)}, u32[]{:S(2)}) %collective-permute-start.2) | collective-permute-done | bytes 135200 | tf_op jit(solution)/shard_map/ppermute | solution.py:50
  16.8 0.0 collective-permute-done.1
  16.9 0.1 broadcast_in_dim.2.scale_ref.refs_3_.refs_5_.refs_1_
  16.9 0.2 shard_map.80
  17.2 1.6 %collective-permute-start.5 = (f16[272,128]{1,0:T(8,128)(2,1)S(1)}, f16[272,128]{1,0:T(8,128)(2,1)S(1)}, u32[]{:S(2)}, u32[]{:S(2)}) collective-permute-start(f16[272,128]{1,0:T(8,128)(2,1)S(1)} %convert_element_type.66), channel_id=1, source_target_pairs={{0,8},{2,10},{4,12},{6,14},{8,0},{10,2},{12,4},{14,6},{16,24},{18,... | collective-permute-start | bytes 208904 | tf_op jit(solution)/shard_map/ppermute | solution.py:50
  18.8 2.3 %collective-permute-start.7 = (f16[272,128]{1,0:T(8,128)(2,1)S(1)}, f16[272,128]{1,0:T(8,128)(2,1)S(1)}, u32[]{:S(2)}, u32[]{:S(2)}) collective-permute-start(f16[272,128]{1,0:T(8,128)(2,1)S(1)} %convert_element_type.68), channel_id=1, source_target_pairs={{0,24},{2,26},{4,28},{6,30},{8,16},{10,18},{12,20},{14,22},{16,8},... | collective-permute-start | bytes 208904 | tf_op jit(solution)/shard_map/ppermute | solution.py:50
  21.1 0.2 collective-permute-start.6
  21.3 0.0 collective-permute-done.5
  21.3 3.5 %collective-permute-done.7 = f16[272,128]{1,0:T(8,128)(2,1)S(1)} collective-permute-done((f16[272,128]{1,0:T(8,128)(2,1)S(1)}, f16[272,128]{1,0:T(8,128)(2,1)S(1)}, u32[]{:S(2)}, u32[]{:S(2)}) %collective-permute-start.7) | collective-permute-done | bytes 69664 | tf_op jit(solution)/shard_map/ppermute | solution.py:50
  24.8 3.8 %collective-permute-done.6 = f16[272,128]{1,0:T(8,128)(2,1)S(1)} collective-permute-done((f16[272,128]{1,0:T(8,128)(2,1)S(1)}, f16[272,128]{1,0:T(8,128)(2,1)S(1)}, u32[]{:S(2)}, u32[]{:S(2)}) %collective-permute-start.6) | collective-permute-done | bytes 69664 | tf_op jit(solution)/shard_map/ppermute | solution.py:50
  28.5 0.2 shard_map.81
  28.8 1.5 %collective-permute-start.10 = (f16[528,128]{1,0:T(8,128)(2,1)S(1)}, f16[528,128]{1,0:T(8,128)(2,1)S(1)}, u32[]{:S(2)}, u32[]{:S(2)}) collective-permute-start(f16[528,128]{1,0:T(8,128)(2,1)S(1)} %convert_element_type.75), channel_id=1, source_target_pairs={{0,6},{2,4},{4,2},{6,0},{8,14},{10,12},{12,10},{14,8},{16,22},{18,... | collective-permute-start | bytes 405512 | tf_op jit(solution)/shard_map/ppermute | solution.py:50
  30.3 1.0 %collective-permute-start.9 = (f16[528,128]{1,0:T(8,128)(2,1)S(1)}, f16[528,128]{1,0:T(8,128)(2,1)S(1)}, u32[]{:S(2)}, u32[]{:S(2)}) collective-permute-start(f16[528,128]{1,0:T(8,128)(2,1)S(1)} %convert_element_type.73), channel_id=1, source_target_pairs={{0,4},{2,6},{4,0},{6,2},{8,12},{10,14},{12,8},{14,10},{16,20},{18,... | collective-permute-start | bytes 405512 | tf_op jit(solution)/shard_map/ppermute | solution.py:50
  31.2 0.3 collective-permute-start.8
  31.6 2.8 %collective-permute-done.10 = f16[528,128]{1,0:T(8,128)(2,1)S(1)} collective-permute-done((f16[528,128]{1,0:T(8,128)(2,1)S(1)}, f16[528,128]{1,0:T(8,128)(2,1)S(1)}, u32[]{:S(2)}, u32[]{:S(2)}) %collective-permute-start.10) | collective-permute-done | bytes 135200 | tf_op jit(solution)/shard_map/ppermute | solution.py:50
  34.4 3.7 %collective-permute-done.9 = f16[528,128]{1,0:T(8,128)(2,1)S(1)} collective-permute-done((f16[528,128]{1,0:T(8,128)(2,1)S(1)}, f16[528,128]{1,0:T(8,128)(2,1)S(1)}, u32[]{:S(2)}, u32[]{:S(2)}) %collective-permute-start.9) | collective-permute-done | bytes 135200 | tf_op jit(solution)/shard_map/ppermute | solution.py:50
  38.1 0.0 collective-permute-done.8
  38.2 0.1 shard_map.82
  38.3 0.1 convert_element_type.77
  38.4 0.6 %collective-permute-start.11 = (f16[1552,128]{1,0:T(8,128)(2,1)S(1)}, f16[1552,128]{1,0:T(8,128)(2,1)S(1)}, u32[]{:S(2)}, u32[]{:S(2)}) collective-permute-start(f16[1552,128]{1,0:T(8,128)(2,1)S(1)} %convert_element_type.77), channel_id=1, source_target_pairs={{0,1},{1,0},{2,3},{3,2},{4,5},{5,4},{6,7},{7,6},{8,9},{9,8},{10,11... | collective-permute-start | bytes 1191944 | tf_op jit(solution)/shard_map/ppermute | solution.py:50
  39.0 0.1 collective-permute-start.12
  39.1 2.6 %shard_map.85.refs_12_.refs_11_.refs_7_ = f32[2,3,256,256]{3,2,1,0:T(8,128)S(1)} custom-call(f32[16,16,128]{2,1,0:T(8,128)S(1)} %broadcast_in_dim.2.scale_ref.refs_3_.refs_5_.refs_1_, bf16[256,1024]{1,0:T(8,128)(2,1)S(1)} %get-tuple-element.49.refs_0_, bf16[256,1024]{1,0:T(8,128)(2,1)S(1)} %get-tuple-element.50.refs_1_.refs_4_.refs_6_, ...), custom_call_target="tpu_custom_call" | custom-call | flops 402653184 | bytes 4325376 | tf_op jit(solution)/shard_map/pallas_call | solution.py:37
  41.7 3.9 %shard_map.84.refs_11_.refs_10_.refs_6_ = f32[3,3,256,256]{3,2,1,0:T(8,128)S(1)} custom-call(f32[16,16,128]{2,1,0:T(8,128)S(1)} %broadcast_in_dim.2.scale_ref.refs_3_.refs_5_.refs_1_, bf16[256,1024]{1,0:T(8,128)(2,1)S(1)} %get-tuple-element.49.refs_0_, bf16[256,1024]{1,0:T(8,128)(2,1)S(1)} %get-tuple-element.50.refs_1_.refs_4_.refs_6_, ...), custom_call_target="tpu_custom_call" | custom-call | flops 603979776 | bytes 4325376 | tf_op jit(solution)/shard_map/pallas_call | solution.py:37
  45.6 3.9 %shard_map.83.refs_10_.refs_9_.refs_5_ = f32[3,3,256,256]{3,2,1,0:T(8,128)S(1)} custom-call(f32[16,16,128]{2,1,0:T(8,128)S(1)} %broadcast_in_dim.2.scale_ref.refs_3_.refs_5_.refs_1_, bf16[256,1024]{1,0:T(8,128)(2,1)S(1)} %get-tuple-element.49.refs_0_, bf16[256,1024]{1,0:T(8,128)(2,1)S(1)} %get-tuple-element.50.refs_1_.refs_4_.refs_6_, ...), custom_call_target="tpu_custom_call" | custom-call | flops 603979776 | bytes 4325376 | tf_op jit(solution)/shard_map/pallas_call | solution.py:37
  49.5 0.0 collective-permute-done.12.refs_2_
  49.5 1.4 %shard_map.87 = (bf16[256,2048]{1,0:T(8,128)(2,1)}, bf16[256,2048]{1,0:T(8,128)(2,1)}, bf16[256,2048]{1,0:T(8,128)(2,1)}) custom-call(f32[3,2,2,128,128]{4,3,2,1,0:T(8,128)S(1)} %collective-permute-done.other_ref.refs_0_, f32[528,128]{1,0:T(8,128)S(1)} %get-tuple-element.54.keep_ref.refs_1_, f32[2,2,128,128]{3,2,1,0:T(8,128)S(1)} %collective-permute-done.12.refs_2_, ...), custom_call_target="tpu_custom_call" | custom-call | flops 201326592 | bytes 10887168 | tf_op jit(solution)/shard_map/pallas_call | solution.py:37
  50.9 1.7 %shard_map.88 = (bf16[256,2048]{1,0:T(8,128)(2,1)}, bf16[256,2048]{1,0:T(8,128)(2,1)}, bf16[256,2048]{1,0:T(8,128)(2,1)}) custom-call(f32[3,2,2,128,128]{4,3,2,1,0:T(8,128)S(1)} %collective-permute-done.other_ref.refs_0_, ...), custom_call_target="tpu_custom_call", output_to_operand_aliasing={{0}: (12, {}), {1}: (13, {}), {2}: (14, {})} | custom-call | flops 301989888 | bytes 13000704 | tf_op jit(solution)/shard_map/pallas_call | solution.py:37
  52.6 0.0 collective-permute-done.11
  52.6 0.1 convert_element_type.78.refs_0_
  52.7 1.6 %shard_map.89 = (bf16[256,2048]{1,0:T(8,128)(2,1)}, bf16[256,2048]{1,0:T(8,128)(2,1)}, bf16[256,2048]{1,0:T(8,128)(2,1)}) custom-call(f32[1552,128]{1,0:T(8,128)S(1)} %convert_element_type.78.refs_0_, f32[16,16,128]{2,1,0:T(8,128)S(1)} %broadcast_in_dim.2.scale_ref.refs_3_.refs_5_.refs_1_, ...), custom_call_target="tpu_custom_call", output_to_operand_aliasing={{0}: (8, {}), {1}: (9, {}), {2}: (10, {})} | custom-call | flops 301989888 | bytes 11935744 | tf_op jit(solution)/shard_map/pallas_call | solution.py:37
  (21 shorter events, 0.4 us)
Async XLA Ops:
  3.4 6.5 %collective-permute-start = (f32[3,2,2,128,128]{4,3,2,1,0:T(8,128)S(1)}, f32[3,2,2,128,128]{4,3,2,1,0:T(8,128)S(1)}, u32[]{:S(2)}, u32[]{:S(2)}) collective-permute-start(f32[3,2,2,128,128]{4,3,2,1,0:T(8,128)S(1)} %get-tuple-element.34), channel_id=1, source_target_pairs={{0,1},{1,0},{2,3},{3,2},{4,5},{5,4},{6,7},{7,6},{8,9},{9,8},{10,11... | collective-permute-start | bytes 2359304 | tf_op jit(solution)/shard_map/ppermute | solution.py:50
  3.5 2.9 %collective-permute-start.3 = (f32[1,2,2,128,128]{4,3,2,1,0:T(8,128)S(1)}, f32[1,2,2,128,128]{4,3,2,1,0:T(8,128)S(1)}, u32[]{:S(2)}, u32[]{:S(2)}) collective-permute-start(f32[1,2,2,128,128]{4,3,2,1,0:T(8,128)S(1)} %get-tuple-element.38), channel_id=1, source_target_pairs={{0,1},{1,0},{2,3},{3,2},{4,5},{5,4},{6,7},{7,6},{8,9},{9,8},{10,11... | collective-permute-start | bytes 786440 | tf_op jit(solution)/shard_map/ppermute | solution.py:50
  6.3 4.3 %copy-start = (f32[16,11]{1,0:T(8,128)S(1)}, f32[16,11]{1,0:T(8,128)}, u32[]{:S(2)}) copy-start(f32[16,11]{1,0:T(8,128)} %param.9) | copy-start | bytes 2116
  6.6 6.8 %collective-permute-start.4 = (f16[528,128]{1,0:T(8,128)(2,1)S(1)}, f16[528,128]{1,0:T(8,128)(2,1)S(1)}, u32[]{:S(2)}, u32[]{:S(2)}) collective-permute-start(f16[528,128]{1,0:T(8,128)(2,1)S(1)} %convert_element_type.64), channel_id=1, source_target_pairs={{0,6},{2,4},{4,2},{6,0},{8,14},{10,12},{12,10},{14,8},{16,22},{18,... | collective-permute-start | bytes 405512 | tf_op jit(solution)/shard_map/ppermute | solution.py:50
  10.2 6.6 %collective-permute-start.2 = (f16[528,128]{1,0:T(8,128)(2,1)S(1)}, f16[528,128]{1,0:T(8,128)(2,1)S(1)}, u32[]{:S(2)}, u32[]{:S(2)}) collective-permute-start(f16[528,128]{1,0:T(8,128)(2,1)S(1)} %convert_element_type.62), channel_id=1, source_target_pairs={{0,4},{2,6},{4,0},{6,2},{8,12},{10,14},{12,8},{14,10},{16,20},{18,... | collective-permute-start | bytes 405512 | tf_op jit(solution)/shard_map/ppermute | solution.py:50
  10.5 6.3 %collective-permute-start.1 = (f16[528,128]{1,0:T(8,128)(2,1)S(1)}, f16[528,128]{1,0:T(8,128)(2,1)S(1)}, u32[]{:S(2)}, u32[]{:S(2)}) collective-permute-start(f16[528,128]{1,0:T(8,128)(2,1)S(1)} %convert_element_type.60), channel_id=1, source_target_pairs={{0,2},{2,0},{4,6},{6,4},{8,10},{10,8},{12,14},{14,12},{16,18},{18,... | collective-permute-start | bytes 405512 | tf_op jit(solution)/shard_map/ppermute | solution.py:50
  17.2 4.0 %collective-permute-start.5 = (f16[272,128]{1,0:T(8,128)(2,1)S(1)}, f16[272,128]{1,0:T(8,128)(2,1)S(1)}, u32[]{:S(2)}, u32[]{:S(2)}) collective-permute-start(f16[272,128]{1,0:T(8,128)(2,1)S(1)} %convert_element_type.66), channel_id=1, source_target_pairs={{0,8},{2,10},{4,12},{6,14},{8,0},{10,2},{12,4},{14,6},{16,24},{18,... | collective-permute-start | bytes 208904 | tf_op jit(solution)/shard_map/ppermute | solution.py:50
  18.8 5.9 %collective-permute-start.7 = (f16[272,128]{1,0:T(8,128)(2,1)S(1)}, f16[272,128]{1,0:T(8,128)(2,1)S(1)}, u32[]{:S(2)}, u32[]{:S(2)}) collective-permute-start(f16[272,128]{1,0:T(8,128)(2,1)S(1)} %convert_element_type.68), channel_id=1, source_target_pairs={{0,24},{2,26},{4,28},{6,30},{8,16},{10,18},{12,20},{14,22},{16,8},... | collective-permute-start | bytes 208904 | tf_op jit(solution)/shard_map/ppermute | solution.py:50
  21.1 7.5 %collective-permute-start.6 = (f16[272,128]{1,0:T(8,128)(2,1)S(1)}, f16[272,128]{1,0:T(8,128)(2,1)S(1)}, u32[]{:S(2)}, u32[]{:S(2)}) collective-permute-start(f16[272,128]{1,0:T(8,128)(2,1)S(1)} %convert_element_type.68), channel_id=1, source_target_pairs={{0,16},{2,18},{4,20},{6,22},{8,24},{10,26},{12,28},{14,30},{16,0},... | collective-permute-start | bytes 208904 | tf_op jit(solution)/shard_map/ppermute | solution.py:50
  28.8 5.6 %collective-permute-start.10 = (f16[528,128]{1,0:T(8,128)(2,1)S(1)}, f16[528,128]{1,0:T(8,128)(2,1)S(1)}, u32[]{:S(2)}, u32[]{:S(2)}) collective-permute-start(f16[528,128]{1,0:T(8,128)(2,1)S(1)} %convert_element_type.75), channel_id=1, source_target_pairs={{0,6},{2,4},{4,2},{6,0},{8,14},{10,12},{12,10},{14,8},{16,22},{18,... | collective-permute-start | bytes 405512 | tf_op jit(solution)/shard_map/ppermute | solution.py:50
  30.3 7.9 %collective-permute-start.9 = (f16[528,128]{1,0:T(8,128)(2,1)S(1)}, f16[528,128]{1,0:T(8,128)(2,1)S(1)}, u32[]{:S(2)}, u32[]{:S(2)}) collective-permute-start(f16[528,128]{1,0:T(8,128)(2,1)S(1)} %convert_element_type.73), channel_id=1, source_target_pairs={{0,4},{2,6},{4,0},{6,2},{8,12},{10,14},{12,8},{14,10},{16,20},{18,... | collective-permute-start | bytes 405512 | tf_op jit(solution)/shard_map/ppermute | solution.py:50
  31.2 6.9 %collective-permute-start.8 = (f16[528,128]{1,0:T(8,128)(2,1)S(1)}, f16[528,128]{1,0:T(8,128)(2,1)S(1)}, u32[]{:S(2)}, u32[]{:S(2)}) collective-permute-start(f16[528,128]{1,0:T(8,128)(2,1)S(1)} %convert_element_type.71), channel_id=1, source_target_pairs={{0,2},{2,0},{4,6},{6,4},{8,10},{10,8},{12,14},{14,12},{16,18},{18,... | collective-permute-start | bytes 405512 | tf_op jit(solution)/shard_map/ppermute | solution.py:50
  38.4 14.2 %collective-permute-start.11 = (f16[1552,128]{1,0:T(8,128)(2,1)S(1)}, f16[1552,128]{1,0:T(8,128)(2,1)S(1)}, u32[]{:S(2)}, u32[]{:S(2)}) collective-permute-start(f16[1552,128]{1,0:T(8,128)(2,1)S(1)} %convert_element_type.77), channel_id=1, source_target_pairs={{0,1},{1,0},{2,3},{3,2},{4,5},{5,4},{6,7},{7,6},{8,9},{9,8},{10,11... | collective-permute-start | bytes 1191944 | tf_op jit(solution)/shard_map/ppermute | solution.py:50
  39.0 10.5 %collective-permute-start.12 = (f32[2,2,128,128]{3,2,1,0:T(8,128)S(1)}, f32[2,2,128,128]{3,2,1,0:T(8,128)S(1)}, u32[]{:S(2)}, u32[]{:S(2)}) collective-permute-start(f32[2,2,128,128]{3,2,1,0:T(8,128)S(1)} %shard_map.86), channel_id=1, source_target_pairs={{0,1},{1,0},{2,3},{3,2},{4,5},{5,4},{6,7},{7,6},{8,9},{9,8},{10,11... | collective-permute-start | bytes 786440 | tf_op jit(solution)/shard_map/ppermute | solution.py:50

commit v7 on v6

--- a/solution.py
+++ b/solution.py
@@ -105,52 +105,60 @@
     return lax.axis_index("seq") & (slices - 1)
 
 
-def state_kernel(half, slices, cuts, counts, *refs):
-    srcs, outs, (mark_ref, q_ref, k_ref, v_ref, o_ref, sems) = refs[:4], refs[4 : 4 + len(counts)], refs[4 + len(counts) :]
-    width = outs[0].shape[2]
-    held = (q_ref, k_ref, v_ref, o_ref)
+def state_kernel(half, cuts, *refs):
+    srcs, refs = refs[:4], refs[4:]
+    if half:
+        (early_ref, late_ref), held, (out_ref, sems) = refs[:2], refs[2:6], refs[6:]
+    else:
+        (out_ref, mark_ref), held, (sems,) = refs[:2], refs[2:6], refs[6:]
+    q_ref, k_ref, v_ref, o_ref = held
+    slices, _, width = out_ref.shape[:3]
     model = q_ref.shape[1]
     place = near_place(slices)
     size = model // cuts
-    per = slices // cuts
-    copies = {}
-    for c in reversed(range(cuts)):
-        at = pl.multiple_of((place // per ^ c) * size, DH)
-        start = pl.multiple_of(first_head(half, model // DH) * DH + at, DH)
+    copies = []
+    for c in range(cuts):
+        start = pl.multiple_of(first_head(half, model // DH) * DH + c * size, DH)
         for i in range(4):
-            copies[c, i] = pltpu.make_async_copy(
-                srcs[i].at[:, pl.ds(start, size)], held[i].at[:, pl.ds(at, size)], sems.at[c, i]
+            copy = pltpu.make_async_copy(
+                srcs[i].at[:, pl.ds(start, size)], held[i].at[:, c * size : (c + 1) * size], sems.at[c, i]
             )
-            copies[c, i].start()
+            copy.start()
+            copies.append(copy)
     most = [jnp.zeros((8, DH), F32)] * 2
-    for d in reversed(range(slices)):
-        if d % per == per - 1:
-            for i in range(4):
-                copies[d // per, i].wait()
-        part = sum(d >= sum(counts[: n + 1]) for n in range(len(counts)))
-        index = d - sum(counts[:part])
-        for j in range(width):
-            cols = pl.ds(pl.multiple_of(((place ^ d) * width + j) * DH, DH), DH)
+    for c in range(cuts):
+        for i in range(4):
+            copies[4 * c + i].wait()
+        for head in range(c * size // DH, (c + 1) * size // DH):
+            d, j = place ^ (head // width), head % width
+            cols = slice(head * DH, (head + 1) * DH)
             pairs = (dot(v_ref[:, cols], k_ref[:, cols], TN), dot(o_ref[:, cols], q_ref[:, cols], TN))
             for t in range(2):
-                outs[part][index, t, j] = pairs[t]
+                out_ref[d, t, j] = pairs[t]
                 if half == 0:
                     most[t] = jnp.maximum(most[t], jnp.max(jnp.abs(pairs[t]).reshape(-1, 8, DH), axis=0))
-    for t in range(2):
-        mark_ref[8 * t : 8 * t + 8] = jnp.full((8, DH), jnp.max(most[t]), F32)
-
-
-def device_states(half, args, slices, width, counts):
+    if half:
+        late_ref[...] = out_ref[: slices - 1]
+        early_ref[0] = out_ref[slices - 1]
+    else:
+        for t in range(2):
+            mark_ref[8 * t : 8 * t + 8] = jnp.full((8, DH), jnp.max(most[t]), F32)
+
+
+def device_states(half, args, slices, width):
     tokens = args[0].shape[0]
     cuts = 2 if slices % 2 == 0 else 1
+
+    def states(count):
+        return pltpu.VMEM((count, 2, width, DH, DH), F32)
+
     return call(
-        functools.partial(state_kernel, half, slices, cuts, counts),
-        [pltpu.VMEM((n, 2, width, DH, DH), F32) for n in counts]
-        + [pltpu.VMEM((16, DH), F32)]
+        functools.partial(state_kernel, half, cuts),
+        ([states(1), states(slices - 1)] if half else [states(slices), pltpu.VMEM((16, DH), F32)])
         + [pltpu.VMEM((tokens, slices * width * DH), BF16)] * 4,
         args,
         specs=[HBM] * 4,
-        scratch=[pltpu.SemaphoreType.DMA((cuts, 4))],
+        scratch=([states(slices)] if half else []) + [pltpu.SemaphoreType.DMA((cuts, 4))],
         flops=4 * slices * width * tokens * DH * DH,
     )
 
@@ -476,10 +484,10 @@
     scales = jnp.broadcast_to(padded[:, :, None], (*padded.shape, DH))
 
     args = [pltpu.with_memory_space_constraint(x, pltpu.HBM) for x in (queries, key_rows, values, out_grad)]
-    sent_b, sent_a, _, *held_there = device_states(1, args, slices, width, (slices - 1, 1))
+    sent_a, sent_b, *held_there = device_states(1, args, slices, width)
     other_a = partner(sent_a, "head", 1)
     other_b = partner(sent_b, "head", 1)
-    own, most, *held_here = device_states(0, args, slices, width, (slices,))
+    own, most, *held_here = device_states(0, args, slices, width)
     held = (held_here, held_there)
     every = [(half, d) for half in range(2) for d in range(slices)]
     ends = [0, 3 * len(every) // 8, 6 * len(every) // 8, len(every)]

time: 55 us -> 54.1 us (0.984)
  Pallas kernels: 21.2 us -> 20.3 us
    pallas_call x14, Pallas kernels: 21.2 us -> 20.3 us  [call(): pl.pallas_call(kernel, in_specs=specs or [VMEM] * len(args), out_specs=ou...]
where the time goes in v7:
time: 54.1 us; the launch traced here: 53.5 us
  Pallas kernels  20.3 us (38%)
  waiting for transfers between devices  20 us (37%)
  starting transfers between devices  11.7 us (22%)
  between operations  0.9 us (2%)
    pallas_call x14, Pallas kernels, call(): pl.pallas_call(kernel, in_specs=specs or [VMEM] * len(args), out_specs=ou...  20.3 us
    ppermute x13, waiting for transfers between devices, partner(): lax.ppermute(array, axis, [(i, i ^ distance) for i in range(lax.axis_size...  20 us
    ppermute x13, starting transfers between devices, partner(): lax.ppermute(array, axis, [(i, i ^ distance) for i in range(lax.axis_size...  11.7 us
  transfers between devices with their start and end apart: 13, of which 6 were waited for; matrix products, arithmetic and copies ran while one was open for 0% of the time, Pallas kernels for 30%

profile of v7, /device:TPU:1, one launch (start us, length us, event | category | flops | bytes accessed | tf_op | source)
XLA Modules:
  0.0 53.5 jit_solution(2013160392802403178)
XLA Ops:
  0.6 2.1 %shard_map.77 = (f32[1,2,2,128,128]{4,3,2,1,0:T(8,128)S(1)}, f32[3,2,2,128,128]{4,3,2,1,0:T(8,128)S(1)}, bf16[256,1024]{1,0:T(8,128)(2,1)S(1)}, bf16[256,1024]{1...) custom-call(bf16[256,2048]{1,0:T(8,128)(2,1)} %refs_0_.3, bf16[256,2048]{1,0:T(8,128)(2,1)} %refs_1_.3, ...), custom_call_target="tpu_custom_call" | custom-call | flops 134217728 | bytes 4194304 | tf_op jit(solution)/shard_map/pallas_call | solution.py:37
  2.7 0.1 collective-permute-start
  2.8 0.5 collective-permute-start.3
  3.3 2.1 %shard_map.76 = (f32[4,2,2,128,128]{4,3,2,1,0:T(8,128)S(1)}, f32[16,128]{1,0:T(8,128)S(1)}, bf16[256,1024]{1,0:T(8,128)(2,1)S(1)}, bf16[256,1024]{1,0:T(8,128)(2...) custom-call(bf16[256,2048]{1,0:T(8,128)(2,1)} %refs_0_.3, bf16[256,2048]{1,0:T(8,128)(2,1)} %refs_1_.3, ...), custom_call_target="tpu_custom_call" | custom-call | flops 134217728 | bytes 4194304 | tf_op jit(solution)/shard_map/pallas_call | solution.py:37
  5.5 0.0 copy-start
  5.5 0.0 collective-permute-done.3.other_ref.refs_1_
  5.5 0.2 shard_map.79
  5.7 3.3 %collective-permute-start.4 = (f16[528,128]{1,0:T(8,128)(2,1)S(1)}, f16[528,128]{1,0:T(8,128)(2,1)S(1)}, u32[]{:S(2)}, u32[]{:S(2)}) collective-permute-start(f16[528,128]{1,0:T(8,128)(2,1)S(1)} %convert_element_type.64), channel_id=1, source_target_pairs={{0,6},{2,4},{4,2},{6,0},{8,14},{10,12},{12,10},{14,8},{16,22},{18,... | collective-permute-start | bytes 405512 | tf_op jit(solution)/shard_map/ppermute | solution.py:50
  9.0 0.0 collective-permute-done.other_ref.refs_0_
  9.0 0.2 shard_map.78
  9.3 0.3 collective-permute-start.2
  9.7 0.1 collective-permute-start.1
  9.8 0.0 copy-done
  9.8 2.8 %collective-permute-done.4 = f16[528,128]{1,0:T(8,128)(2,1)S(1)} collective-permute-done((f16[528,128]{1,0:T(8,128)(2,1)S(1)}, f16[528,128]{1,0:T(8,128)(2,1)S(1)}, u32[]{:S(2)}, u32[]{:S(2)}) %collective-permute-start.4) | collective-permute-done | bytes 135200 | tf_op jit(solution)/shard_map/ppermute | solution.py:50
  12.6 3.4 %collective-permute-done.2 = f16[528,128]{1,0:T(8,128)(2,1)S(1)} collective-permute-done((f16[528,128]{1,0:T(8,128)(2,1)S(1)}, f16[528,128]{1,0:T(8,128)(2,1)S(1)}, u32[]{:S(2)}, u32[]{:S(2)}) %collective-permute-start.2) | collective-permute-done | bytes 135200 | tf_op jit(solution)/shard_map/ppermute | solution.py:50
  16.0 0.0 collective-permute-done.1
  16.0 0.1 broadcast_in_dim.2.scale_ref.refs_3_.refs_5_.refs_1_
  16.1 0.2 shard_map.80
  16.4 1.6 %collective-permute-start.5 = (f16[272,128]{1,0:T(8,128)(2,1)S(1)}, f16[272,128]{1,0:T(8,128)(2,1)S(1)}, u32[]{:S(2)}, u32[]{:S(2)}) collective-permute-start(f16[272,128]{1,0:T(8,128)(2,1)S(1)} %convert_element_type.66), channel_id=1, source_target_pairs={{0,8},{2,10},{4,12},{6,14},{8,0},{10,2},{12,4},{14,6},{16,24},{18,... | collective-permute-start | bytes 208904 | tf_op jit(solution)/shard_map/ppermute | solution.py:50
  18.0 2.3 %collective-permute-start.7 = (f16[272,128]{1,0:T(8,128)(2,1)S(1)}, f16[272,128]{1,0:T(8,128)(2,1)S(1)}, u32[]{:S(2)}, u32[]{:S(2)}) collective-permute-start(f16[272,128]{1,0:T(8,128)(2,1)S(1)} %convert_element_type.68), channel_id=1, source_target_pairs={{0,24},{2,26},{4,28},{6,30},{8,16},{10,18},{12,20},{14,22},{16,8},... | collective-permute-start | bytes 208904 | tf_op jit(solution)/shard_map/ppermute | solution.py:50
  20.2 0.2 collective-permute-start.6
  20.4 0.0 collective-permute-done.5
  20.4 3.5 %collective-permute-done.7 = f16[272,128]{1,0:T(8,128)(2,1)S(1)} collective-permute-done((f16[272,128]{1,0:T(8,128)(2,1)S(1)}, f16[272,128]{1,0:T(8,128)(2,1)S(1)}, u32[]{:S(2)}, u32[]{:S(2)}) %collective-permute-start.7) | collective-permute-done | bytes 69664 | tf_op jit(solution)/shard_map/ppermute | solution.py:50
  23.9 3.8 %collective-permute-done.6 = f16[272,128]{1,0:T(8,128)(2,1)S(1)} collective-permute-done((f16[272,128]{1,0:T(8,128)(2,1)S(1)}, f16[272,128]{1,0:T(8,128)(2,1)S(1)}, u32[]{:S(2)}, u32[]{:S(2)}) %collective-permute-start.6) | collective-permute-done | bytes 69664 | tf_op jit(solution)/shard_map/ppermute | solution.py:50
  27.7 0.2 shard_map.81
  27.9 1.5 %collective-permute-start.10 = (f16[528,128]{1,0:T(8,128)(2,1)S(1)}, f16[528,128]{1,0:T(8,128)(2,1)S(1)}, u32[]{:S(2)}, u32[]{:S(2)}) collective-permute-start(f16[528,128]{1,0:T(8,128)(2,1)S(1)} %convert_element_type.75), channel_id=1, source_target_pairs={{0,6},{2,4},{4,2},{6,0},{8,14},{10,12},{12,10},{14,8},{16,22},{18,... | collective-permute-start | bytes 405512 | tf_op jit(solution)/shard_map/ppermute | solution.py:50
  29.4 1.0 %collective-permute-start.9 = (f16[528,128]{1,0:T(8,128)(2,1)S(1)}, f16[528,128]{1,0:T(8,128)(2,1)S(1)}, u32[]{:S(2)}, u32[]{:S(2)}) collective-permute-start(f16[528,128]{1,0:T(8,128)(2,1)S(1)} %convert_element_type.73), channel_id=1, source_target_pairs={{0,4},{2,6},{4,0},{6,2},{8,12},{10,14},{12,8},{14,10},{16,20},{18,... | collective-permute-start | bytes 405512 | tf_op jit(solution)/shard_map/ppermute | solution.py:50
  30.4 0.3 collective-permute-start.8
  30.7 2.8 %collective-permute-done.10 = f16[528,128]{1,0:T(8,128)(2,1)S(1)} collective-permute-done((f16[528,128]{1,0:T(8,128)(2,1)S(1)}, f16[528,128]{1,0:T(8,128)(2,1)S(1)}, u32[]{:S(2)}, u32[]{:S(2)}) %collective-permute-start.10) | collective-permute-done | bytes 135200 | tf_op jit(solution)/shard_map/ppermute | solution.py:50
  33.6 3.7 %collective-permute-done.9 = f16[528,128]{1,0:T(8,128)(2,1)S(1)} collective-permute-done((f16[528,128]{1,0:T(8,128)(2,1)S(1)}, f16[528,128]{1,0:T(8,128)(2,1)S(1)}, u32[]{:S(2)}, u32[]{:S(2)}) %collective-permute-start.9) | collective-permute-done | bytes 135200 | tf_op jit(solution)/shard_map/ppermute | solution.py:50
  37.3 0.0 collective-permute-done.8
  37.3 0.1 shard_map.82
  37.5 0.1 convert_element_type.77
  37.6 0.6 %collective-permute-start.11 = (f16[1552,128]{1,0:T(8,128)(2,1)S(1)}, f16[1552,128]{1,0:T(8,128)(2,1)S(1)}, u32[]{:S(2)}, u32[]{:S(2)}) collective-permute-start(f16[1552,128]{1,0:T(8,128)(2,1)S(1)} %convert_element_type.77), channel_id=1, source_target_pairs={{0,1},{1,0},{2,3},{3,2},{4,5},{5,4},{6,7},{7,6},{8,9},{9,8},{10,11... | collective-permute-start | bytes 1191944 | tf_op jit(solution)/shard_map/ppermute | solution.py:50
  38.2 0.1 collective-permute-start.12
  38.3 2.6 %shard_map.85.refs_12_.refs_11_.refs_7_ = f32[2,3,256,256]{3,2,1,0:T(8,128)S(1)} custom-call(f32[16,16,128]{2,1,0:T(8,128)S(1)} %broadcast_in_dim.2.scale_ref.refs_3_.refs_5_.refs_1_, bf16[256,1024]{1,0:T(8,128)(2,1)S(1)} %get-tuple-element.49.refs_0_, bf16[256,1024]{1,0:T(8,128)(2,1)S(1)} %get-tuple-element.50.refs_1_.refs_4_.refs_6_, ...), custom_call_target="tpu_custom_call" | custom-call | flops 402653184 | bytes 4325376 | tf_op jit(solution)/shard_map/pallas_call | solution.py:37
  40.9 3.9 %shard_map.84.refs_11_.refs_10_.refs_6_ = f32[3,3,256,256]{3,2,1,0:T(8,128)S(1)} custom-call(f32[16,16,128]{2,1,0:T(8,128)S(1)} %broadcast_in_dim.2.scale_ref.refs_3_.refs_5_.refs_1_, bf16[256,1024]{1,0:T(8,128)(2,1)S(1)} %get-tuple-element.49.refs_0_, bf16[256,1024]{1,0:T(8,128)(2,1)S(1)} %get-tuple-element.50.refs_1_.refs_4_.refs_6_, ...), custom_call_target="tpu_custom_call" | custom-call | flops 603979776 | bytes 4325376 | tf_op jit(solution)/shard_map/pallas_call | solution.py:37
  44.8 3.9 %shard_map.83.refs_10_.refs_9_.refs_5_ = f32[3,3,256,256]{3,2,1,0:T(8,128)S(1)} custom-call(f32[16,16,128]{2,1,0:T(8,128)S(1)} %broadcast_in_dim.2.scale_ref.refs_3_.refs_5_.refs_1_, bf16[256,1024]{1,0:T(8,128)(2,1)S(1)} %get-tuple-element.49.refs_0_, bf16[256,1024]{1,0:T(8,128)(2,1)S(1)} %get-tuple-element.50.refs_1_.refs_4_.refs_6_, ...), custom_call_target="tpu_custom_call" | custom-call | flops 603979776 | bytes 4325376 | tf_op jit(solution)/shard_map/pallas_call | solution.py:37
  48.7 0.0 collective-permute-done.12.refs_2_
  48.7 1.4 %shard_map.87 = (bf16[256,2048]{1,0:T(8,128)(2,1)}, bf16[256,2048]{1,0:T(8,128)(2,1)}, bf16[256,2048]{1,0:T(8,128)(2,1)}) custom-call(f32[3,2,2,128,128]{4,3,2,1,0:T(8,128)S(1)} %collective-permute-done.other_ref.refs_0_, f32[528,128]{1,0:T(8,128)S(1)} %get-tuple-element.54.keep_ref.refs_1_, f32[2,2,128,128]{3,2,1,0:T(8,128)S(1)} %collective-permute-done.12.refs_2_, ...), custom_call_target="tpu_custom_call" | custom-call | flops 201326592 | bytes 10887168 | tf_op jit(solution)/shard_map/pallas_call | solution.py:37
  50.1 1.7 %shard_map.88 = (bf16[256,2048]{1,0:T(8,128)(2,1)}, bf16[256,2048]{1,0:T(8,128)(2,1)}, bf16[256,2048]{1,0:T(8,128)(2,1)}) custom-call(f32[3,2,2,128,128]{4,3,2,1,0:T(8,128)S(1)} %collective-permute-done.other_ref.refs_0_, ...), custom_call_target="tpu_custom_call", output_to_operand_aliasing={{0}: (12, {}), {1}: (13, {}), {2}: (14, {})} | custom-call | flops 301989888 | bytes 13000704 | tf_op jit(solution)/shard_map/pallas_call | solution.py:37
  51.8 0.0 collective-permute-done.11
  51.8 0.1 convert_element_type.78.refs_0_
  51.8 1.6 %shard_map.89 = (bf16[256,2048]{1,0:T(8,128)(2,1)}, bf16[256,2048]{1,0:T(8,128)(2,1)}, bf16[256,2048]{1,0:T(8,128)(2,1)}) custom-call(f32[1552,128]{1,0:T(8,128)S(1)} %convert_element_type.78.refs_0_, f32[16,16,128]{2,1,0:T(8,128)S(1)} %broadcast_in_dim.2.scale_ref.refs_3_.refs_5_.refs_1_, ...), custom_call_target="tpu_custom_call", output_to_operand_aliasing={{0}: (8, {}), {1}: (9, {}), {2}: (10, {})} | custom-call | flops 301989888 | bytes 11935744 | tf_op jit(solution)/shard_map/pallas_call | solution.py:37
  (21 shorter events, 0.4 us)
Async XLA Ops:
  2.7 6.3 %collective-permute-start = (f32[3,2,2,128,128]{4,3,2,1,0:T(8,128)S(1)}, f32[3,2,2,128,128]{4,3,2,1,0:T(8,128)S(1)}, u32[]{:S(2)}, u32[]{:S(2)}) collective-permute-start(f32[3,2,2,128,128]{4,3,2,1,0:T(8,128)S(1)} %get-tuple-element.34), channel_id=1, source_target_pairs={{0,1},{1,0},{2,3},{3,2},{4,5},{5,4},{6,7},{7,6},{8,9},{9,8},{10,11... | collective-permute-start | bytes 2359304 | tf_op jit(solution)/shard_map/ppermute | solution.py:50
  2.8 2.7 %collective-permute-start.3 = (f32[1,2,2,128,128]{4,3,2,1,0:T(8,128)S(1)}, f32[1,2,2,128,128]{4,3,2,1,0:T(8,128)S(1)}, u32[]{:S(2)}, u32[]{:S(2)}) collective-permute-start(f32[1,2,2,128,128]{4,3,2,1,0:T(8,128)S(1)} %get-tuple-element.38), channel_id=1, source_target_pairs={{0,1},{1,0},{2,3},{3,2},{4,5},{5,4},{6,7},{7,6},{8,9},{9,8},{10,11... | collective-permute-start | bytes 786440 | tf_op jit(solution)/shard_map/ppermute | solution.py:50
  5.5 4.3 %copy-start = (f32[16,11]{1,0:T(8,128)S(1)}, f32[16,11]{1,0:T(8,128)}, u32[]{:S(2)}) copy-start(f32[16,11]{1,0:T(8,128)} %param.9) | copy-start | bytes 2116
  5.7 6.9 %collective-permute-start.4 = (f16[528,128]{1,0:T(8,128)(2,1)S(1)}, f16[528,128]{1,0:T(8,128)(2,1)S(1)}, u32[]{:S(2)}, u32[]{:S(2)}) collective-permute-start(f16[528,128]{1,0:T(8,128)(2,1)S(1)} %convert_element_type.64), channel_id=1, source_target_pairs={{0,6},{2,4},{4,2},{6,0},{8,14},{10,12},{12,10},{14,8},{16,22},{18,... | collective-permute-start | bytes 405512 | tf_op jit(solution)/shard_map/ppermute | solution.py:50
  9.3 6.6 %collective-permute-start.2 = (f16[528,128]{1,0:T(8,128)(2,1)S(1)}, f16[528,128]{1,0:T(8,128)(2,1)S(1)}, u32[]{:S(2)}, u32[]{:S(2)}) collective-permute-start(f16[528,128]{1,0:T(8,128)(2,1)S(1)} %convert_element_type.62), channel_id=1, source_target_pairs={{0,4},{2,6},{4,0},{6,2},{8,12},{10,14},{12,8},{14,10},{16,20},{18,... | collective-permute-start | bytes 405512 | tf_op jit(solution)/shard_map/ppermute | solution.py:50
  9.7 6.3 %collective-permute-start.1 = (f16[528,128]{1,0:T(8,128)(2,1)S(1)}, f16[528,128]{1,0:T(8,128)(2,1)S(1)}, u32[]{:S(2)}, u32[]{:S(2)}) collective-permute-start(f16[528,128]{1,0:T(8,128)(2,1)S(1)} %convert_element_type.60), channel_id=1, source_target_pairs={{0,2},{2,0},{4,6},{6,4},{8,10},{10,8},{12,14},{14,12},{16,18},{18,... | collective-permute-start | bytes 405512 | tf_op jit(solution)/shard_map/ppermute | solution.py:50
  16.4 4.0 %collective-permute-start.5 = (f16[272,128]{1,0:T(8,128)(2,1)S(1)}, f16[272,128]{1,0:T(8,128)(2,1)S(1)}, u32[]{:S(2)}, u32[]{:S(2)}) collective-permute-start(f16[272,128]{1,0:T(8,128)(2,1)S(1)} %convert_element_type.66), channel_id=1, source_target_pairs={{0,8},{2,10},{4,12},{6,14},{8,0},{10,2},{12,4},{14,6},{16,24},{18,... | collective-permute-start | bytes 208904 | tf_op jit(solution)/shard_map/ppermute | solution.py:50
  18.0 5.9 %collective-permute-start.7 = (f16[272,128]{1,0:T(8,128)(2,1)S(1)}, f16[272,128]{1,0:T(8,128)(2,1)S(1)}, u32[]{:S(2)}, u32[]{:S(2)}) collective-permute-start(f16[272,128]{1,0:T(8,128)(2,1)S(1)} %convert_element_type.68), channel_id=1, source_target_pairs={{0,24},{2,26},{4,28},{6,30},{8,16},{10,18},{12,20},{14,22},{16,8},... | collective-permute-start | bytes 208904 | tf_op jit(solution)/shard_map/ppermute | solution.py:50
  20.2 7.5 %collective-permute-start.6 = (f16[272,128]{1,0:T(8,128)(2,1)S(1)}, f16[272,128]{1,0:T(8,128)(2,1)S(1)}, u32[]{:S(2)}, u32[]{:S(2)}) collective-permute-start(f16[272,128]{1,0:T(8,128)(2,1)S(1)} %convert_element_type.68), channel_id=1, source_target_pairs={{0,16},{2,18},{4,20},{6,22},{8,24},{10,26},{12,28},{14,30},{16,0},... | collective-permute-start | bytes 208904 | tf_op jit(solution)/shard_map/ppermute | solution.py:50
  27.9 5.6 %collective-permute-start.10 = (f16[528,128]{1,0:T(8,128)(2,1)S(1)}, f16[528,128]{1,0:T(8,128)(2,1)S(1)}, u32[]{:S(2)}, u32[]{:S(2)}) collective-permute-start(f16[528,128]{1,0:T(8,128)(2,1)S(1)} %convert_element_type.75), channel_id=1, source_target_pairs={{0,6},{2,4},{4,2},{6,0},{8,14},{10,12},{12,10},{14,8},{16,22},{18,... | collective-permute-start | bytes 405512 | tf_op jit(solution)/shard_map/ppermute | solution.py:50
  29.4 7.9 %collective-permute-start.9 = (f16[528,128]{1,0:T(8,128)(2,1)S(1)}, f16[528,128]{1,0:T(8,128)(2,1)S(1)}, u32[]{:S(2)}, u32[]{:S(2)}) collective-permute-start(f16[528,128]{1,0:T(8,128)(2,1)S(1)} %convert_element_type.73), channel_id=1, source_target_pairs={{0,4},{2,6},{4,0},{6,2},{8,12},{10,14},{12,8},{14,10},{16,20},{18,... | collective-permute-start | bytes 405512 | tf_op jit(solution)/shard_map/ppermute | solution.py:50
  30.4 6.9 %collective-permute-start.8 = (f16[528,128]{1,0:T(8,128)(2,1)S(1)}, f16[528,128]{1,0:T(8,128)(2,1)S(1)}, u32[]{:S(2)}, u32[]{:S(2)}) collective-permute-start(f16[528,128]{1,0:T(8,128)(2,1)S(1)} %convert_element_type.71), channel_id=1, source_target_pairs={{0,2},{2,0},{4,6},{6,4},{8,10},{10,8},{12,14},{14,12},{16,18},{18,... | collective-permute-start | bytes 405512 | tf_op jit(solution)/shard_map/ppermute | solution.py:50
  37.6 14.2 %collective-permute-start.11 = (f16[1552,128]{1,0:T(8,128)(2,1)S(1)}, f16[1552,128]{1,0:T(8,128)(2,1)S(1)}, u32[]{:S(2)}, u32[]{:S(2)}) collective-permute-start(f16[1552,128]{1,0:T(8,128)(2,1)S(1)} %convert_element_type.77), channel_id=1, source_target_pairs={{0,1},{1,0},{2,3},{3,2},{4,5},{5,4},{6,7},{7,6},{8,9},{9,8},{10,11... | collective-permute-start | bytes 1191944 | tf_op jit(solution)/shard_map/ppermute | solution.py:50
  38.2 10.5 %collective-permute-start.12 = (f32[2,2,128,128]{3,2,1,0:T(8,128)S(1)}, f32[2,2,128,128]{3,2,1,0:T(8,128)S(1)}, u32[]{:S(2)}, u32[]{:S(2)}) collective-permute-start(f32[2,2,128,128]{3,2,1,0:T(8,128)S(1)} %shard_map.86), channel_id=1, source_target_pairs={{0,1},{1,0},{2,3},{3,2},{4,5},{5,4},{6,7},{7,6},{8,9},{9,8},{10,11... | collective-permute-start | bytes 786440 | tf_op jit(solution)/shard_map/ppermute | solution.py:50

commit v8 on v7

--- a/solution.py
+++ b/solution.py
@@ -105,61 +105,85 @@
     return lax.axis_index("seq") & (slices - 1)
 
 
-def state_kernel(half, cuts, *refs):
-    srcs, refs = refs[:4], refs[4:]
-    if half:
-        (early_ref, late_ref), held, (out_ref, sems) = refs[:2], refs[2:6], refs[6:]
-    else:
-        (out_ref, mark_ref), held, (sems,) = refs[:2], refs[2:6], refs[6:]
+def form_states(heads, held, out_ref, visit=None):
     q_ref, k_ref, v_ref, o_ref = held
     slices, _, width = out_ref.shape[:3]
-    model = q_ref.shape[1]
     place = near_place(slices)
+    for head in heads:
+        d, j = place ^ (head // width), head % width
+        cols = slice(head * DH, (head + 1) * DH)
+        pairs = (dot(v_ref[:, cols], k_ref[:, cols], TN), dot(o_ref[:, cols], q_ref[:, cols], TN))
+        for t in range(2):
+            out_ref[d, t, j] = pairs[t]
+            if visit:
+                visit(t, pairs[t])
+
+
+def first_kernel(cuts, *refs):
+    srcs, (early_ref, late_ref), there, here, (out_ref, sems) = refs[:4], refs[4:6], refs[6:10], refs[10:14], refs[14:]
+    slices = out_ref.shape[0]
+    model = there[0].shape[1]
     size = model // cuts
     copies = []
     for c in range(cuts):
-        start = pl.multiple_of(first_head(half, model // DH) * DH + c * size, DH)
+        start = pl.multiple_of(first_head(1, model // DH) * DH + c * size, DH)
         for i in range(4):
-            copy = pltpu.make_async_copy(
-                srcs[i].at[:, pl.ds(start, size)], held[i].at[:, c * size : (c + 1) * size], sems.at[c, i]
+            copies.append(
+                pltpu.make_async_copy(
+                    srcs[i].at[:, pl.ds(start, size)], there[i].at[:, c * size : (c + 1) * size], sems.at[c, i]
+                )
             )
-            copy.start()
-            copies.append(copy)
+    start = pl.multiple_of(first_head(0, model // DH) * DH, DH)
+    for i in range(4):
+        copies.append(pltpu.make_async_copy(srcs[i].at[:, pl.ds(start, model)], here[i], sems.at[cuts, i]))
+    for copy in copies:
+        copy.start()
+    for c in range(cuts):
+        for copy in copies[4 * c : 4 * c + 4]:
+            copy.wait()
+        form_states(range(c * size // DH, (c + 1) * size // DH), there, out_ref)
+    late_ref[...] = out_ref[: slices - 1]
+    early_ref[0] = out_ref[slices - 1]
+    for copy in copies[4 * cuts :]:
+        copy.wait()
+
+
+def second_kernel(*refs):
+    held, (out_ref, mark_ref) = refs[:4], refs[4:]
     most = [jnp.zeros((8, DH), F32)] * 2
-    for c in range(cuts):
-        for i in range(4):
-            copies[4 * c + i].wait()
-        for head in range(c * size // DH, (c + 1) * size // DH):
-            d, j = place ^ (head // width), head % width
-            cols = slice(head * DH, (head + 1) * DH)
-            pairs = (dot(v_ref[:, cols], k_ref[:, cols], TN), dot(o_ref[:, cols], q_ref[:, cols], TN))
-            for t in range(2):
-                out_ref[d, t, j] = pairs[t]
-                if half == 0:
-                    most[t] = jnp.maximum(most[t], jnp.max(jnp.abs(pairs[t]).reshape(-1, 8, DH), axis=0))
-    if half:
-        late_ref[...] = out_ref[: slices - 1]
-        early_ref[0] = out_ref[slices - 1]
-    else:
-        for t in range(2):
-            mark_ref[8 * t : 8 * t + 8] = jnp.full((8, DH), jnp.max(most[t]), F32)
-
-
-def device_states(half, args, slices, width):
+
+    def visit(t, value):
+        most[t] = jnp.maximum(most[t], jnp.max(jnp.abs(value).reshape(-1, 8, DH), axis=0))
+
+    form_states(range(held[0].shape[1] // DH), held, out_ref, visit)
+    for t in range(2):
+        mark_ref[8 * t : 8 * t + 8] = jnp.full((8, DH), jnp.max(most[t]), F32)
+
+
+def device_states(args, slices, width):
     tokens = args[0].shape[0]
     cuts = 2 if slices % 2 == 0 else 1
 
     def states(count):
         return pltpu.VMEM((count, 2, width, DH, DH), F32)
 
-    return call(
-        functools.partial(state_kernel, half, cuts),
-        ([states(1), states(slices - 1)] if half else [states(slices), pltpu.VMEM((16, DH), F32)])
-        + [pltpu.VMEM((tokens, slices * width * DH), BF16)] * 4,
+    early, late, *held = call(
+        functools.partial(first_kernel, cuts),
+        [states(1), states(slices - 1)] + [pltpu.VMEM((tokens, slices * width * DH), BF16)] * 8,
         args,
         specs=[HBM] * 4,
-        scratch=([states(slices)] if half else []) + [pltpu.SemaphoreType.DMA((cuts, 4))],
+        scratch=[states(slices), pltpu.SemaphoreType.DMA((cuts + 1, 4))],
         flops=4 * slices * width * tokens * DH * DH,
+    )
+    return early, late, held[4:], held[:4]
+
+
+def own_states(held, slices, width):
+    return call(
+        second_kernel,
+        [pltpu.VMEM((slices, 2, width, DH, DH), F32), pltpu.VMEM((16, DH), F32)],
+        held,
+        flops=4 * slices * width * held[0].shape[0] * DH * DH,
     )
 
 
@@ -484,10 +508,10 @@
     scales = jnp.broadcast_to(padded[:, :, None], (*padded.shape, DH))
 
     args = [pltpu.with_memory_space_constraint(x, pltpu.HBM) for x in (queries, key_rows, values, out_grad)]
-    sent_a, sent_b, *held_there = device_states(1, args, slices, width)
+    sent_a, sent_b, held_here, held_there = device_states(args, slices, width)
     other_a = partner(sent_a, "head", 1)
     other_b = partner(sent_b, "head", 1)
-    own, most, *held_here = device_states(0, args, slices, width)
+    own, most = own_states(held_here, slices, width)
     held = (held_here, held_there)
     every = [(half, d) for half in range(2) for d in range(slices)]
     ends = [0, 3 * len(every) // 8, 6 * len(every) // 8, len(every)]

time: 54.1 us -> 54.3 us (level)
  waiting for transfers between devices: 20 us -> 21.4 us
  Pallas kernels: 20.3 us -> 19 us
    ppermute x13, waiting for transfers between devices: 20 us -> 21.4 us  [partner(): lax.ppermute(array, axis, [(i, i ^ distance) for i in range(lax.axis_size...]
    pallas_call x14, Pallas kernels: 20.3 us -> 19 us  [call(): pl.pallas_call(kernel, in_specs=specs or [VMEM] * len(args), out_specs=ou...]
  transfers between devices with their start and end apart: 13 -> 13, of which waited for: 6 -> 7; matrix products, arithmetic and copies ran while one was open for 0% -> 0% of each run, Pallas kernels for 30% -> 27%
where the time goes in v8:
time: 54.3 us; the launch traced here: 53.7 us
  waiting for transfers between devices  21.4 us (39%)
  Pallas kernels  19 us (35%)
  starting transfers between devices  11.8 us (22%)
  between operations  0.89 us (2%)
    ppermute x13, waiting for transfers between devices, partner(): lax.ppermute(array, axis, [(i, i ^ distance) for i in range(lax.axis_size...  21.4 us
    pallas_call x14, Pallas kernels, call(): pl.pallas_call(kernel, in_specs=specs or [VMEM] * len(args), out_specs=ou...  19 us
    ppermute x13, starting transfers between devices, partner(): lax.ppermute(array, axis, [(i, i ^ distance) for i in range(lax.axis_size...  11.8 us
  transfers between devices with their start and end apart: 13, of which 7 were waited for; matrix products, arithmetic and copies ran while one was open for 0% of the time, Pallas kernels for 27%

profile of v8, /device:TPU:1, one launch (start us, length us, event | category | flops | bytes accessed | tf_op | source)
XLA Modules:
  0.0 53.7 jit_solution(3306540486333416532)
XLA Ops:
  0.6 2.3 %shard_map.76 = (f32[1,2,2,128,128]{4,3,2,1,0:T(8,128)S(1)}, f32[3,2,2,128,128]{4,3,2,1,0:T(8,128)S(1)}, bf16[256,1024]{1,0:T(8,128)(2,1)S(1)}, bf16[256,1024]{1...) custom-call(bf16[256,2048]{1,0:T(8,128)(2,1)} %refs_0_.1, ...), custom_call_target="tpu_custom_call" | custom-call | flops 134217728 | bytes 4194304 | tf_op jit(solution)/shard_map/pallas_call | solution.py:37
  2.9 0.1 collective-permute-start
  3.0 0.5 collective-permute-start.3
  3.5 0.6 %shard_map.77 = (f32[4,2,2,128,128]{4,3,2,1,0:T(8,128)S(1)}, f32[16,128]{1,0:T(8,128)S(1)}) custom-call(bf16[256,1024]{1,0:T(8,128)(2,1)S(1)} %get-tuple-element.32.refs_0_, bf16[256,1024]{1,0:T(8,128)(2,1)S(1)} %get-tuple-element.33.refs_1_.refs_4_.refs_6_, bf16[256,1024]{1,0:T(8,128)(2,1)S(1)} %get-tuple-element.34.refs_2_.refs_5_.refs_7_, ...), custom_call_target="tpu_custom_call" | custom-call | flops 134217728 | bytes 2097152 | tf_op jit(solution)/shard_map/pallas_call | solution.py:37
  4.2 0.0 copy-start
  4.2 1.5 %collective-permute-done.3.other_ref.refs_1_ = f32[1,2,2,128,128]{4,3,2,1,0:T(8,128)S(1)} collective-permute-done((f32[1,2,2,128,128]{4,3,2,1,0:T(8,128)S(1)}, f32[1,2,2,128,128]{4,3,2,1,0:T(8,128)S(1)}, u32[]{:S(2)}, u32[]{:S(2)}) %collective-permute-start.3) | collective-permute-done | bytes 262176 | tf_op jit(solution)/shard_map/ppermute | solution.py:50
  5.6 0.2 shard_map.79
  5.9 3.4 %collective-permute-start.4 = (f16[528,128]{1,0:T(8,128)(2,1)S(1)}, f16[528,128]{1,0:T(8,128)(2,1)S(1)}, u32[]{:S(2)}, u32[]{:S(2)}) collective-permute-start(f16[528,128]{1,0:T(8,128)(2,1)S(1)} %convert_element_type.64), channel_id=1, source_target_pairs={{0,6},{2,4},{4,2},{6,0},{8,14},{10,12},{12,10},{14,8},{16,22},{18,... | collective-permute-start | bytes 405512 | tf_op jit(solution)/shard_map/ppermute | solution.py:50
  9.2 0.0 collective-permute-done.other_ref.refs_0_
  9.2 0.2 shard_map.78
  9.5 0.3 collective-permute-start.2
  9.8 0.1 collective-permute-start.1
  9.9 0.0 copy-done
  9.9 2.9 %collective-permute-done.4 = f16[528,128]{1,0:T(8,128)(2,1)S(1)} collective-permute-done((f16[528,128]{1,0:T(8,128)(2,1)S(1)}, f16[528,128]{1,0:T(8,128)(2,1)S(1)}, u32[]{:S(2)}, u32[]{:S(2)}) %collective-permute-start.4) | collective-permute-done | bytes 135200 | tf_op jit(solution)/shard_map/ppermute | solution.py:50
  12.8 3.3 %collective-permute-done.2 = f16[528,128]{1,0:T(8,128)(2,1)S(1)} collective-permute-done((f16[528,128]{1,0:T(8,128)(2,1)S(1)}, f16[528,128]{1,0:T(8,128)(2,1)S(1)}, u32[]{:S(2)}, u32[]{:S(2)}) %collective-permute-start.2) | collective-permute-done | bytes 135200 | tf_op jit(solution)/shard_map/ppermute | solution.py:50
  16.2 0.0 collective-permute-done.1
  16.2 0.1 broadcast_in_dim.2.scale_ref.refs_3_.refs_5_.refs_1_
  16.3 0.2 shard_map.80
  16.6 1.6 %collective-permute-start.5 = (f16[272,128]{1,0:T(8,128)(2,1)S(1)}, f16[272,128]{1,0:T(8,128)(2,1)S(1)}, u32[]{:S(2)}, u32[]{:S(2)}) collective-permute-start(f16[272,128]{1,0:T(8,128)(2,1)S(1)} %convert_element_type.66), channel_id=1, source_target_pairs={{0,8},{2,10},{4,12},{6,14},{8,0},{10,2},{12,4},{14,6},{16,24},{18,... | collective-permute-start | bytes 208904 | tf_op jit(solution)/shard_map/ppermute | solution.py:50
  18.1 2.3 %collective-permute-start.7 = (f16[272,128]{1,0:T(8,128)(2,1)S(1)}, f16[272,128]{1,0:T(8,128)(2,1)S(1)}, u32[]{:S(2)}, u32[]{:S(2)}) collective-permute-start(f16[272,128]{1,0:T(8,128)(2,1)S(1)} %convert_element_type.68), channel_id=1, source_target_pairs={{0,24},{2,26},{4,28},{6,30},{8,16},{10,18},{12,20},{14,22},{16,8},... | collective-permute-start | bytes 208904 | tf_op jit(solution)/shard_map/ppermute | solution.py:50
  20.4 0.2 collective-permute-start.6
  20.6 0.0 collective-permute-done.5
  20.6 3.5 %collective-permute-done.7 = f16[272,128]{1,0:T(8,128)(2,1)S(1)} collective-permute-done((f16[272,128]{1,0:T(8,128)(2,1)S(1)}, f16[272,128]{1,0:T(8,128)(2,1)S(1)}, u32[]{:S(2)}, u32[]{:S(2)}) %collective-permute-start.7) | collective-permute-done | bytes 69664 | tf_op jit(solution)/shard_map/ppermute | solution.py:50
  24.1 3.8 %collective-permute-done.6 = f16[272,128]{1,0:T(8,128)(2,1)S(1)} collective-permute-done((f16[272,128]{1,0:T(8,128)(2,1)S(1)}, f16[272,128]{1,0:T(8,128)(2,1)S(1)}, u32[]{:S(2)}, u32[]{:S(2)}) %collective-permute-start.6) | collective-permute-done | bytes 69664 | tf_op jit(solution)/shard_map/ppermute | solution.py:50
  27.9 0.2 shard_map.81
  28.1 1.5 %collective-permute-start.10 = (f16[528,128]{1,0:T(8,128)(2,1)S(1)}, f16[528,128]{1,0:T(8,128)(2,1)S(1)}, u32[]{:S(2)}, u32[]{:S(2)}) collective-permute-start(f16[528,128]{1,0:T(8,128)(2,1)S(1)} %convert_element_type.75), channel_id=1, source_target_pairs={{0,6},{2,4},{4,2},{6,0},{8,14},{10,12},{12,10},{14,8},{16,22},{18,... | collective-permute-start | bytes 405512 | tf_op jit(solution)/shard_map/ppermute | solution.py:50
  29.6 1.0 %collective-permute-start.9 = (f16[528,128]{1,0:T(8,128)(2,1)S(1)}, f16[528,128]{1,0:T(8,128)(2,1)S(1)}, u32[]{:S(2)}, u32[]{:S(2)}) collective-permute-start(f16[528,128]{1,0:T(8,128)(2,1)S(1)} %convert_element_type.73), channel_id=1, source_target_pairs={{0,4},{2,6},{4,0},{6,2},{8,12},{10,14},{12,8},{14,10},{16,20},{18,... | collective-permute-start | bytes 405512 | tf_op jit(solution)/shard_map/ppermute | solution.py:50
  30.6 0.3 collective-permute-start.8
  30.9 2.8 %collective-permute-done.10 = f16[528,128]{1,0:T(8,128)(2,1)S(1)} collective-permute-done((f16[528,128]{1,0:T(8,128)(2,1)S(1)}, f16[528,128]{1,0:T(8,128)(2,1)S(1)}, u32[]{:S(2)}, u32[]{:S(2)}) %collective-permute-start.10) | collective-permute-done | bytes 135200 | tf_op jit(solution)/shard_map/ppermute | solution.py:50
  33.7 3.7 %collective-permute-done.9 = f16[528,128]{1,0:T(8,128)(2,1)S(1)} collective-permute-done((f16[528,128]{1,0:T(8,128)(2,1)S(1)}, f16[528,128]{1,0:T(8,128)(2,1)S(1)}, u32[]{:S(2)}, u32[]{:S(2)}) %collective-permute-start.9) | collective-permute-done | bytes 135200 | tf_op jit(solution)/shard_map/ppermute | solution.py:50
  37.5 0.0 collective-permute-done.8
  37.5 0.1 shard_map.82
  37.7 0.1 convert_element_type.77
  37.7 0.6 %collective-permute-start.11 = (f16[1552,128]{1,0:T(8,128)(2,1)S(1)}, f16[1552,128]{1,0:T(8,128)(2,1)S(1)}, u32[]{:S(2)}, u32[]{:S(2)}) collective-permute-start(f16[1552,128]{1,0:T(8,128)(2,1)S(1)} %convert_element_type.77), channel_id=1, source_target_pairs={{0,1},{1,0},{2,3},{3,2},{4,5},{5,4},{6,7},{7,6},{8,9},{9,8},{10,11... | collective-permute-start | bytes 1191944 | tf_op jit(solution)/shard_map/ppermute | solution.py:50
  38.3 0.1 collective-permute-start.12
  38.4 2.6 %shard_map.85.refs_12_.refs_11_.refs_7_ = f32[2,3,256,256]{3,2,1,0:T(8,128)S(1)} custom-call(f32[16,16,128]{2,1,0:T(8,128)S(1)} %broadcast_in_dim.2.scale_ref.refs_3_.refs_5_.refs_1_, bf16[256,1024]{1,0:T(8,128)(2,1)S(1)} %get-tuple-element.32.refs_0_, bf16[256,1024]{1,0:T(8,128)(2,1)S(1)} %get-tuple-element.33.refs_1_.refs_4_.refs_6_, ...), custom_call_target="tpu_custom_call" | custom-call | flops 402653184 | bytes 4325376 | tf_op jit(solution)/shard_map/pallas_call | solution.py:37
  41.1 3.9 %shard_map.84.refs_11_.refs_10_.refs_6_ = f32[3,3,256,256]{3,2,1,0:T(8,128)S(1)} custom-call(f32[16,16,128]{2,1,0:T(8,128)S(1)} %broadcast_in_dim.2.scale_ref.refs_3_.refs_5_.refs_1_, bf16[256,1024]{1,0:T(8,128)(2,1)S(1)} %get-tuple-element.32.refs_0_, bf16[256,1024]{1,0:T(8,128)(2,1)S(1)} %get-tuple-element.33.refs_1_.refs_4_.refs_6_, ...), custom_call_target="tpu_custom_call" | custom-call | flops 603979776 | bytes 4325376 | tf_op jit(solution)/shard_map/pallas_call | solution.py:37
  45.0 3.9 %shard_map.83.refs_10_.refs_9_.refs_5_ = f32[3,3,256,256]{3,2,1,0:T(8,128)S(1)} custom-call(f32[16,16,128]{2,1,0:T(8,128)S(1)} %broadcast_in_dim.2.scale_ref.refs_3_.refs_5_.refs_1_, bf16[256,1024]{1,0:T(8,128)(2,1)S(1)} %get-tuple-element.32.refs_0_, bf16[256,1024]{1,0:T(8,128)(2,1)S(1)} %get-tuple-element.33.refs_1_.refs_4_.refs_6_, ...), custom_call_target="tpu_custom_call" | custom-call | flops 603979776 | bytes 4325376 | tf_op jit(solution)/shard_map/pallas_call | solution.py:37
  48.8 0.0 collective-permute-done.12.refs_2_
  48.8 1.4 %shard_map.87 = (bf16[256,2048]{1,0:T(8,128)(2,1)}, bf16[256,2048]{1,0:T(8,128)(2,1)}, bf16[256,2048]{1,0:T(8,128)(2,1)}) custom-call(f32[3,2,2,128,128]{4,3,2,1,0:T(8,128)S(1)} %collective-permute-done.other_ref.refs_0_, f32[528,128]{1,0:T(8,128)S(1)} %get-tuple-element.54.keep_ref.refs_1_, f32[2,2,128,128]{3,2,1,0:T(8,128)S(1)} %collective-permute-done.12.refs_2_, ...), custom_call_target="tpu_custom_call" | custom-call | flops 201326592 | bytes 10887168 | tf_op jit(solution)/shard_map/pallas_call | solution.py:37
  50.3 1.7 %shard_map.88 = (bf16[256,2048]{1,0:T(8,128)(2,1)}, bf16[256,2048]{1,0:T(8,128)(2,1)}, bf16[256,2048]{1,0:T(8,128)(2,1)}) custom-call(f32[3,2,2,128,128]{4,3,2,1,0:T(8,128)S(1)} %collective-permute-done.other_ref.refs_0_, ...), custom_call_target="tpu_custom_call", output_to_operand_aliasing={{0}: (12, {}), {1}: (13, {}), {2}: (14, {})} | custom-call | flops 301989888 | bytes 13000704 | tf_op jit(solution)/shard_map/pallas_call | solution.py:37
  51.9 0.0 collective-permute-done.11
  52.0 0.1 convert_element_type.78.refs_0_
  52.0 1.6 %shard_map.89 = (bf16[256,2048]{1,0:T(8,128)(2,1)}, bf16[256,2048]{1,0:T(8,128)(2,1)}, bf16[256,2048]{1,0:T(8,128)(2,1)}) custom-call(f32[1552,128]{1,0:T(8,128)S(1)} %convert_element_type.78.refs_0_, f32[16,16,128]{2,1,0:T(8,128)S(1)} %broadcast_in_dim.2.scale_ref.refs_3_.refs_5_.refs_1_, ...), custom_call_target="tpu_custom_call", output_to_operand_aliasing={{0}: (8, {}), {1}: (9, {}), {2}: (10, {})} | custom-call | flops 301989888 | bytes 11935744 | tf_op jit(solution)/shard_map/pallas_call | solution.py:37
  (21 shorter events, 0.4 us)
Async XLA Ops:
  2.9 6.3 %collective-permute-start = (f32[3,2,2,128,128]{4,3,2,1,0:T(8,128)S(1)}, f32[3,2,2,128,128]{4,3,2,1,0:T(8,128)S(1)}, u32[]{:S(2)}, u32[]{:S(2)}) collective-permute-start(f32[3,2,2,128,128]{4,3,2,1,0:T(8,128)S(1)} %get-tuple-element.38), channel_id=1, source_target_pairs={{0,1},{1,0},{2,3},{3,2},{4,5},{5,4},{6,7},{7,6},{8,9},{9,8},{10,11... | collective-permute-start | bytes 2359304 | tf_op jit(solution)/shard_map/ppermute | solution.py:50
  3.0 2.6 %collective-permute-start.3 = (f32[1,2,2,128,128]{4,3,2,1,0:T(8,128)S(1)}, f32[1,2,2,128,128]{4,3,2,1,0:T(8,128)S(1)}, u32[]{:S(2)}, u32[]{:S(2)}) collective-permute-start(f32[1,2,2,128,128]{4,3,2,1,0:T(8,128)S(1)} %get-tuple-element.42), channel_id=1, source_target_pairs={{0,1},{1,0},{2,3},{3,2},{4,5},{5,4},{6,7},{7,6},{8,9},{9,8},{10,11... | collective-permute-start | bytes 786440 | tf_op jit(solution)/shard_map/ppermute | solution.py:50
  4.2 5.8 %copy-start = (f32[16,11]{1,0:T(8,128)S(1)}, f32[16,11]{1,0:T(8,128)}, u32[]{:S(2)}) copy-start(f32[16,11]{1,0:T(8,128)} %param.9) | copy-start | bytes 2116
  5.9 6.9 %collective-permute-start.4 = (f16[528,128]{1,0:T(8,128)(2,1)S(1)}, f16[528,128]{1,0:T(8,128)(2,1)S(1)}, u32[]{:S(2)}, u32[]{:S(2)}) collective-permute-start(f16[528,128]{1,0:T(8,128)(2,1)S(1)} %convert_element_type.64), channel_id=1, source_target_pairs={{0,6},{2,4},{4,2},{6,0},{8,14},{10,12},{12,10},{14,8},{16,22},{18,... | collective-permute-start | bytes 405512 | tf_op jit(solution)/shard_map/ppermute | solution.py:50
  9.5 6.6 %collective-permute-start.2 = (f16[528,128]{1,0:T(8,128)(2,1)S(1)}, f16[528,128]{1,0:T(8,128)(2,1)S(1)}, u32[]{:S(2)}, u32[]{:S(2)}) collective-permute-start(f16[528,128]{1,0:T(8,128)(2,1)S(1)} %convert_element_type.62), channel_id=1, source_target_pairs={{0,4},{2,6},{4,0},{6,2},{8,12},{10,14},{12,8},{14,10},{16,20},{18,... | collective-permute-start | bytes 405512 | tf_op jit(solution)/shard_map/ppermute | solution.py:50
  9.8 6.4 %collective-permute-start.1 = (f16[528,128]{1,0:T(8,128)(2,1)S(1)}, f16[528,128]{1,0:T(8,128)(2,1)S(1)}, u32[]{:S(2)}, u32[]{:S(2)}) collective-permute-start(f16[528,128]{1,0:T(8,128)(2,1)S(1)} %convert_element_type.60), channel_id=1, source_target_pairs={{0,2},{2,0},{4,6},{6,4},{8,10},{10,8},{12,14},{14,12},{16,18},{18,... | collective-permute-start | bytes 405512 | tf_op jit(solution)/shard_map/ppermute | solution.py:50
  16.6 4.0 %collective-permute-start.5 = (f16[272,128]{1,0:T(8,128)(2,1)S(1)}, f16[272,128]{1,0:T(8,128)(2,1)S(1)}, u32[]{:S(2)}, u32[]{:S(2)}) collective-permute-start(f16[272,128]{1,0:T(8,128)(2,1)S(1)} %convert_element_type.66), channel_id=1, source_target_pairs={{0,8},{2,10},{4,12},{6,14},{8,0},{10,2},{12,4},{14,6},{16,24},{18,... | collective-permute-start | bytes 208904 | tf_op jit(solution)/shard_map/ppermute | solution.py:50
  18.1 5.9 %collective-permute-start.7 = (f16[272,128]{1,0:T(8,128)(2,1)S(1)}, f16[272,128]{1,0:T(8,128)(2,1)S(1)}, u32[]{:S(2)}, u32[]{:S(2)}) collective-permute-start(f16[272,128]{1,0:T(8,128)(2,1)S(1)} %convert_element_type.68), channel_id=1, source_target_pairs={{0,24},{2,26},{4,28},{6,30},{8,16},{10,18},{12,20},{14,22},{16,8},... | collective-permute-start | bytes 208904 | tf_op jit(solution)/shard_map/ppermute | solution.py:50
  20.4 7.5 %collective-permute-start.6 = (f16[272,128]{1,0:T(8,128)(2,1)S(1)}, f16[272,128]{1,0:T(8,128)(2,1)S(1)}, u32[]{:S(2)}, u32[]{:S(2)}) collective-permute-start(f16[272,128]{1,0:T(8,128)(2,1)S(1)} %convert_element_type.68), channel_id=1, source_target_pairs={{0,16},{2,18},{4,20},{6,22},{8,24},{10,26},{12,28},{14,30},{16,0},... | collective-permute-start | bytes 208904 | tf_op jit(solution)/shard_map/ppermute | solution.py:50
  28.1 5.6 %collective-permute-start.10 = (f16[528,128]{1,0:T(8,128)(2,1)S(1)}, f16[528,128]{1,0:T(8,128)(2,1)S(1)}, u32[]{:S(2)}, u32[]{:S(2)}) collective-permute-start(f16[528,128]{1,0:T(8,128)(2,1)S(1)} %convert_element_type.75), channel_id=1, source_target_pairs={{0,6},{2,4},{4,2},{6,0},{8,14},{10,12},{12,10},{14,8},{16,22},{18,... | collective-permute-start | bytes 405512 | tf_op jit(solution)/shard_map/ppermute | solution.py:50
  29.6 7.9 %collective-permute-start.9 = (f16[528,128]{1,0:T(8,128)(2,1)S(1)}, f16[528,128]{1,0:T(8,128)(2,1)S(1)}, u32[]{:S(2)}, u32[]{:S(2)}) collective-permute-start(f16[528,128]{1,0:T(8,128)(2,1)S(1)} %convert_element_type.73), channel_id=1, source_target_pairs={{0,4},{2,6},{4,0},{6,2},{8,12},{10,14},{12,8},{14,10},{16,20},{18,... | collective-permute-start | bytes 405512 | tf_op jit(solution)/shard_map/ppermute | solution.py:50
  30.6 6.9 %collective-permute-start.8 = (f16[528,128]{1,0:T(8,128)(2,1)S(1)}, f16[528,128]{1,0:T(8,128)(2,1)S(1)}, u32[]{:S(2)}, u32[]{:S(2)}) collective-permute-start(f16[528,128]{1,0:T(8,128)(2,1)S(1)} %convert_element_type.71), channel_id=1, source_target_pairs={{0,2},{2,0},{4,6},{6,4},{8,10},{10,8},{12,14},{14,12},{16,18},{18,... | collective-permute-start | bytes 405512 | tf_op jit(solution)/shard_map/ppermute | solution.py:50
  37.7 14.2 %collective-permute-start.11 = (f16[1552,128]{1,0:T(8,128)(2,1)S(1)}, f16[1552,128]{1,0:T(8,128)(2,1)S(1)}, u32[]{:S(2)}, u32[]{:S(2)}) collective-permute-start(f16[1552,128]{1,0:T(8,128)(2,1)S(1)} %convert_element_type.77), channel_id=1, source_target_pairs={{0,1},{1,0},{2,3},{3,2},{4,5},{5,4},{6,7},{7,6},{8,9},{9,8},{10,11... | collective-permute-start | bytes 1191944 | tf_op jit(solution)/shard_map/ppermute | solution.py:50
  38.3 10.5 %collective-permute-start.12 = (f32[2,2,128,128]{3,2,1,0:T(8,128)S(1)}, f32[2,2,128,128]{3,2,1,0:T(8,128)S(1)}, u32[]{:S(2)}, u32[]{:S(2)}) collective-permute-start(f32[2,2,128,128]{3,2,1,0:T(8,128)S(1)} %shard_map.86), channel_id=1, source_target_pairs={{0,1},{1,0},{2,3},{3,2},{4,5},{5,4},{6,7},{7,6},{8,9},{9,8},{10,11... | collective-permute-start | bytes 786440 | tf_op jit(solution)/shard_map/ppermute | solution.py:50

commit v9 on v8

--- a/solution.py
+++ b/solution.py
@@ -162,7 +162,7 @@
 
 def device_states(args, slices, width):
     tokens = args[0].shape[0]
-    cuts = 2 if slices % 2 == 0 else 1
+    cuts = 1
 
     def states(count):
         return pltpu.VMEM((count, 2, width, DH, DH), F32)
@@ -197,21 +197,31 @@
     def blk(n, m=None):
         return slice(n * BLOCK, (n + 1 if m is None else m) * BLOCK)
 
-    def product(left, right, weight, values, n, low, high, mask):
-        raw = dot(left[blk(n)], right[blk(low, high)], NT)
-        parts, rest = [], []
-        for m in range(low, high):
-            part = raw[:, blk(m - low)]
-            if m == n:
-                parts.append(jnp.where(mask, part * weight(0), 0.0).astype(BF16))
-            else:
-                hi, lo = split(part * weight((m ^ n).bit_length()))
-                parts.append(hi)
-                rest.append((m, lo))
-        out = dot(jnp.concatenate(parts, axis=1) if len(parts) > 1 else parts[0], values[blk(low, high)])
-        for m, lo in rest:
-            out = out + dot(lo, values[blk(m)])
-        return out
+    def spread(raw, weight, mask, cross):
+        zero = jnp.zeros((BLOCK, BLOCK), BF16)
+        high, low = [], []
+        for n in range(blocks):
+            tops, rests = [], []
+            for m in range(blocks):
+                part = raw[blk(n), blk(m)]
+                top = rest = zero
+                if m == n:
+                    top = jnp.where(mask, part * weight(0), 0.0).astype(BF16)
+                elif cross(n, m):
+                    top, rest = split(part * weight((m ^ n).bit_length()))
+                tops.append(top)
+                rests.append(rest)
+            high.append(jnp.concatenate(tops, axis=1) if blocks > 1 else tops[0])
+            if any(cross(n, m) for m in range(blocks)):
+                low.append((n, jnp.concatenate(rests, axis=1)))
+        return high, low
+
+    def product(high, low, values):
+        out = dot(jnp.concatenate(high + [x for _, x in low], axis=0), values)
+        rows = [out[blk(n)] for n in range(blocks)]
+        for i, (n, _) in enumerate(low):
+            rows[n] = rows[n] + out[blk(blocks + i)]
+        return rows
 
     place = near_place(model // (width * DH))
     for index, (half, d) in enumerate(lot):
@@ -225,10 +235,16 @@
             def weight(level, head=head):
                 return scale_ref[head, level : level + 1]
 
-            for n in range(blocks):
-                out_ref[index, 2, blk(n), to] = product(k, q, weight, o, n, n, blocks, rows <= cols)
-                out_ref[index, 1, blk(n), to] = product(v, o, weight, q, n, n, blocks, rows <= cols)
-                out_ref[index, 0, blk(n), to] = product(o, v, weight, k, n, 0, n + 1, rows >= cols)
+            high, low = spread(dot(k, q, NT), weight, rows <= cols, lambda n, m: m > n)
+            for n, value in enumerate(product(high, low, o)):
+                out_ref[index, 2, blk(n), to] = value
+            high, low = spread(dot(o, v, NT), weight, rows >= cols, lambda n, m: m < n)
+            for n, value in enumerate(product(high, low, k)):
+                out_ref[index, 0, blk(n), to] = value
+            key_grad = dot(jnp.concatenate(high, axis=0), q, TN)
+            for n, value in low:
+                key_grad = key_grad + dot(value, q[blk(n)], TN)
+            out_ref[index, 1, :, to] = key_grad
 
 
 def local_grads(lot, scales, held, width):
@@ -467,12 +483,13 @@
                 vg = dot(k, hi, NT) + dot(k, lo, NT)
                 for i, cross in enumerate((qg, kg, vg)):
                     temps[index, i, :, to] = (cross + local_refs[part][at_part, i, :, to]).astype(BF16)
-            start = first_head(half, cols // DH) * DH + group * (width * DH)
-            wide = pl.ds(pl.multiple_of(start, DH), width * DH)
-            for i in range(3):
-                copy = pltpu.make_async_copy(temps.at[index, i], outs[i].at[:, wide], sems.at[index, i])
-                copy.start()
-                copies.append(copy)
+                wide = pl.ds(pl.multiple_of((first_head(half, cols // DH) + group * width + j) * DH, DH), DH)
+                for i in range(3):
+                    copy = pltpu.make_async_copy(
+                        temps.at[index, i, :, to], outs[i].at[:, wide], sems.at[index * width + j, i]
+                    )
+                    copy.start()
+                    copies.append(copy)
         for copy in copies:
             copy.wait()
 
@@ -482,7 +499,7 @@
         args + list(before),
         specs=specs,
         out_specs=[HBM] * 3,
-        scratch=[pltpu.VMEM((len(items), 3, tokens, width * DH), BF16), pltpu.SemaphoreType.DMA((len(items), 3))],
+        scratch=[pltpu.VMEM((len(items), 3, tokens, width * DH), BF16), pltpu.SemaphoreType.DMA((len(items) * width, 3))],
         flops=12 * tokens * DH * width * DH * len(items),
         limit=4,
         aliases={len(args) + i: i for i in range(len(before))},

time: 54.3 us -> 49.8 us (0.917)
  Pallas kernels: 19 us -> 14.6 us
    pallas_call x14, Pallas kernels: 19 us -> 14.6 us  [call(): pl.pallas_call(kernel, in_specs=specs or [VMEM] * len(args), out_specs=ou...]
  transfers between devices with their start and end apart: 13 -> 13, of which waited for: 7 -> 7; matrix products, arithmetic and copies ran while one was open for 0% -> 0% of each run, Pallas kernels for 27% -> 21%
where the time goes in v9:
time: 49.8 us; the launch traced here: 49.2 us
  waiting for transfers between devices  21.4 us (43%)
  Pallas kernels  14.6 us (29%)
  starting transfers between devices  11.8 us (24%)
  between operations  0.9 us (2%)
    ppermute x13, waiting for transfers between devices, partner(): lax.ppermute(array, axis, [(i, i ^ distance) for i in range(lax.axis_size...  21.4 us
    pallas_call x14, Pallas kernels, call(): pl.pallas_call(kernel, in_specs=specs or [VMEM] * len(args), out_specs=ou...  14.6 us
    ppermute x13, starting transfers between devices, partner(): lax.ppermute(array, axis, [(i, i ^ distance) for i in range(lax.axis_size...  11.8 us
  transfers between devices with their start and end apart: 13, of which 7 were waited for; matrix products, arithmetic and copies ran while one was open for 0% of the time, Pallas kernels for 21%

profile of v9, /device:TPU:1, one launch (start us, length us, event | category | flops | bytes accessed | tf_op | source)
XLA Modules:
  0.0 49.2 jit_solution(18055856200906148521)
XLA Ops:
  0.6 2.2 %shard_map.76 = (f32[1,2,2,128,128]{4,3,2,1,0:T(8,128)S(1)}, f32[3,2,2,128,128]{4,3,2,1,0:T(8,128)S(1)}, bf16[256,1024]{1,0:T(8,128)(2,1)S(1)}, bf16[256,1024]{1...) custom-call(bf16[256,2048]{1,0:T(8,128)(2,1)} %refs_0_.1, ...), custom_call_target="tpu_custom_call" | custom-call | flops 134217728 | bytes 4194304 | tf_op jit(solution)/shard_map/pallas_call | solution.py:37
  2.9 0.1 collective-permute-start
  2.9 0.5 %collective-permute-start.3 = (f32[1,2,2,128,128]{4,3,2,1,0:T(8,128)S(1)}, f32[1,2,2,128,128]{4,3,2,1,0:T(8,128)S(1)}, u32[]{:S(2)}, u32[]{:S(2)}) collective-permute-start(f32[1,2,2,128,128]{4,3,2,1,0:T(8,128)S(1)} %get-tuple-element.42), channel_id=1, source_target_pairs={{0,1},{1,0},{2,3},{3,2},{4,5},{5,4},{6,7},{7,6},{8,9},{9,8},{10,11... | collective-permute-start | bytes 786440 | tf_op jit(solution)/shard_map/ppermute | solution.py:50
  3.4 0.6 %shard_map.77 = (f32[4,2,2,128,128]{4,3,2,1,0:T(8,128)S(1)}, f32[16,128]{1,0:T(8,128)S(1)}) custom-call(bf16[256,1024]{1,0:T(8,128)(2,1)S(1)} %get-tuple-element.32.refs_0_, bf16[256,1024]{1,0:T(8,128)(2,1)S(1)} %get-tuple-element.33.refs_1_.refs_4_.refs_6_, bf16[256,1024]{1,0:T(8,128)(2,1)S(1)} %get-tuple-element.34.refs_2_.refs_5_.refs_7_, ...), custom_call_target="tpu_custom_call" | custom-call | flops 134217728 | bytes 2097152 | tf_op jit(solution)/shard_map/pallas_call | solution.py:37
  4.1 0.0 copy-start
  4.1 1.5 %collective-permute-done.3.other_ref.refs_1_ = f32[1,2,2,128,128]{4,3,2,1,0:T(8,128)S(1)} collective-permute-done((f32[1,2,2,128,128]{4,3,2,1,0:T(8,128)S(1)}, f32[1,2,2,128,128]{4,3,2,1,0:T(8,128)S(1)}, u32[]{:S(2)}, u32[]{:S(2)}) %collective-permute-start.3) | collective-permute-done | bytes 262176 | tf_op jit(solution)/shard_map/ppermute | solution.py:50
  5.6 0.2 shard_map.79
  5.8 3.4 %collective-permute-start.4 = (f16[528,128]{1,0:T(8,128)(2,1)S(1)}, f16[528,128]{1,0:T(8,128)(2,1)S(1)}, u32[]{:S(2)}, u32[]{:S(2)}) collective-permute-start(f16[528,128]{1,0:T(8,128)(2,1)S(1)} %convert_element_type.64), channel_id=1, source_target_pairs={{0,6},{2,4},{4,2},{6,0},{8,14},{10,12},{12,10},{14,8},{16,22},{18,... | collective-permute-start | bytes 405512 | tf_op jit(solution)/shard_map/ppermute | solution.py:50
  9.2 0.0 collective-permute-done.other_ref.refs_0_
  9.2 0.2 shard_map.78
  9.5 0.3 collective-permute-start.2
  9.8 0.1 collective-permute-start.1
  9.9 0.0 copy-done
  9.9 2.9 %collective-permute-done.4 = f16[528,128]{1,0:T(8,128)(2,1)S(1)} collective-permute-done((f16[528,128]{1,0:T(8,128)(2,1)S(1)}, f16[528,128]{1,0:T(8,128)(2,1)S(1)}, u32[]{:S(2)}, u32[]{:S(2)}) %collective-permute-start.4) | collective-permute-done | bytes 135200 | tf_op jit(solution)/shard_map/ppermute | solution.py:50
  12.8 3.3 %collective-permute-done.2 = f16[528,128]{1,0:T(8,128)(2,1)S(1)} collective-permute-done((f16[528,128]{1,0:T(8,128)(2,1)S(1)}, f16[528,128]{1,0:T(8,128)(2,1)S(1)}, u32[]{:S(2)}, u32[]{:S(2)}) %collective-permute-start.2) | collective-permute-done | bytes 135200 | tf_op jit(solution)/shard_map/ppermute | solution.py:50
  16.1 0.0 collective-permute-done.1
  16.2 0.1 broadcast_in_dim.2.scale_ref.refs_3_.refs_5_.refs_1_
  16.3 0.2 shard_map.80
  16.5 1.6 %collective-permute-start.5 = (f16[272,128]{1,0:T(8,128)(2,1)S(1)}, f16[272,128]{1,0:T(8,128)(2,1)S(1)}, u32[]{:S(2)}, u32[]{:S(2)}) collective-permute-start(f16[272,128]{1,0:T(8,128)(2,1)S(1)} %convert_element_type.66), channel_id=1, source_target_pairs={{0,8},{2,10},{4,12},{6,14},{8,0},{10,2},{12,4},{14,6},{16,24},{18,... | collective-permute-start | bytes 208904 | tf_op jit(solution)/shard_map/ppermute | solution.py:50
  18.1 2.3 %collective-permute-start.7 = (f16[272,128]{1,0:T(8,128)(2,1)S(1)}, f16[272,128]{1,0:T(8,128)(2,1)S(1)}, u32[]{:S(2)}, u32[]{:S(2)}) collective-permute-start(f16[272,128]{1,0:T(8,128)(2,1)S(1)} %convert_element_type.68), channel_id=1, source_target_pairs={{0,24},{2,26},{4,28},{6,30},{8,16},{10,18},{12,20},{14,22},{16,8},... | collective-permute-start | bytes 208904 | tf_op jit(solution)/shard_map/ppermute | solution.py:50
  20.4 0.2 collective-permute-start.6
  20.5 0.0 collective-permute-done.5
  20.6 3.5 %collective-permute-done.7 = f16[272,128]{1,0:T(8,128)(2,1)S(1)} collective-permute-done((f16[272,128]{1,0:T(8,128)(2,1)S(1)}, f16[272,128]{1,0:T(8,128)(2,1)S(1)}, u32[]{:S(2)}, u32[]{:S(2)}) %collective-permute-start.7) | collective-permute-done | bytes 69664 | tf_op jit(solution)/shard_map/ppermute | solution.py:50
  24.1 3.8 %collective-permute-done.6 = f16[272,128]{1,0:T(8,128)(2,1)S(1)} collective-permute-done((f16[272,128]{1,0:T(8,128)(2,1)S(1)}, f16[272,128]{1,0:T(8,128)(2,1)S(1)}, u32[]{:S(2)}, u32[]{:S(2)}) %collective-permute-start.6) | collective-permute-done | bytes 69664 | tf_op jit(solution)/shard_map/ppermute | solution.py:50
  27.8 0.2 shard_map.81
  28.0 1.5 %collective-permute-start.10 = (f16[528,128]{1,0:T(8,128)(2,1)S(1)}, f16[528,128]{1,0:T(8,128)(2,1)S(1)}, u32[]{:S(2)}, u32[]{:S(2)}) collective-permute-start(f16[528,128]{1,0:T(8,128)(2,1)S(1)} %convert_element_type.75), channel_id=1, source_target_pairs={{0,6},{2,4},{4,2},{6,0},{8,14},{10,12},{12,10},{14,8},{16,22},{18,... | collective-permute-start | bytes 405512 | tf_op jit(solution)/shard_map/ppermute | solution.py:50
  29.6 1.0 %collective-permute-start.9 = (f16[528,128]{1,0:T(8,128)(2,1)S(1)}, f16[528,128]{1,0:T(8,128)(2,1)S(1)}, u32[]{:S(2)}, u32[]{:S(2)}) collective-permute-start(f16[528,128]{1,0:T(8,128)(2,1)S(1)} %convert_element_type.73), channel_id=1, source_target_pairs={{0,4},{2,6},{4,0},{6,2},{8,12},{10,14},{12,8},{14,10},{16,20},{18,... | collective-permute-start | bytes 405512 | tf_op jit(solution)/shard_map/ppermute | solution.py:50
  30.5 0.3 collective-permute-start.8
  30.9 2.8 %collective-permute-done.10 = f16[528,128]{1,0:T(8,128)(2,1)S(1)} collective-permute-done((f16[528,128]{1,0:T(8,128)(2,1)S(1)}, f16[528,128]{1,0:T(8,128)(2,1)S(1)}, u32[]{:S(2)}, u32[]{:S(2)}) %collective-permute-start.10) | collective-permute-done | bytes 135200 | tf_op jit(solution)/shard_map/ppermute | solution.py:50
  33.7 3.7 %collective-permute-done.9 = f16[528,128]{1,0:T(8,128)(2,1)S(1)} collective-permute-done((f16[528,128]{1,0:T(8,128)(2,1)S(1)}, f16[528,128]{1,0:T(8,128)(2,1)S(1)}, u32[]{:S(2)}, u32[]{:S(2)}) %collective-permute-start.9) | collective-permute-done | bytes 135200 | tf_op jit(solution)/shard_map/ppermute | solution.py:50
  37.4 0.0 collective-permute-done.8
  37.5 0.1 shard_map.82
  37.6 0.1 convert_element_type.77
  37.7 0.6 %collective-permute-start.11 = (f16[1552,128]{1,0:T(8,128)(2,1)S(1)}, f16[1552,128]{1,0:T(8,128)(2,1)S(1)}, u32[]{:S(2)}, u32[]{:S(2)}) collective-permute-start(f16[1552,128]{1,0:T(8,128)(2,1)S(1)} %convert_element_type.77), channel_id=1, source_target_pairs={{0,1},{1,0},{2,3},{3,2},{4,5},{5,4},{6,7},{7,6},{8,9},{9,8},{10,11... | collective-permute-start | bytes 1191944 | tf_op jit(solution)/shard_map/ppermute | solution.py:50
  38.3 0.1 collective-permute-start.12
  38.4 1.5 %shard_map.85.refs_12_.refs_11_.refs_7_ = f32[2,3,256,256]{3,2,1,0:T(8,128)S(1)} custom-call(f32[16,16,128]{2,1,0:T(8,128)S(1)} %broadcast_in_dim.2.scale_ref.refs_3_.refs_5_.refs_1_, bf16[256,1024]{1,0:T(8,128)(2,1)S(1)} %get-tuple-element.32.refs_0_, bf16[256,1024]{1,0:T(8,128)(2,1)S(1)} %get-tuple-element.33.refs_1_.refs_4_.refs_6_, ...), custom_call_target="tpu_custom_call" | custom-call | flops 402653184 | bytes 4325376 | tf_op jit(solution)/shard_map/pallas_call | solution.py:37
  39.9 2.2 %shard_map.84.refs_11_.refs_10_.refs_6_ = f32[3,3,256,256]{3,2,1,0:T(8,128)S(1)} custom-call(f32[16,16,128]{2,1,0:T(8,128)S(1)} %broadcast_in_dim.2.scale_ref.refs_3_.refs_5_.refs_1_, bf16[256,1024]{1,0:T(8,128)(2,1)S(1)} %get-tuple-element.32.refs_0_, bf16[256,1024]{1,0:T(8,128)(2,1)S(1)} %get-tuple-element.33.refs_1_.refs_4_.refs_6_, ...), custom_call_target="tpu_custom_call" | custom-call | flops 603979776 | bytes 4325376 | tf_op jit(solution)/shard_map/pallas_call | solution.py:37
  42.2 2.2 %shard_map.83.refs_10_.refs_9_.refs_5_ = f32[3,3,256,256]{3,2,1,0:T(8,128)S(1)} custom-call(f32[16,16,128]{2,1,0:T(8,128)S(1)} %broadcast_in_dim.2.scale_ref.refs_3_.refs_5_.refs_1_, bf16[256,1024]{1,0:T(8,128)(2,1)S(1)} %get-tuple-element.32.refs_0_, bf16[256,1024]{1,0:T(8,128)(2,1)S(1)} %get-tuple-element.33.refs_1_.refs_4_.refs_6_, ...), custom_call_target="tpu_custom_call" | custom-call | flops 603979776 | bytes 4325376 | tf_op jit(solution)/shard_map/pallas_call | solution.py:37
  44.4 0.0 collective-permute-done.12.refs_2_
  44.4 1.4 %shard_map.87 = (bf16[256,2048]{1,0:T(8,128)(2,1)}, bf16[256,2048]{1,0:T(8,128)(2,1)}, bf16[256,2048]{1,0:T(8,128)(2,1)}) custom-call(f32[3,2,2,128,128]{4,3,2,1,0:T(8,128)S(1)} %collective-permute-done.other_ref.refs_0_, f32[528,128]{1,0:T(8,128)S(1)} %get-tuple-element.54.keep_ref.refs_1_, f32[2,2,128,128]{3,2,1,0:T(8,128)S(1)} %collective-permute-done.12.refs_2_, ...), custom_call_target="tpu_custom_call" | custom-call | flops 201326592 | bytes 10887168 | tf_op jit(solution)/shard_map/pallas_call | solution.py:37
  45.8 1.7 %shard_map.88 = (bf16[256,2048]{1,0:T(8,128)(2,1)}, bf16[256,2048]{1,0:T(8,128)(2,1)}, bf16[256,2048]{1,0:T(8,128)(2,1)}) custom-call(f32[3,2,2,128,128]{4,3,2,1,0:T(8,128)S(1)} %collective-permute-done.other_ref.refs_0_, ...), custom_call_target="tpu_custom_call", output_to_operand_aliasing={{0}: (12, {}), {1}: (13, {}), {2}: (14, {})} | custom-call | flops 301989888 | bytes 13000704 | tf_op jit(solution)/shard_map/pallas_call | solution.py:37
  47.5 0.0 collective-permute-done.11
  47.5 0.1 convert_element_type.78.refs_0_
  47.6 1.7 %shard_map.89 = (bf16[256,2048]{1,0:T(8,128)(2,1)}, bf16[256,2048]{1,0:T(8,128)(2,1)}, bf16[256,2048]{1,0:T(8,128)(2,1)}) custom-call(f32[1552,128]{1,0:T(8,128)S(1)} %convert_element_type.78.refs_0_, f32[16,16,128]{2,1,0:T(8,128)S(1)} %broadcast_in_dim.2.scale_ref.refs_3_.refs_5_.refs_1_, ...), custom_call_target="tpu_custom_call", output_to_operand_aliasing={{0}: (8, {}), {1}: (9, {}), {2}: (10, {})} | custom-call | flops 301989888 | bytes 11935744 | tf_op jit(solution)/shard_map/pallas_call | solution.py:37
  (21 shorter events, 0.4 us)
Async XLA Ops:
  2.9 6.3 %collective-permute-start = (f32[3,2,2,128,128]{4,3,2,1,0:T(8,128)S(1)}, f32[3,2,2,128,128]{4,3,2,1,0:T(8,128)S(1)}, u32[]{:S(2)}, u32[]{:S(2)}) collective-permute-start(f32[3,2,2,128,128]{4,3,2,1,0:T(8,128)S(1)} %get-tuple-element.38), channel_id=1, source_target_pairs={{0,1},{1,0},{2,3},{3,2},{4,5},{5,4},{6,7},{7,6},{8,9},{9,8},{10,11... | collective-permute-start | bytes 2359304 | tf_op jit(solution)/shard_map/ppermute | solution.py:50
  2.9 2.6 %collective-permute-start.3 = (f32[1,2,2,128,128]{4,3,2,1,0:T(8,128)S(1)}, f32[1,2,2,128,128]{4,3,2,1,0:T(8,128)S(1)}, u32[]{:S(2)}, u32[]{:S(2)}) collective-permute-start(f32[1,2,2,128,128]{4,3,2,1,0:T(8,128)S(1)} %get-tuple-element.42), channel_id=1, source_target_pairs={{0,1},{1,0},{2,3},{3,2},{4,5},{5,4},{6,7},{7,6},{8,9},{9,8},{10,11... | collective-permute-start | bytes 786440 | tf_op jit(solution)/shard_map/ppermute | solution.py:50
  4.1 5.8 %copy-start = (f32[16,11]{1,0:T(8,128)S(1)}, f32[16,11]{1,0:T(8,128)}, u32[]{:S(2)}) copy-start(f32[16,11]{1,0:T(8,128)} %param.9) | copy-start | bytes 2116
  5.8 6.9 %collective-permute-start.4 = (f16[528,128]{1,0:T(8,128)(2,1)S(1)}, f16[528,128]{1,0:T(8,128)(2,1)S(1)}, u32[]{:S(2)}, u32[]{:S(2)}) collective-permute-start(f16[528,128]{1,0:T(8,128)(2,1)S(1)} %convert_element_type.64), channel_id=1, source_target_pairs={{0,6},{2,4},{4,2},{6,0},{8,14},{10,12},{12,10},{14,8},{16,22},{18,... | collective-permute-start | bytes 405512 | tf_op jit(solution)/shard_map/ppermute | solution.py:50
  9.5 6.6 %collective-permute-start.2 = (f16[528,128]{1,0:T(8,128)(2,1)S(1)}, f16[528,128]{1,0:T(8,128)(2,1)S(1)}, u32[]{:S(2)}, u32[]{:S(2)}) collective-permute-start(f16[528,128]{1,0:T(8,128)(2,1)S(1)} %convert_element_type.62), channel_id=1, source_target_pairs={{0,4},{2,6},{4,0},{6,2},{8,12},{10,14},{12,8},{14,10},{16,20},{18,... | collective-permute-start | bytes 405512 | tf_op jit(solution)/shard_map/ppermute | solution.py:50
  9.8 6.4 %collective-permute-start.1 = (f16[528,128]{1,0:T(8,128)(2,1)S(1)}, f16[528,128]{1,0:T(8,128)(2,1)S(1)}, u32[]{:S(2)}, u32[]{:S(2)}) collective-permute-start(f16[528,128]{1,0:T(8,128)(2,1)S(1)} %convert_element_type.60), channel_id=1, source_target_pairs={{0,2},{2,0},{4,6},{6,4},{8,10},{10,8},{12,14},{14,12},{16,18},{18,... | collective-permute-start | bytes 405512 | tf_op jit(solution)/shard_map/ppermute | solution.py:50
  16.5 4.0 %collective-permute-start.5 = (f16[272,128]{1,0:T(8,128)(2,1)S(1)}, f16[272,128]{1,0:T(8,128)(2,1)S(1)}, u32[]{:S(2)}, u32[]{:S(2)}) collective-permute-start(f16[272,128]{1,0:T(8,128)(2,1)S(1)} %convert_element_type.66), channel_id=1, source_target_pairs={{0,8},{2,10},{4,12},{6,14},{8,0},{10,2},{12,4},{14,6},{16,24},{18,... | collective-permute-start | bytes 208904 | tf_op jit(solution)/shard_map/ppermute | solution.py:50
  18.1 5.9 %collective-permute-start.7 = (f16[272,128]{1,0:T(8,128)(2,1)S(1)}, f16[272,128]{1,0:T(8,128)(2,1)S(1)}, u32[]{:S(2)}, u32[]{:S(2)}) collective-permute-start(f16[272,128]{1,0:T(8,128)(2,1)S(1)} %convert_element_type.68), channel_id=1, source_target_pairs={{0,24},{2,26},{4,28},{6,30},{8,16},{10,18},{12,20},{14,22},{16,8},... | collective-permute-start | bytes 208904 | tf_op jit(solution)/shard_map/ppermute | solution.py:50
  20.4 7.5 %collective-permute-start.6 = (f16[272,128]{1,0:T(8,128)(2,1)S(1)}, f16[272,128]{1,0:T(8,128)(2,1)S(1)}, u32[]{:S(2)}, u32[]{:S(2)}) collective-permute-start(f16[272,128]{1,0:T(8,128)(2,1)S(1)} %convert_element_type.68), channel_id=1, source_target_pairs={{0,16},{2,18},{4,20},{6,22},{8,24},{10,26},{12,28},{14,30},{16,0},... | collective-permute-start | bytes 208904 | tf_op jit(solution)/shard_map/ppermute | solution.py:50
  28.0 5.6 %collective-permute-start.10 = (f16[528,128]{1,0:T(8,128)(2,1)S(1)}, f16[528,128]{1,0:T(8,128)(2,1)S(1)}, u32[]{:S(2)}, u32[]{:S(2)}) collective-permute-start(f16[528,128]{1,0:T(8,128)(2,1)S(1)} %convert_element_type.75), channel_id=1, source_target_pairs={{0,6},{2,4},{4,2},{6,0},{8,14},{10,12},{12,10},{14,8},{16,22},{18,... | collective-permute-start | bytes 405512 | tf_op jit(solution)/shard_map/ppermute | solution.py:50
  29.6 7.9 %collective-permute-start.9 = (f16[528,128]{1,0:T(8,128)(2,1)S(1)}, f16[528,128]{1,0:T(8,128)(2,1)S(1)}, u32[]{:S(2)}, u32[]{:S(2)}) collective-permute-start(f16[528,128]{1,0:T(8,128)(2,1)S(1)} %convert_element_type.73), channel_id=1, source_target_pairs={{0,4},{2,6},{4,0},{6,2},{8,12},{10,14},{12,8},{14,10},{16,20},{18,... | collective-permute-start | bytes 405512 | tf_op jit(solution)/shard_map/ppermute | solution.py:50
  30.5 6.9 %collective-permute-start.8 = (f16[528,128]{1,0:T(8,128)(2,1)S(1)}, f16[528,128]{1,0:T(8,128)(2,1)S(1)}, u32[]{:S(2)}, u32[]{:S(2)}) collective-permute-start(f16[528,128]{1,0:T(8,128)(2,1)S(1)} %convert_element_type.71), channel_id=1, source_target_pairs={{0,2},{2,0},{4,6},{6,4},{8,10},{10,8},{12,14},{14,12},{16,18},{18,... | collective-permute-start | bytes 405512 | tf_op jit(solution)/shard_map/ppermute | solution.py:50
  37.7 9.8 %collective-permute-start.11 = (f16[1552,128]{1,0:T(8,128)(2,1)S(1)}, f16[1552,128]{1,0:T(8,128)(2,1)S(1)}, u32[]{:S(2)}, u32[]{:S(2)}) collective-permute-start(f16[1552,128]{1,0:T(8,128)(2,1)S(1)} %convert_element_type.77), channel_id=1, source_target_pairs={{0,1},{1,0},{2,3},{3,2},{4,5},{5,4},{6,7},{7,6},{8,9},{9,8},{10,11... | collective-permute-start | bytes 1191944 | tf_op jit(solution)/shard_map/ppermute | solution.py:50
  38.3 6.1 %collective-permute-start.12 = (f32[2,2,128,128]{3,2,1,0:T(8,128)S(1)}, f32[2,2,128,128]{3,2,1,0:T(8,128)S(1)}, u32[]{:S(2)}, u32[]{:S(2)}) collective-permute-start(f32[2,2,128,128]{3,2,1,0:T(8,128)S(1)} %shard_map.86), channel_id=1, source_target_pairs={{0,1},{1,0},{2,3},{3,2},{4,5},{5,4},{6,7},{7,6},{8,9},{9,8},{10,11... | collective-permute-start | bytes 786440 | tf_op jit(solution)/shard_map/ppermute | solution.py:50

commit v10 on v9

--- a/solution.py
+++ b/solution.py
@@ -483,13 +483,12 @@
                 vg = dot(k, hi, NT) + dot(k, lo, NT)
                 for i, cross in enumerate((qg, kg, vg)):
                     temps[index, i, :, to] = (cross + local_refs[part][at_part, i, :, to]).astype(BF16)
-                wide = pl.ds(pl.multiple_of((first_head(half, cols // DH) + group * width + j) * DH, DH), DH)
-                for i in range(3):
-                    copy = pltpu.make_async_copy(
-                        temps.at[index, i, :, to], outs[i].at[:, wide], sems.at[index * width + j, i]
-                    )
-                    copy.start()
-                    copies.append(copy)
+            start = first_head(half, cols // DH) * DH + group * (width * DH)
+            wide = pl.ds(pl.multiple_of(start, DH), width * DH)
+            for i in range(3):
+                copy = pltpu.make_async_copy(temps.at[index, i], outs[i].at[:, wide], sems.at[index, i])
+                copy.start()
+                copies.append(copy)
         for copy in copies:
             copy.wait()
 
@@ -499,7 +498,7 @@
         args + list(before),
         specs=specs,
         out_specs=[HBM] * 3,
-        scratch=[pltpu.VMEM((len(items), 3, tokens, width * DH), BF16), pltpu.SemaphoreType.DMA((len(items) * width, 3))],
+        scratch=[pltpu.VMEM((len(items), 3, tokens, width * DH), BF16), pltpu.SemaphoreType.DMA((len(items), 3))],
         flops=12 * tokens * DH * width * DH * len(items),
         limit=4,
         aliases={len(args) + i: i for i in range(len(before))},

time: 49.8 us -> 49.8 us (level)
  no operation moved by 1% of the time
where the time goes in v10:
time: 49.8 us; the launch traced here: 49.2 us
  waiting for transfers between devices  21.4 us (43%)
  Pallas kernels  14.6 us (29%)
  starting transfers between devices  11.8 us (24%)
  between operations  0.9 us (2%)
    ppermute x13, waiting for transfers between devices, partner(): lax.ppermute(array, axis, [(i, i ^ distance) for i in range(lax.axis_size...  21.4 us
    pallas_call x14, Pallas kernels, call(): pl.pallas_call(kernel, in_specs=specs or [VMEM] * len(args), out_specs=ou...  14.6 us
    ppermute x13, starting transfers between devices, partner(): lax.ppermute(array, axis, [(i, i ^ distance) for i in range(lax.axis_size...  11.8 us
  transfers between devices with their start and end apart: 13, of which 7 were waited for; matrix products, arithmetic and copies ran while one was open for 0% of the time, Pallas kernels for 21%

profile of v10, /device:TPU:1, one launch (start us, length us, event | category | flops | bytes accessed | tf_op | source)
XLA Modules:
  0.0 49.2 jit_solution(13193615569894954369)
XLA Ops:
  0.6 2.2 %shard_map.76 = (f32[1,2,2,128,128]{4,3,2,1,0:T(8,128)S(1)}, f32[3,2,2,128,128]{4,3,2,1,0:T(8,128)S(1)}, bf16[256,1024]{1,0:T(8,128)(2,1)S(1)}, bf16[256,1024]{1...) custom-call(bf16[256,2048]{1,0:T(8,128)(2,1)} %refs_0_.1, ...), custom_call_target="tpu_custom_call" | custom-call | flops 134217728 | bytes 4194304 | tf_op jit(solution)/shard_map/pallas_call | solution.py:37
  2.9 0.1 collective-permute-start
  2.9 0.5 %collective-permute-start.3 = (f32[1,2,2,128,128]{4,3,2,1,0:T(8,128)S(1)}, f32[1,2,2,128,128]{4,3,2,1,0:T(8,128)S(1)}, u32[]{:S(2)}, u32[]{:S(2)}) collective-permute-start(f32[1,2,2,128,128]{4,3,2,1,0:T(8,128)S(1)} %get-tuple-element.42), channel_id=1, source_target_pairs={{0,1},{1,0},{2,3},{3,2},{4,5},{5,4},{6,7},{7,6},{8,9},{9,8},{10,11... | collective-permute-start | bytes 786440 | tf_op jit(solution)/shard_map/ppermute | solution.py:50
  3.4 0.6 %shard_map.77 = (f32[4,2,2,128,128]{4,3,2,1,0:T(8,128)S(1)}, f32[16,128]{1,0:T(8,128)S(1)}) custom-call(bf16[256,1024]{1,0:T(8,128)(2,1)S(1)} %get-tuple-element.32.refs_0_, bf16[256,1024]{1,0:T(8,128)(2,1)S(1)} %get-tuple-element.33.refs_1_.refs_4_.refs_6_, bf16[256,1024]{1,0:T(8,128)(2,1)S(1)} %get-tuple-element.34.refs_2_.refs_5_.refs_7_, ...), custom_call_target="tpu_custom_call" | custom-call | flops 134217728 | bytes 2097152 | tf_op jit(solution)/shard_map/pallas_call | solution.py:37
  4.1 0.0 copy-start
  4.1 1.5 %collective-permute-done.3.other_ref.refs_1_ = f32[1,2,2,128,128]{4,3,2,1,0:T(8,128)S(1)} collective-permute-done((f32[1,2,2,128,128]{4,3,2,1,0:T(8,128)S(1)}, f32[1,2,2,128,128]{4,3,2,1,0:T(8,128)S(1)}, u32[]{:S(2)}, u32[]{:S(2)}) %collective-permute-start.3) | collective-permute-done | bytes 262176 | tf_op jit(solution)/shard_map/ppermute | solution.py:50
  5.6 0.2 shard_map.79
  5.8 3.4 %collective-permute-start.4 = (f16[528,128]{1,0:T(8,128)(2,1)S(1)}, f16[528,128]{1,0:T(8,128)(2,1)S(1)}, u32[]{:S(2)}, u32[]{:S(2)}) collective-permute-start(f16[528,128]{1,0:T(8,128)(2,1)S(1)} %convert_element_type.64), channel_id=1, source_target_pairs={{0,6},{2,4},{4,2},{6,0},{8,14},{10,12},{12,10},{14,8},{16,22},{18,... | collective-permute-start | bytes 405512 | tf_op jit(solution)/shard_map/ppermute | solution.py:50
  9.2 0.0 collective-permute-done.other_ref.refs_0_
  9.2 0.2 shard_map.78
  9.5 0.3 collective-permute-start.2
  9.8 0.1 collective-permute-start.1
  9.9 0.0 copy-done
  9.9 2.9 %collective-permute-done.4 = f16[528,128]{1,0:T(8,128)(2,1)S(1)} collective-permute-done((f16[528,128]{1,0:T(8,128)(2,1)S(1)}, f16[528,128]{1,0:T(8,128)(2,1)S(1)}, u32[]{:S(2)}, u32[]{:S(2)}) %collective-permute-start.4) | collective-permute-done | bytes 135200 | tf_op jit(solution)/shard_map/ppermute | solution.py:50
  12.8 3.3 %collective-permute-done.2 = f16[528,128]{1,0:T(8,128)(2,1)S(1)} collective-permute-done((f16[528,128]{1,0:T(8,128)(2,1)S(1)}, f16[528,128]{1,0:T(8,128)(2,1)S(1)}, u32[]{:S(2)}, u32[]{:S(2)}) %collective-permute-start.2) | collective-permute-done | bytes 135200 | tf_op jit(solution)/shard_map/ppermute | solution.py:50
  16.1 0.0 collective-permute-done.1
  16.2 0.1 broadcast_in_dim.2.scale_ref.refs_3_.refs_5_.refs_1_
  16.3 0.2 shard_map.80
  16.5 1.6 %collective-permute-start.5 = (f16[272,128]{1,0:T(8,128)(2,1)S(1)}, f16[272,128]{1,0:T(8,128)(2,1)S(1)}, u32[]{:S(2)}, u32[]{:S(2)}) collective-permute-start(f16[272,128]{1,0:T(8,128)(2,1)S(1)} %convert_element_type.66), channel_id=1, source_target_pairs={{0,8},{2,10},{4,12},{6,14},{8,0},{10,2},{12,4},{14,6},{16,24},{18,... | collective-permute-start | bytes 208904 | tf_op jit(solution)/shard_map/ppermute | solution.py:50
  18.1 2.3 %collective-permute-start.7 = (f16[272,128]{1,0:T(8,128)(2,1)S(1)}, f16[272,128]{1,0:T(8,128)(2,1)S(1)}, u32[]{:S(2)}, u32[]{:S(2)}) collective-permute-start(f16[272,128]{1,0:T(8,128)(2,1)S(1)} %convert_element_type.68), channel_id=1, source_target_pairs={{0,24},{2,26},{4,28},{6,30},{8,16},{10,18},{12,20},{14,22},{16,8},... | collective-permute-start | bytes 208904 | tf_op jit(solution)/shard_map/ppermute | solution.py:50
  20.4 0.2 collective-permute-start.6
  20.5 0.0 collective-permute-done.5
  20.6 3.5 %collective-permute-done.7 = f16[272,128]{1,0:T(8,128)(2,1)S(1)} collective-permute-done((f16[272,128]{1,0:T(8,128)(2,1)S(1)}, f16[272,128]{1,0:T(8,128)(2,1)S(1)}, u32[]{:S(2)}, u32[]{:S(2)}) %collective-permute-start.7) | collective-permute-done | bytes 69664 | tf_op jit(solution)/shard_map/ppermute | solution.py:50
  24.1 3.8 %collective-permute-done.6 = f16[272,128]{1,0:T(8,128)(2,1)S(1)} collective-permute-done((f16[272,128]{1,0:T(8,128)(2,1)S(1)}, f16[272,128]{1,0:T(8,128)(2,1)S(1)}, u32[]{:S(2)}, u32[]{:S(2)}) %collective-permute-start.6) | collective-permute-done | bytes 69664 | tf_op jit(solution)/shard_map/ppermute | solution.py:50
  27.8 0.2 shard_map.81
  28.0 1.5 %collective-permute-start.10 = (f16[528,128]{1,0:T(8,128)(2,1)S(1)}, f16[528,128]{1,0:T(8,128)(2,1)S(1)}, u32[]{:S(2)}, u32[]{:S(2)}) collective-permute-start(f16[528,128]{1,0:T(8,128)(2,1)S(1)} %convert_element_type.75), channel_id=1, source_target_pairs={{0,6},{2,4},{4,2},{6,0},{8,14},{10,12},{12,10},{14,8},{16,22},{18,... | collective-permute-start | bytes 405512 | tf_op jit(solution)/shard_map/ppermute | solution.py:50
  29.6 1.0 %collective-permute-start.9 = (f16[528,128]{1,0:T(8,128)(2,1)S(1)}, f16[528,128]{1,0:T(8,128)(2,1)S(1)}, u32[]{:S(2)}, u32[]{:S(2)}) collective-permute-start(f16[528,128]{1,0:T(8,128)(2,1)S(1)} %convert_element_type.73), channel_id=1, source_target_pairs={{0,4},{2,6},{4,0},{6,2},{8,12},{10,14},{12,8},{14,10},{16,20},{18,... | collective-permute-start | bytes 405512 | tf_op jit(solution)/shard_map/ppermute | solution.py:50
  30.5 0.3 collective-permute-start.8
  30.9 2.8 %collective-permute-done.10 = f16[528,128]{1,0:T(8,128)(2,1)S(1)} collective-permute-done((f16[528,128]{1,0:T(8,128)(2,1)S(1)}, f16[528,128]{1,0:T(8,128)(2,1)S(1)}, u32[]{:S(2)}, u32[]{:S(2)}) %collective-permute-start.10) | collective-permute-done | bytes 135200 | tf_op jit(solution)/shard_map/ppermute | solution.py:50
  33.7 3.7 %collective-permute-done.9 = f16[528,128]{1,0:T(8,128)(2,1)S(1)} collective-permute-done((f16[528,128]{1,0:T(8,128)(2,1)S(1)}, f16[528,128]{1,0:T(8,128)(2,1)S(1)}, u32[]{:S(2)}, u32[]{:S(2)}) %collective-permute-start.9) | collective-permute-done | bytes 135200 | tf_op jit(solution)/shard_map/ppermute | solution.py:50
  37.4 0.0 collective-permute-done.8
  37.5 0.1 shard_map.82
  37.6 0.1 convert_element_type.77
  37.7 0.6 %collective-permute-start.11 = (f16[1552,128]{1,0:T(8,128)(2,1)S(1)}, f16[1552,128]{1,0:T(8,128)(2,1)S(1)}, u32[]{:S(2)}, u32[]{:S(2)}) collective-permute-start(f16[1552,128]{1,0:T(8,128)(2,1)S(1)} %convert_element_type.77), channel_id=1, source_target_pairs={{0,1},{1,0},{2,3},{3,2},{4,5},{5,4},{6,7},{7,6},{8,9},{9,8},{10,11... | collective-permute-start | bytes 1191944 | tf_op jit(solution)/shard_map/ppermute | solution.py:50
  38.3 0.1 collective-permute-start.12
  38.4 1.5 %shard_map.85.refs_12_.refs_11_.refs_7_ = f32[2,3,256,256]{3,2,1,0:T(8,128)S(1)} custom-call(f32[16,16,128]{2,1,0:T(8,128)S(1)} %broadcast_in_dim.2.scale_ref.refs_3_.refs_5_.refs_1_, bf16[256,1024]{1,0:T(8,128)(2,1)S(1)} %get-tuple-element.32.refs_0_, bf16[256,1024]{1,0:T(8,128)(2,1)S(1)} %get-tuple-element.33.refs_1_.refs_4_.refs_6_, ...), custom_call_target="tpu_custom_call" | custom-call | flops 402653184 | bytes 4325376 | tf_op jit(solution)/shard_map/pallas_call | solution.py:37
  39.9 2.2 %shard_map.84.refs_11_.refs_10_.refs_6_ = f32[3,3,256,256]{3,2,1,0:T(8,128)S(1)} custom-call(f32[16,16,128]{2,1,0:T(8,128)S(1)} %broadcast_in_dim.2.scale_ref.refs_3_.refs_5_.refs_1_, bf16[256,1024]{1,0:T(8,128)(2,1)S(1)} %get-tuple-element.32.refs_0_, bf16[256,1024]{1,0:T(8,128)(2,1)S(1)} %get-tuple-element.33.refs_1_.refs_4_.refs_6_, ...), custom_call_target="tpu_custom_call" | custom-call | flops 603979776 | bytes 4325376 | tf_op jit(solution)/shard_map/pallas_call | solution.py:37
  42.2 2.2 %shard_map.83.refs_10_.refs_9_.refs_5_ = f32[3,3,256,256]{3,2,1,0:T(8,128)S(1)} custom-call(f32[16,16,128]{2,1,0:T(8,128)S(1)} %broadcast_in_dim.2.scale_ref.refs_3_.refs_5_.refs_1_, bf16[256,1024]{1,0:T(8,128)(2,1)S(1)} %get-tuple-element.32.refs_0_, bf16[256,1024]{1,0:T(8,128)(2,1)S(1)} %get-tuple-element.33.refs_1_.refs_4_.refs_6_, ...), custom_call_target="tpu_custom_call" | custom-call | flops 603979776 | bytes 4325376 | tf_op jit(solution)/shard_map/pallas_call | solution.py:37
  44.4 0.0 collective-permute-done.12.refs_2_
  44.4 1.4 %shard_map.87 = (bf16[256,2048]{1,0:T(8,128)(2,1)}, bf16[256,2048]{1,0:T(8,128)(2,1)}, bf16[256,2048]{1,0:T(8,128)(2,1)}) custom-call(f32[3,2,2,128,128]{4,3,2,1,0:T(8,128)S(1)} %collective-permute-done.other_ref.refs_0_, f32[528,128]{1,0:T(8,128)S(1)} %get-tuple-element.54.keep_ref.refs_1_, f32[2,2,128,128]{3,2,1,0:T(8,128)S(1)} %collective-permute-done.12.refs_2_, ...), custom_call_target="tpu_custom_call" | custom-call | flops 201326592 | bytes 10887168 | tf_op jit(solution)/shard_map/pallas_call | solution.py:37
  45.8 1.7 %shard_map.88 = (bf16[256,2048]{1,0:T(8,128)(2,1)}, bf16[256,2048]{1,0:T(8,128)(2,1)}, bf16[256,2048]{1,0:T(8,128)(2,1)}) custom-call(f32[3,2,2,128,128]{4,3,2,1,0:T(8,128)S(1)} %collective-permute-done.other_ref.refs_0_, ...), custom_call_target="tpu_custom_call", output_to_operand_aliasing={{0}: (12, {}), {1}: (13, {}), {2}: (14, {})} | custom-call | flops 301989888 | bytes 13000704 | tf_op jit(solution)/shard_map/pallas_call | solution.py:37
  47.5 0.0 collective-permute-done.11
  47.5 0.1 convert_element_type.78.refs_0_
  47.6 1.6 %shard_map.89 = (bf16[256,2048]{1,0:T(8,128)(2,1)}, bf16[256,2048]{1,0:T(8,128)(2,1)}, bf16[256,2048]{1,0:T(8,128)(2,1)}) custom-call(f32[1552,128]{1,0:T(8,128)S(1)} %convert_element_type.78.refs_0_, f32[16,16,128]{2,1,0:T(8,128)S(1)} %broadcast_in_dim.2.scale_ref.refs_3_.refs_5_.refs_1_, ...), custom_call_target="tpu_custom_call", output_to_operand_aliasing={{0}: (8, {}), {1}: (9, {}), {2}: (10, {})} | custom-call | flops 301989888 | bytes 11935744 | tf_op jit(solution)/shard_map/pallas_call | solution.py:37
  (21 shorter events, 0.4 us)
Async XLA Ops:
  2.9 6.3 %collective-permute-start = (f32[3,2,2,128,128]{4,3,2,1,0:T(8,128)S(1)}, f32[3,2,2,128,128]{4,3,2,1,0:T(8,128)S(1)}, u32[]{:S(2)}, u32[]{:S(2)}) collective-permute-start(f32[3,2,2,128,128]{4,3,2,1,0:T(8,128)S(1)} %get-tuple-element.38), channel_id=1, source_target_pairs={{0,1},{1,0},{2,3},{3,2},{4,5},{5,4},{6,7},{7,6},{8,9},{9,8},{10,11... | collective-permute-start | bytes 2359304 | tf_op jit(solution)/shard_map/ppermute | solution.py:50
  2.9 2.6 %collective-permute-start.3 = (f32[1,2,2,128,128]{4,3,2,1,0:T(8,128)S(1)}, f32[1,2,2,128,128]{4,3,2,1,0:T(8,128)S(1)}, u32[]{:S(2)}, u32[]{:S(2)}) collective-permute-start(f32[1,2,2,128,128]{4,3,2,1,0:T(8,128)S(1)} %get-tuple-element.42), channel_id=1, source_target_pairs={{0,1},{1,0},{2,3},{3,2},{4,5},{5,4},{6,7},{7,6},{8,9},{9,8},{10,11... | collective-permute-start | bytes 786440 | tf_op jit(solution)/shard_map/ppermute | solution.py:50
  4.1 5.8 %copy-start = (f32[16,11]{1,0:T(8,128)S(1)}, f32[16,11]{1,0:T(8,128)}, u32[]{:S(2)}) copy-start(f32[16,11]{1,0:T(8,128)} %param.9) | copy-start | bytes 2116
  5.8 6.9 %collective-permute-start.4 = (f16[528,128]{1,0:T(8,128)(2,1)S(1)}, f16[528,128]{1,0:T(8,128)(2,1)S(1)}, u32[]{:S(2)}, u32[]{:S(2)}) collective-permute-start(f16[528,128]{1,0:T(8,128)(2,1)S(1)} %convert_element_type.64), channel_id=1, source_target_pairs={{0,6},{2,4},{4,2},{6,0},{8,14},{10,12},{12,10},{14,8},{16,22},{18,... | collective-permute-start | bytes 405512 | tf_op jit(solution)/shard_map/ppermute | solution.py:50
  9.5 6.6 %collective-permute-start.2 = (f16[528,128]{1,0:T(8,128)(2,1)S(1)}, f16[528,128]{1,0:T(8,128)(2,1)S(1)}, u32[]{:S(2)}, u32[]{:S(2)}) collective-permute-start(f16[528,128]{1,0:T(8,128)(2,1)S(1)} %convert_element_type.62), channel_id=1, source_target_pairs={{0,4},{2,6},{4,0},{6,2},{8,12},{10,14},{12,8},{14,10},{16,20},{18,... | collective-permute-start | bytes 405512 | tf_op jit(solution)/shard_map/ppermute | solution.py:50
  9.8 6.4 %collective-permute-start.1 = (f16[528,128]{1,0:T(8,128)(2,1)S(1)}, f16[528,128]{1,0:T(8,128)(2,1)S(1)}, u32[]{:S(2)}, u32[]{:S(2)}) collective-permute-start(f16[528,128]{1,0:T(8,128)(2,1)S(1)} %convert_element_type.60), channel_id=1, source_target_pairs={{0,2},{2,0},{4,6},{6,4},{8,10},{10,8},{12,14},{14,12},{16,18},{18,... | collective-permute-start | bytes 405512 | tf_op jit(solution)/shard_map/ppermute | solution.py:50
  16.5 4.0 %collective-permute-start.5 = (f16[272,128]{1,0:T(8,128)(2,1)S(1)}, f16[272,128]{1,0:T(8,128)(2,1)S(1)}, u32[]{:S(2)}, u32[]{:S(2)}) collective-permute-start(f16[272,128]{1,0:T(8,128)(2,1)S(1)} %convert_element_type.66), channel_id=1, source_target_pairs={{0,8},{2,10},{4,12},{6,14},{8,0},{10,2},{12,4},{14,6},{16,24},{18,... | collective-permute-start | bytes 208904 | tf_op jit(solution)/shard_map/ppermute | solution.py:50
  18.1 5.9 %collective-permute-start.7 = (f16[272,128]{1,0:T(8,128)(2,1)S(1)}, f16[272,128]{1,0:T(8,128)(2,1)S(1)}, u32[]{:S(2)}, u32[]{:S(2)}) collective-permute-start(f16[272,128]{1,0:T(8,128)(2,1)S(1)} %convert_element_type.68), channel_id=1, source_target_pairs={{0,24},{2,26},{4,28},{6,30},{8,16},{10,18},{12,20},{14,22},{16,8},... | collective-permute-start | bytes 208904 | tf_op jit(solution)/shard_map/ppermute | solution.py:50
  20.4 7.5 %collective-permute-start.6 = (f16[272,128]{1,0:T(8,128)(2,1)S(1)}, f16[272,128]{1,0:T(8,128)(2,1)S(1)}, u32[]{:S(2)}, u32[]{:S(2)}) collective-permute-start(f16[272,128]{1,0:T(8,128)(2,1)S(1)} %convert_element_type.68), channel_id=1, source_target_pairs={{0,16},{2,18},{4,20},{6,22},{8,24},{10,26},{12,28},{14,30},{16,0},... | collective-permute-start | bytes 208904 | tf_op jit(solution)/shard_map/ppermute | solution.py:50
  28.0 5.6 %collective-permute-start.10 = (f16[528,128]{1,0:T(8,128)(2,1)S(1)}, f16[528,128]{1,0:T(8,128)(2,1)S(1)}, u32[]{:S(2)}, u32[]{:S(2)}) collective-permute-start(f16[528,128]{1,0:T(8,128)(2,1)S(1)} %convert_element_type.75), channel_id=1, source_target_pairs={{0,6},{2,4},{4,2},{6,0},{8,14},{10,12},{12,10},{14,8},{16,22},{18,... | collective-permute-start | bytes 405512 | tf_op jit(solution)/shard_map/ppermute | solution.py:50
  29.6 7.9 %collective-permute-start.9 = (f16[528,128]{1,0:T(8,128)(2,1)S(1)}, f16[528,128]{1,0:T(8,128)(2,1)S(1)}, u32[]{:S(2)}, u32[]{:S(2)}) collective-permute-start(f16[528,128]{1,0:T(8,128)(2,1)S(1)} %convert_element_type.73), channel_id=1, source_target_pairs={{0,4},{2,6},{4,0},{6,2},{8,12},{10,14},{12,8},{14,10},{16,20},{18,... | collective-permute-start | bytes 405512 | tf_op jit(solution)/shard_map/ppermute | solution.py:50
  30.5 6.9 %collective-permute-start.8 = (f16[528,128]{1,0:T(8,128)(2,1)S(1)}, f16[528,128]{1,0:T(8,128)(2,1)S(1)}, u32[]{:S(2)}, u32[]{:S(2)}) collective-permute-start(f16[528,128]{1,0:T(8,128)(2,1)S(1)} %convert_element_type.71), channel_id=1, source_target_pairs={{0,2},{2,0},{4,6},{6,4},{8,10},{10,8},{12,14},{14,12},{16,18},{18,... | collective-permute-start | bytes 405512 | tf_op jit(solution)/shard_map/ppermute | solution.py:50
  37.7 9.8 %collective-permute-start.11 = (f16[1552,128]{1,0:T(8,128)(2,1)S(1)}, f16[1552,128]{1,0:T(8,128)(2,1)S(1)}, u32[]{:S(2)}, u32[]{:S(2)}) collective-permute-start(f16[1552,128]{1,0:T(8,128)(2,1)S(1)} %convert_element_type.77), channel_id=1, source_target_pairs={{0,1},{1,0},{2,3},{3,2},{4,5},{5,4},{6,7},{7,6},{8,9},{9,8},{10,11... | collective-permute-start | bytes 1191944 | tf_op jit(solution)/shard_map/ppermute | solution.py:50
  38.3 6.1 %collective-permute-start.12 = (f32[2,2,128,128]{3,2,1,0:T(8,128)S(1)}, f32[2,2,128,128]{3,2,1,0:T(8,128)S(1)}, u32[]{:S(2)}, u32[]{:S(2)}) collective-permute-start(f32[2,2,128,128]{3,2,1,0:T(8,128)S(1)} %shard_map.86), channel_id=1, source_target_pairs={{0,1},{1,0},{2,3},{3,2},{4,5},{5,4},{6,7},{7,6},{8,9},{9,8},{10,11... | collective-permute-start | bytes 786440 | tf_op jit(solution)/shard_map/ppermute | solution.py:50
